TPU v7x, 32 devices: a whole 2x2x4 slice. The times are simulated.
32 devices in a mesh: dp: 8 (over y, x, core), seq: 4 (over z).
Axes of the slice: x: 2, y: 2, z: 4, core: 2. Of those that a mesh axis runs over, the one named last changes fastest.
Arguments:
- query: bfloat16 [8, 512, 2048], P('dp', 'seq'), may hold values from -8 to 8
- key_value: bfloat16 [2, 8, 512, 2048], P(None, 'dp', 'seq'), may hold values from -8 to 8
- grad_y: bfloat16 [8, 512, 2048], P('dp', 'seq'), may hold values from -6 to 6
- tags: int32 [8, 512], P('dp', 'seq'), may hold values 0 or 1
- segments: int32 [8, 512], P('dp'), may hold values from 0 to 3, never falling along the last dimension, each value on 1 to 256 neighbouring positions
- out_weight: bfloat16 [2, 2048, 2048], P(None, None, 'dp'), may hold values from -0.125 to 0.125
Outputs:
- grad_query: bfloat16 [8, 512, 2048], P('dp', 'seq')
- grad_key_value: bfloat16 [2, 8, 512, 2048], P(None, 'dp', 'seq')
Inputs may be any that keep to these rules, and one draw needn't show every extreme that they name: `segments`: sample numbers never fall along a sequence; a sample holds at most 256 positions and some sample holds exactly 256.
All inputs are finite; a program needn't handle non-finite values. No bound on the sum of `tags` on one device may be relied on, other than what follows from the above.
Results may differ from a plain program's by a relative error of at most 0.0075.
Values may be sent and summed in bfloat16 or wider, within the bound.
No kernel may reach another device: no remote copies, remote signals or barrier semaphores. Data moves between devices by JAX's collectives and lax.ppermute only.
A program may use at most 128 MiB of HBM per device.

v0:
```python
import functools
import jax
import jax.numpy as jnp
from jax import lax
from jax.experimental import pallas as pl
from jax.experimental.pallas import tpu as pltpu
from jax.sharding import PartitionSpec as P


HEAD_DIM = 128
CHUNKS = 2

NEG = -1e30
LANES = 128
BF16 = jnp.bfloat16
F32 = jnp.float32
NT = (((1,), (1,)), ((), ()))
TN = (((0,), (0,)), ((), ()))


def params(mib):
    return pltpu.CompilerParams(vmem_limit_bytes=mib << 20)


def lane_slice(start, size):
    return pl.ds(pl.multiple_of(start, LANES), size)


def swap(value, axis, bits):
    return lax.ppermute(value, axis, [(i, i ^ bits) for i in range(lax.axis_size(axis))])


def column_of(row):
    n = row.shape[1]
    same = lax.broadcasted_iota(jnp.int32, (n, n), 0) == lax.broadcasted_iota(jnp.int32, (n, n), 1)
    return jnp.sum(jnp.where(same, row.astype(F32), 0.0), axis=1, keepdims=True)


def grad_slices_kernel(grad_ref, tags_ref, *outs):
    chip = lax.axis_index("dp") // 2
    width = outs[0].shape[1] - LANES
    tag = jnp.broadcast_to(column_of(tags_ref[...]), (grad_ref.shape[1], LANES)).astype(BF16)
    for k, out in enumerate(outs):
        out[:, :width] = grad_ref[0, :, lane_slice((chip ^ k) * width, width)]
        out[:, width:] = tag


def project_kernel(chips, *refs):
    grads, (own_w, other_w), (mine, *parts, lhs) = refs[:chips], refs[chips : chips + 2], refs[chips + 2 :]
    rows = grads[0].shape[0]
    depth = own_w.shape[2]
    core = lax.axis_index("dp") % 2

    @pl.when(pl.program_id(0) == 0)
    def _():
        for k, grad in enumerate(grads):
            text = grad[:, 2 * depth : 2 * depth + 1] == 1
            for side in range(2):
                g = grad[:, lane_slice((core ^ side) * depth, depth)]
                lhs[side, 0, k * rows : (k + 1) * rows] = jnp.where(text, jnp.zeros_like(g), g)
                lhs[side, 1, k * rows : (k + 1) * rows] = jnp.where(text, g, jnp.zeros_like(g))

    total = None
    for side, w in enumerate((own_w, other_w)):
        for kind in range(2):
            term = lax.dot_general(lhs[side, kind], w[kind], NT, preferred_element_type=F32)
            total = term if total is None else total + term
    mine[...] = total[:rows]
    for k, part in enumerate(parts):
        part[...] = total[(k + 1) * rows : (k + 2) * rows].astype(BF16)


def neighbour_slices_kernel(q_ref, kv_ref, *outs):
    even = lax.axis_index("seq") % 2 == 0

    def up(out):
        out[...] = kv_ref[:, 0]

    def down(out):
        out[0] = q_ref[0]
        out[1] = q_ref[0]

    send(even, outs, down, up)


def send(even, outs, down, up):
    @pl.when(even)
    def _():
        up(outs[0])
        down(outs[1])

    @pl.when(jnp.logical_not(even))
    def _():
        down(outs[0])
        up(outs[1])


def collect_kernel(terms, mine, *refs):
    parts, out = refs[:terms], refs[terms]
    total = mine[...]
    for part in parts:
        total = total + part[...].astype(F32)
    out[...] = total.astype(BF16)


def masks(count, segs, index, rows):
    def segment(back):
        at = jnp.clip(index + back, 0, count - 1)
        return segs[:, lane_slice(at * rows, rows)].astype(F32)

    left, own, right = segment(-1), segment(0), segment(1)
    left_at, own_at = column_of(left), column_of(own)
    first, last = index == 0, index == count - 1
    key = lax.broadcasted_iota(jnp.int32, (rows, rows), 0)
    query = lax.broadcasted_iota(jnp.int32, (rows, rows), 1)
    return (
        (left_at == own) & jnp.logical_not(first),
        (left_at == right) & jnp.logical_not(first | last),
        (own_at == own) & (key <= query),
    )


def gather_sides(even, first, second, left_kv, right_q, lanes):
    def fill(from_left, from_right):
        left_kv[...] = from_left[:, :, lanes]
        right_q[...] = from_right[0, :, lanes]

    @pl.when(even)
    def _():
        fill(second, first)

    @pl.when(jnp.logical_not(even))
    def _():
        fill(first, second)


def block_terms(h, lanes, scale, kv_ref, left_kv, both_q, both_g, mask):
    at = slice(h * HEAD_DIM, (h + 1) * HEAD_DIM)
    wide = slice(lanes.start + at.start, lanes.start + at.stop)
    kl, vl = left_kv[0, :, at], left_kv[1, :, at]
    k, v = kv_ref[0, 0, :, wide], kv_ref[1, 0, :, wide]
    q2, g2 = both_q[:, at], both_g[:, at]
    rows = k.shape[0]
    s_left = lax.dot_general(kl, q2, NT, preferred_element_type=F32) * scale
    s_own = lax.dot_general(k, q2[:rows], NT, preferred_element_type=F32) * scale
    d_left = lax.dot_general(vl, g2, NT, preferred_element_type=F32)
    d_own = lax.dot_general(v, g2[:rows], NT, preferred_element_type=F32)
    s_pre = jnp.where(mask[0], s_left[:, :rows], NEG)
    s_far = jnp.where(mask[1], s_left[:, rows:], NEG)
    s_own = jnp.where(mask[2], s_own, NEG)
    return (kl, k, q2, g2), (s_pre, s_far, s_own), (d_left[:, :rows], d_left[:, rows:], d_own)


def fill_both(even, lanes, q_ref, g_ref, side1, side2, right_g, left_kv, both_q, both_g):
    rows = q_ref.shape[1]
    gather_sides(even, side1, side2, left_kv, both_q.at[rows:], lanes)
    both_g[rows:] = right_g[...]
    both_q[:rows] = q_ref[0, :, lanes]
    both_g[:rows] = g_ref[...]


def stats_kernel(count, chunk, scale, q_ref, kv_ref, g_ref, side1, side2, right_g, segs,
                 own_out, far_out, left_kv, both_q, both_g):
    index = lax.axis_index("seq")
    even = index % 2 == 0
    rows, span = g_ref.shape
    lanes = slice(chunk * span, (chunk + 1) * span)
    fill_both(even, lanes, q_ref, g_ref, side1, side2, right_g, left_kv, both_q, both_g)
    mask = masks(count, segs, index, rows)
    for h in range(span // HEAD_DIM):
        _, (s_pre, s_far, s_own), (d_pre, d_far, d_own) = block_terms(
            h, lanes, scale, kv_ref, left_kv, both_q, both_g, mask)
        top = jnp.maximum(jnp.max(s_pre, axis=0, keepdims=True), jnp.max(s_own, axis=0, keepdims=True))
        e_pre, e_own = jnp.exp(s_pre - top), jnp.exp(s_own - top)
        own_out[0, h : h + 1] = top
        own_out[1, h : h + 1] = jnp.sum(e_pre + e_own, axis=0, keepdims=True)
        own_out[2, h : h + 1] = jnp.sum(e_pre * d_pre + e_own * d_own, axis=0, keepdims=True)
        top = jnp.max(s_far, axis=0, keepdims=True)
        e_far = jnp.exp(s_far - top)
        far_out[0, h : h + 1] = top
        far_out[1, h : h + 1] = jnp.sum(e_far, axis=0, keepdims=True)
        far_out[2, h : h + 1] = jnp.sum(e_far * d_far, axis=0, keepdims=True)


def merged(one, two):
    top = jnp.maximum(one[0], two[0])
    first, second = jnp.exp(one[0] - top), jnp.exp(two[0] - top)
    total = 1.0 / (one[1] * first + two[1] * second)
    return top, total, (one[2] * first + two[2] * second) * total


def grads_kernel(count, chunk, scale, q_ref, kv_ref, g_ref, side1, side2, right_g, segs,
                 own_stats, far_stats, from_left, from_right, dq_out, dkv_out, to1, to2,
                 left_kv, both_q, both_g):
    index = lax.axis_index("seq")
    even = index % 2 == 0
    rows, span = g_ref.shape
    lanes = slice(chunk * span, (chunk + 1) * span)
    fill_both(even, lanes, q_ref, g_ref, side1, side2, right_g, left_kv, both_q, both_g)
    mask = masks(count, segs, index, rows)
    first, last = index == 0, index == count - 1
    own_l = (jnp.where(first, NEG, from_left[0]), jnp.where(first, 0.0, from_left[1]), jnp.where(first, 0.0, from_left[2]))
    top, inv, delta = merged(own_stats, own_l)
    right = (jnp.where(last, 0.0, from_right[0]), jnp.where(last, 1.0, from_right[1]), jnp.where(last, 0.0, from_right[2]))
    far_top, far_inv, far_delta = merged(right, far_stats)

    def near(up_out, down_out):
        for h in range(span // HEAD_DIM):
            (kl, k, q2, g2), (s_pre, s_far, s_own), (d_pre, d_far, d_own) = block_terms(
                h, lanes, scale, kv_ref, left_kv, both_q, both_g, mask)
            row = slice(h, h + 1)
            at = slice(h * HEAD_DIM, (h + 1) * HEAD_DIM)
            p_pre = jnp.exp(s_pre - top[row]) * inv[row]
            p_own = jnp.exp(s_own - top[row]) * inv[row]
            p_far = jnp.exp(s_far - far_top[row]) * far_inv[row]
            ds_pre = (p_pre * (d_pre - delta[row]) * scale).astype(BF16)
            ds_own = (p_own * (d_own - delta[row]) * scale).astype(BF16)
            ds_far = (p_far * (d_far - far_delta[row]) * scale).astype(BF16)
            ds_left = jnp.concatenate([ds_pre, ds_far], axis=1)
            p_left = jnp.concatenate([p_pre.astype(BF16), p_far.astype(BF16)], axis=1)
            dkv_out[0, :, at] = jnp.dot(ds_own, q2[:rows], preferred_element_type=F32)
            dkv_out[1, :, at] = jnp.dot(p_own.astype(BF16), g2[:rows], preferred_element_type=F32)
            down_out[0, :, at] = jnp.dot(ds_left, q2, preferred_element_type=F32).astype(BF16)
            down_out[1, :, at] = jnp.dot(p_left, g2, preferred_element_type=F32).astype(BF16)
            dq_out[:, at] = lax.dot_general(ds_pre, kl, TN, preferred_element_type=F32) + lax.dot_general(
                ds_own, k, TN, preferred_element_type=F32)
            up_out[0, :, at] = lax.dot_general(ds_far, kl, TN, preferred_element_type=F32).astype(BF16)

    @pl.when(even)
    def _():
        near(to1, to2)

    @pl.when(jnp.logical_not(even))
    def _():
        near(to2, to1)


def finish_kernel(count, dq_ref, dkv_ref, got1, got2, *refs):
    grad_q, grad_kv = refs[-2:]
    index = lax.axis_index("seq")
    even = index % 2 == 0

    def add(from_left, from_right):
        grad_q[0] = (dq_ref[...] + jnp.where(index == 0, 0.0, from_left[0].astype(F32))).astype(BF16)
        for n in range(2):
            more = jnp.where(index == count - 1, 0.0, from_right[n].astype(F32))
            grad_kv[n, 0] = (dkv_ref[n] + more).astype(BF16)

    @pl.when(even)
    def _():
        add(got2, got1)

    @pl.when(jnp.logical_not(even))
    def _():
        add(got1, got2)


def shifted(value, steps):
    count = lax.axis_size("seq")
    return lax.ppermute(value, "seq", [(i, (i + steps) % count) for i in range(count)])


def neighbour_swaps(first, second):
    count = lax.axis_size("seq")
    one = [(i, min(i ^ 1, count - 1)) for i in range(count)]
    two = [(i, ((i + 1) ^ 1) - 1) for i in range(count)]
    two = [(i, j if 0 <= j < count else i) for i, j in two]
    return lax.ppermute(first, "seq", one), lax.ppermute(second, "seq", two)


def shape(dims, dtype=BF16):
    return jax.ShapeDtypeStruct(dims, dtype)


def cost(flops, moved):
    return pl.CostEstimate(flops=int(flops), bytes_accessed=int(moved), transcendentals=0)


def step(query, key_value, grad_y, tags, segments, out_weight):
    _, rows, hc = query.shape
    depth = out_weight.shape[2]
    chips = lax.axis_size("dp") // 2
    count = lax.axis_size("seq")
    span = hc // CHUNKS
    heads = span // HEAD_DIM
    scale = HEAD_DIM ** (-0.5)

    other_weight = swap(out_weight, "dp", 1)
    slices = pl.pallas_call(
        grad_slices_kernel,
        out_shape=[shape((rows, 2 * depth + LANES))] * chips,
        compiler_params=params(4),
        name="grad_slices",
        cost_estimate=cost(0, 4 * grad_y.size),
    )(grad_y, tags)
    grads = [slices[0]] + [swap(slices[k], "dp", 2 * k) for k in range(1, chips)]
    pair = shape((2, rows, hc))
    sides = pl.pallas_call(
        neighbour_slices_kernel,
        out_shape=[pair, pair],
        compiler_params=params(8),
        name="neighbour_slices",
        cost_estimate=cost(0, 16 * query.size),
    )(query, key_value)
    sides = neighbour_swaps(*sides)

    tile = min(512, span)
    steps = span // tile
    gouts, right_gs = [], []
    for c in range(CHUNKS):
        w_spec = pl.BlockSpec((2, tile, depth), lambda t, c=c: (0, c * steps + t, 0))
        mine, *parts = pl.pallas_call(
            functools.partial(project_kernel, chips),
            grid=(steps,),
            in_specs=[pl.BlockSpec((rows, 2 * depth + LANES), lambda t: (0, 0))] * chips + [w_spec] * 2,
            out_specs=[pl.BlockSpec((rows, tile), lambda t: (0, t))] * chips,
            out_shape=[shape((rows, span), F32)] + [shape((rows, span))] * (chips - 1),
            scratch_shapes=[pltpu.VMEM((2, 2, chips * rows, depth), BF16)],
            compiler_params=params(12),
            cost_estimate=cost(8 * chips * rows * depth * span, 8 * span * depth),
        )(*grads, out_weight, other_weight)
        parts = [swap(part, "dp", 2 * k) for k, part in enumerate(parts, 1)]
        gout = pl.pallas_call(
            functools.partial(collect_kernel, chips - 1),
            out_shape=shape((rows, span)),
            compiler_params=params(4),
            cost_estimate=cost(0, 12 * rows * span),
        )(mine, *parts)
        gouts.append(gout)
        right_gs.append(shifted(gout, -1))

    small = shape((3, heads, rows), F32)
    sides_scratch = [
        pltpu.VMEM((2, rows, span), BF16), pltpu.VMEM((2 * rows, span), BF16), pltpu.VMEM((2 * rows, span), BF16)]
    half = shape((2, rows, span))
    parts = []
    for c in range(CHUNKS):
        common = (query, key_value, gouts[c], *sides, right_gs[c], segments)
        own, far = pl.pallas_call(
            functools.partial(stats_kernel, count, c, scale),
            out_shape=[small] * 2,
            scratch_shapes=sides_scratch,
            compiler_params=params(8),
            cost_estimate=cost(4 * 3 * rows * rows * span, 20 * rows * span),
        )(*common)
        from_right, from_left = shifted(own, -1), shifted(far, 1)
        dq, dkv, to1, to2 = pl.pallas_call(
            functools.partial(grads_kernel, count, c, scale),
            out_shape=[shape((rows, span), F32), shape((2, rows, span), F32), half, half],
            scratch_shapes=sides_scratch,
            compiler_params=params(12),
            cost_estimate=cost(10 * 3 * rows * rows * span, 40 * rows * span),
        )(*common, own, far, from_left, from_right)
        parts.append((dq, dkv, *neighbour_swaps(to1, to2)))

    results = ()
    for c in range(CHUNKS):
        block = pl.BlockSpec((rows, span), lambda t: (0, 0))
        blocks = pl.BlockSpec((2, rows, span), lambda t: (0, 0, 0))
        results = pl.pallas_call(
            functools.partial(finish_kernel, count),
            grid=(1,),
            in_specs=[block, blocks, blocks, blocks] + [pl.BlockSpec(memory_space=pl.ANY)] * len(results),
            out_specs=[
                pl.BlockSpec((1, rows, span), lambda t, c=c: (0, 0, c)),
                pl.BlockSpec((2, 1, rows, span), lambda t, c=c: (0, 0, 0, c)),
            ],
            out_shape=[shape(query.shape), shape(key_value.shape)],
            input_output_aliases={4 + n: n for n in range(len(results))},
            compiler_params=params(12),
            cost_estimate=cost(0, 20 * rows * span),
        )(*parts[c], *results)
    return tuple(results)


def solution(mesh):
    return jax.shard_map(
        step,
        mesh=mesh,
        in_specs=(
            P("dp", "seq", None),
            P(None, "dp", "seq", None),
            P("dp", "seq", None),
            P("dp", "seq"),
            P("dp", None),
            P(None, None, "dp"),
        ),
        out_specs=(P("dp", "seq", None), P(None, "dp", "seq", None)),
        check_vma=False,
    )
```

profile of v0, /device:TPU:20, one launch (start us, length us, event | category | flops | bytes accessed | tf_op | source)
XLA Modules:
  0.0 86.7 jit_solution(4479264759629005351)
XLA Ops:
  0.7 1.0 %copy-done.5 = bf16[1,128,2048]{2,1,0:T(8,128)(2,1)S(1)} copy-done((bf16[1,128,2048]{2,1,0:T(8,128)(2,1)S(1)}, bf16[1,128,2048]{2,1,0:T(8,128)(2,1)}, u32[]{:S(2)}) %copy-start.5) | copy-done | bytes 524312
  1.8 0.7 copy-done.7
  2.5 1.6 %collective-permute-start = (bf16[128,640]{1,0:T(8,128)(2,1)S(1)}, bf16[128,640]{1,0:T(8,128)(2,1)S(1)}, u32[]{:S(2)}, u32[]{:S(2)}) collective-permute-start(bf16[128,640]{1,0:T(8,128)(2,1)S(1)} %get-tuple-element.31), channel_id=1, source_target_pairs={{0,8},{4,12},{8,0},{12,4},{16,24},{20,28},{24,16},{28,20},{1,9},{5... | collective-permute-start | bytes 491528 | tf_op jit(solution)/shard_map/ppermute | solution.py:30
  4.1 0.5 collective-permute-start.1
  4.6 1.5 %collective-permute-start.2 = (bf16[128,640]{1,0:T(8,128)(2,1)S(1)}, bf16[128,640]{1,0:T(8,128)(2,1)S(1)}, u32[]{:S(2)}, u32[]{:S(2)}) collective-permute-start(bf16[128,640]{1,0:T(8,128)(2,1)S(1)} %get-tuple-element.33), channel_id=1, source_target_pairs={{0,24},{4,28},{8,16},{12,20},{16,8},{20,12},{24,0},{28,4},{1,25},{... | collective-permute-start | bytes 491528 | tf_op jit(solution)/shard_map/ppermute | solution.py:30
  6.1 1.2 %copy-done = bf16[2,1,128,2048]{3,2,1,0:T(8,128)(2,1)S(1)} copy-done((bf16[2,1,128,2048]{3,2,1,0:T(8,128)(2,1)S(1)}, bf16[2,1,128,2048]{3,2,1,0:T(8,128)(2,1)}, u32[]{:S(2)}) %copy-start) | copy-done | bytes 1048600
  7.3 1.0 %copy-done.2 = bf16[1,128,2048]{2,1,0:T(8,128)(2,1)S(1)} copy-done((bf16[1,128,2048]{2,1,0:T(8,128)(2,1)S(1)}, bf16[1,128,2048]{2,1,0:T(8,128)(2,1)}, u32[]{:S(2)}) %copy-start.2) | copy-done | bytes 524312
  8.3 0.1 neighbour_slices.1
  8.5 1.6 %collective-permute-start.7 = (bf16[2,128,2048]{2,1,0:T(8,128)(2,1)S(1)}, bf16[2,128,2048]{2,1,0:T(8,128)(2,1)S(1)}, u32[]{:S(2)}, u32[]{:S(2)}) collective-permute-start(bf16[2,128,2048]{2,1,0:T(8,128)(2,1)S(1)} %get-tuple-element.38), channel_id=1, source_target_pairs={{0,1},{1,0},{2,3},{3,2},{4,5},{5,4},{6,7},{7,6},{8,9},{9,8},{10,11... | collective-permute-start | bytes 3145736 | tf_op jit(solution)/shard_map/ppermute | solution.py:268
  10.1 1.9 %collective-permute-start.8 = (bf16[2,128,2048]{2,1,0:T(8,128)(2,1)S(1)}, bf16[2,128,2048]{2,1,0:T(8,128)(2,1)S(1)}, u32[]{:S(2)}, u32[]{:S(2)}) collective-permute-start(bf16[2,128,2048]{2,1,0:T(8,128)(2,1)S(1)} %get-tuple-element.39), channel_id=1, source_target_pairs={{0,0},{1,2},{2,1},{3,3},{4,4},{5,6},{6,5},{7,7},{8,8},{9,10},{10,9... | collective-permute-start | bytes 3145736 | tf_op jit(solution)/shard_map/ppermute | solution.py:268
  12.0 1.9 %collective-permute-done.1.refs_2_ = bf16[128,640]{1,0:T(8,128)(2,1)S(1)} collective-permute-done((bf16[128,640]{1,0:T(8,128)(2,1)S(1)}, bf16[128,640]{1,0:T(8,128)(2,1)S(1)}, u32[]{:S(2)}, u32[]{:S(2)}) %collective-permute-start.1) | collective-permute-done | bytes 163872 | tf_op jit(solution)/shard_map/ppermute | solution.py:30
  13.9 1.6 %copy-done.4 = bf16[2,2048,256]{2,1,0:T(8,128)(2,1)S(1)} copy-done((bf16[2,2048,256]{2,1,0:T(8,128)(2,1)S(1)}, bf16[2,2048,256]{2,1,0:T(8,128)(2,1)}, u32[]{:S(2)}) %copy-start.4) | copy-done | bytes 2097176
  15.5 1.9 %shard_map.81 = (f32[128,1024]{1,0:T(8,128)S(1)}, bf16[128,1024]{1,0:T(8,128)(2,1)S(1)}, bf16[128,1024]{1,0:T(8,128)(2,1)S(1)}, bf16[128,1024]{1,0:T(8,128)(2,1)S(1)}) custom-call(bf16[128,640]{1,0:T(8,128)(2,1)S(1)} %get-tuple-element.30.refs_0_, bf16[128,640]{1,0:T(8,128)(2,1)S(1)} %collective-permute-done.refs_1_, ...), custom_call_target="tpu_custom_call" | custom-call | flops 1073741824 | bytes 2097152 | tf_op jit(solution)/shard_map/pallas_call | solution.py:312
  17.5 0.6 collective-permute-start.14
  18.1 1.2 %collective-permute-start.15 = (bf16[128,1024]{1,0:T(8,128)(2,1)S(1)}, bf16[128,1024]{1,0:T(8,128)(2,1)S(1)}, u32[]{:S(2)}, u32[]{:S(2)}) collective-permute-start(bf16[128,1024]{1,0:T(8,128)(2,1)S(1)} %get-tuple-element.48), channel_id=1, source_target_pairs={{0,16},{4,20},{8,24},{12,28},{16,0},{20,4},{24,8},{28,12},{1,17},{... | collective-permute-start | bytes 786440 | tf_op jit(solution)/shard_map/ppermute | solution.py:30
  19.3 1.8 %collective-permute-start.16 = (bf16[128,1024]{1,0:T(8,128)(2,1)S(1)}, bf16[128,1024]{1,0:T(8,128)(2,1)S(1)}, u32[]{:S(2)}, u32[]{:S(2)}) collective-permute-start(bf16[128,1024]{1,0:T(8,128)(2,1)S(1)} %get-tuple-element.49), channel_id=1, source_target_pairs={{0,24},{4,28},{8,16},{12,20},{16,8},{20,12},{24,0},{28,4},{1,25},{... | collective-permute-start | bytes 786440 | tf_op jit(solution)/shard_map/ppermute | solution.py:30
  21.0 2.0 %shard_map.77 = (f32[128,1024]{1,0:T(8,128)S(1)}, bf16[128,1024]{1,0:T(8,128)(2,1)S(1)}, bf16[128,1024]{1,0:T(8,128)(2,1)S(1)}, bf16[128,1024]{1,0:T(8,128)(2,1)S(1)}) custom-call(bf16[128,640]{1,0:T(8,128)(2,1)S(1)} %get-tuple-element.30.refs_0_, bf16[128,640]{1,0:T(8,128)(2,1)S(1)} %collective-permute-done.refs_1_, ...), custom_call_target="tpu_custom_call" | custom-call | flops 1073741824 | bytes 2097152 | tf_op jit(solution)/shard_map/pallas_call | solution.py:312
  23.0 3.7 %collective-permute-done.14.refs_0_ = bf16[128,1024]{1,0:T(8,128)(2,1)S(1)} collective-permute-done((bf16[128,1024]{1,0:T(8,128)(2,1)S(1)}, bf16[128,1024]{1,0:T(8,128)(2,1)S(1)}, u32[]{:S(2)}, u32[]{:S(2)}) %collective-permute-start.14) | collective-permute-done | bytes 262176 | tf_op jit(solution)/shard_map/ppermute | solution.py:30
  26.7 0.5 collective-permute-start.4
  27.2 3.1 %collective-permute-done.15.refs_1_ = bf16[128,1024]{1,0:T(8,128)(2,1)S(1)} collective-permute-done((bf16[128,1024]{1,0:T(8,128)(2,1)S(1)}, bf16[128,1024]{1,0:T(8,128)(2,1)S(1)}, u32[]{:S(2)}, u32[]{:S(2)}) %collective-permute-start.15) | collective-permute-done | bytes 262176 | tf_op jit(solution)/shard_map/ppermute | solution.py:30
  30.3 1.2 %collective-permute-start.5 = (bf16[128,1024]{1,0:T(8,128)(2,1)S(1)}, bf16[128,1024]{1,0:T(8,128)(2,1)S(1)}, u32[]{:S(2)}, u32[]{:S(2)}) collective-permute-start(bf16[128,1024]{1,0:T(8,128)(2,1)S(1)} %get-tuple-element.36), channel_id=1, source_target_pairs={{0,16},{4,20},{8,24},{12,28},{16,0},{20,4},{24,8},{28,12},{1,17},{... | collective-permute-start | bytes 786440 | tf_op jit(solution)/shard_map/ppermute | solution.py:30
  31.5 0.8 collective-permute-done.16.refs_2_
  32.3 1.5 %collective-permute-start.6 = (bf16[128,1024]{1,0:T(8,128)(2,1)S(1)}, bf16[128,1024]{1,0:T(8,128)(2,1)S(1)}, u32[]{:S(2)}, u32[]{:S(2)}) collective-permute-start(bf16[128,1024]{1,0:T(8,128)(2,1)S(1)} %get-tuple-element.37), channel_id=1, source_target_pairs={{0,24},{4,28},{8,16},{12,20},{16,8},{20,12},{24,0},{28,4},{1,25},{... | collective-permute-start | bytes 786440 | tf_op jit(solution)/shard_map/ppermute | solution.py:30
  33.8 0.1 shard_map.82.g_ref
  33.9 4.1 %collective-permute-done.4.refs_0_ = bf16[128,1024]{1,0:T(8,128)(2,1)S(1)} collective-permute-done((bf16[128,1024]{1,0:T(8,128)(2,1)S(1)}, bf16[128,1024]{1,0:T(8,128)(2,1)S(1)}, u32[]{:S(2)}, u32[]{:S(2)}) %collective-permute-start.4) | collective-permute-done | bytes 262176 | tf_op jit(solution)/shard_map/ppermute | solution.py:30
  38.0 0.4 collective-permute-start.17
  38.4 3.9 %collective-permute-done.5.refs_1_ = bf16[128,1024]{1,0:T(8,128)(2,1)S(1)} collective-permute-done((bf16[128,1024]{1,0:T(8,128)(2,1)S(1)}, bf16[128,1024]{1,0:T(8,128)(2,1)S(1)}, u32[]{:S(2)}, u32[]{:S(2)}) %collective-permute-start.5) | collective-permute-done | bytes 262176 | tf_op jit(solution)/shard_map/ppermute | solution.py:30
  42.3 0.1 shard_map.78.g_ref
  42.4 1.7 %collective-permute-start.9 = (bf16[128,1024]{1,0:T(8,128)(2,1)S(1)}, bf16[128,1024]{1,0:T(8,128)(2,1)S(1)}, u32[]{:S(2)}, u32[]{:S(2)}) collective-permute-start(bf16[128,1024]{1,0:T(8,128)(2,1)S(1)} %shard_map.78.g_ref), channel_id=1, source_target_pairs={{0,3},{1,0},{2,1},{3,2},{4,7},{5,4},{6,5},{7,6},{8,11},{9,8},{10,9... | collective-permute-start | bytes 786440 | tf_op jit(solution)/shard_map/ppermute | solution.py:260
  44.2 1.2 %collective-permute-done.17.right_g = bf16[128,1024]{1,0:T(8,128)(2,1)S(1)} collective-permute-done((bf16[128,1024]{1,0:T(8,128)(2,1)S(1)}, bf16[128,1024]{1,0:T(8,128)(2,1)S(1)}, u32[]{:S(2)}, u32[]{:S(2)}) %collective-permute-start.17) | collective-permute-done | bytes 262176 | tf_op jit(solution)/shard_map/ppermute | solution.py:260
  45.4 1.1 %shard_map.83 = (f32[3,8,128]{2,1,0:T(8,128)S(1)}, f32[3,8,128]{2,1,0:T(8,128)S(1)}) custom-call(bf16[1,128,2048]{2,1,0:T(8,128)(2,1)S(1)} %copy-done.3, bf16[2,1,128,2048]{3,2,1,0:T(8,128)(2,1)S(1)} %copy-done.1, bf16[128,1024]{1,0:T(8,128)(2,1)S(1)} %shard_map.82.g_ref, bf16[2,128,2048]{2,1,0:T(8,128)(2,1)S(1)} %collective-permute-done.7.side1, ...), custom_call_target="tpu_custom_call" | custom-call | flops 201326592 | bytes 2621440 | tf_op jit(solution)/shard_map/pallas_call | solution.py:339
  46.5 0.5 collective-permute-start.19
  47.0 3.1 %collective-permute-start.18 = (f32[3,8,128]{2,1,0:T(8,128)S(1)}, f32[3,8,128]{2,1,0:T(8,128)S(1)}, u32[]{:S(2)}, u32[]{:S(2)}) collective-permute-start(f32[3,8,128]{2,1,0:T(8,128)S(1)} %get-tuple-element.51.far_stats), channel_id=1, source_target_pairs={{0,1},{1,2},{2,3},{3,0},{4,5},{5,6},{6,7},{7,4},{8,9},{9,10},{10,1... | collective-permute-start | bytes 36872 | tf_op jit(solution)/shard_map/ppermute | solution.py:260
  50.1 0.2 collective-permute-done.9.right_g
  50.2 1.1 %shard_map.79 = (f32[3,8,128]{2,1,0:T(8,128)S(1)}, f32[3,8,128]{2,1,0:T(8,128)S(1)}) custom-call(bf16[1,128,2048]{2,1,0:T(8,128)(2,1)S(1)} %copy-done.3, bf16[2,1,128,2048]{3,2,1,0:T(8,128)(2,1)S(1)} %copy-done.1, bf16[128,1024]{1,0:T(8,128)(2,1)S(1)} %shard_map.78.g_ref, bf16[2,128,2048]{2,1,0:T(8,128)(2,1)S(1)} %collective-permute-done.7.side1, ...), custom_call_target="tpu_custom_call" | custom-call | flops 201326592 | bytes 2621440 | tf_op jit(solution)/shard_map/pallas_call | solution.py:339
  51.3 0.5 collective-permute-start.11
  51.8 3.2 %collective-permute-start.10 = (f32[3,8,128]{2,1,0:T(8,128)S(1)}, f32[3,8,128]{2,1,0:T(8,128)S(1)}, u32[]{:S(2)}, u32[]{:S(2)}) collective-permute-start(f32[3,8,128]{2,1,0:T(8,128)S(1)} %get-tuple-element.41.far_stats), channel_id=1, source_target_pairs={{0,1},{1,2},{2,3},{3,0},{4,5},{5,6},{6,7},{7,4},{8,9},{9,10},{10,1... | collective-permute-start | bytes 36872 | tf_op jit(solution)/shard_map/ppermute | solution.py:260
  55.1 2.7 %shard_map.84 = (f32[128,1024]{1,0:T(8,128)S(1)}, f32[2,128,1024]{2,1,0:T(8,128)S(1)}, bf16[2,128,1024]{2,1,0:T(8,128)(2,1)S(1)}, bf16[2,128,1024]{2,1,0:T(8,128)(2,1)S(1)}) custom-call(bf16[1,128,2048]{2,1,0:T(8,128)(2,1)S(1)} %copy-done.3, bf16[2,1,128,2048]{3,2,1,0:T(8,128)(2,1)S(1)} %copy-done.1, bf16[128,1024]{1,0:T(8,128)(2,1)S(1)} %shard_map.82.g_ref, ...), custom_call_target="tpu_custom_call" | custom-call | flops 503316480 | bytes 5242880 | tf_op jit(solution)/shard_map/pallas_call | solution.py:347
  57.7 3.8 %collective-permute-start.20 = (bf16[2,128,1024]{2,1,0:T(8,128)(2,1)S(1)}, bf16[2,128,1024]{2,1,0:T(8,128)(2,1)S(1)}, u32[]{:S(2)}, u32[]{:S(2)}) collective-permute-start(bf16[2,128,1024]{2,1,0:T(8,128)(2,1)S(1)} %get-tuple-element.54), channel_id=1, source_target_pairs={{0,1},{1,0},{2,3},{3,2},{4,5},{5,4},{6,7},{7,6},{8,9},{9,8},{10,11... | collective-permute-start | bytes 1572872 | tf_op jit(solution)/shard_map/ppermute | solution.py:268
  61.6 1.9 %collective-permute-start.21 = (bf16[2,128,1024]{2,1,0:T(8,128)(2,1)S(1)}, bf16[2,128,1024]{2,1,0:T(8,128)(2,1)S(1)}, u32[]{:S(2)}, u32[]{:S(2)}) collective-permute-start(bf16[2,128,1024]{2,1,0:T(8,128)(2,1)S(1)} %get-tuple-element.55), channel_id=1, source_target_pairs={{0,0},{1,2},{2,1},{3,3},{4,4},{5,6},{6,5},{7,7},{8,8},{9,10},{10,9... | collective-permute-start | bytes 1572872 | tf_op jit(solution)/shard_map/ppermute | solution.py:268
  63.5 2.9 %shard_map.80 = (f32[128,1024]{1,0:T(8,128)S(1)}, f32[2,128,1024]{2,1,0:T(8,128)S(1)}, bf16[2,128,1024]{2,1,0:T(8,128)(2,1)S(1)}, bf16[2,128,1024]{2,1,0:T(8,128)(2,1)S(1)}) custom-call(bf16[1,128,2048]{2,1,0:T(8,128)(2,1)S(1)} %copy-done.3, bf16[2,1,128,2048]{3,2,1,0:T(8,128)(2,1)S(1)} %copy-done.1, bf16[128,1024]{1,0:T(8,128)(2,1)S(1)} %shard_map.78.g_ref, ...), custom_call_target="tpu_custom_call" | custom-call | flops 503316480 | bytes 5242880 | tf_op jit(solution)/shard_map/pallas_call | solution.py:347
  66.4 3.9 %collective-permute-start.13 = (bf16[2,128,1024]{2,1,0:T(8,128)(2,1)S(1)}, bf16[2,128,1024]{2,1,0:T(8,128)(2,1)S(1)}, u32[]{:S(2)}, u32[]{:S(2)}) collective-permute-start(bf16[2,128,1024]{2,1,0:T(8,128)(2,1)S(1)} %get-tuple-element.45), channel_id=1, source_target_pairs={{0,0},{1,2},{2,1},{3,3},{4,4},{5,6},{6,5},{7,7},{8,8},{9,10},{10,9... | collective-permute-start | bytes 1572872 | tf_op jit(solution)/shard_map/ppermute | solution.py:268
  70.4 4.0 %collective-permute-done.20.got1 = bf16[2,128,1024]{2,1,0:T(8,128)(2,1)S(1)} collective-permute-done((bf16[2,128,1024]{2,1,0:T(8,128)(2,1)S(1)}, bf16[2,128,1024]{2,1,0:T(8,128)(2,1)S(1)}, u32[]{:S(2)}, u32[]{:S(2)}) %collective-permute-start.20) | collective-permute-done | bytes 524320 | tf_op jit(solution)/shard_map/ppermute | solution.py:268
  74.3 3.9 %collective-permute-done.21.got2 = bf16[2,128,1024]{2,1,0:T(8,128)(2,1)S(1)} collective-permute-done((bf16[2,128,1024]{2,1,0:T(8,128)(2,1)S(1)}, bf16[2,128,1024]{2,1,0:T(8,128)(2,1)S(1)}, u32[]{:S(2)}, u32[]{:S(2)}) %collective-permute-start.21) | collective-permute-done | bytes 524320 | tf_op jit(solution)/shard_map/ppermute | solution.py:268
  78.2 1.1 %shard_map.85 = (bf16[1,128,2048]{2,1,0:T(8,128)(2,1)}, bf16[2,1,128,2048]{3,2,1,0:T(8,128)(2,1)}) custom-call(f32[128,1024]{1,0:T(8,128)S(1)} %get-tuple-element.52.dq_ref, f32[2,128,1024]{2,1,0:T(8,128)S(1)} %get-tuple-element.53.dkv_ref, bf16[2,128,1024]{2,1,0:T(8,128)(2,1)S(1)} %collective-permute-done.20.got1, ...), custom_call_target="tpu_custom_call" | custom-call | bytes 2621440 | tf_op jit(solution)/shard_map/pallas_call | solution.py:360
  79.3 3.1 %collective-permute-done.12.got1 = bf16[2,128,1024]{2,1,0:T(8,128)(2,1)S(1)} collective-permute-done((bf16[2,128,1024]{2,1,0:T(8,128)(2,1)S(1)}, bf16[2,128,1024]{2,1,0:T(8,128)(2,1)S(1)}, u32[]{:S(2)}, u32[]{:S(2)}) %collective-permute-start.12) | collective-permute-done | bytes 524320 | tf_op jit(solution)/shard_map/ppermute | solution.py:268
  82.4 3.2 %collective-permute-done.13.got2 = bf16[2,128,1024]{2,1,0:T(8,128)(2,1)S(1)} collective-permute-done((bf16[2,128,1024]{2,1,0:T(8,128)(2,1)S(1)}, bf16[2,128,1024]{2,1,0:T(8,128)(2,1)S(1)}, u32[]{:S(2)}, u32[]{:S(2)}) %collective-permute-start.13) | collective-permute-done | bytes 524320 | tf_op jit(solution)/shard_map/ppermute | solution.py:268
  85.6 1.1 %shard_map.86 = (bf16[1,128,2048]{2,1,0:T(8,128)(2,1)}, bf16[2,1,128,2048]{3,2,1,0:T(8,128)(2,1)}) custom-call(f32[128,1024]{1,0:T(8,128)S(1)} %get-tuple-element.42.dq_ref, f32[2,128,1024]{2,1,0:T(8,128)S(1)} %get-tuple-element.43.dkv_ref, bf16[2,128,1024]{2,1,0:T(8,128)(2,1)S(1)} %collective-permute-done.12.got1, ...), custom_call_target="tpu_custom_call", output_to_operand_aliasing={{0}: (4, {}), {1}: (5, {})} | custom-call | bytes 2621440 | tf_op jit(solution)/shard_map/pallas_call | solution.py:360
  (24 shorter events, 0.3 us)
Async XLA Ops:
  0.6 13.3 %collective-permute-start.3 = (bf16[2,2048,256]{2,1,0:T(8,128)(2,1)}, bf16[2,2048,256]{2,1,0:T(8,128)(2,1)S(1)}, u32[]{:S(2)}, u32[]{:S(2)}) collective-permute-start(bf16[2,2048,256]{2,1,0:T(8,128)(2,1)} %refs_4_.3), channel_id=1, source_target_pairs={{0,4},{4,0},{8,12},{12,8},{16,20},{20,16},{24,28},{28,24},{1,5},{5... | collective-permute-start | bytes 6291464 | tf_op jit(solution)/shard_map/ppermute | solution.py:30
  0.7 1.0 %copy-start.5 = (bf16[1,128,2048]{2,1,0:T(8,128)(2,1)S(1)}, bf16[1,128,2048]{2,1,0:T(8,128)(2,1)}, u32[]{:S(2)}) copy-start(bf16[1,128,2048]{2,1,0:T(8,128)(2,1)} %grad_ref.1) | copy-start | bytes 1572868
  1.8 0.7 copy-start.7
  2.5 7.6 %collective-permute-start = (bf16[128,640]{1,0:T(8,128)(2,1)S(1)}, bf16[128,640]{1,0:T(8,128)(2,1)S(1)}, u32[]{:S(2)}, u32[]{:S(2)}) collective-permute-start(bf16[128,640]{1,0:T(8,128)(2,1)S(1)} %get-tuple-element.31), channel_id=1, source_target_pairs={{0,8},{4,12},{8,0},{12,4},{16,24},{20,28},{24,16},{28,20},{1,9},{5... | collective-permute-start | bytes 491528 | tf_op jit(solution)/shard_map/ppermute | solution.py:30
  4.1 9.8 %collective-permute-start.1 = (bf16[128,640]{1,0:T(8,128)(2,1)S(1)}, bf16[128,640]{1,0:T(8,128)(2,1)S(1)}, u32[]{:S(2)}, u32[]{:S(2)}) collective-permute-start(bf16[128,640]{1,0:T(8,128)(2,1)S(1)} %get-tuple-element.32), channel_id=1, source_target_pairs={{0,16},{4,20},{8,24},{12,28},{16,0},{20,4},{24,8},{28,12},{1,17},{... | collective-permute-start | bytes 491528 | tf_op jit(solution)/shard_map/ppermute | solution.py:30
  4.6 9.3 %collective-permute-start.2 = (bf16[128,640]{1,0:T(8,128)(2,1)S(1)}, bf16[128,640]{1,0:T(8,128)(2,1)S(1)}, u32[]{:S(2)}, u32[]{:S(2)}) collective-permute-start(bf16[128,640]{1,0:T(8,128)(2,1)S(1)} %get-tuple-element.33), channel_id=1, source_target_pairs={{0,24},{4,28},{8,16},{12,20},{16,8},{20,12},{24,0},{28,4},{1,25},{... | collective-permute-start | bytes 491528 | tf_op jit(solution)/shard_map/ppermute | solution.py:30
  6.1 1.2 %copy-start = (bf16[2,1,128,2048]{3,2,1,0:T(8,128)(2,1)S(1)}, bf16[2,1,128,2048]{3,2,1,0:T(8,128)(2,1)}, u32[]{:S(2)}) copy-start(bf16[2,1,128,2048]{3,2,1,0:T(8,128)(2,1)} %kv_ref.9) | copy-start | bytes 3145732
  7.3 1.0 %copy-start.2 = (bf16[1,128,2048]{2,1,0:T(8,128)(2,1)S(1)}, bf16[1,128,2048]{2,1,0:T(8,128)(2,1)}, u32[]{:S(2)}) copy-start(bf16[1,128,2048]{2,1,0:T(8,128)(2,1)} %q_ref.9) | copy-start | bytes 1572868
  8.5 35.7 %collective-permute-start.7 = (bf16[2,128,2048]{2,1,0:T(8,128)(2,1)S(1)}, bf16[2,128,2048]{2,1,0:T(8,128)(2,1)S(1)}, u32[]{:S(2)}, u32[]{:S(2)}) collective-permute-start(bf16[2,128,2048]{2,1,0:T(8,128)(2,1)S(1)} %get-tuple-element.38), channel_id=1, source_target_pairs={{0,1},{1,0},{2,3},{3,2},{4,5},{5,4},{6,7},{7,6},{8,9},{9,8},{10,11... | collective-permute-start | bytes 3145736 | tf_op jit(solution)/shard_map/ppermute | solution.py:268
  10.1 34.0 %collective-permute-start.8 = (bf16[2,128,2048]{2,1,0:T(8,128)(2,1)S(1)}, bf16[2,128,2048]{2,1,0:T(8,128)(2,1)S(1)}, u32[]{:S(2)}, u32[]{:S(2)}) collective-permute-start(bf16[2,128,2048]{2,1,0:T(8,128)(2,1)S(1)} %get-tuple-element.39), channel_id=1, source_target_pairs={{0,0},{1,2},{2,1},{3,3},{4,4},{5,6},{6,5},{7,7},{8,8},{9,10},{10,9... | collective-permute-start | bytes 3145736 | tf_op jit(solution)/shard_map/ppermute | solution.py:268
  13.9 1.6 %copy-start.4 = (bf16[2,2048,256]{2,1,0:T(8,128)(2,1)S(1)}, bf16[2,2048,256]{2,1,0:T(8,128)(2,1)}, u32[]{:S(2)}) copy-start(bf16[2,2048,256]{2,1,0:T(8,128)(2,1)} %refs_4_.3) | copy-start | bytes 6291460
  17.5 9.2 %collective-permute-start.14 = (bf16[128,1024]{1,0:T(8,128)(2,1)S(1)}, bf16[128,1024]{1,0:T(8,128)(2,1)S(1)}, u32[]{:S(2)}, u32[]{:S(2)}) collective-permute-start(bf16[128,1024]{1,0:T(8,128)(2,1)S(1)} %get-tuple-element.47), channel_id=1, source_target_pairs={{0,8},{4,12},{8,0},{12,4},{16,24},{20,28},{24,16},{28,20},{1,9},{5... | collective-permute-start | bytes 786440 | tf_op jit(solution)/shard_map/ppermute | solution.py:30
  18.1 12.3 %collective-permute-start.15 = (bf16[128,1024]{1,0:T(8,128)(2,1)S(1)}, bf16[128,1024]{1,0:T(8,128)(2,1)S(1)}, u32[]{:S(2)}, u32[]{:S(2)}) collective-permute-start(bf16[128,1024]{1,0:T(8,128)(2,1)S(1)} %get-tuple-element.48), channel_id=1, source_target_pairs={{0,16},{4,20},{8,24},{12,28},{16,0},{20,4},{24,8},{28,12},{1,17},{... | collective-permute-start | bytes 786440 | tf_op jit(solution)/shard_map/ppermute | solution.py:30
  19.3 13.0 %collective-permute-start.16 = (bf16[128,1024]{1,0:T(8,128)(2,1)S(1)}, bf16[128,1024]{1,0:T(8,128)(2,1)S(1)}, u32[]{:S(2)}, u32[]{:S(2)}) collective-permute-start(bf16[128,1024]{1,0:T(8,128)(2,1)S(1)} %get-tuple-element.49), channel_id=1, source_target_pairs={{0,24},{4,28},{8,16},{12,20},{16,8},{20,12},{24,0},{28,4},{1,25},{... | collective-permute-start | bytes 786440 | tf_op jit(solution)/shard_map/ppermute | solution.py:30
  23.0 22.4 %copy-start.1 = (bf16[2,1,128,2048]{3,2,1,0:T(8,128)(2,1)S(1)}, bf16[2,1,128,2048]{3,2,1,0:T(8,128)(2,1)}, u32[]{:S(2)}) copy-start(bf16[2,1,128,2048]{3,2,1,0:T(8,128)(2,1)} %kv_ref.9) | copy-start | bytes 3145732
  23.0 22.4 %copy-start.3 = (bf16[1,128,2048]{2,1,0:T(8,128)(2,1)S(1)}, bf16[1,128,2048]{2,1,0:T(8,128)(2,1)}, u32[]{:S(2)}) copy-start(bf16[1,128,2048]{2,1,0:T(8,128)(2,1)} %q_ref.9) | copy-start | bytes 1572868
  23.0 22.4 %copy-start.6 = (s32[1,512]{1,0:T(1,128)S(1)}, s32[1,512]{1,0:T(1,128)}, u32[]{:S(2)}) copy-start(s32[1,512]{1,0:T(1,128)} %segs.7) | copy-start | bytes 6148
  26.7 11.3 %collective-permute-start.4 = (bf16[128,1024]{1,0:T(8,128)(2,1)S(1)}, bf16[128,1024]{1,0:T(8,128)(2,1)S(1)}, u32[]{:S(2)}, u32[]{:S(2)}) collective-permute-start(bf16[128,1024]{1,0:T(8,128)(2,1)S(1)} %get-tuple-element.35), channel_id=1, source_target_pairs={{0,8},{4,12},{8,0},{12,4},{16,24},{20,28},{24,16},{28,20},{1,9},{5... | collective-permute-start | bytes 786440 | tf_op jit(solution)/shard_map/ppermute | solution.py:30
  30.3 12.0 %collective-permute-start.5 = (bf16[128,1024]{1,0:T(8,128)(2,1)S(1)}, bf16[128,1024]{1,0:T(8,128)(2,1)S(1)}, u32[]{:S(2)}, u32[]{:S(2)}) collective-permute-start(bf16[128,1024]{1,0:T(8,128)(2,1)S(1)} %get-tuple-element.36), channel_id=1, source_target_pairs={{0,16},{4,20},{8,24},{12,28},{16,0},{20,4},{24,8},{28,12},{1,17},{... | collective-permute-start | bytes 786440 | tf_op jit(solution)/shard_map/ppermute | solution.py:30
  32.3 10.0 %collective-permute-start.6 = (bf16[128,1024]{1,0:T(8,128)(2,1)S(1)}, bf16[128,1024]{1,0:T(8,128)(2,1)S(1)}, u32[]{:S(2)}, u32[]{:S(2)}) collective-permute-start(bf16[128,1024]{1,0:T(8,128)(2,1)S(1)} %get-tuple-element.37), channel_id=1, source_target_pairs={{0,24},{4,28},{8,16},{12,20},{16,8},{20,12},{24,0},{28,4},{1,25},{... | collective-permute-start | bytes 786440 | tf_op jit(solution)/shard_map/ppermute | solution.py:30
  38.0 7.4 %collective-permute-start.17 = (bf16[128,1024]{1,0:T(8,128)(2,1)S(1)}, bf16[128,1024]{1,0:T(8,128)(2,1)S(1)}, u32[]{:S(2)}, u32[]{:S(2)}) collective-permute-start(bf16[128,1024]{1,0:T(8,128)(2,1)S(1)} %shard_map.82.g_ref), channel_id=1, source_target_pairs={{0,3},{1,0},{2,1},{3,2},{4,7},{5,4},{6,5},{7,6},{8,11},{9,8},{10,9... | collective-permute-start | bytes 786440 | tf_op jit(solution)/shard_map/ppermute | solution.py:260
  42.4 7.8 %collective-permute-start.9 = (bf16[128,1024]{1,0:T(8,128)(2,1)S(1)}, bf16[128,1024]{1,0:T(8,128)(2,1)S(1)}, u32[]{:S(2)}, u32[]{:S(2)}) collective-permute-start(bf16[128,1024]{1,0:T(8,128)(2,1)S(1)} %shard_map.78.g_ref), channel_id=1, source_target_pairs={{0,3},{1,0},{2,1},{3,2},{4,7},{5,4},{6,5},{7,6},{8,11},{9,8},{10,9... | collective-permute-start | bytes 786440 | tf_op jit(solution)/shard_map/ppermute | solution.py:260
  46.5 8.6 %collective-permute-start.19 = (f32[3,8,128]{2,1,0:T(8,128)S(1)}, f32[3,8,128]{2,1,0:T(8,128)S(1)}, u32[]{:S(2)}, u32[]{:S(2)}) collective-permute-start(f32[3,8,128]{2,1,0:T(8,128)S(1)} %get-tuple-element.50.own_stats), channel_id=1, source_target_pairs={{0,3},{1,0},{2,1},{3,2},{4,7},{5,4},{6,5},{7,6},{8,11},{9,8},{10,9... | collective-permute-start | bytes 36872 | tf_op jit(solution)/shard_map/ppermute | solution.py:260
  47.0 8.1 %collective-permute-start.18 = (f32[3,8,128]{2,1,0:T(8,128)S(1)}, f32[3,8,128]{2,1,0:T(8,128)S(1)}, u32[]{:S(2)}, u32[]{:S(2)}) collective-permute-start(f32[3,8,128]{2,1,0:T(8,128)S(1)} %get-tuple-element.51.far_stats), channel_id=1, source_target_pairs={{0,1},{1,2},{2,3},{3,0},{4,5},{5,6},{6,7},{7,4},{8,9},{9,10},{10,1... | collective-permute-start | bytes 36872 | tf_op jit(solution)/shard_map/ppermute | solution.py:260
  51.3 12.1 %collective-permute-start.11 = (f32[3,8,128]{2,1,0:T(8,128)S(1)}, f32[3,8,128]{2,1,0:T(8,128)S(1)}, u32[]{:S(2)}, u32[]{:S(2)}) collective-permute-start(f32[3,8,128]{2,1,0:T(8,128)S(1)} %get-tuple-element.40.own_stats), channel_id=1, source_target_pairs={{0,3},{1,0},{2,1},{3,2},{4,7},{5,4},{6,5},{7,6},{8,11},{9,8},{10,9... | collective-permute-start | bytes 36872 | tf_op jit(solution)/shard_map/ppermute | solution.py:260
  51.8 11.6 %collective-permute-start.10 = (f32[3,8,128]{2,1,0:T(8,128)S(1)}, f32[3,8,128]{2,1,0:T(8,128)S(1)}, u32[]{:S(2)}, u32[]{:S(2)}) collective-permute-start(f32[3,8,128]{2,1,0:T(8,128)S(1)} %get-tuple-element.41.far_stats), channel_id=1, source_target_pairs={{0,1},{1,2},{2,3},{3,0},{4,5},{5,6},{6,7},{7,4},{8,9},{9,10},{10,1... | collective-permute-start | bytes 36872 | tf_op jit(solution)/shard_map/ppermute | solution.py:260
  57.7 16.6 %collective-permute-start.20 = (bf16[2,128,1024]{2,1,0:T(8,128)(2,1)S(1)}, bf16[2,128,1024]{2,1,0:T(8,128)(2,1)S(1)}, u32[]{:S(2)}, u32[]{:S(2)}) collective-permute-start(bf16[2,128,1024]{2,1,0:T(8,128)(2,1)S(1)} %get-tuple-element.54), channel_id=1, source_target_pairs={{0,1},{1,0},{2,3},{3,2},{4,5},{5,4},{6,7},{7,6},{8,9},{9,8},{10,11... | collective-permute-start | bytes 1572872 | tf_op jit(solution)/shard_map/ppermute | solution.py:268
  61.6 16.7 %collective-permute-start.21 = (bf16[2,128,1024]{2,1,0:T(8,128)(2,1)S(1)}, bf16[2,128,1024]{2,1,0:T(8,128)(2,1)S(1)}, u32[]{:S(2)}, u32[]{:S(2)}) collective-permute-start(bf16[2,128,1024]{2,1,0:T(8,128)(2,1)S(1)} %get-tuple-element.55), channel_id=1, source_target_pairs={{0,0},{1,2},{2,1},{3,3},{4,4},{5,6},{6,5},{7,7},{8,8},{9,10},{10,9... | collective-permute-start | bytes 1572872 | tf_op jit(solution)/shard_map/ppermute | solution.py:268
  66.4 16.1 %collective-permute-start.12 = (bf16[2,128,1024]{2,1,0:T(8,128)(2,1)S(1)}, bf16[2,128,1024]{2,1,0:T(8,128)(2,1)S(1)}, u32[]{:S(2)}, u32[]{:S(2)}) collective-permute-start(bf16[2,128,1024]{2,1,0:T(8,128)(2,1)S(1)} %get-tuple-element.44), channel_id=1, source_target_pairs={{0,1},{1,0},{2,3},{3,2},{4,5},{5,4},{6,7},{7,6},{8,9},{9,8},{10,11... | collective-permute-start | bytes 1572872 | tf_op jit(solution)/shard_map/ppermute | solution.py:268
  66.4 19.2 %collective-permute-start.13 = (bf16[2,128,1024]{2,1,0:T(8,128)(2,1)S(1)}, bf16[2,128,1024]{2,1,0:T(8,128)(2,1)S(1)}, u32[]{:S(2)}, u32[]{:S(2)}) collective-permute-start(bf16[2,128,1024]{2,1,0:T(8,128)(2,1)S(1)} %get-tuple-element.45), channel_id=1, source_target_pairs={{0,0},{1,2},{2,1},{3,3},{4,4},{5,6},{6,5},{7,7},{8,8},{9,10},{10,9... | collective-permute-start | bytes 1572872 | tf_op jit(solution)/shard_map/ppermute | solution.py:268
where the time goes:
time: 87 us; the launch traced here: 86.7 us
  starting transfers between devices  33.1 us (38%)
  waiting for transfers between devices  32.9 us (38%)
  Pallas kernels  14.3 us (16%)
  local copies, waits for them, and re-layouts  5.56 us (6%)
    ppermute x10, waiting for transfers between devices, swap(): lax.ppermute(value, axis, [(i, i ^ bits) for i in range(lax.axis_size(axi...  17.4 us
    ppermute x6, waiting for transfers between devices, neighbour_swaps(): return (lax.ppermute(first, 'seq', one), lax.ppermute(second, 'seq', two))  14.2 us
    ppermute x6, starting transfers between devices, neighbour_swaps(): return (lax.ppermute(first, 'seq', one), lax.ppermute(second, 'seq', two))  13.3 us
    ppermute x10, starting transfers between devices, swap(): lax.ppermute(value, axis, [(i, i ^ bits) for i in range(lax.axis_size(axi...  10.4 us
    ppermute x6, starting transfers between devices, shifted(): lax.ppermute(value, 'seq', [(i, (i + steps) % count) for i in range(count)])  9.46 us
    unnamed x16, local copies, waits for them, and re-layouts  5.56 us
    pallas_call x2, Pallas kernels, step(): pl.pallas_call(functools.partial(grads_kernel, count, c, scale), out_shap...  5.52 us
    pallas_call x2, Pallas kernels, step(): pl.pallas_call(functools.partial(project_kernel, chips), grid=(steps,), i...  3.9 us
  transfers between devices with their start and end apart: 22, of which 12 were waited for; matrix products, arithmetic and copies ran while one was open for 0% of the time, Pallas kernels for 15%

commit v1 on v0

--- a/solution.py
+++ b/solution.py
@@ -36,13 +36,23 @@
     return jnp.sum(jnp.where(same, row.astype(F32), 0.0), axis=1, keepdims=True)
 
 
-def grad_slices_kernel(grad_ref, tags_ref, *outs):
+def grad_slices_kernel(grad_ref, tags_ref, *refs):
+    outs, (tags, tag_sem, sem) = refs[:-3], refs[-3:]
     chip = lax.axis_index("dp") // 2
     width = outs[0].shape[1] - LANES
-    tag = jnp.broadcast_to(column_of(tags_ref[...]), (grad_ref.shape[1], LANES)).astype(BF16)
-    for k, out in enumerate(outs):
-        out[:, :width] = grad_ref[0, :, lane_slice((chip ^ k) * width, width)]
+    tag_copy = pltpu.make_async_copy(tags_ref, tags, tag_sem)
+    copies = [
+        pltpu.make_async_copy(grad_ref.at[0, :, lane_slice((chip ^ k) * width, width)], out.at[:, :width], sem.at[k])
+        for k, out in enumerate(outs)
+    ]
+    for copy in [tag_copy] + copies:
+        copy.start()
+    tag_copy.wait()
+    tag = jnp.broadcast_to(column_of(tags[...]), (grad_ref.shape[1], LANES)).astype(BF16)
+    for out in outs:
         out[:, width:] = tag
+    for copy in copies:
+        copy.wait()
 
 
 def project_kernel(chips, *refs):
@@ -70,29 +80,27 @@
         part[...] = total[(k + 1) * rows : (k + 2) * rows].astype(BF16)
 
 
-def neighbour_slices_kernel(q_ref, kv_ref, *outs):
+def neighbour_slices_kernel(q_ref, kv_ref, out1, out2, sem):
+    def fill(up, down):
+        copies = [
+            pltpu.make_async_copy(kv_ref.at[:, 0], up, sem.at[0]),
+            pltpu.make_async_copy(q_ref.at[0], down.at[0], sem.at[1]),
+            pltpu.make_async_copy(q_ref.at[0], down.at[1], sem.at[2]),
+        ]
+        for copy in copies:
+            copy.start()
+        for copy in copies:
+            copy.wait()
+
     even = lax.axis_index("seq") % 2 == 0
 
-    def up(out):
-        out[...] = kv_ref[:, 0]
-
-    def down(out):
-        out[0] = q_ref[0]
-        out[1] = q_ref[0]
-
-    send(even, outs, down, up)
-
-
-def send(even, outs, down, up):
     @pl.when(even)
     def _():
-        up(outs[0])
-        down(outs[1])
+        fill(out1, out2)
 
     @pl.when(jnp.logical_not(even))
     def _():
-        down(outs[0])
-        up(outs[1])
+        fill(out2, out1)
 
 
 def collect_kernel(terms, mine, *refs):
@@ -268,6 +276,10 @@
     return lax.ppermute(first, "seq", one), lax.ppermute(second, "seq", two)
 
 
+def in_hbm(value):
+    return pltpu.with_memory_space_constraint(value, pltpu.HBM)
+
+
 def shape(dims, dtype=BF16):
     return jax.ShapeDtypeStruct(dims, dtype)
 
@@ -288,20 +300,25 @@
     other_weight = swap(out_weight, "dp", 1)
     slices = pl.pallas_call(
         grad_slices_kernel,
+        in_specs=[pl.BlockSpec(memory_space=pltpu.HBM)] * 2,
         out_shape=[shape((rows, 2 * depth + LANES))] * chips,
+        scratch_shapes=[
+            pltpu.VMEM(tags.shape, tags.dtype), pltpu.SemaphoreType.DMA, pltpu.SemaphoreType.DMA((chips,))],
         compiler_params=params(4),
         name="grad_slices",
         cost_estimate=cost(0, 4 * grad_y.size),
-    )(grad_y, tags)
+    )(in_hbm(grad_y), in_hbm(tags))
     grads = [slices[0]] + [swap(slices[k], "dp", 2 * k) for k in range(1, chips)]
     pair = shape((2, rows, hc))
     sides = pl.pallas_call(
         neighbour_slices_kernel,
+        in_specs=[pl.BlockSpec(memory_space=pltpu.HBM)] * 2,
         out_shape=[pair, pair],
+        scratch_shapes=[pltpu.SemaphoreType.DMA((3,))],
         compiler_params=params(8),
         name="neighbour_slices",
         cost_estimate=cost(0, 16 * query.size),
-    )(query, key_value)
+    )(in_hbm(query), in_hbm(key_value))
     sides = neighbour_swaps(*sides)
 
     tile = min(512, span)

time: 87 us -> 84.8 us (0.975)
  local copies, waits for them, and re-layouts: 5.56 us -> 0.02 us
  Pallas kernels: 14.3 us -> 16.9 us
  waiting for transfers between devices: 32.9 us -> 34.3 us
    unnamed x16 -> x8, local copies, waits for them, and re-layouts: 5.56 us -> 0.02 us
    pallas_call x2, Pallas kernels: 0.23 us -> 2.83 us  [the longest x1 1.54 us: step(): pl.pallas_call(neighbour_slices_kernel, in_specs=[pl.BlockSpec(memory_spa...]
    ppermute x6, waiting for transfers between devices: 1.36 us -> 2.72 us  [shifted(): lax.ppermute(value, 'seq', [(i, (i + steps) % count) for i in range(count)])]
    ppermute x6, starting transfers between devices: 9.46 us -> 8.43 us  [shifted(): lax.ppermute(value, 'seq', [(i, (i + steps) % count) for i in range(count)])]
  transfers between devices with their start and end apart: 22 -> 22, of which waited for: 12 -> 12; matrix products, arithmetic and copies ran while one was open for 0% -> 0% of each run, Pallas kernels for 15% -> 19%
where the time goes in v1:
time: 84.8 us; the launch traced here: 84.6 us
  waiting for transfers between devices  34.3 us (40%)
  starting transfers between devices  32.5 us (38%)
  Pallas kernels  16.9 us (20%)
    ppermute x10, waiting for transfers between devices, swap(): lax.ppermute(value, axis, [(i, i ^ bits) for i in range(lax.axis_size(axi...  17.7 us
    ppermute x6, waiting for transfers between devices, neighbour_swaps(): return (lax.ppermute(first, 'seq', one), lax.ppermute(second, 'seq', two))  13.9 us
    ppermute x6, starting transfers between devices, neighbour_swaps(): return (lax.ppermute(first, 'seq', one), lax.ppermute(second, 'seq', two))  13.7 us
    ppermute x10, starting transfers between devices, swap(): lax.ppermute(value, axis, [(i, i ^ bits) for i in range(lax.axis_size(axi...  10.4 us
    ppermute x6, starting transfers between devices, shifted(): lax.ppermute(value, 'seq', [(i, (i + steps) % count) for i in range(count)])  8.43 us
    pallas_call x2, Pallas kernels, step(): pl.pallas_call(functools.partial(grads_kernel, count, c, scale), out_shap...  5.52 us
    pallas_call x2, Pallas kernels, step(): pl.pallas_call(functools.partial(project_kernel, chips), grid=(steps,), i...  3.92 us
    ppermute x6, waiting for transfers between devices, shifted(): lax.ppermute(value, 'seq', [(i, (i + steps) % count) for i in range(count)])  2.72 us
  transfers between devices with their start and end apart: 22, of which 12 were waited for; matrix products, arithmetic and copies ran while one was open for 0% of the time, Pallas kernels for 19%

profile of v1, /device:TPU:20, one launch (start us, length us, event | category | flops | bytes accessed | tf_op | source)
XLA Modules:
  0.0 84.6 jit_solution(14321163994222154652)
XLA Ops:
  0.6 0.1 collective-permute-start.3
  0.7 1.3 %grad_slices.1 = (bf16[128,640]{1,0:T(8,128)(2,1)S(1)}, bf16[128,640]{1,0:T(8,128)(2,1)S(1)}, bf16[128,640]{1,0:T(8,128)(2,1)S(1)}, bf16[128,640]{1,0:T(8,128)(2,1)S(1)}) custom-call(bf16[1,128,2048]{2,1,0:T(8,128)(2,1)} %grad_ref.1, s32[1,128]{1,0:T(1,128)} %tags_ref.1), custom_call_target="tpu_custom_call" | custom-call | bytes 1048576 | tf_op jit(solution)/shard_map/grad_slices/pallas_call | solution.py:301
  2.0 1.6 %collective-permute-start = (bf16[128,640]{1,0:T(8,128)(2,1)S(1)}, bf16[128,640]{1,0:T(8,128)(2,1)S(1)}, u32[]{:S(2)}, u32[]{:S(2)}) collective-permute-start(bf16[128,640]{1,0:T(8,128)(2,1)S(1)} %get-tuple-element.31), channel_id=1, source_target_pairs={{0,8},{4,12},{8,0},{12,4},{16,24},{20,28},{24,16},{28,20},{1,9},{5... | collective-permute-start | bytes 491528 | tf_op jit(solution)/shard_map/ppermute | solution.py:30
  3.6 0.5 collective-permute-start.1
  4.1 1.5 %collective-permute-start.2 = (bf16[128,640]{1,0:T(8,128)(2,1)S(1)}, bf16[128,640]{1,0:T(8,128)(2,1)S(1)}, u32[]{:S(2)}, u32[]{:S(2)}) collective-permute-start(bf16[128,640]{1,0:T(8,128)(2,1)S(1)} %get-tuple-element.33), channel_id=1, source_target_pairs={{0,24},{4,28},{8,16},{12,20},{16,8},{20,12},{24,0},{28,4},{1,25},{... | collective-permute-start | bytes 491528 | tf_op jit(solution)/shard_map/ppermute | solution.py:30
  5.6 1.5 %neighbour_slices.1 = (bf16[2,128,2048]{2,1,0:T(8,128)(2,1)S(1)}, bf16[2,128,2048]{2,1,0:T(8,128)(2,1)S(1)}) custom-call(bf16[1,128,2048]{2,1,0:T(8,128)(2,1)} %q_ref.9, bf16[2,1,128,2048]{3,2,1,0:T(8,128)(2,1)} %kv_ref.9), custom_call_target="tpu_custom_call" | custom-call | bytes 4194304 | tf_op jit(solution)/shard_map/neighbour_slices/pallas_call | solution.py:313
  7.1 1.6 %collective-permute-start.7 = (bf16[2,128,2048]{2,1,0:T(8,128)(2,1)S(1)}, bf16[2,128,2048]{2,1,0:T(8,128)(2,1)S(1)}, u32[]{:S(2)}, u32[]{:S(2)}) collective-permute-start(bf16[2,128,2048]{2,1,0:T(8,128)(2,1)S(1)} %get-tuple-element.38), channel_id=1, source_target_pairs={{0,1},{1,0},{2,3},{3,2},{4,5},{5,4},{6,7},{7,6},{8,9},{9,8},{10,11... | collective-permute-start | bytes 3145736 | tf_op jit(solution)/shard_map/ppermute | solution.py:276
  8.8 0.4 collective-permute-done.refs_1_
  9.2 2.3 %collective-permute-start.8 = (bf16[2,128,2048]{2,1,0:T(8,128)(2,1)S(1)}, bf16[2,128,2048]{2,1,0:T(8,128)(2,1)S(1)}, u32[]{:S(2)}, u32[]{:S(2)}) collective-permute-start(bf16[2,128,2048]{2,1,0:T(8,128)(2,1)S(1)} %get-tuple-element.39), channel_id=1, source_target_pairs={{0,0},{1,2},{2,1},{3,3},{4,4},{5,6},{6,5},{7,7},{8,8},{9,10},{10,9... | collective-permute-start | bytes 3145736 | tf_op jit(solution)/shard_map/ppermute | solution.py:276
  11.5 1.8 %collective-permute-done.1.refs_2_ = bf16[128,640]{1,0:T(8,128)(2,1)S(1)} collective-permute-done((bf16[128,640]{1,0:T(8,128)(2,1)S(1)}, bf16[128,640]{1,0:T(8,128)(2,1)S(1)}, u32[]{:S(2)}, u32[]{:S(2)}) %collective-permute-start.1) | collective-permute-done | bytes 163872 | tf_op jit(solution)/shard_map/ppermute | solution.py:30
  13.3 2.0 %shard_map.81 = (f32[128,1024]{1,0:T(8,128)S(1)}, bf16[128,1024]{1,0:T(8,128)(2,1)S(1)}, bf16[128,1024]{1,0:T(8,128)(2,1)S(1)}, bf16[128,1024]{1,0:T(8,128)(2,1)S(1)}) custom-call(bf16[128,640]{1,0:T(8,128)(2,1)S(1)} %get-tuple-element.30.refs_0_, bf16[128,640]{1,0:T(8,128)(2,1)S(1)} %collective-permute-done.refs_1_, ...), custom_call_target="tpu_custom_call" | custom-call | flops 1073741824 | bytes 2097152 | tf_op jit(solution)/shard_map/pallas_call | solution.py:329
  15.3 0.6 collective-permute-start.14
  15.9 1.2 %collective-permute-start.15 = (bf16[128,1024]{1,0:T(8,128)(2,1)S(1)}, bf16[128,1024]{1,0:T(8,128)(2,1)S(1)}, u32[]{:S(2)}, u32[]{:S(2)}) collective-permute-start(bf16[128,1024]{1,0:T(8,128)(2,1)S(1)} %get-tuple-element.48), channel_id=1, source_target_pairs={{0,16},{4,20},{8,24},{12,28},{16,0},{20,4},{24,8},{28,12},{1,17},{... | collective-permute-start | bytes 786440 | tf_op jit(solution)/shard_map/ppermute | solution.py:30
  17.0 1.8 %collective-permute-start.16 = (bf16[128,1024]{1,0:T(8,128)(2,1)S(1)}, bf16[128,1024]{1,0:T(8,128)(2,1)S(1)}, u32[]{:S(2)}, u32[]{:S(2)}) collective-permute-start(bf16[128,1024]{1,0:T(8,128)(2,1)S(1)} %get-tuple-element.49), channel_id=1, source_target_pairs={{0,24},{4,28},{8,16},{12,20},{16,8},{20,12},{24,0},{28,4},{1,25},{... | collective-permute-start | bytes 786440 | tf_op jit(solution)/shard_map/ppermute | solution.py:30
  18.8 2.0 %shard_map.77 = (f32[128,1024]{1,0:T(8,128)S(1)}, bf16[128,1024]{1,0:T(8,128)(2,1)S(1)}, bf16[128,1024]{1,0:T(8,128)(2,1)S(1)}, bf16[128,1024]{1,0:T(8,128)(2,1)S(1)}) custom-call(bf16[128,640]{1,0:T(8,128)(2,1)S(1)} %get-tuple-element.30.refs_0_, bf16[128,640]{1,0:T(8,128)(2,1)S(1)} %collective-permute-done.refs_1_, ...), custom_call_target="tpu_custom_call" | custom-call | flops 1073741824 | bytes 2097152 | tf_op jit(solution)/shard_map/pallas_call | solution.py:329
  20.8 0.0 copy-start.1
  20.8 0.0 copy-start.3
  20.8 3.7 %collective-permute-done.14.refs_0_ = bf16[128,1024]{1,0:T(8,128)(2,1)S(1)} collective-permute-done((bf16[128,1024]{1,0:T(8,128)(2,1)S(1)}, bf16[128,1024]{1,0:T(8,128)(2,1)S(1)}, u32[]{:S(2)}, u32[]{:S(2)}) %collective-permute-start.14) | collective-permute-done | bytes 262176 | tf_op jit(solution)/shard_map/ppermute | solution.py:30
  24.5 0.5 collective-permute-start.4
  25.0 3.1 %collective-permute-done.15.refs_1_ = bf16[128,1024]{1,0:T(8,128)(2,1)S(1)} collective-permute-done((bf16[128,1024]{1,0:T(8,128)(2,1)S(1)}, bf16[128,1024]{1,0:T(8,128)(2,1)S(1)}, u32[]{:S(2)}, u32[]{:S(2)}) %collective-permute-start.15) | collective-permute-done | bytes 262176 | tf_op jit(solution)/shard_map/ppermute | solution.py:30
  28.1 1.2 %collective-permute-start.5 = (bf16[128,1024]{1,0:T(8,128)(2,1)S(1)}, bf16[128,1024]{1,0:T(8,128)(2,1)S(1)}, u32[]{:S(2)}, u32[]{:S(2)}) collective-permute-start(bf16[128,1024]{1,0:T(8,128)(2,1)S(1)} %get-tuple-element.36), channel_id=1, source_target_pairs={{0,16},{4,20},{8,24},{12,28},{16,0},{20,4},{24,8},{28,12},{1,17},{... | collective-permute-start | bytes 786440 | tf_op jit(solution)/shard_map/ppermute | solution.py:30
  29.3 0.8 collective-permute-done.16.refs_2_
  30.1 1.5 %collective-permute-start.6 = (bf16[128,1024]{1,0:T(8,128)(2,1)S(1)}, bf16[128,1024]{1,0:T(8,128)(2,1)S(1)}, u32[]{:S(2)}, u32[]{:S(2)}) collective-permute-start(bf16[128,1024]{1,0:T(8,128)(2,1)S(1)} %get-tuple-element.37), channel_id=1, source_target_pairs={{0,24},{4,28},{8,16},{12,20},{16,8},{20,12},{24,0},{28,4},{1,25},{... | collective-permute-start | bytes 786440 | tf_op jit(solution)/shard_map/ppermute | solution.py:30
  31.6 0.1 shard_map.82.g_ref
  31.7 4.1 %collective-permute-done.4.refs_0_ = bf16[128,1024]{1,0:T(8,128)(2,1)S(1)} collective-permute-done((bf16[128,1024]{1,0:T(8,128)(2,1)S(1)}, bf16[128,1024]{1,0:T(8,128)(2,1)S(1)}, u32[]{:S(2)}, u32[]{:S(2)}) %collective-permute-start.4) | collective-permute-done | bytes 262176 | tf_op jit(solution)/shard_map/ppermute | solution.py:30
  35.8 0.5 collective-permute-start.17
  36.2 3.9 %collective-permute-done.5.refs_1_ = bf16[128,1024]{1,0:T(8,128)(2,1)S(1)} collective-permute-done((bf16[128,1024]{1,0:T(8,128)(2,1)S(1)}, bf16[128,1024]{1,0:T(8,128)(2,1)S(1)}, u32[]{:S(2)}, u32[]{:S(2)}) %collective-permute-start.5) | collective-permute-done | bytes 262176 | tf_op jit(solution)/shard_map/ppermute | solution.py:30
  40.1 0.1 shard_map.78.g_ref
  40.2 0.5 collective-permute-start.9
  40.7 2.7 %collective-permute-done.17.right_g = bf16[128,1024]{1,0:T(8,128)(2,1)S(1)} collective-permute-done((bf16[128,1024]{1,0:T(8,128)(2,1)S(1)}, bf16[128,1024]{1,0:T(8,128)(2,1)S(1)}, u32[]{:S(2)}, u32[]{:S(2)}) %collective-permute-start.17) | collective-permute-done | bytes 262176 | tf_op jit(solution)/shard_map/ppermute | solution.py:268
  43.5 1.1 %shard_map.83 = (f32[3,8,128]{2,1,0:T(8,128)S(1)}, f32[3,8,128]{2,1,0:T(8,128)S(1)}) custom-call(bf16[1,128,2048]{2,1,0:T(8,128)(2,1)S(1)} %copy-done.1, bf16[2,1,128,2048]{3,2,1,0:T(8,128)(2,1)S(1)} %copy-done, bf16[128,1024]{1,0:T(8,128)(2,1)S(1)} %shard_map.82.g_ref, bf16[2,128,2048]{2,1,0:T(8,128)(2,1)S(1)} %collective-permute-done.7.side1, ...), custom_call_target="tpu_custom_call" | custom-call | flops 201326592 | bytes 2621440 | tf_op jit(solution)/shard_map/pallas_call | solution.py:356
  44.6 0.5 collective-permute-start.19
  45.1 3.1 %collective-permute-start.18 = (f32[3,8,128]{2,1,0:T(8,128)S(1)}, f32[3,8,128]{2,1,0:T(8,128)S(1)}, u32[]{:S(2)}, u32[]{:S(2)}) collective-permute-start(f32[3,8,128]{2,1,0:T(8,128)S(1)} %get-tuple-element.51.far_stats), channel_id=1, source_target_pairs={{0,1},{1,2},{2,3},{3,0},{4,5},{5,6},{6,7},{7,4},{8,9},{9,10},{10,1... | collective-permute-start | bytes 36872 | tf_op jit(solution)/shard_map/ppermute | solution.py:268
  48.2 1.1 %shard_map.79 = (f32[3,8,128]{2,1,0:T(8,128)S(1)}, f32[3,8,128]{2,1,0:T(8,128)S(1)}) custom-call(bf16[1,128,2048]{2,1,0:T(8,128)(2,1)S(1)} %copy-done.1, bf16[2,1,128,2048]{3,2,1,0:T(8,128)(2,1)S(1)} %copy-done, bf16[128,1024]{1,0:T(8,128)(2,1)S(1)} %shard_map.78.g_ref, bf16[2,128,2048]{2,1,0:T(8,128)(2,1)S(1)} %collective-permute-done.7.side1, ...), custom_call_target="tpu_custom_call" | custom-call | flops 201326592 | bytes 2621440 | tf_op jit(solution)/shard_map/pallas_call | solution.py:356
  49.3 0.4 collective-permute-start.11
  49.7 3.5 %collective-permute-start.10 = (f32[3,8,128]{2,1,0:T(8,128)S(1)}, f32[3,8,128]{2,1,0:T(8,128)S(1)}, u32[]{:S(2)}, u32[]{:S(2)}) collective-permute-start(f32[3,8,128]{2,1,0:T(8,128)S(1)} %get-tuple-element.41.far_stats), channel_id=1, source_target_pairs={{0,1},{1,2},{2,3},{3,0},{4,5},{5,6},{6,7},{7,4},{8,9},{9,10},{10,1... | collective-permute-start | bytes 36872 | tf_op jit(solution)/shard_map/ppermute | solution.py:268
  53.2 2.7 %shard_map.84 = (f32[128,1024]{1,0:T(8,128)S(1)}, f32[2,128,1024]{2,1,0:T(8,128)S(1)}, bf16[2,128,1024]{2,1,0:T(8,128)(2,1)S(1)}, bf16[2,128,1024]{2,1,0:T(8,128)(2,1)S(1)}) custom-call(bf16[1,128,2048]{2,1,0:T(8,128)(2,1)S(1)} %copy-done.1, bf16[2,1,128,2048]{3,2,1,0:T(8,128)(2,1)S(1)} %copy-done, bf16[128,1024]{1,0:T(8,128)(2,1)S(1)} %shard_map.82.g_ref, ...), custom_call_target="tpu_custom_call" | custom-call | flops 503316480 | bytes 5242880 | tf_op jit(solution)/shard_map/pallas_call | solution.py:364
  55.8 3.8 %collective-permute-start.20 = (bf16[2,128,1024]{2,1,0:T(8,128)(2,1)S(1)}, bf16[2,128,1024]{2,1,0:T(8,128)(2,1)S(1)}, u32[]{:S(2)}, u32[]{:S(2)}) collective-permute-start(bf16[2,128,1024]{2,1,0:T(8,128)(2,1)S(1)} %get-tuple-element.54), channel_id=1, source_target_pairs={{0,1},{1,0},{2,3},{3,2},{4,5},{5,4},{6,7},{7,6},{8,9},{9,8},{10,11... | collective-permute-start | bytes 1572872 | tf_op jit(solution)/shard_map/ppermute | solution.py:276
  59.7 1.9 %collective-permute-start.21 = (bf16[2,128,1024]{2,1,0:T(8,128)(2,1)S(1)}, bf16[2,128,1024]{2,1,0:T(8,128)(2,1)S(1)}, u32[]{:S(2)}, u32[]{:S(2)}) collective-permute-start(bf16[2,128,1024]{2,1,0:T(8,128)(2,1)S(1)} %get-tuple-element.55), channel_id=1, source_target_pairs={{0,0},{1,2},{2,1},{3,3},{4,4},{5,6},{6,5},{7,7},{8,8},{9,10},{10,9... | collective-permute-start | bytes 1572872 | tf_op jit(solution)/shard_map/ppermute | solution.py:276
  61.6 2.9 %shard_map.80 = (f32[128,1024]{1,0:T(8,128)S(1)}, f32[2,128,1024]{2,1,0:T(8,128)S(1)}, bf16[2,128,1024]{2,1,0:T(8,128)(2,1)S(1)}, bf16[2,128,1024]{2,1,0:T(8,128)(2,1)S(1)}) custom-call(bf16[1,128,2048]{2,1,0:T(8,128)(2,1)S(1)} %copy-done.1, bf16[2,1,128,2048]{3,2,1,0:T(8,128)(2,1)S(1)} %copy-done, bf16[128,1024]{1,0:T(8,128)(2,1)S(1)} %shard_map.78.g_ref, ...), custom_call_target="tpu_custom_call" | custom-call | flops 503316480 | bytes 5242880 | tf_op jit(solution)/shard_map/pallas_call | solution.py:364
  64.5 0.1 collective-permute-start.12
  64.5 3.9 %collective-permute-start.13 = (bf16[2,128,1024]{2,1,0:T(8,128)(2,1)S(1)}, bf16[2,128,1024]{2,1,0:T(8,128)(2,1)S(1)}, u32[]{:S(2)}, u32[]{:S(2)}) collective-permute-start(bf16[2,128,1024]{2,1,0:T(8,128)(2,1)S(1)} %get-tuple-element.45), channel_id=1, source_target_pairs={{0,0},{1,2},{2,1},{3,3},{4,4},{5,6},{6,5},{7,7},{8,8},{9,10},{10,9... | collective-permute-start | bytes 1572872 | tf_op jit(solution)/shard_map/ppermute | solution.py:276
  68.5 4.0 %collective-permute-done.20.got1 = bf16[2,128,1024]{2,1,0:T(8,128)(2,1)S(1)} collective-permute-done((bf16[2,128,1024]{2,1,0:T(8,128)(2,1)S(1)}, bf16[2,128,1024]{2,1,0:T(8,128)(2,1)S(1)}, u32[]{:S(2)}, u32[]{:S(2)}) %collective-permute-start.20) | collective-permute-done | bytes 524320 | tf_op jit(solution)/shard_map/ppermute | solution.py:276
  72.4 3.9 %collective-permute-done.21.got2 = bf16[2,128,1024]{2,1,0:T(8,128)(2,1)S(1)} collective-permute-done((bf16[2,128,1024]{2,1,0:T(8,128)(2,1)S(1)}, bf16[2,128,1024]{2,1,0:T(8,128)(2,1)S(1)}, u32[]{:S(2)}, u32[]{:S(2)}) %collective-permute-start.21) | collective-permute-done | bytes 524320 | tf_op jit(solution)/shard_map/ppermute | solution.py:276
  76.3 1.1 %shard_map.85 = (bf16[1,128,2048]{2,1,0:T(8,128)(2,1)}, bf16[2,1,128,2048]{3,2,1,0:T(8,128)(2,1)}) custom-call(f32[128,1024]{1,0:T(8,128)S(1)} %get-tuple-element.52.dq_ref, f32[2,128,1024]{2,1,0:T(8,128)S(1)} %get-tuple-element.53.dkv_ref, bf16[2,128,1024]{2,1,0:T(8,128)(2,1)S(1)} %collective-permute-done.20.got1, ...), custom_call_target="tpu_custom_call" | custom-call | bytes 2621440 | tf_op jit(solution)/shard_map/pallas_call | solution.py:377
  77.4 2.8 %collective-permute-done.12.got1 = bf16[2,128,1024]{2,1,0:T(8,128)(2,1)S(1)} collective-permute-done((bf16[2,128,1024]{2,1,0:T(8,128)(2,1)S(1)}, bf16[2,128,1024]{2,1,0:T(8,128)(2,1)S(1)}, u32[]{:S(2)}, u32[]{:S(2)}) %collective-permute-start.12) | collective-permute-done | bytes 524320 | tf_op jit(solution)/shard_map/ppermute | solution.py:276
  80.2 3.2 %collective-permute-done.13.got2 = bf16[2,128,1024]{2,1,0:T(8,128)(2,1)S(1)} collective-permute-done((bf16[2,128,1024]{2,1,0:T(8,128)(2,1)S(1)}, bf16[2,128,1024]{2,1,0:T(8,128)(2,1)S(1)}, u32[]{:S(2)}, u32[]{:S(2)}) %collective-permute-start.13) | collective-permute-done | bytes 524320 | tf_op jit(solution)/shard_map/ppermute | solution.py:276
  83.5 1.1 %shard_map.86 = (bf16[1,128,2048]{2,1,0:T(8,128)(2,1)}, bf16[2,1,128,2048]{3,2,1,0:T(8,128)(2,1)}) custom-call(f32[128,1024]{1,0:T(8,128)S(1)} %get-tuple-element.42.dq_ref, f32[2,128,1024]{2,1,0:T(8,128)S(1)} %get-tuple-element.43.dkv_ref, bf16[2,128,1024]{2,1,0:T(8,128)(2,1)S(1)} %collective-permute-done.12.got1, ...), custom_call_target="tpu_custom_call", output_to_operand_aliasing={{0}: (4, {}), {1}: (5, {})} | custom-call | bytes 2621440 | tf_op jit(solution)/shard_map/pallas_call | solution.py:377
  (16 shorter events, 0.0 us)
Async XLA Ops:
  0.6 12.6 %copy-start.2 = (bf16[2,2048,256]{2,1,0:T(8,128)(2,1)S(1)}, bf16[2,2048,256]{2,1,0:T(8,128)(2,1)}, u32[]{:S(2)}) copy-start(bf16[2,2048,256]{2,1,0:T(8,128)(2,1)} %refs_4_.3) | copy-start | bytes 6291460
  0.6 12.6 %collective-permute-start.3 = (bf16[2,2048,256]{2,1,0:T(8,128)(2,1)}, bf16[2,2048,256]{2,1,0:T(8,128)(2,1)S(1)}, u32[]{:S(2)}, u32[]{:S(2)}) collective-permute-start(bf16[2,2048,256]{2,1,0:T(8,128)(2,1)} %refs_4_.3), channel_id=1, source_target_pairs={{0,4},{4,0},{8,12},{12,8},{16,20},{20,16},{24,28},{28,24},{1,5},{5... | collective-permute-start | bytes 6291464 | tf_op jit(solution)/shard_map/ppermute | solution.py:30
  2.0 7.1 %collective-permute-start = (bf16[128,640]{1,0:T(8,128)(2,1)S(1)}, bf16[128,640]{1,0:T(8,128)(2,1)S(1)}, u32[]{:S(2)}, u32[]{:S(2)}) collective-permute-start(bf16[128,640]{1,0:T(8,128)(2,1)S(1)} %get-tuple-element.31), channel_id=1, source_target_pairs={{0,8},{4,12},{8,0},{12,4},{16,24},{20,28},{24,16},{28,20},{1,9},{5... | collective-permute-start | bytes 491528 | tf_op jit(solution)/shard_map/ppermute | solution.py:30
  3.6 9.7 %collective-permute-start.1 = (bf16[128,640]{1,0:T(8,128)(2,1)S(1)}, bf16[128,640]{1,0:T(8,128)(2,1)S(1)}, u32[]{:S(2)}, u32[]{:S(2)}) collective-permute-start(bf16[128,640]{1,0:T(8,128)(2,1)S(1)} %get-tuple-element.32), channel_id=1, source_target_pairs={{0,16},{4,20},{8,24},{12,28},{16,0},{20,4},{24,8},{28,12},{1,17},{... | collective-permute-start | bytes 491528 | tf_op jit(solution)/shard_map/ppermute | solution.py:30
  4.1 9.2 %collective-permute-start.2 = (bf16[128,640]{1,0:T(8,128)(2,1)S(1)}, bf16[128,640]{1,0:T(8,128)(2,1)S(1)}, u32[]{:S(2)}, u32[]{:S(2)}) collective-permute-start(bf16[128,640]{1,0:T(8,128)(2,1)S(1)} %get-tuple-element.33), channel_id=1, source_target_pairs={{0,24},{4,28},{8,16},{12,20},{16,8},{20,12},{24,0},{28,4},{1,25},{... | collective-permute-start | bytes 491528 | tf_op jit(solution)/shard_map/ppermute | solution.py:30
  7.1 33.6 %collective-permute-start.7 = (bf16[2,128,2048]{2,1,0:T(8,128)(2,1)S(1)}, bf16[2,128,2048]{2,1,0:T(8,128)(2,1)S(1)}, u32[]{:S(2)}, u32[]{:S(2)}) collective-permute-start(bf16[2,128,2048]{2,1,0:T(8,128)(2,1)S(1)} %get-tuple-element.38), channel_id=1, source_target_pairs={{0,1},{1,0},{2,3},{3,2},{4,5},{5,4},{6,7},{7,6},{8,9},{9,8},{10,11... | collective-permute-start | bytes 3145736 | tf_op jit(solution)/shard_map/ppermute | solution.py:276
  9.2 31.6 %collective-permute-start.8 = (bf16[2,128,2048]{2,1,0:T(8,128)(2,1)S(1)}, bf16[2,128,2048]{2,1,0:T(8,128)(2,1)S(1)}, u32[]{:S(2)}, u32[]{:S(2)}) collective-permute-start(bf16[2,128,2048]{2,1,0:T(8,128)(2,1)S(1)} %get-tuple-element.39), channel_id=1, source_target_pairs={{0,0},{1,2},{2,1},{3,3},{4,4},{5,6},{6,5},{7,7},{8,8},{9,10},{10,9... | collective-permute-start | bytes 3145736 | tf_op jit(solution)/shard_map/ppermute | solution.py:276
  15.3 9.2 %collective-permute-start.14 = (bf16[128,1024]{1,0:T(8,128)(2,1)S(1)}, bf16[128,1024]{1,0:T(8,128)(2,1)S(1)}, u32[]{:S(2)}, u32[]{:S(2)}) collective-permute-start(bf16[128,1024]{1,0:T(8,128)(2,1)S(1)} %get-tuple-element.47), channel_id=1, source_target_pairs={{0,8},{4,12},{8,0},{12,4},{16,24},{20,28},{24,16},{28,20},{1,9},{5... | collective-permute-start | bytes 786440 | tf_op jit(solution)/shard_map/ppermute | solution.py:30
  15.9 12.3 %collective-permute-start.15 = (bf16[128,1024]{1,0:T(8,128)(2,1)S(1)}, bf16[128,1024]{1,0:T(8,128)(2,1)S(1)}, u32[]{:S(2)}, u32[]{:S(2)}) collective-permute-start(bf16[128,1024]{1,0:T(8,128)(2,1)S(1)} %get-tuple-element.48), channel_id=1, source_target_pairs={{0,16},{4,20},{8,24},{12,28},{16,0},{20,4},{24,8},{28,12},{1,17},{... | collective-permute-start | bytes 786440 | tf_op jit(solution)/shard_map/ppermute | solution.py:30
  17.0 13.1 %collective-permute-start.16 = (bf16[128,1024]{1,0:T(8,128)(2,1)S(1)}, bf16[128,1024]{1,0:T(8,128)(2,1)S(1)}, u32[]{:S(2)}, u32[]{:S(2)}) collective-permute-start(bf16[128,1024]{1,0:T(8,128)(2,1)S(1)} %get-tuple-element.49), channel_id=1, source_target_pairs={{0,24},{4,28},{8,16},{12,20},{16,8},{20,12},{24,0},{28,4},{1,25},{... | collective-permute-start | bytes 786440 | tf_op jit(solution)/shard_map/ppermute | solution.py:30
  20.8 22.7 %copy-start = (bf16[2,1,128,2048]{3,2,1,0:T(8,128)(2,1)S(1)}, bf16[2,1,128,2048]{3,2,1,0:T(8,128)(2,1)}, u32[]{:S(2)}) copy-start(bf16[2,1,128,2048]{3,2,1,0:T(8,128)(2,1)} %kv_ref.9) | copy-start | bytes 3145732
  20.8 22.7 %copy-start.1 = (bf16[1,128,2048]{2,1,0:T(8,128)(2,1)S(1)}, bf16[1,128,2048]{2,1,0:T(8,128)(2,1)}, u32[]{:S(2)}) copy-start(bf16[1,128,2048]{2,1,0:T(8,128)(2,1)} %q_ref.9) | copy-start | bytes 1572868
  20.8 22.7 %copy-start.3 = (s32[1,512]{1,0:T(1,128)S(1)}, s32[1,512]{1,0:T(1,128)}, u32[]{:S(2)}) copy-start(s32[1,512]{1,0:T(1,128)} %segs.7) | copy-start | bytes 6148
  24.5 11.3 %collective-permute-start.4 = (bf16[128,1024]{1,0:T(8,128)(2,1)S(1)}, bf16[128,1024]{1,0:T(8,128)(2,1)S(1)}, u32[]{:S(2)}, u32[]{:S(2)}) collective-permute-start(bf16[128,1024]{1,0:T(8,128)(2,1)S(1)} %get-tuple-element.35), channel_id=1, source_target_pairs={{0,8},{4,12},{8,0},{12,4},{16,24},{20,28},{24,16},{28,20},{1,9},{5... | collective-permute-start | bytes 786440 | tf_op jit(solution)/shard_map/ppermute | solution.py:30
  28.1 12.0 %collective-permute-start.5 = (bf16[128,1024]{1,0:T(8,128)(2,1)S(1)}, bf16[128,1024]{1,0:T(8,128)(2,1)S(1)}, u32[]{:S(2)}, u32[]{:S(2)}) collective-permute-start(bf16[128,1024]{1,0:T(8,128)(2,1)S(1)} %get-tuple-element.36), channel_id=1, source_target_pairs={{0,16},{4,20},{8,24},{12,28},{16,0},{20,4},{24,8},{28,12},{1,17},{... | collective-permute-start | bytes 786440 | tf_op jit(solution)/shard_map/ppermute | solution.py:30
  30.1 10.0 %collective-permute-start.6 = (bf16[128,1024]{1,0:T(8,128)(2,1)S(1)}, bf16[128,1024]{1,0:T(8,128)(2,1)S(1)}, u32[]{:S(2)}, u32[]{:S(2)}) collective-permute-start(bf16[128,1024]{1,0:T(8,128)(2,1)S(1)} %get-tuple-element.37), channel_id=1, source_target_pairs={{0,24},{4,28},{8,16},{12,20},{16,8},{20,12},{24,0},{28,4},{1,25},{... | collective-permute-start | bytes 786440 | tf_op jit(solution)/shard_map/ppermute | solution.py:30
  35.8 7.7 %collective-permute-start.17 = (bf16[128,1024]{1,0:T(8,128)(2,1)S(1)}, bf16[128,1024]{1,0:T(8,128)(2,1)S(1)}, u32[]{:S(2)}, u32[]{:S(2)}) collective-permute-start(bf16[128,1024]{1,0:T(8,128)(2,1)S(1)} %shard_map.82.g_ref), channel_id=1, source_target_pairs={{0,3},{1,0},{2,1},{3,2},{4,7},{5,4},{6,5},{7,6},{8,11},{9,8},{10,9... | collective-permute-start | bytes 786440 | tf_op jit(solution)/shard_map/ppermute | solution.py:268
  40.2 7.9 %collective-permute-start.9 = (bf16[128,1024]{1,0:T(8,128)(2,1)S(1)}, bf16[128,1024]{1,0:T(8,128)(2,1)S(1)}, u32[]{:S(2)}, u32[]{:S(2)}) collective-permute-start(bf16[128,1024]{1,0:T(8,128)(2,1)S(1)} %shard_map.78.g_ref), channel_id=1, source_target_pairs={{0,3},{1,0},{2,1},{3,2},{4,7},{5,4},{6,5},{7,6},{8,11},{9,8},{10,9... | collective-permute-start | bytes 786440 | tf_op jit(solution)/shard_map/ppermute | solution.py:268
  44.6 8.6 %collective-permute-start.19 = (f32[3,8,128]{2,1,0:T(8,128)S(1)}, f32[3,8,128]{2,1,0:T(8,128)S(1)}, u32[]{:S(2)}, u32[]{:S(2)}) collective-permute-start(f32[3,8,128]{2,1,0:T(8,128)S(1)} %get-tuple-element.50.own_stats), channel_id=1, source_target_pairs={{0,3},{1,0},{2,1},{3,2},{4,7},{5,4},{6,5},{7,6},{8,11},{9,8},{10,9... | collective-permute-start | bytes 36872 | tf_op jit(solution)/shard_map/ppermute | solution.py:268
  45.1 8.1 %collective-permute-start.18 = (f32[3,8,128]{2,1,0:T(8,128)S(1)}, f32[3,8,128]{2,1,0:T(8,128)S(1)}, u32[]{:S(2)}, u32[]{:S(2)}) collective-permute-start(f32[3,8,128]{2,1,0:T(8,128)S(1)} %get-tuple-element.51.far_stats), channel_id=1, source_target_pairs={{0,1},{1,2},{2,3},{3,0},{4,5},{5,6},{6,7},{7,4},{8,9},{9,10},{10,1... | collective-permute-start | bytes 36872 | tf_op jit(solution)/shard_map/ppermute | solution.py:268
  49.3 12.3 %collective-permute-start.11 = (f32[3,8,128]{2,1,0:T(8,128)S(1)}, f32[3,8,128]{2,1,0:T(8,128)S(1)}, u32[]{:S(2)}, u32[]{:S(2)}) collective-permute-start(f32[3,8,128]{2,1,0:T(8,128)S(1)} %get-tuple-element.40.own_stats), channel_id=1, source_target_pairs={{0,3},{1,0},{2,1},{3,2},{4,7},{5,4},{6,5},{7,6},{8,11},{9,8},{10,9... | collective-permute-start | bytes 36872 | tf_op jit(solution)/shard_map/ppermute | solution.py:268
  49.7 11.9 %collective-permute-start.10 = (f32[3,8,128]{2,1,0:T(8,128)S(1)}, f32[3,8,128]{2,1,0:T(8,128)S(1)}, u32[]{:S(2)}, u32[]{:S(2)}) collective-permute-start(f32[3,8,128]{2,1,0:T(8,128)S(1)} %get-tuple-element.41.far_stats), channel_id=1, source_target_pairs={{0,1},{1,2},{2,3},{3,0},{4,5},{5,6},{6,7},{7,4},{8,9},{9,10},{10,1... | collective-permute-start | bytes 36872 | tf_op jit(solution)/shard_map/ppermute | solution.py:268
  55.8 16.6 %collective-permute-start.20 = (bf16[2,128,1024]{2,1,0:T(8,128)(2,1)S(1)}, bf16[2,128,1024]{2,1,0:T(8,128)(2,1)S(1)}, u32[]{:S(2)}, u32[]{:S(2)}) collective-permute-start(bf16[2,128,1024]{2,1,0:T(8,128)(2,1)S(1)} %get-tuple-element.54), channel_id=1, source_target_pairs={{0,1},{1,0},{2,3},{3,2},{4,5},{5,4},{6,7},{7,6},{8,9},{9,8},{10,11... | collective-permute-start | bytes 1572872 | tf_op jit(solution)/shard_map/ppermute | solution.py:276
  59.7 16.7 %collective-permute-start.21 = (bf16[2,128,1024]{2,1,0:T(8,128)(2,1)S(1)}, bf16[2,128,1024]{2,1,0:T(8,128)(2,1)S(1)}, u32[]{:S(2)}, u32[]{:S(2)}) collective-permute-start(bf16[2,128,1024]{2,1,0:T(8,128)(2,1)S(1)} %get-tuple-element.55), channel_id=1, source_target_pairs={{0,0},{1,2},{2,1},{3,3},{4,4},{5,6},{6,5},{7,7},{8,8},{9,10},{10,9... | collective-permute-start | bytes 1572872 | tf_op jit(solution)/shard_map/ppermute | solution.py:276
  64.5 15.8 %collective-permute-start.12 = (bf16[2,128,1024]{2,1,0:T(8,128)(2,1)S(1)}, bf16[2,128,1024]{2,1,0:T(8,128)(2,1)S(1)}, u32[]{:S(2)}, u32[]{:S(2)}) collective-permute-start(bf16[2,128,1024]{2,1,0:T(8,128)(2,1)S(1)} %get-tuple-element.44), channel_id=1, source_target_pairs={{0,1},{1,0},{2,3},{3,2},{4,5},{5,4},{6,7},{7,6},{8,9},{9,8},{10,11... | collective-permute-start | bytes 1572872 | tf_op jit(solution)/shard_map/ppermute | solution.py:276
  64.5 18.9 %collective-permute-start.13 = (bf16[2,128,1024]{2,1,0:T(8,128)(2,1)S(1)}, bf16[2,128,1024]{2,1,0:T(8,128)(2,1)S(1)}, u32[]{:S(2)}, u32[]{:S(2)}) collective-permute-start(bf16[2,128,1024]{2,1,0:T(8,128)(2,1)S(1)} %get-tuple-element.45), channel_id=1, source_target_pairs={{0,0},{1,2},{2,1},{3,3},{4,4},{5,6},{6,5},{7,7},{8,8},{9,10},{10,9... | collective-permute-start | bytes 1572872 | tf_op jit(solution)/shard_map/ppermute | solution.py:276

commit v2 on v1

v2 whole, which is shorter than its diff:
```python
import functools
import jax
import jax.numpy as jnp
from jax import lax
from jax.experimental import pallas as pl
from jax.experimental.pallas import tpu as pltpu
from jax.sharding import PartitionSpec as P


HEADS = 16
HEAD_DIM = 128
CHUNKS = 2

NEG = -1e30
LANES = 128
BF16 = jnp.bfloat16
F32 = jnp.float32
NT = (((1,), (1,)), ((), ()))
TN = (((0,), (0,)), ((), ()))


def params(mib):
    return pltpu.CompilerParams(vmem_limit_bytes=mib << 20)


def lane_slice(start, size):
    return pl.ds(pl.multiple_of(start, LANES), size)


def swap(value, axis, bits):
    return lax.ppermute(value, axis, [(i, i ^ bits) for i in range(lax.axis_size(axis))])


def column_of(row):
    n = row.shape[1]
    same = lax.broadcasted_iota(jnp.int32, (n, n), 0) == lax.broadcasted_iota(jnp.int32, (n, n), 1)
    return jnp.sum(jnp.where(same, row.astype(F32), 0.0), axis=1, keepdims=True)


def slices_kernel(grad_ref, tags_ref, q_ref, kv_ref, *refs):
    outs, (first, second, v_out), (tags, tag_sem, sem) = refs[:-6], refs[-6:-3], refs[-3:]
    chip = lax.axis_index("dp") // 2
    even = lax.axis_index("seq") % 2 == 0
    width = outs[0].shape[1] - LANES
    tag_copy = pltpu.make_async_copy(tags_ref, tags, tag_sem)
    copies = [
        pltpu.make_async_copy(grad_ref.at[0, :, lane_slice((chip ^ k) * width, width)], out.at[:, :width], sem.at[k])
        for k, out in enumerate(outs)
    ]
    count = len(outs)
    v_copy = pltpu.make_async_copy(kv_ref.at[1, 0], v_out, sem.at[count])
    for copy in [tag_copy] + copies:
        copy.start()

    def sides(up, down):
        both = [
            pltpu.make_async_copy(kv_ref.at[0, 0], up, sem.at[count + 1]),
            pltpu.make_async_copy(q_ref.at[0], down, sem.at[count + 2]),
        ]
        for copy in both:
            copy.start()
        for copy in both:
            copy.wait()

    @pl.when(even)
    def _():
        sides(first, second)

    @pl.when(jnp.logical_not(even))
    def _():
        sides(second, first)

    v_copy.start()
    tag_copy.wait()
    tag = jnp.broadcast_to(column_of(tags[...]), (grad_ref.shape[1], LANES)).astype(BF16)
    for out in outs:
        out[:, width:] = tag
    for copy in copies + [v_copy]:
        copy.wait()


def project_kernel(chips, *refs):
    grads, (own_w, other_w), (mine, *parts, lhs) = refs[:chips], refs[chips : chips + 2], refs[chips + 2 :]
    rows = grads[0].shape[0]
    depth = own_w.shape[2]
    core = lax.axis_index("dp") % 2

    @pl.when(pl.program_id(0) == 0)
    def _():
        for k, grad in enumerate(grads):
            text = grad[:, 2 * depth : 2 * depth + 1] == 1
            for side in range(2):
                g = grad[:, lane_slice((core ^ side) * depth, depth)]
                lhs[side, 0, k * rows : (k + 1) * rows] = jnp.where(text, jnp.zeros_like(g), g)
                lhs[side, 1, k * rows : (k + 1) * rows] = jnp.where(text, g, jnp.zeros_like(g))

    total = None
    for side, w in enumerate((own_w, other_w)):
        for kind in range(2):
            term = lax.dot_general(lhs[side, kind], w[kind], NT, preferred_element_type=F32)
            total = term if total is None else total + term
    mine[...] = total[:rows]
    for k, part in enumerate(parts):
        part[...] = total[(k + 1) * rows : (k + 2) * rows].astype(BF16)


def split(values):
    high = values.astype(BF16)
    return jnp.concatenate([high, (values - high.astype(F32)).astype(BF16)], axis=0)


def joined(pieces):
    half = pieces.shape[0] // 2
    return pieces[:half].astype(F32) + pieces[half:].astype(F32)


def masks(count, segs, index, rows):
    def segment(back):
        at = jnp.clip(index + back, 0, count - 1)
        return segs[:, lane_slice(at * rows, rows)].astype(F32)

    left, own, right = segment(-1), segment(0), segment(1)
    left_at, own_at = column_of(left), column_of(own)
    no_left, no_right = index == 0, index == count - 1
    key = lax.broadcasted_iota(jnp.int32, (rows, rows), 0)
    query = lax.broadcasted_iota(jnp.int32, (rows, rows), 1)
    return (
        (left_at == own) & jnp.logical_not(no_left),
        (left_at == right) & jnp.logical_not(no_left | no_right),
        (own_at == own) & (key <= query),
        (own_at == right) & jnp.logical_not(no_right),
    )


def score(keys, queries, scale, mask):
    s = lax.dot_general(keys, queries, NT, preferred_element_type=F32) * scale
    return jnp.where(mask, s, NEG)


def pair_of(even, to_even, to_odd):
    def copy(items):
        for source, target in items:
            target[...] = source[...]

    @pl.when(even)
    def _():
        copy(to_even)

    @pl.when(jnp.logical_not(even))
    def _():
        copy(to_odd)


def stats_kernel(count, scale, q_ref, kv_ref, got1, got2, segs, own_out, far_out, left_k, right_q):
    index = lax.axis_index("seq")
    rows, hc = left_k.shape
    pair_of(index % 2 == 0, [(got2, left_k), (got1, right_q)], [(got1, left_k), (got2, right_q)])
    pre, far, own, _ = masks(count, segs, index, rows)
    for h in range(hc // HEAD_DIM):
        at = slice(h * HEAD_DIM, (h + 1) * HEAD_DIM)
        kl, q = left_k[:, at], q_ref[0, :, at]
        s_pre = score(kl, q, scale, pre)
        s_own = score(kv_ref[0, 0, :, at], q, scale, own)
        s_far = score(kl, right_q[:, at], scale, far)
        top = jnp.max(jnp.maximum(s_pre, s_own), axis=0, keepdims=True)
        own_out[0, h : h + 1] = top
        own_out[1, h : h + 1] = jnp.sum(jnp.exp(s_pre - top) + jnp.exp(s_own - top), axis=0, keepdims=True)
        top = jnp.max(s_far, axis=0, keepdims=True)
        far_out[0, h : h + 1] = top
        far_out[1, h : h + 1] = jnp.sum(jnp.exp(s_far - top), axis=0, keepdims=True)


def merged(one, two):
    top = jnp.maximum(one[0], two[0])
    return top, 1.0 / (one[1] * jnp.exp(one[0] - top) + two[1] * jnp.exp(two[0] - top))


def own_rows(index, own_stats, from_left, heads):
    no_left = index == 0
    far = (jnp.where(no_left, NEG, from_left[0, heads]), jnp.where(no_left, 0.0, from_left[1, heads]))
    return merged((own_stats[0, heads], own_stats[1, heads]), far)


def right_rows(index, count, far_stats, from_right, heads):
    no_right = index == count - 1
    own = (jnp.where(no_right, 0.0, from_right[0, heads]), jnp.where(no_right, 1.0, from_right[1, heads]))
    return merged(own, (far_stats[0, heads], far_stats[1, heads]))


def delta_kernel(count, chunk, terms, scale, mine, *refs):
    parts = refs[:terms]
    q_ref, kv_ref, left_k, got1, got2, segs, own_stats, from_left, g_out, d_out, left_v = refs[terms:]
    rows, span = mine.shape
    index = lax.axis_index("seq")
    first = chunk * span
    lanes = slice(first, first + span)
    pair_of(index % 2 == 0, [(got2.at[:, lanes], left_v)], [(got1.at[:, lanes], left_v)])
    total = mine[...]
    for part in parts:
        total = total + part[...].astype(F32)
    g_out[:rows] = total.astype(BF16)
    pre, _, own, _ = masks(count, segs, index, rows)
    heads = span // HEAD_DIM
    top, inv = own_rows(index, own_stats, from_left, slice(chunk * heads, (chunk + 1) * heads))
    for h in range(heads):
        at = slice(h * HEAD_DIM, (h + 1) * HEAD_DIM)
        wide = slice(first + at.start, first + at.stop)
        row = slice(h, h + 1)
        q, g = q_ref[0, :, wide], g_out[:rows, at]
        s_pre = score(left_k[:, wide], q, scale, pre)
        s_own = score(kv_ref[0, 0, :, wide], q, scale, own)
        d_pre = lax.dot_general(left_v[:, at], g, NT, preferred_element_type=F32)
        d_own = lax.dot_general(kv_ref[1, 0, :, wide], g, NT, preferred_element_type=F32)
        terms_ = jnp.exp(s_pre - top[row]) * d_pre + jnp.exp(s_own - top[row]) * d_own
        d_out[row] = jnp.sum(terms_, axis=0, keepdims=True) * inv[row]
    g_out[rows:] = jnp.zeros((2 * heads, span), BF16)
    g_out[rows:, :LANES] = split(d_out[...])


def grads_kernel(count, chunk, scale, q_ref, kv_ref, left_k, left_v, right_q, g_ref, right_g, segs,
                 own_stats, far_stats, from_left, from_right, delta_own,
                 dq_out, dkv_out, p_out, to1, to2, far_delta):
    index = lax.axis_index("seq")
    rows, span = left_v.shape
    first = chunk * span
    heads = span // HEAD_DIM
    chosen = slice(chunk * heads, (chunk + 1) * heads)
    pre, far, own, nxt = masks(count, segs, index, rows)
    top, inv = own_rows(index, own_stats, from_left, chosen)
    r_top, r_inv = right_rows(index, count, far_stats, from_right, chosen)
    right_delta = joined(right_g[rows:, :LANES])

    def run(up_out, down_out):
        for h in range(heads):
            at = slice(h * HEAD_DIM, (h + 1) * HEAD_DIM)
            wide = slice(first + at.start, first + at.stop)
            row = slice(h, h + 1)
            q2 = jnp.concatenate([q_ref[0, :, wide], right_q[:, wide]], axis=0)
            g2 = jnp.concatenate([g_ref[:rows, at], right_g[:rows, at]], axis=0)
            k, kl = kv_ref[0, 0, :, wide], left_k[:, wide]
            s_left = lax.dot_general(kl, q2, NT, preferred_element_type=F32) * scale
            s_here = lax.dot_general(k, q2, NT, preferred_element_type=F32) * scale
            d_left = lax.dot_general(left_v[:, at], g2, NT, preferred_element_type=F32)
            d_own = lax.dot_general(kv_ref[1, 0, :, wide], g2[:rows], NT, preferred_element_type=F32)
            p_pre = jnp.exp(jnp.where(pre, s_left[:, :rows], NEG) - top[row]) * inv[row]
            p_own = jnp.exp(jnp.where(own, s_here[:, :rows], NEG) - top[row]) * inv[row]
            p_far = jnp.exp(jnp.where(far, s_left[:, rows:], NEG) - r_top[row]) * r_inv[row]
            p_nxt = jnp.exp(jnp.where(nxt, s_here[:, rows:], NEG) - r_top[row]) * r_inv[row]
            d_pre, d_far = d_left[:, :rows], d_left[:, rows:]
            extra = jnp.sum(p_far * d_far, axis=0, keepdims=True)
            far_delta[row] = extra
            ds_pre = (p_pre * (d_pre - delta_own[row]) * scale).astype(BF16)
            ds_own = (p_own * (d_own - delta_own[row]) * scale).astype(BF16)
            ds_far = (p_far * (d_far - (right_delta[row] + extra)) * scale).astype(BF16)
            ds_nxt = (p_nxt * (extra * -scale)).astype(BF16)
            p_low = p_pre.astype(BF16)
            p_here = p_own.astype(BF16)
            p_out[h, :rows] = p_low
            p_out[h, rows:] = p_here
            dkv_out[0, :, at] = jnp.dot(
                jnp.concatenate([ds_own, ds_nxt], axis=1), q2, preferred_element_type=F32)
            dkv_out[1, :, at] = jnp.dot(p_here, g2[:rows], preferred_element_type=F32)
            down_out[0, :, at] = jnp.dot(
                jnp.concatenate([ds_pre, ds_far], axis=1), q2, preferred_element_type=F32).astype(BF16)
            down_out[1, :, at] = jnp.dot(
                jnp.concatenate([p_low, p_far.astype(BF16)], axis=1), g2, preferred_element_type=F32).astype(BF16)
            dq_out[:, at] = lax.dot_general(ds_pre, kl, TN, preferred_element_type=F32) + lax.dot_general(
                ds_own, k, TN, preferred_element_type=F32)
            up_out[0, :, at] = lax.dot_general(ds_far, kl, TN, preferred_element_type=F32).astype(BF16)
        up_out[1, : 2 * heads, :LANES] = split(far_delta[...])

    @pl.when(index % 2 == 0)
    def _():
        run(to1, to2)

    @pl.when(index % 2 == 1)
    def _():
        run(to2, to1)


def finish_kernel(count, chunk, scale, dq_ref, dkv_ref, p_ref, q_ref, kv_ref, left_k, got1, got2, *refs):
    grad_q, grad_kv = refs[-2:]
    index = lax.axis_index("seq")
    rows, span = dq_ref.shape
    heads = span // HEAD_DIM
    first = chunk * span

    def add(from_left, from_right):
        no_left, no_right = index == 0, index == count - 1
        delta = jnp.where(no_left, 0.0, joined(from_left[1, : 2 * heads, :LANES]))
        for h in range(heads):
            at = slice(h * HEAD_DIM, (h + 1) * HEAD_DIM)
            wide = slice(first + at.start, first + at.stop)
            factor = delta[h : h + 1] * -scale
            ds_pre = (p_ref[h, :rows].astype(F32) * factor).astype(BF16)
            ds_own = (p_ref[h, rows:].astype(F32) * factor).astype(BF16)
            dq = dq_ref[:, at] + jnp.where(no_left, 0.0, from_left[0, :, at].astype(F32))
            dq = dq + lax.dot_general(ds_pre, left_k[:, wide], TN, preferred_element_type=F32)
            dq = dq + lax.dot_general(ds_own, kv_ref[0, 0, :, wide], TN, preferred_element_type=F32)
            grad_q[0, :, at] = dq.astype(BF16)
            dk = dkv_ref[0, :, at] + jnp.where(no_right, 0.0, from_right[0, :, at].astype(F32))
            dk = dk + jnp.dot(ds_own, q_ref[0, :, wide], preferred_element_type=F32)
            grad_kv[0, 0, :, at] = dk.astype(BF16)
            dv = dkv_ref[1, :, at] + jnp.where(no_right, 0.0, from_right[1, :, at].astype(F32))
            grad_kv[1, 0, :, at] = dv.astype(BF16)

    @pl.when(index % 2 == 0)
    def _():
        add(got2, got1)

    @pl.when(index % 2 == 1)
    def _():
        add(got1, got2)


def shifted(value, steps):
    count = lax.axis_size("seq")
    return lax.ppermute(value, "seq", [(i, (i + steps) % count) for i in range(count)])


def neighbour_swaps(first, second):
    count = lax.axis_size("seq")
    one = [(i, min(i ^ 1, count - 1)) for i in range(count)]
    two = [(i, ((i + 1) ^ 1) - 1) for i in range(count)]
    two = [(i, j if 0 <= j < count else i) for i, j in two]
    return lax.ppermute(first, "seq", one), lax.ppermute(second, "seq", two)


def in_hbm(value):
    return pltpu.with_memory_space_constraint(value, pltpu.HBM)


def shape(dims, dtype=BF16):
    return jax.ShapeDtypeStruct(dims, dtype)


def cost(flops, moved):
    return pl.CostEstimate(flops=int(flops), bytes_accessed=int(moved), transcendentals=0)


def step(query, key_value, grad_y, tags, segments, out_weight):
    _, rows, hc = query.shape
    depth = out_weight.shape[2]
    chips = lax.axis_size("dp") // 2
    count = lax.axis_size("seq")
    span = hc // CHUNKS
    heads = span // HEAD_DIM
    scale = HEAD_DIM ** (-0.5)

    other_weight = swap(out_weight, "dp", 1)
    *slices, first, second, own_v = pl.pallas_call(
        slices_kernel,
        in_specs=[pl.BlockSpec(memory_space=pltpu.HBM)] * 4,
        out_shape=[shape((rows, 2 * depth + LANES))] * chips + [shape((rows, hc))] * 3,
        scratch_shapes=[
            pltpu.VMEM(tags.shape, tags.dtype), pltpu.SemaphoreType.DMA, pltpu.SemaphoreType.DMA((chips + 3,))],
        compiler_params=params(8),
        name="slices",
        cost_estimate=cost(0, 4 * grad_y.size),
    )(in_hbm(grad_y), in_hbm(tags), in_hbm(query), in_hbm(key_value))
    grads = [slices[0]] + [swap(slices[k], "dp", 2 * k) for k in range(1, chips)]
    sides = neighbour_swaps(first, second)
    values = neighbour_swaps(own_v, own_v)

    tile = min(512, span)
    steps = span // tile
    sums = []
    for c in range(CHUNKS):
        w_spec = pl.BlockSpec((2, tile, depth), lambda t, c=c: (0, c * steps + t, 0))
        mine, *parts = pl.pallas_call(
            functools.partial(project_kernel, chips),
            grid=(steps,),
            in_specs=[pl.BlockSpec((rows, 2 * depth + LANES), lambda t: (0, 0))] * chips + [w_spec] * 2,
            out_specs=[pl.BlockSpec((rows, tile), lambda t: (0, t))] * chips,
            out_shape=[shape((rows, span), F32)] + [shape((rows, span))] * (chips - 1),
            scratch_shapes=[pltpu.VMEM((2, 2, chips * rows, depth), BF16)],
            compiler_params=params(12),
            cost_estimate=cost(8 * chips * rows * depth * span, 8 * span * depth),
        )(*grads, out_weight, other_weight)
        sums.append([mine] + [swap(part, "dp", 2 * k) for k, part in enumerate(parts, 1)])

    small = shape((2, HEADS, rows), F32)
    own, far, left_k, right_q = pl.pallas_call(
        functools.partial(stats_kernel, count, scale),
        out_shape=[small] * 2 + [shape((rows, hc))] * 2,
        compiler_params=params(8),
        name="stats",
        cost_estimate=cost(2 * 3 * rows * rows * hc, 20 * rows * hc),
    )(query, key_value, *sides, segments)
    from_right, from_left = shifted(own, -1), shifted(far, 1)

    pieces = []
    for c in range(CHUNKS):
        gout, delta, left_v = pl.pallas_call(
            functools.partial(delta_kernel, count, c, chips - 1, scale),
            out_shape=[shape((rows + 2 * heads, span)), shape((heads, rows), F32), shape((rows, span))],
            compiler_params=params(8),
            cost_estimate=cost(4 * 2 * rows * rows * span, 20 * rows * span),
        )(*sums[c], query, key_value, left_k, *values, segments, own, from_left)
        pieces.append((gout, delta, left_v, shifted(gout, -1)))

    half = shape((2, rows, span))
    parts = []
    for c in range(CHUNKS):
        gout, delta, left_v, right_g = pieces[c]
        *kept, to1, to2 = pl.pallas_call(
            functools.partial(grads_kernel, count, c, scale),
            out_shape=[
                shape((rows, span), F32), shape((2, rows, span), F32), shape((heads, 2 * rows, rows)), half, half],
            scratch_shapes=[pltpu.VMEM((heads, rows), F32)],
            compiler_params=params(12),
            cost_estimate=cost(10 * 3 * rows * rows * span, 40 * rows * span),
        )(query, key_value, left_k, left_v, right_q, gout, right_g, segments, own, far, from_left, from_right, delta)
        parts.append((*kept, query, key_value, left_k, *neighbour_swaps(to1, to2)))

    results = ()
    for c in range(CHUNKS):
        results = pl.pallas_call(
            functools.partial(finish_kernel, count, c, scale),
            grid=(1,),
            in_specs=[pl.BlockSpec(memory_space=pltpu.VMEM)] * len(parts[c])
            + [pl.BlockSpec(memory_space=pl.ANY)] * len(results),
            out_specs=[
                pl.BlockSpec((1, rows, span), lambda t, c=c: (0, 0, c)),
                pl.BlockSpec((2, 1, rows, span), lambda t, c=c: (0, 0, 0, c)),
            ],
            out_shape=[shape(query.shape), shape(key_value.shape)],
            input_output_aliases={len(parts[c]) + n: n for n in range(len(results))},
            compiler_params=params(12),
            cost_estimate=cost(0, 20 * rows * span),
        )(*parts[c], *results)
    return tuple(results)


def solution(mesh):
    return jax.shard_map(
        step,
        mesh=mesh,
        in_specs=(
            P("dp", "seq", None),
            P(None, "dp", "seq", None),
            P("dp", "seq", None),
            P("dp", "seq"),
            P("dp", None),
            P(None, None, "dp"),
        ),
        out_specs=(P("dp", "seq", None), P(None, "dp", "seq", None)),
        check_vma=False,
    )
```

time: 84.8 us -> 91.8 us (1.083)
  the two profiles are of different devices: /device:TPU:20 before, /device:TPU:0 now
where the time goes in v2:
time: 91.8 us; the launch traced here: 90.8 us
  starting transfers between devices  41 us (45%)
  waiting for transfers between devices  30.2 us (33%)
  Pallas kernels  18.8 us (20%)
    ppermute x10, waiting for transfers between devices, swap(): lax.ppermute(value, axis, [(i, i ^ bits) for i in range(lax.axis_size(axi...  16.7 us
    ppermute x4, starting transfers between devices, shifted(): lax.ppermute(value, 'seq', [(i, (i + steps) % count) for i in range(count)])  15.2 us
    ppermute x8, starting transfers between devices, neighbour_swaps(): return (lax.ppermute(first, 'seq', one), lax.ppermute(second, 'seq', two))  14.5 us
    ppermute x10, starting transfers between devices, swap(): lax.ppermute(value, axis, [(i, i ^ bits) for i in range(lax.axis_size(axi...  11.3 us
    ppermute x8, waiting for transfers between devices, neighbour_swaps(): return (lax.ppermute(first, 'seq', one), lax.ppermute(second, 'seq', two))  10.8 us
    pallas_call x2, Pallas kernels, step(): pl.pallas_call(functools.partial(grads_kernel, count, c, scale), out_shap...  5.91 us
    pallas_call x2, Pallas kernels, step(): pl.pallas_call(functools.partial(project_kernel, chips), grid=(steps,), i...  3.92 us
    pallas_call x2, Pallas kernels, step(): pl.pallas_call(functools.partial(finish_kernel, count, c, scale), grid=(1...  2.93 us
  transfers between devices with their start and end apart: 22, of which 7 were waited for; matrix products, arithmetic and copies ran while one was open for 0% of the time, Pallas kernels for 19%

profile of v2, /device:TPU:0, one launch (start us, length us, event | category | flops | bytes accessed | tf_op | source)
XLA Modules:
  0.0 90.8 jit_solution(3322005079170501087)
XLA Ops:
  0.6 0.6 collective-permute-start.5
  1.2 2.6 %slices.1 = (bf16[128,640]{1,0:T(8,128)(2,1)S(1)}, bf16[128,640]{1,0:T(8,128)(2,1)S(1)}, bf16[128,640]{1,0:T(8,128)(2,1)S(1)}, bf16[128,640]{1,0:T(8,128)(2,1)S(...) custom-call(bf16[1,128,2048]{2,1,0:T(8,128)(2,1)} %grad_ref.1, ...), custom_call_target="tpu_custom_call" | custom-call | bytes 1048576 | tf_op jit(solution)/shard_map/slices/pallas_call | solution.py:351
  3.8 2.6 %collective-permute-start.2 = (bf16[128,640]{1,0:T(8,128)(2,1)S(1)}, bf16[128,640]{1,0:T(8,128)(2,1)S(1)}, u32[]{:S(2)}, u32[]{:S(2)}) collective-permute-start(bf16[128,640]{1,0:T(8,128)(2,1)S(1)} %get-tuple-element.43), channel_id=1, source_target_pairs={{0,8},{4,12},{8,0},{12,4},{16,24},{20,28},{24,16},{28,20},{1,9},{5... | collective-permute-start | bytes 491528 | tf_op jit(solution)/shard_map/ppermute | solution.py:31
  6.5 1.5 %collective-permute-start.3 = (bf16[128,640]{1,0:T(8,128)(2,1)S(1)}, bf16[128,640]{1,0:T(8,128)(2,1)S(1)}, u32[]{:S(2)}, u32[]{:S(2)}) collective-permute-start(bf16[128,640]{1,0:T(8,128)(2,1)S(1)} %get-tuple-element.44), channel_id=1, source_target_pairs={{0,16},{4,20},{8,24},{12,28},{16,0},{20,4},{24,8},{28,12},{1,17},{... | collective-permute-start | bytes 491528 | tf_op jit(solution)/shard_map/ppermute | solution.py:31
  8.0 0.0 collective-permute-start.4
  8.0 2.0 %collective-permute-start = (bf16[128,2048]{1,0:T(8,128)(2,1)S(1)}, bf16[128,2048]{1,0:T(8,128)(2,1)S(1)}, u32[]{:S(2)}, u32[]{:S(2)}) collective-permute-start(bf16[128,2048]{1,0:T(8,128)(2,1)S(1)} %get-tuple-element.39), channel_id=1, source_target_pairs={{0,1},{1,0},{2,3},{3,2},{4,5},{5,4},{6,7},{7,6},{8,9},{9,8},{10,11... | collective-permute-start | bytes 1572872 | tf_op jit(solution)/shard_map/ppermute | solution.py:326
  10.1 1.5 %collective-permute-done.2.refs_1_ = bf16[128,640]{1,0:T(8,128)(2,1)S(1)} collective-permute-done((bf16[128,640]{1,0:T(8,128)(2,1)S(1)}, bf16[128,640]{1,0:T(8,128)(2,1)S(1)}, u32[]{:S(2)}, u32[]{:S(2)}) %collective-permute-start.2) | collective-permute-done | bytes 163872 | tf_op jit(solution)/shard_map/ppermute | solution.py:31
  11.5 0.7 collective-permute-start.1
  12.2 4.0 %collective-permute-done.3.refs_2_ = bf16[128,640]{1,0:T(8,128)(2,1)S(1)} collective-permute-done((bf16[128,640]{1,0:T(8,128)(2,1)S(1)}, bf16[128,640]{1,0:T(8,128)(2,1)S(1)}, u32[]{:S(2)}, u32[]{:S(2)}) %collective-permute-start.3) | collective-permute-done | bytes 163872 | tf_op jit(solution)/shard_map/ppermute | solution.py:31
  16.2 0.7 collective-permute-start.10
  16.9 0.0 collective-permute-done.4.refs_3_
  16.9 4.4 %collective-permute-start.9 = (bf16[128,2048]{1,0:T(8,128)(2,1)S(1)}, bf16[128,2048]{1,0:T(8,128)(2,1)S(1)}, u32[]{:S(2)}, u32[]{:S(2)}) collective-permute-start(bf16[128,2048]{1,0:T(8,128)(2,1)S(1)} %get-tuple-element.50), channel_id=1, source_target_pairs={{0,1},{1,0},{2,3},{3,2},{4,5},{5,4},{6,7},{7,6},{8,9},{9,8},{10,11... | collective-permute-start | bytes 1572872 | tf_op jit(solution)/shard_map/ppermute | solution.py:326
  21.3 0.0 collective-permute-done.5.refs_5_
  21.3 0.0 copy-start.3
  21.3 2.0 %shard_map.80 = (f32[128,1024]{1,0:T(8,128)S(1)}, bf16[128,1024]{1,0:T(8,128)(2,1)S(1)}, bf16[128,1024]{1,0:T(8,128)(2,1)S(1)}, bf16[128,1024]{1,0:T(8,128)(2,1)S(1)}) custom-call(bf16[128,640]{1,0:T(8,128)(2,1)S(1)} %get-tuple-element.42.refs_0_, bf16[128,640]{1,0:T(8,128)(2,1)S(1)} %collective-permute-done.2.refs_1_, ...), custom_call_target="tpu_custom_call" | custom-call | flops 1073741824 | bytes 2097152 | tf_op jit(solution)/shard_map/pallas_call | solution.py:370
  23.3 0.1 collective-permute-start.16
  23.4 0.0 collective-permute-done.1.got2
  23.5 1.5 %stats.1 = (f32[2,16,128]{2,1,0:T(8,128)S(1)}, f32[2,16,128]{2,1,0:T(8,128)S(1)}, bf16[128,2048]{1,0:T(8,128)(2,1)S(1)}, bf16[128,2048]{1,0:T(8,128)(2,1)S(1)}) custom-call(bf16[1,128,2048]{2,1,0:T(8,128)(2,1)S(1)} %copy-done.1, bf16[2,1,128,2048]{3,2,1,0:T(8,128)(2,1)S(1)} %copy-done, bf16[128,2048]{1,0:T(8,128)(2,1)S(1)} %collective-permute-done.got1, ...), custom_call_target="tpu_custom_call" | custom-call | flops 201326592 | bytes 5242880 | tf_op jit(solution)/shard_map/stats/pallas_call | solution.py:383
  25.0 6.9 %collective-permute-start.11 = (f32[2,16,128]{2,1,0:T(8,128)S(1)}, f32[2,16,128]{2,1,0:T(8,128)S(1)}, u32[]{:S(2)}, u32[]{:S(2)}) collective-permute-start(f32[2,16,128]{2,1,0:T(8,128)S(1)} %get-tuple-element.52.far_stats), channel_id=1, source_target_pairs={{0,1},{1,2},{2,3},{3,0},{4,5},{5,6},{6,7},{7,4},{8,9},{9,10},{10,1... | collective-permute-start | bytes 49160 | tf_op jit(solution)/shard_map/ppermute | solution.py:318
  31.9 1.5 %collective-permute-start.17 = (bf16[128,1024]{1,0:T(8,128)(2,1)S(1)}, bf16[128,1024]{1,0:T(8,128)(2,1)S(1)}, u32[]{:S(2)}, u32[]{:S(2)}) collective-permute-start(bf16[128,1024]{1,0:T(8,128)(2,1)S(1)} %get-tuple-element.64), channel_id=1, source_target_pairs={{0,16},{4,20},{8,24},{12,28},{16,0},{20,4},{24,8},{28,12},{1,17},{... | collective-permute-start | bytes 786440 | tf_op jit(solution)/shard_map/ppermute | solution.py:31
  33.4 0.0 collective-permute-done.10.refs_7_
  33.4 1.4 %collective-permute-start.18 = (bf16[128,1024]{1,0:T(8,128)(2,1)S(1)}, bf16[128,1024]{1,0:T(8,128)(2,1)S(1)}, u32[]{:S(2)}, u32[]{:S(2)}) collective-permute-start(bf16[128,1024]{1,0:T(8,128)(2,1)S(1)} %get-tuple-element.65), channel_id=1, source_target_pairs={{0,24},{4,28},{8,16},{12,20},{16,8},{20,12},{24,0},{28,4},{1,25},{... | collective-permute-start | bytes 786440 | tf_op jit(solution)/shard_map/ppermute | solution.py:31
  34.9 2.0 %shard_map.77 = (f32[128,1024]{1,0:T(8,128)S(1)}, bf16[128,1024]{1,0:T(8,128)(2,1)S(1)}, bf16[128,1024]{1,0:T(8,128)(2,1)S(1)}, bf16[128,1024]{1,0:T(8,128)(2,1)S(1)}) custom-call(bf16[128,640]{1,0:T(8,128)(2,1)S(1)} %get-tuple-element.42.refs_0_, bf16[128,640]{1,0:T(8,128)(2,1)S(1)} %collective-permute-done.2.refs_1_, ...), custom_call_target="tpu_custom_call" | custom-call | flops 1073741824 | bytes 2097152 | tf_op jit(solution)/shard_map/pallas_call | solution.py:370
  36.9 0.6 collective-permute-start.6
  37.5 0.0 collective-permute-done.11.refs_10_.from_left
  37.5 1.5 %collective-permute-start.7 = (bf16[128,1024]{1,0:T(8,128)(2,1)S(1)}, bf16[128,1024]{1,0:T(8,128)(2,1)S(1)}, u32[]{:S(2)}, u32[]{:S(2)}) collective-permute-start(bf16[128,1024]{1,0:T(8,128)(2,1)S(1)} %get-tuple-element.48), channel_id=1, source_target_pairs={{0,16},{4,20},{8,24},{12,28},{16,0},{20,4},{24,8},{28,12},{1,17},{... | collective-permute-start | bytes 786440 | tf_op jit(solution)/shard_map/ppermute | solution.py:31
  39.0 0.0 collective-permute-done.16.refs_0_
  39.0 1.4 %collective-permute-start.8 = (bf16[128,1024]{1,0:T(8,128)(2,1)S(1)}, bf16[128,1024]{1,0:T(8,128)(2,1)S(1)}, u32[]{:S(2)}, u32[]{:S(2)}) collective-permute-start(bf16[128,1024]{1,0:T(8,128)(2,1)S(1)} %get-tuple-element.49), channel_id=1, source_target_pairs={{0,24},{4,28},{8,16},{12,20},{16,8},{20,12},{24,0},{28,4},{1,25},{... | collective-permute-start | bytes 786440 | tf_op jit(solution)/shard_map/ppermute | solution.py:31
  40.4 7.8 %collective-permute-done.17.refs_1_ = bf16[128,1024]{1,0:T(8,128)(2,1)S(1)} collective-permute-done((bf16[128,1024]{1,0:T(8,128)(2,1)S(1)}, bf16[128,1024]{1,0:T(8,128)(2,1)S(1)}, u32[]{:S(2)}, u32[]{:S(2)}) %collective-permute-start.17) | collective-permute-done | bytes 262176 | tf_op jit(solution)/shard_map/ppermute | solution.py:31
  48.2 0.0 collective-permute-done.18.refs_2_
  48.2 0.9 %shard_map.81 = (bf16[144,1024]{1,0:T(8,128)(2,1)S(1)}, f32[8,128]{1,0:T(8,128)S(1)}, bf16[128,1024]{1,0:T(8,128)(2,1)S(1)}) custom-call(f32[128,1024]{1,0:T(8,128)S(1)} %get-tuple-element.62.mine, bf16[128,1024]{1,0:T(8,128)(2,1)S(1)} %collective-permute-done.16.refs_0_, bf16[128,1024]{1,0:T(8,128)(2,1)S(1)} %collective-permute-done.17.refs_1_, ...), custom_call_target="tpu_custom_call" | custom-call | flops 134217728 | bytes 2621440 | tf_op jit(solution)/shard_map/pallas_call | solution.py:394
  49.1 0.1 collective-permute-start.19
  49.2 3.5 %collective-permute-done.7.refs_1_ = bf16[128,1024]{1,0:T(8,128)(2,1)S(1)} collective-permute-done((bf16[128,1024]{1,0:T(8,128)(2,1)S(1)}, bf16[128,1024]{1,0:T(8,128)(2,1)S(1)}, u32[]{:S(2)}, u32[]{:S(2)}) %collective-permute-start.7) | collective-permute-done | bytes 262176 | tf_op jit(solution)/shard_map/ppermute | solution.py:31
  52.7 0.9 %shard_map.78 = (bf16[144,1024]{1,0:T(8,128)(2,1)S(1)}, f32[8,128]{1,0:T(8,128)S(1)}, bf16[128,1024]{1,0:T(8,128)(2,1)S(1)}) custom-call(f32[128,1024]{1,0:T(8,128)S(1)} %get-tuple-element.46.mine, bf16[128,1024]{1,0:T(8,128)(2,1)S(1)} %collective-permute-done.6.refs_0_, bf16[128,1024]{1,0:T(8,128)(2,1)S(1)} %collective-permute-done.7.refs_1_, ...), custom_call_target="tpu_custom_call" | custom-call | flops 134217728 | bytes 2621440 | tf_op jit(solution)/shard_map/pallas_call | solution.py:394
  53.6 0.4 collective-permute-start.12
  54.1 7.7 %collective-permute-start.13 = (f32[2,16,128]{2,1,0:T(8,128)S(1)}, f32[2,16,128]{2,1,0:T(8,128)S(1)}, u32[]{:S(2)}, u32[]{:S(2)}) collective-permute-start(f32[2,16,128]{2,1,0:T(8,128)S(1)} %get-tuple-element.51.refs_9_.own_stats), channel_id=1, source_target_pairs={{0,3},{1,0},{2,1},{3,2},{4,7},{5,4},{6,5},{7,6},{8,11},{9,8},{10,9... | collective-permute-start | bytes 49160 | tf_op jit(solution)/shard_map/ppermute | solution.py:318
  61.8 2.7 %collective-permute-done.13.from_right = f32[2,16,128]{2,1,0:T(8,128)S(1)} collective-permute-done((f32[2,16,128]{2,1,0:T(8,128)S(1)}, f32[2,16,128]{2,1,0:T(8,128)S(1)}, u32[]{:S(2)}, u32[]{:S(2)}) %collective-permute-start.13) | collective-permute-done | bytes 16416 | tf_op jit(solution)/shard_map/ppermute | solution.py:318
  64.5 0.0 collective-permute-done.19.right_g
  64.5 2.9 %shard_map.82 = (f32[128,1024]{1,0:T(8,128)S(1)}, f32[2,128,1024]{2,1,0:T(8,128)S(1)}, bf16[8,256,128]{2,1,0:T(8,128)(2,1)S(1)}, bf16[2,128,1024]{2,1,0:T(8,128)(2,1)S(1)}, bf16[2,128,1024]{2,1,0:T(8,128)(2,1)S(1)}) custom-call(bf16[1,128,2048]{2,1,0:T(8,128)(2,1)S(1)} %copy-done.1, bf16[2,1,128,2048]{3,2,1,0:T(8,128)(2,1)S(1)} %copy-done, ...), custom_call_target="tpu_custom_call" | custom-call | flops 503316480 | bytes 5242880 | tf_op jit(solution)/shard_map/pallas_call | solution.py:406
  67.4 2.0 %collective-permute-start.20 = (bf16[2,128,1024]{2,1,0:T(8,128)(2,1)S(1)}, bf16[2,128,1024]{2,1,0:T(8,128)(2,1)S(1)}, u32[]{:S(2)}, u32[]{:S(2)}) collective-permute-start(bf16[2,128,1024]{2,1,0:T(8,128)(2,1)S(1)} %get-tuple-element.72), channel_id=1, source_target_pairs={{0,1},{1,0},{2,3},{3,2},{4,5},{5,4},{6,7},{7,6},{8,9},{9,8},{10,11... | collective-permute-start | bytes 1572872 | tf_op jit(solution)/shard_map/ppermute | solution.py:326
  69.3 0.7 collective-permute-start.21
  70.0 3.0 %shard_map.79 = (f32[128,1024]{1,0:T(8,128)S(1)}, f32[2,128,1024]{2,1,0:T(8,128)S(1)}, bf16[8,256,128]{2,1,0:T(8,128)(2,1)S(1)}, bf16[2,128,1024]{2,1,0:T(8,128)(2,1)S(1)}, bf16[2,128,1024]{2,1,0:T(8,128)(2,1)S(1)}) custom-call(bf16[1,128,2048]{2,1,0:T(8,128)(2,1)S(1)} %copy-done.1, bf16[2,1,128,2048]{3,2,1,0:T(8,128)(2,1)S(1)} %copy-done, ...), custom_call_target="tpu_custom_call" | custom-call | flops 503316480 | bytes 5242880 | tf_op jit(solution)/shard_map/pallas_call | solution.py:406
  73.1 3.4 %collective-permute-start.14 = (bf16[2,128,1024]{2,1,0:T(8,128)(2,1)S(1)}, bf16[2,128,1024]{2,1,0:T(8,128)(2,1)S(1)}, u32[]{:S(2)}, u32[]{:S(2)}) collective-permute-start(bf16[2,128,1024]{2,1,0:T(8,128)(2,1)S(1)} %get-tuple-element.60), channel_id=1, source_target_pairs={{0,1},{1,0},{2,3},{3,2},{4,5},{5,4},{6,7},{7,6},{8,9},{9,8},{10,11... | collective-permute-start | bytes 1572872 | tf_op jit(solution)/shard_map/ppermute | solution.py:326
  76.5 0.7 collective-permute-start.15
  77.1 5.1 %collective-permute-done.20.got1 = bf16[2,128,1024]{2,1,0:T(8,128)(2,1)S(1)} collective-permute-done((bf16[2,128,1024]{2,1,0:T(8,128)(2,1)S(1)}, bf16[2,128,1024]{2,1,0:T(8,128)(2,1)S(1)}, u32[]{:S(2)}, u32[]{:S(2)}) %collective-permute-start.20) | collective-permute-done | bytes 524320 | tf_op jit(solution)/shard_map/ppermute | solution.py:326
  82.2 1.5 %shard_map.83 = (bf16[1,128,2048]{2,1,0:T(8,128)(2,1)}, bf16[2,1,128,2048]{3,2,1,0:T(8,128)(2,1)}) custom-call(f32[128,1024]{1,0:T(8,128)S(1)} %get-tuple-element.69.dq_ref, f32[2,128,1024]{2,1,0:T(8,128)S(1)} %get-tuple-element.70.dkv_ref, bf16[8,256,128]{2,1,0:T(8,128)(2,1)S(1)} %get-tuple-element.71.p_ref, bf16[1,128,2048]{2,1,0:T(8,128)(2,1)S(1)} %copy-done.1, ...), custom_call_target="tpu_custom_call" | custom-call | bytes 2621440 | tf_op jit(solution)/shard_map/pallas_call | solution.py:418
  83.7 5.7 %collective-permute-done.14.got1 = bf16[2,128,1024]{2,1,0:T(8,128)(2,1)S(1)} collective-permute-done((bf16[2,128,1024]{2,1,0:T(8,128)(2,1)S(1)}, bf16[2,128,1024]{2,1,0:T(8,128)(2,1)S(1)}, u32[]{:S(2)}, u32[]{:S(2)}) %collective-permute-start.14) | collective-permute-done | bytes 524320 | tf_op jit(solution)/shard_map/ppermute | solution.py:326
  89.4 1.5 %shard_map.84 = (bf16[1,128,2048]{2,1,0:T(8,128)(2,1)}, bf16[2,1,128,2048]{3,2,1,0:T(8,128)(2,1)}) custom-call(f32[128,1024]{1,0:T(8,128)S(1)} %get-tuple-element.57.dq_ref, f32[2,128,1024]{2,1,0:T(8,128)S(1)} %get-tuple-element.58.dkv_ref, bf16[8,256,128]{2,1,0:T(8,128)(2,1)S(1)} %get-tuple-element.59.p_ref, ...), custom_call_target="tpu_custom_call", output_to_operand_aliasing={{0}: (8, {}), {1}: (9, {})} | custom-call | bytes 2621440 | tf_op jit(solution)/shard_map/pallas_call | solution.py:418
  (14 shorter events, 0.0 us)
Async XLA Ops:
  0.6 20.7 %copy-start.2 = (bf16[2,2048,256]{2,1,0:T(8,128)(2,1)S(1)}, bf16[2,2048,256]{2,1,0:T(8,128)(2,1)}, u32[]{:S(2)}) copy-start(bf16[2,2048,256]{2,1,0:T(8,128)(2,1)} %refs_4_.6) | copy-start | bytes 6291460
  0.6 20.7 %collective-permute-start.5 = (bf16[2,2048,256]{2,1,0:T(8,128)(2,1)}, bf16[2,2048,256]{2,1,0:T(8,128)(2,1)S(1)}, u32[]{:S(2)}, u32[]{:S(2)}) collective-permute-start(bf16[2,2048,256]{2,1,0:T(8,128)(2,1)} %refs_4_.6), channel_id=1, source_target_pairs={{0,4},{4,0},{8,12},{12,8},{16,20},{20,16},{24,28},{28,24},{1,5},{5... | collective-permute-start | bytes 6291464 | tf_op jit(solution)/shard_map/ppermute | solution.py:31
  3.8 7.7 %collective-permute-start.2 = (bf16[128,640]{1,0:T(8,128)(2,1)S(1)}, bf16[128,640]{1,0:T(8,128)(2,1)S(1)}, u32[]{:S(2)}, u32[]{:S(2)}) collective-permute-start(bf16[128,640]{1,0:T(8,128)(2,1)S(1)} %get-tuple-element.43), channel_id=1, source_target_pairs={{0,8},{4,12},{8,0},{12,4},{16,24},{20,28},{24,16},{28,20},{1,9},{5... | collective-permute-start | bytes 491528 | tf_op jit(solution)/shard_map/ppermute | solution.py:31
  6.5 9.7 %collective-permute-start.3 = (bf16[128,640]{1,0:T(8,128)(2,1)S(1)}, bf16[128,640]{1,0:T(8,128)(2,1)S(1)}, u32[]{:S(2)}, u32[]{:S(2)}) collective-permute-start(bf16[128,640]{1,0:T(8,128)(2,1)S(1)} %get-tuple-element.44), channel_id=1, source_target_pairs={{0,16},{4,20},{8,24},{12,28},{16,0},{20,4},{24,8},{28,12},{1,17},{... | collective-permute-start | bytes 491528 | tf_op jit(solution)/shard_map/ppermute | solution.py:31
  8.0 8.9 %collective-permute-start.4 = (bf16[128,640]{1,0:T(8,128)(2,1)S(1)}, bf16[128,640]{1,0:T(8,128)(2,1)S(1)}, u32[]{:S(2)}, u32[]{:S(2)}) collective-permute-start(bf16[128,640]{1,0:T(8,128)(2,1)S(1)} %get-tuple-element.45), channel_id=1, source_target_pairs={{0,24},{4,28},{8,16},{12,20},{16,8},{20,12},{24,0},{28,4},{1,25},{... | collective-permute-start | bytes 491528 | tf_op jit(solution)/shard_map/ppermute | solution.py:31
  8.0 15.4 %collective-permute-start = (bf16[128,2048]{1,0:T(8,128)(2,1)S(1)}, bf16[128,2048]{1,0:T(8,128)(2,1)S(1)}, u32[]{:S(2)}, u32[]{:S(2)}) collective-permute-start(bf16[128,2048]{1,0:T(8,128)(2,1)S(1)} %get-tuple-element.39), channel_id=1, source_target_pairs={{0,1},{1,0},{2,3},{3,2},{4,5},{5,4},{6,7},{7,6},{8,9},{9,8},{10,11... | collective-permute-start | bytes 1572872 | tf_op jit(solution)/shard_map/ppermute | solution.py:326
  11.5 11.9 %collective-permute-start.1 = (bf16[128,2048]{1,0:T(8,128)(2,1)S(1)}, bf16[128,2048]{1,0:T(8,128)(2,1)S(1)}, u32[]{:S(2)}, u32[]{:S(2)}) collective-permute-start(bf16[128,2048]{1,0:T(8,128)(2,1)S(1)} %get-tuple-element.40), channel_id=1, source_target_pairs={{0,0},{1,2},{2,1},{3,3},{4,4},{5,6},{6,5},{7,7},{8,8},{9,10},{10,9... | collective-permute-start | bytes 1572872 | tf_op jit(solution)/shard_map/ppermute | solution.py:326
  16.2 17.3 %collective-permute-start.10 = (bf16[128,2048]{1,0:T(8,128)(2,1)S(1)}, bf16[128,2048]{1,0:T(8,128)(2,1)S(1)}, u32[]{:S(2)}, u32[]{:S(2)}) collective-permute-start(bf16[128,2048]{1,0:T(8,128)(2,1)S(1)} %get-tuple-element.50), channel_id=1, source_target_pairs={{0,0},{1,2},{2,1},{3,3},{4,4},{5,6},{6,5},{7,7},{8,8},{9,10},{10,9... | collective-permute-start | bytes 1572872 | tf_op jit(solution)/shard_map/ppermute | solution.py:326
  16.9 20.0 %collective-permute-start.9 = (bf16[128,2048]{1,0:T(8,128)(2,1)S(1)}, bf16[128,2048]{1,0:T(8,128)(2,1)S(1)}, u32[]{:S(2)}, u32[]{:S(2)}) collective-permute-start(bf16[128,2048]{1,0:T(8,128)(2,1)S(1)} %get-tuple-element.50), channel_id=1, source_target_pairs={{0,1},{1,0},{2,3},{3,2},{4,5},{5,4},{6,7},{7,6},{8,9},{9,8},{10,11... | collective-permute-start | bytes 1572872 | tf_op jit(solution)/shard_map/ppermute | solution.py:326
  21.3 2.1 %copy-start = (bf16[2,1,128,2048]{3,2,1,0:T(8,128)(2,1)S(1)}, bf16[2,1,128,2048]{3,2,1,0:T(8,128)(2,1)}, u32[]{:S(2)}) copy-start(bf16[2,1,128,2048]{3,2,1,0:T(8,128)(2,1)} %kv_ref.11) | copy-start | bytes 3145732
  21.3 2.1 %copy-start.1 = (bf16[1,128,2048]{2,1,0:T(8,128)(2,1)S(1)}, bf16[1,128,2048]{2,1,0:T(8,128)(2,1)}, u32[]{:S(2)}) copy-start(bf16[1,128,2048]{2,1,0:T(8,128)(2,1)} %q_ref.11) | copy-start | bytes 1572868
  21.3 2.1 %copy-start.3 = (s32[1,512]{1,0:T(1,128)S(1)}, s32[1,512]{1,0:T(1,128)}, u32[]{:S(2)}) copy-start(s32[1,512]{1,0:T(1,128)} %segs.5) | copy-start | bytes 6148
  23.3 15.7 %collective-permute-start.16 = (bf16[128,1024]{1,0:T(8,128)(2,1)S(1)}, bf16[128,1024]{1,0:T(8,128)(2,1)S(1)}, u32[]{:S(2)}, u32[]{:S(2)}) collective-permute-start(bf16[128,1024]{1,0:T(8,128)(2,1)S(1)} %get-tuple-element.63), channel_id=1, source_target_pairs={{0,8},{4,12},{8,0},{12,4},{16,24},{20,28},{24,16},{28,20},{1,9},{5... | collective-permute-start | bytes 786440 | tf_op jit(solution)/shard_map/ppermute | solution.py:31
  25.0 12.5 %collective-permute-start.11 = (f32[2,16,128]{2,1,0:T(8,128)S(1)}, f32[2,16,128]{2,1,0:T(8,128)S(1)}, u32[]{:S(2)}, u32[]{:S(2)}) collective-permute-start(f32[2,16,128]{2,1,0:T(8,128)S(1)} %get-tuple-element.52.far_stats), channel_id=1, source_target_pairs={{0,1},{1,2},{2,3},{3,0},{4,5},{5,6},{6,7},{7,4},{8,9},{9,10},{10,1... | collective-permute-start | bytes 49160 | tf_op jit(solution)/shard_map/ppermute | solution.py:318
  31.9 16.3 %collective-permute-start.17 = (bf16[128,1024]{1,0:T(8,128)(2,1)S(1)}, bf16[128,1024]{1,0:T(8,128)(2,1)S(1)}, u32[]{:S(2)}, u32[]{:S(2)}) collective-permute-start(bf16[128,1024]{1,0:T(8,128)(2,1)S(1)} %get-tuple-element.64), channel_id=1, source_target_pairs={{0,16},{4,20},{8,24},{12,28},{16,0},{20,4},{24,8},{28,12},{1,17},{... | collective-permute-start | bytes 786440 | tf_op jit(solution)/shard_map/ppermute | solution.py:31
  33.4 14.7 %collective-permute-start.18 = (bf16[128,1024]{1,0:T(8,128)(2,1)S(1)}, bf16[128,1024]{1,0:T(8,128)(2,1)S(1)}, u32[]{:S(2)}, u32[]{:S(2)}) collective-permute-start(bf16[128,1024]{1,0:T(8,128)(2,1)S(1)} %get-tuple-element.65), channel_id=1, source_target_pairs={{0,24},{4,28},{8,16},{12,20},{16,8},{20,12},{24,0},{28,4},{1,25},{... | collective-permute-start | bytes 786440 | tf_op jit(solution)/shard_map/ppermute | solution.py:31
  36.9 12.3 %collective-permute-start.6 = (bf16[128,1024]{1,0:T(8,128)(2,1)S(1)}, bf16[128,1024]{1,0:T(8,128)(2,1)S(1)}, u32[]{:S(2)}, u32[]{:S(2)}) collective-permute-start(bf16[128,1024]{1,0:T(8,128)(2,1)S(1)} %get-tuple-element.47), channel_id=1, source_target_pairs={{0,8},{4,12},{8,0},{12,4},{16,24},{20,28},{24,16},{28,20},{1,9},{5... | collective-permute-start | bytes 786440 | tf_op jit(solution)/shard_map/ppermute | solution.py:31
  37.5 15.2 %collective-permute-start.7 = (bf16[128,1024]{1,0:T(8,128)(2,1)S(1)}, bf16[128,1024]{1,0:T(8,128)(2,1)S(1)}, u32[]{:S(2)}, u32[]{:S(2)}) collective-permute-start(bf16[128,1024]{1,0:T(8,128)(2,1)S(1)} %get-tuple-element.48), channel_id=1, source_target_pairs={{0,16},{4,20},{8,24},{12,28},{16,0},{20,4},{24,8},{28,12},{1,17},{... | collective-permute-start | bytes 786440 | tf_op jit(solution)/shard_map/ppermute | solution.py:31
  39.0 13.7 %collective-permute-start.8 = (bf16[128,1024]{1,0:T(8,128)(2,1)S(1)}, bf16[128,1024]{1,0:T(8,128)(2,1)S(1)}, u32[]{:S(2)}, u32[]{:S(2)}) collective-permute-start(bf16[128,1024]{1,0:T(8,128)(2,1)S(1)} %get-tuple-element.49), channel_id=1, source_target_pairs={{0,24},{4,28},{8,16},{12,20},{16,8},{20,12},{24,0},{28,4},{1,25},{... | collective-permute-start | bytes 786440 | tf_op jit(solution)/shard_map/ppermute | solution.py:31
  49.1 15.4 %collective-permute-start.19 = (bf16[144,1024]{1,0:T(8,128)(2,1)S(1)}, bf16[144,1024]{1,0:T(8,128)(2,1)S(1)}, u32[]{:S(2)}, u32[]{:S(2)}) collective-permute-start(bf16[144,1024]{1,0:T(8,128)(2,1)S(1)} %get-tuple-element.67.g_ref), channel_id=1, source_target_pairs={{0,3},{1,0},{2,1},{3,2},{4,7},{5,4},{6,5},{7,6},{8,11},{9,8},{10,9... | collective-permute-start | bytes 884744 | tf_op jit(solution)/shard_map/ppermute | solution.py:318
  53.6 16.4 %collective-permute-start.12 = (bf16[144,1024]{1,0:T(8,128)(2,1)S(1)}, bf16[144,1024]{1,0:T(8,128)(2,1)S(1)}, u32[]{:S(2)}, u32[]{:S(2)}) collective-permute-start(bf16[144,1024]{1,0:T(8,128)(2,1)S(1)} %get-tuple-element.55.g_ref), channel_id=1, source_target_pairs={{0,3},{1,0},{2,1},{3,2},{4,7},{5,4},{6,5},{7,6},{8,11},{9,8},{10,9... | collective-permute-start | bytes 884744 | tf_op jit(solution)/shard_map/ppermute | solution.py:318
  54.1 10.4 %collective-permute-start.13 = (f32[2,16,128]{2,1,0:T(8,128)S(1)}, f32[2,16,128]{2,1,0:T(8,128)S(1)}, u32[]{:S(2)}, u32[]{:S(2)}) collective-permute-start(f32[2,16,128]{2,1,0:T(8,128)S(1)} %get-tuple-element.51.refs_9_.own_stats), channel_id=1, source_target_pairs={{0,3},{1,0},{2,1},{3,2},{4,7},{5,4},{6,5},{7,6},{8,11},{9,8},{10,9... | collective-permute-start | bytes 49160 | tf_op jit(solution)/shard_map/ppermute | solution.py:318
  67.4 14.9 %collective-permute-start.20 = (bf16[2,128,1024]{2,1,0:T(8,128)(2,1)S(1)}, bf16[2,128,1024]{2,1,0:T(8,128)(2,1)S(1)}, u32[]{:S(2)}, u32[]{:S(2)}) collective-permute-start(bf16[2,128,1024]{2,1,0:T(8,128)(2,1)S(1)} %get-tuple-element.72), channel_id=1, source_target_pairs={{0,1},{1,0},{2,3},{3,2},{4,5},{5,4},{6,7},{7,6},{8,9},{9,8},{10,11... | collective-permute-start | bytes 1572872 | tf_op jit(solution)/shard_map/ppermute | solution.py:326
  69.3 12.9 %collective-permute-start.21 = (bf16[2,128,1024]{2,1,0:T(8,128)(2,1)S(1)}, bf16[2,128,1024]{2,1,0:T(8,128)(2,1)S(1)}, u32[]{:S(2)}, u32[]{:S(2)}) collective-permute-start(bf16[2,128,1024]{2,1,0:T(8,128)(2,1)S(1)} %get-tuple-element.73), channel_id=1, source_target_pairs={{0,0},{1,2},{2,1},{3,3},{4,4},{5,6},{6,5},{7,7},{8,8},{9,10},{10,9... | collective-permute-start | bytes 1572872 | tf_op jit(solution)/shard_map/ppermute | solution.py:326
  73.1 16.3 %collective-permute-start.14 = (bf16[2,128,1024]{2,1,0:T(8,128)(2,1)S(1)}, bf16[2,128,1024]{2,1,0:T(8,128)(2,1)S(1)}, u32[]{:S(2)}, u32[]{:S(2)}) collective-permute-start(bf16[2,128,1024]{2,1,0:T(8,128)(2,1)S(1)} %get-tuple-element.60), channel_id=1, source_target_pairs={{0,1},{1,0},{2,3},{3,2},{4,5},{5,4},{6,7},{7,6},{8,9},{9,8},{10,11... | collective-permute-start | bytes 1572872 | tf_op jit(solution)/shard_map/ppermute | solution.py:326
  76.5 12.9 %collective-permute-start.15 = (bf16[2,128,1024]{2,1,0:T(8,128)(2,1)S(1)}, bf16[2,128,1024]{2,1,0:T(8,128)(2,1)S(1)}, u32[]{:S(2)}, u32[]{:S(2)}) collective-permute-start(bf16[2,128,1024]{2,1,0:T(8,128)(2,1)S(1)} %get-tuple-element.61), channel_id=1, source_target_pairs={{0,0},{1,2},{2,1},{3,3},{4,4},{5,6},{6,5},{7,7},{8,8},{9,10},{10,9... | collective-permute-start | bytes 1572872 | tf_op jit(solution)/shard_map/ppermute | solution.py:326

commit v3 on v2

--- a/solution.py
+++ b/solution.py
@@ -9,7 +9,7 @@
 
 HEADS = 16
 HEAD_DIM = 128
-CHUNKS = 2
+PARTS = 2
 
 NEG = -1e30
 LANES = 128
@@ -37,67 +37,68 @@
     return jnp.sum(jnp.where(same, row.astype(F32), 0.0), axis=1, keepdims=True)
 
 
-def slices_kernel(grad_ref, tags_ref, q_ref, kv_ref, *refs):
-    outs, (first, second, v_out), (tags, tag_sem, sem) = refs[:-6], refs[-6:-3], refs[-3:]
+def grad_slices_kernel(grad_ref, tags_ref, *refs):
+    outs, (tags, tag_sem, sem) = refs[:-3], refs[-3:]
     chip = lax.axis_index("dp") // 2
-    even = lax.axis_index("seq") % 2 == 0
     width = outs[0].shape[1] - LANES
     tag_copy = pltpu.make_async_copy(tags_ref, tags, tag_sem)
     copies = [
         pltpu.make_async_copy(grad_ref.at[0, :, lane_slice((chip ^ k) * width, width)], out.at[:, :width], sem.at[k])
         for k, out in enumerate(outs)
     ]
-    count = len(outs)
-    v_copy = pltpu.make_async_copy(kv_ref.at[1, 0], v_out, sem.at[count])
     for copy in [tag_copy] + copies:
         copy.start()
-
-    def sides(up, down):
-        both = [
-            pltpu.make_async_copy(kv_ref.at[0, 0], up, sem.at[count + 1]),
-            pltpu.make_async_copy(q_ref.at[0], down, sem.at[count + 2]),
-        ]
-        for copy in both:
-            copy.start()
-        for copy in both:
-            copy.wait()
-
-    @pl.when(even)
-    def _():
-        sides(first, second)
-
-    @pl.when(jnp.logical_not(even))
-    def _():
-        sides(second, first)
-
-    v_copy.start()
     tag_copy.wait()
     tag = jnp.broadcast_to(column_of(tags[...]), (grad_ref.shape[1], LANES)).astype(BF16)
     for out in outs:
         out[:, width:] = tag
-    for copy in copies + [v_copy]:
+    for copy in copies:
         copy.wait()
 
 
-def project_kernel(chips, *refs):
+def side_slices_kernel(q_ref, kv_ref, first, second, v_out, sem):
+    v_copy = pltpu.make_async_copy(kv_ref.at[1, 0], v_out, sem.at[0])
+
+    def sides(up, down):
+        copies = [
+            pltpu.make_async_copy(kv_ref.at[0, 0], up, sem.at[1]),
+            pltpu.make_async_copy(q_ref.at[0], down, sem.at[2]),
+            v_copy,
+        ]
+        for copy in copies:
+            copy.start()
+        for copy in copies:
+            copy.wait()
+
+    even = lax.axis_index("seq") % 2 == 0
+
+    @pl.when(even)
+    def _():
+        sides(first, second)
+
+    @pl.when(jnp.logical_not(even))
+    def _():
+        sides(second, first)
+
+
+def project_kernel(chips, first, *refs):
     grads, (own_w, other_w), (mine, *parts, lhs) = refs[:chips], refs[chips : chips + 2], refs[chips + 2 :]
     rows = grads[0].shape[0]
     depth = own_w.shape[2]
     core = lax.axis_index("dp") % 2
 
-    @pl.when(pl.program_id(0) == 0)
-    def _():
-        for k, grad in enumerate(grads):
-            text = grad[:, 2 * depth : 2 * depth + 1] == 1
-            for side in range(2):
-                g = grad[:, lane_slice((core ^ side) * depth, depth)]
-                lhs[side, 0, k * rows : (k + 1) * rows] = jnp.where(text, jnp.zeros_like(g), g)
-                lhs[side, 1, k * rows : (k + 1) * rows] = jnp.where(text, g, jnp.zeros_like(g))
+    for k, grad in enumerate(grads):
+        text = grad[:, 2 * depth : 2 * depth + 1] == 1
+        for side in range(2):
+            g = grad[:, lane_slice((core ^ side) * depth, depth)]
+            lhs[side, 0, k * rows : (k + 1) * rows] = jnp.where(text, jnp.zeros_like(g), g)
+            lhs[side, 1, k * rows : (k + 1) * rows] = jnp.where(text, g, jnp.zeros_like(g))
 
     total = None
     for side, w in enumerate((own_w, other_w)):
         for kind in range(2):
-            term = lax.dot_general(lhs[side, kind], w[kind], NT, preferred_element_type=F32)
+            rhs = w[kind, first : first + mine.shape[1]]
+            term = lax.dot_general(lhs[side, kind], rhs, NT, preferred_element_type=F32)
             total = term if total is None else total + term
     mine[...] = total[:rows]
     for k, part in enumerate(parts):
@@ -187,12 +188,11 @@
     return merged(own, (far_stats[0, heads], far_stats[1, heads]))
 
 
-def delta_kernel(count, chunk, terms, scale, mine, *refs):
+def delta_kernel(count, first, terms, scale, mine, *refs):
     parts = refs[:terms]
     q_ref, kv_ref, left_k, got1, got2, segs, own_stats, from_left, g_out, d_out, left_v = refs[terms:]
     rows, span = mine.shape
     index = lax.axis_index("seq")
-    first = chunk * span
     lanes = slice(first, first + span)
     pair_of(index % 2 == 0, [(got2.at[:, lanes], left_v)], [(got1.at[:, lanes], left_v)])
     total = mine[...]
@@ -201,7 +201,7 @@
     g_out[:rows] = total.astype(BF16)
     pre, _, own, _ = masks(count, segs, index, rows)
     heads = span // HEAD_DIM
-    top, inv = own_rows(index, own_stats, from_left, slice(chunk * heads, (chunk + 1) * heads))
+    top, inv = own_rows(index, own_stats, from_left, slice(first // HEAD_DIM, first // HEAD_DIM + heads))
     for h in range(heads):
         at = slice(h * HEAD_DIM, (h + 1) * HEAD_DIM)
         wide = slice(first + at.start, first + at.stop)
@@ -217,14 +217,13 @@
     g_out[rows:, :LANES] = split(d_out[...])
 
 
-def grads_kernel(count, chunk, scale, q_ref, kv_ref, left_k, left_v, right_q, g_ref, right_g, segs,
+def grads_kernel(count, first, scale, q_ref, kv_ref, left_k, left_v, right_q, g_ref, right_g, segs,
                  own_stats, far_stats, from_left, from_right, delta_own,
                  dq_out, dkv_out, p_out, to1, to2, far_delta):
     index = lax.axis_index("seq")
     rows, span = left_v.shape
-    first = chunk * span
     heads = span // HEAD_DIM
-    chosen = slice(chunk * heads, (chunk + 1) * heads)
+    chosen = slice(first // HEAD_DIM, first // HEAD_DIM + heads)
     pre, far, own, nxt = masks(count, segs, index, rows)
     top, inv = own_rows(index, own_stats, from_left, chosen)
     r_top, r_inv = right_rows(index, count, far_stats, from_right, chosen)
@@ -278,12 +277,11 @@
         run(to2, to1)
 
 
-def finish_kernel(count, chunk, scale, dq_ref, dkv_ref, p_ref, q_ref, kv_ref, left_k, got1, got2, *refs):
-    grad_q, grad_kv = refs[-2:]
+def finish_kernel(count, first, scale, dq_ref, dkv_ref, p_ref, q_ref, kv_ref, left_k, got1, got2, *refs):
+    grad_q, grad_kv, done, sem = refs[-4:]
     index = lax.axis_index("seq")
     rows, span = dq_ref.shape
     heads = span // HEAD_DIM
-    first = chunk * span
 
     def add(from_left, from_right):
         no_left, no_right = index == 0, index == count - 1
@@ -297,12 +295,12 @@
             dq = dq_ref[:, at] + jnp.where(no_left, 0.0, from_left[0, :, at].astype(F32))
             dq = dq + lax.dot_general(ds_pre, left_k[:, wide], TN, preferred_element_type=F32)
             dq = dq + lax.dot_general(ds_own, kv_ref[0, 0, :, wide], TN, preferred_element_type=F32)
-            grad_q[0, :, at] = dq.astype(BF16)
+            done[0, :, at] = dq.astype(BF16)
             dk = dkv_ref[0, :, at] + jnp.where(no_right, 0.0, from_right[0, :, at].astype(F32))
             dk = dk + jnp.dot(ds_own, q_ref[0, :, wide], preferred_element_type=F32)
-            grad_kv[0, 0, :, at] = dk.astype(BF16)
+            done[1, :, at] = dk.astype(BF16)
             dv = dkv_ref[1, :, at] + jnp.where(no_right, 0.0, from_right[1, :, at].astype(F32))
-            grad_kv[1, 0, :, at] = dv.astype(BF16)
+            done[2, :, at] = dv.astype(BF16)
 
     @pl.when(index % 2 == 0)
     def _():
@@ -311,6 +309,16 @@
     @pl.when(index % 2 == 1)
     def _():
         add(got1, got2)
+
+    lanes = slice(first, first + span)
+    copies = [
+        pltpu.make_async_copy(done.at[0], grad_q.at[0, :, lanes], sem.at[0]),
+        pltpu.make_async_copy(done.at[1:], grad_kv.at[:, 0, :, lanes], sem.at[1]),
+    ]
+    for copy in copies:
+        copy.start()
+    for copy in copies:
+        copy.wait()
 
 
 def shifted(value, steps):
@@ -338,40 +346,47 @@
     return pl.CostEstimate(flops=int(flops), bytes_accessed=int(moved), transcendentals=0)
 
 
+def chunks(hc):
+    heads = hc // HEAD_DIM
+    cuts = [heads * n // PARTS for n in range(PARTS + 1)]
+    return [(HEAD_DIM * a, HEAD_DIM * (b - a)) for a, b in zip(cuts, cuts[1:])]
+
+
 def step(query, key_value, grad_y, tags, segments, out_weight):
     _, rows, hc = query.shape
     depth = out_weight.shape[2]
     chips = lax.axis_size("dp") // 2
     count = lax.axis_size("seq")
-    span = hc // CHUNKS
-    heads = span // HEAD_DIM
     scale = HEAD_DIM ** (-0.5)
 
     other_weight = swap(out_weight, "dp", 1)
-    *slices, first, second, own_v = pl.pallas_call(
-        slices_kernel,
-        in_specs=[pl.BlockSpec(memory_space=pltpu.HBM)] * 4,
-        out_shape=[shape((rows, 2 * depth + LANES))] * chips + [shape((rows, hc))] * 3,
+    slices = pl.pallas_call(
+        grad_slices_kernel,
+        in_specs=[pl.BlockSpec(memory_space=pltpu.HBM)] * 2,
+        out_shape=[shape((rows, 2 * depth + LANES))] * chips,
         scratch_shapes=[
-            pltpu.VMEM(tags.shape, tags.dtype), pltpu.SemaphoreType.DMA, pltpu.SemaphoreType.DMA((chips + 3,))],
+            pltpu.VMEM(tags.shape, tags.dtype), pltpu.SemaphoreType.DMA, pltpu.SemaphoreType.DMA((chips,))],
+        compiler_params=params(4),
+        name="grad_slices",
+        cost_estimate=cost(0, 4 * grad_y.size),
+    )(in_hbm(grad_y), in_hbm(tags))
+    grads = [slices[0]] + [swap(slices[k], "dp", 2 * k) for k in range(1, chips)]
+    first, second, own_v = pl.pallas_call(
+        side_slices_kernel,
+        in_specs=[pl.BlockSpec(memory_space=pltpu.HBM)] * 2,
+        out_shape=[shape((rows, hc))] * 3,
+        scratch_shapes=[pltpu.SemaphoreType.DMA((3,))],
         compiler_params=params(8),
-        name="slices",
-        cost_estimate=cost(0, 4 * grad_y.size),
-    )(in_hbm(grad_y), in_hbm(tags), in_hbm(query), in_hbm(key_value))
-    grads = [slices[0]] + [swap(slices[k], "dp", 2 * k) for k in range(1, chips)]
+        name="side_slices",
+        cost_estimate=cost(0, 12 * query.size),
+    )(in_hbm(query), in_hbm(key_value))
     sides = neighbour_swaps(first, second)
     values = neighbour_swaps(own_v, own_v)
 
-    tile = min(512, span)
-    steps = span // tile
     sums = []
-    for c in range(CHUNKS):
-        w_spec = pl.BlockSpec((2, tile, depth), lambda t, c=c: (0, c * steps + t, 0))
+    for first, span in chunks(hc):
         mine, *parts = pl.pallas_call(
-            functools.partial(project_kernel, chips),
-            grid=(steps,),
-            in_specs=[pl.BlockSpec((rows, 2 * depth + LANES), lambda t: (0, 0))] * chips + [w_spec] * 2,
-            out_specs=[pl.BlockSpec((rows, tile), lambda t: (0, t))] * chips,
+            functools.partial(project_kernel, chips, first),
             out_shape=[shape((rows, span), F32)] + [shape((rows, span))] * (chips - 1),
             scratch_shapes=[pltpu.VMEM((2, 2, chips * rows, depth), BF16)],
             compiler_params=params(12),
@@ -390,21 +405,22 @@
     from_right, from_left = shifted(own, -1), shifted(far, 1)
 
     pieces = []
-    for c in range(CHUNKS):
+    for c, (first, span) in enumerate(chunks(hc)):
+        heads = span // HEAD_DIM
         gout, delta, left_v = pl.pallas_call(
-            functools.partial(delta_kernel, count, c, chips - 1, scale),
+            functools.partial(delta_kernel, count, first, chips - 1, scale),
             out_shape=[shape((rows + 2 * heads, span)), shape((heads, rows), F32), shape((rows, span))],
             compiler_params=params(8),
             cost_estimate=cost(4 * 2 * rows * rows * span, 20 * rows * span),
         )(*sums[c], query, key_value, left_k, *values, segments, own, from_left)
         pieces.append((gout, delta, left_v, shifted(gout, -1)))
 
-    half = shape((2, rows, span))
     parts = []
-    for c in range(CHUNKS):
+    for c, (first, span) in enumerate(chunks(hc)):
+        heads, half = span // HEAD_DIM, shape((2, rows, span))
         gout, delta, left_v, right_g = pieces[c]
         *kept, to1, to2 = pl.pallas_call(
-            functools.partial(grads_kernel, count, c, scale),
+            functools.partial(grads_kernel, count, first, scale),
             out_shape=[
                 shape((rows, span), F32), shape((2, rows, span), F32), shape((heads, 2 * rows, rows)), half, half],
             scratch_shapes=[pltpu.VMEM((heads, rows), F32)],
@@ -414,17 +430,14 @@
         parts.append((*kept, query, key_value, left_k, *neighbour_swaps(to1, to2)))
 
     results = ()
-    for c in range(CHUNKS):
+    anywhere = pl.BlockSpec(memory_space=pl.ANY)
+    for c, (first, span) in enumerate(chunks(hc)):
         results = pl.pallas_call(
-            functools.partial(finish_kernel, count, c, scale),
-            grid=(1,),
-            in_specs=[pl.BlockSpec(memory_space=pltpu.VMEM)] * len(parts[c])
-            + [pl.BlockSpec(memory_space=pl.ANY)] * len(results),
-            out_specs=[
-                pl.BlockSpec((1, rows, span), lambda t, c=c: (0, 0, c)),
-                pl.BlockSpec((2, 1, rows, span), lambda t, c=c: (0, 0, 0, c)),
-            ],
+            functools.partial(finish_kernel, count, first, scale),
+            in_specs=[pl.BlockSpec(memory_space=pltpu.VMEM)] * len(parts[c]) + [anywhere] * len(results),
+            out_specs=[anywhere] * 2,
             out_shape=[shape(query.shape), shape(key_value.shape)],
+            scratch_shapes=[pltpu.VMEM((3, rows, span), BF16), pltpu.SemaphoreType.DMA((2,))],
             input_output_aliases={len(parts[c]) + n: n for n in range(len(results))},
             compiler_params=params(12),
             cost_estimate=cost(0, 20 * rows * span),

time: 91.8 us -> 89.2 us (0.972)
  Pallas kernels: 18.8 us -> 17.5 us
  starting transfers between devices: 41 us -> 39.8 us
    pallas_call x9 -> x10, Pallas kernels: 17.3 us -> 15.9 us  [the longest x2 5.9 us: step(): pl.pallas_call(functools.partial(grads_kernel, count, first, scale), out_...]
    ppermute x4, starting transfers between devices: 15.2 us -> 13.9 us  [shifted(): lax.ppermute(value, 'seq', [(i, (i + steps) % count) for i in range(count)])]
    ppermute x10, waiting for transfers between devices: 16.7 us -> 15.7 us  [swap(): lax.ppermute(value, axis, [(i, i ^ bits) for i in range(lax.axis_size(axi...]
  transfers between devices with their start and end apart: 22 -> 22, of which waited for: 7 -> 10; matrix products, arithmetic and copies ran while one was open for 0% -> 0% of each run, Pallas kernels for 19% -> 18%
where the time goes in v3:
time: 89.2 us; the launch traced here: 88.4 us
  starting transfers between devices  39.8 us (45%)
  waiting for transfers between devices  30.1 us (34%)
  Pallas kernels  17.5 us (20%)
  between operations  0.97 us (1%)
    ppermute x10, waiting for transfers between devices, swap(): lax.ppermute(value, axis, [(i, i ^ bits) for i in range(lax.axis_size(axi...  15.7 us
    ppermute x8, starting transfers between devices, neighbour_swaps(): return (lax.ppermute(first, 'seq', one), lax.ppermute(second, 'seq', two))  14.5 us
    ppermute x4, starting transfers between devices, shifted(): lax.ppermute(value, 'seq', [(i, (i + steps) % count) for i in range(count)])  13.9 us
    ppermute x8, waiting for transfers between devices, neighbour_swaps(): return (lax.ppermute(first, 'seq', one), lax.ppermute(second, 'seq', two))  11.4 us
    ppermute x10, starting transfers between devices, swap(): lax.ppermute(value, axis, [(i, i ^ bits) for i in range(lax.axis_size(axi...  11.3 us
    pallas_call x2, Pallas kernels, step(): pl.pallas_call(functools.partial(grads_kernel, count, first, scale), out_...  5.9 us
    ppermute x4, waiting for transfers between devices, shifted(): lax.ppermute(value, 'seq', [(i, (i + steps) % count) for i in range(count)])  2.96 us
    pallas_call x2, Pallas kernels, step(): pl.pallas_call(functools.partial(finish_kernel, count, first, scale), in_...  2.96 us
  transfers between devices with their start and end apart: 22, of which 10 were waited for; matrix products, arithmetic and copies ran while one was open for 0% of the time, Pallas kernels for 18%

profile of v3, /device:TPU:0, one launch (start us, length us, event | category | flops | bytes accessed | tf_op | source)
XLA Modules:
  0.0 88.4 jit_solution(894578122755544004)
XLA Ops:
  0.6 0.6 collective-permute-start.5
  1.2 1.2 %grad_slices.1 = (bf16[128,640]{1,0:T(8,128)(2,1)S(1)}, bf16[128,640]{1,0:T(8,128)(2,1)S(1)}, bf16[128,640]{1,0:T(8,128)(2,1)S(1)}, bf16[128,640]{1,0:T(8,128)(2,1)S(1)}) custom-call(bf16[1,128,2048]{2,1,0:T(8,128)(2,1)} %grad_ref.1, s32[1,128]{1,0:T(1,128)} %tags_ref.1), custom_call_target="tpu_custom_call" | custom-call | bytes 1048576 | tf_op jit(solution)/shard_map/grad_slices/pallas_call | solution.py:363
  2.4 2.6 %collective-permute-start.2 = (bf16[128,640]{1,0:T(8,128)(2,1)S(1)}, bf16[128,640]{1,0:T(8,128)(2,1)S(1)}, u32[]{:S(2)}, u32[]{:S(2)}) collective-permute-start(bf16[128,640]{1,0:T(8,128)(2,1)S(1)} %get-tuple-element.43), channel_id=1, source_target_pairs={{0,8},{4,12},{8,0},{12,4},{16,24},{20,28},{24,16},{28,20},{1,9},{5... | collective-permute-start | bytes 491528 | tf_op jit(solution)/shard_map/ppermute | solution.py:31
  5.0 1.5 %collective-permute-start.3 = (bf16[128,640]{1,0:T(8,128)(2,1)S(1)}, bf16[128,640]{1,0:T(8,128)(2,1)S(1)}, u32[]{:S(2)}, u32[]{:S(2)}) collective-permute-start(bf16[128,640]{1,0:T(8,128)(2,1)S(1)} %get-tuple-element.44), channel_id=1, source_target_pairs={{0,16},{4,20},{8,24},{12,28},{16,0},{20,4},{24,8},{28,12},{1,17},{... | collective-permute-start | bytes 491528 | tf_op jit(solution)/shard_map/ppermute | solution.py:31
  6.6 0.0 collective-permute-start.4
  6.6 1.4 %side_slices.1 = (bf16[128,2048]{1,0:T(8,128)(2,1)S(1)}, bf16[128,2048]{1,0:T(8,128)(2,1)S(1)}, bf16[128,2048]{1,0:T(8,128)(2,1)S(1)}) custom-call(bf16[1,128,2048]{2,1,0:T(8,128)(2,1)} %q_ref.11, bf16[2,1,128,2048]{3,2,1,0:T(8,128)(2,1)} %kv_ref.11), custom_call_target="tpu_custom_call" | custom-call | bytes 3145728 | tf_op jit(solution)/shard_map/side_slices/pallas_call | solution.py:374
  8.0 2.1 %collective-permute-start = (bf16[128,2048]{1,0:T(8,128)(2,1)S(1)}, bf16[128,2048]{1,0:T(8,128)(2,1)S(1)}, u32[]{:S(2)}, u32[]{:S(2)}) collective-permute-start(bf16[128,2048]{1,0:T(8,128)(2,1)S(1)} %get-tuple-element.39), channel_id=1, source_target_pairs={{0,1},{1,0},{2,3},{3,2},{4,5},{5,4},{6,7},{7,6},{8,9},{9,8},{10,11... | collective-permute-start | bytes 1572872 | tf_op jit(solution)/shard_map/ppermute | solution.py:334
  10.1 0.0 collective-permute-done.2.refs_1_
  10.1 0.7 collective-permute-start.1
  10.8 4.0 %collective-permute-done.3.refs_2_ = bf16[128,640]{1,0:T(8,128)(2,1)S(1)} collective-permute-done((bf16[128,640]{1,0:T(8,128)(2,1)S(1)}, bf16[128,640]{1,0:T(8,128)(2,1)S(1)}, u32[]{:S(2)}, u32[]{:S(2)}) %collective-permute-start.3) | collective-permute-done | bytes 163872 | tf_op jit(solution)/shard_map/ppermute | solution.py:31
  14.7 0.7 collective-permute-start.10
  15.4 0.0 collective-permute-done.4.refs_3_
  15.4 4.4 %collective-permute-start.9 = (bf16[128,2048]{1,0:T(8,128)(2,1)S(1)}, bf16[128,2048]{1,0:T(8,128)(2,1)S(1)}, u32[]{:S(2)}, u32[]{:S(2)}) collective-permute-start(bf16[128,2048]{1,0:T(8,128)(2,1)S(1)} %get-tuple-element.50), channel_id=1, source_target_pairs={{0,1},{1,0},{2,3},{3,2},{4,5},{5,4},{6,7},{7,6},{8,9},{9,8},{10,11... | collective-permute-start | bytes 1572872 | tf_op jit(solution)/shard_map/ppermute | solution.py:334
  19.9 0.0 collective-permute-done.5.refs_5_
  19.9 0.0 copy-start.3
  19.9 1.3 %shard_map.80 = (f32[128,1024]{1,0:T(8,128)S(1)}, bf16[128,1024]{1,0:T(8,128)(2,1)S(1)}, bf16[128,1024]{1,0:T(8,128)(2,1)S(1)}, bf16[128,1024]{1,0:T(8,128)(2,1)S(1)}) custom-call(bf16[128,640]{1,0:T(8,128)(2,1)S(1)} %get-tuple-element.42.refs_0_, bf16[128,640]{1,0:T(8,128)(2,1)S(1)} %collective-permute-done.2.refs_1_, ...), custom_call_target="tpu_custom_call" | custom-call | flops 1073741824 | bytes 2097152 | tf_op jit(solution)/shard_map/pallas_call | solution.py:388
  21.2 0.1 collective-permute-start.16
  21.3 1.5 %collective-permute-done.got1 = bf16[128,2048]{1,0:T(8,128)(2,1)S(1)} collective-permute-done((bf16[128,2048]{1,0:T(8,128)(2,1)S(1)}, bf16[128,2048]{1,0:T(8,128)(2,1)S(1)}, u32[]{:S(2)}, u32[]{:S(2)}) %collective-permute-start) | collective-permute-done | bytes 524320 | tf_op jit(solution)/shard_map/ppermute | solution.py:334
  22.9 0.0 collective-permute-done.1.got2
  22.9 1.5 %stats.1 = (f32[2,16,128]{2,1,0:T(8,128)S(1)}, f32[2,16,128]{2,1,0:T(8,128)S(1)}, bf16[128,2048]{1,0:T(8,128)(2,1)S(1)}, bf16[128,2048]{1,0:T(8,128)(2,1)S(1)}) custom-call(bf16[1,128,2048]{2,1,0:T(8,128)(2,1)S(1)} %copy-done.1, bf16[2,1,128,2048]{3,2,1,0:T(8,128)(2,1)S(1)} %copy-done, bf16[128,2048]{1,0:T(8,128)(2,1)S(1)} %collective-permute-done.got1, ...), custom_call_target="tpu_custom_call" | custom-call | flops 201326592 | bytes 5242880 | tf_op jit(solution)/shard_map/stats/pallas_call | solution.py:398
  24.4 6.1 %collective-permute-start.11 = (f32[2,16,128]{2,1,0:T(8,128)S(1)}, f32[2,16,128]{2,1,0:T(8,128)S(1)}, u32[]{:S(2)}, u32[]{:S(2)}) collective-permute-start(f32[2,16,128]{2,1,0:T(8,128)S(1)} %get-tuple-element.52.far_stats), channel_id=1, source_target_pairs={{0,1},{1,2},{2,3},{3,0},{4,5},{5,6},{6,7},{7,4},{8,9},{9,10},{10,1... | collective-permute-start | bytes 49160 | tf_op jit(solution)/shard_map/ppermute | solution.py:326
  30.5 1.5 %collective-permute-start.17 = (bf16[128,1024]{1,0:T(8,128)(2,1)S(1)}, bf16[128,1024]{1,0:T(8,128)(2,1)S(1)}, u32[]{:S(2)}, u32[]{:S(2)}) collective-permute-start(bf16[128,1024]{1,0:T(8,128)(2,1)S(1)} %get-tuple-element.64), channel_id=1, source_target_pairs={{0,16},{4,20},{8,24},{12,28},{16,0},{20,4},{24,8},{28,12},{1,17},{... | collective-permute-start | bytes 786440 | tf_op jit(solution)/shard_map/ppermute | solution.py:31
  32.0 1.4 %collective-permute-start.18 = (bf16[128,1024]{1,0:T(8,128)(2,1)S(1)}, bf16[128,1024]{1,0:T(8,128)(2,1)S(1)}, u32[]{:S(2)}, u32[]{:S(2)}) collective-permute-start(bf16[128,1024]{1,0:T(8,128)(2,1)S(1)} %get-tuple-element.65), channel_id=1, source_target_pairs={{0,24},{4,28},{8,16},{12,20},{16,8},{20,12},{24,0},{28,4},{1,25},{... | collective-permute-start | bytes 786440 | tf_op jit(solution)/shard_map/ppermute | solution.py:31
  33.4 1.3 %shard_map.77 = (f32[128,1024]{1,0:T(8,128)S(1)}, bf16[128,1024]{1,0:T(8,128)(2,1)S(1)}, bf16[128,1024]{1,0:T(8,128)(2,1)S(1)}, bf16[128,1024]{1,0:T(8,128)(2,1)S(1)}) custom-call(bf16[128,640]{1,0:T(8,128)(2,1)S(1)} %get-tuple-element.42.refs_0_, bf16[128,640]{1,0:T(8,128)(2,1)S(1)} %collective-permute-done.2.refs_1_, ...), custom_call_target="tpu_custom_call" | custom-call | flops 1073741824 | bytes 2097152 | tf_op jit(solution)/shard_map/pallas_call | solution.py:388
  34.8 0.6 collective-permute-start.6
  35.4 0.2 collective-permute-done.11.refs_10_.from_left
  35.6 1.5 %collective-permute-start.7 = (bf16[128,1024]{1,0:T(8,128)(2,1)S(1)}, bf16[128,1024]{1,0:T(8,128)(2,1)S(1)}, u32[]{:S(2)}, u32[]{:S(2)}) collective-permute-start(bf16[128,1024]{1,0:T(8,128)(2,1)S(1)} %get-tuple-element.48), channel_id=1, source_target_pairs={{0,16},{4,20},{8,24},{12,28},{16,0},{20,4},{24,8},{28,12},{1,17},{... | collective-permute-start | bytes 786440 | tf_op jit(solution)/shard_map/ppermute | solution.py:31
  37.1 1.4 %collective-permute-start.8 = (bf16[128,1024]{1,0:T(8,128)(2,1)S(1)}, bf16[128,1024]{1,0:T(8,128)(2,1)S(1)}, u32[]{:S(2)}, u32[]{:S(2)}) collective-permute-start(bf16[128,1024]{1,0:T(8,128)(2,1)S(1)} %get-tuple-element.49), channel_id=1, source_target_pairs={{0,24},{4,28},{8,16},{12,20},{16,8},{20,12},{24,0},{28,4},{1,25},{... | collective-permute-start | bytes 786440 | tf_op jit(solution)/shard_map/ppermute | solution.py:31
  38.5 3.6 %collective-permute-done.17.refs_1_ = bf16[128,1024]{1,0:T(8,128)(2,1)S(1)} collective-permute-done((bf16[128,1024]{1,0:T(8,128)(2,1)S(1)}, bf16[128,1024]{1,0:T(8,128)(2,1)S(1)}, u32[]{:S(2)}, u32[]{:S(2)}) %collective-permute-start.17) | collective-permute-done | bytes 262176 | tf_op jit(solution)/shard_map/ppermute | solution.py:31
  42.1 0.1 collective-permute-done.18.refs_2_
  42.2 0.9 %shard_map.81 = (bf16[144,1024]{1,0:T(8,128)(2,1)S(1)}, f32[8,128]{1,0:T(8,128)S(1)}, bf16[128,1024]{1,0:T(8,128)(2,1)S(1)}) custom-call(f32[128,1024]{1,0:T(8,128)S(1)} %get-tuple-element.62.mine, bf16[128,1024]{1,0:T(8,128)(2,1)S(1)} %collective-permute-done.16.refs_0_, bf16[128,1024]{1,0:T(8,128)(2,1)S(1)} %collective-permute-done.17.refs_1_, ...), custom_call_target="tpu_custom_call" | custom-call | flops 134217728 | bytes 2621440 | tf_op jit(solution)/shard_map/pallas_call | solution.py:410
  43.1 0.1 collective-permute-start.19
  43.2 2.6 %collective-permute-done.6.refs_0_ = bf16[128,1024]{1,0:T(8,128)(2,1)S(1)} collective-permute-done((bf16[128,1024]{1,0:T(8,128)(2,1)S(1)}, bf16[128,1024]{1,0:T(8,128)(2,1)S(1)}, u32[]{:S(2)}, u32[]{:S(2)}) %collective-permute-start.6) | collective-permute-done | bytes 262176 | tf_op jit(solution)/shard_map/ppermute | solution.py:31
  45.7 5.5 %collective-permute-done.7.refs_1_ = bf16[128,1024]{1,0:T(8,128)(2,1)S(1)} collective-permute-done((bf16[128,1024]{1,0:T(8,128)(2,1)S(1)}, bf16[128,1024]{1,0:T(8,128)(2,1)S(1)}, u32[]{:S(2)}, u32[]{:S(2)}) %collective-permute-start.7) | collective-permute-done | bytes 262176 | tf_op jit(solution)/shard_map/ppermute | solution.py:31
  51.3 1.0 %shard_map.78 = (bf16[144,1024]{1,0:T(8,128)(2,1)S(1)}, f32[8,128]{1,0:T(8,128)S(1)}, bf16[128,1024]{1,0:T(8,128)(2,1)S(1)}) custom-call(f32[128,1024]{1,0:T(8,128)S(1)} %get-tuple-element.46.mine, bf16[128,1024]{1,0:T(8,128)(2,1)S(1)} %collective-permute-done.6.refs_0_, bf16[128,1024]{1,0:T(8,128)(2,1)S(1)} %collective-permute-done.7.refs_1_, ...), custom_call_target="tpu_custom_call" | custom-call | flops 134217728 | bytes 2621440 | tf_op jit(solution)/shard_map/pallas_call | solution.py:410
  52.2 0.7 collective-permute-start.12
  52.9 7.1 %collective-permute-start.13 = (f32[2,16,128]{2,1,0:T(8,128)S(1)}, f32[2,16,128]{2,1,0:T(8,128)S(1)}, u32[]{:S(2)}, u32[]{:S(2)}) collective-permute-start(f32[2,16,128]{2,1,0:T(8,128)S(1)} %get-tuple-element.51.refs_9_.own_stats), channel_id=1, source_target_pairs={{0,3},{1,0},{2,1},{3,2},{4,7},{5,4},{6,5},{7,6},{8,11},{9,8},{10,9... | collective-permute-start | bytes 49160 | tf_op jit(solution)/shard_map/ppermute | solution.py:326
  60.0 2.8 %collective-permute-done.13.from_right = f32[2,16,128]{2,1,0:T(8,128)S(1)} collective-permute-done((f32[2,16,128]{2,1,0:T(8,128)S(1)}, f32[2,16,128]{2,1,0:T(8,128)S(1)}, u32[]{:S(2)}, u32[]{:S(2)}) %collective-permute-start.13) | collective-permute-done | bytes 16416 | tf_op jit(solution)/shard_map/ppermute | solution.py:326
  62.8 2.9 %shard_map.82 = (f32[128,1024]{1,0:T(8,128)S(1)}, f32[2,128,1024]{2,1,0:T(8,128)S(1)}, bf16[8,256,128]{2,1,0:T(8,128)(2,1)S(1)}, bf16[2,128,1024]{2,1,0:T(8,128)(2,1)S(1)}, bf16[2,128,1024]{2,1,0:T(8,128)(2,1)S(1)}) custom-call(bf16[1,128,2048]{2,1,0:T(8,128)(2,1)S(1)} %copy-done.1, bf16[2,1,128,2048]{3,2,1,0:T(8,128)(2,1)S(1)} %copy-done, ...), custom_call_target="tpu_custom_call" | custom-call | flops 503316480 | bytes 5242880 | tf_op jit(solution)/shard_map/pallas_call | solution.py:422
  65.6 2.1 %collective-permute-start.20 = (bf16[2,128,1024]{2,1,0:T(8,128)(2,1)S(1)}, bf16[2,128,1024]{2,1,0:T(8,128)(2,1)S(1)}, u32[]{:S(2)}, u32[]{:S(2)}) collective-permute-start(bf16[2,128,1024]{2,1,0:T(8,128)(2,1)S(1)} %get-tuple-element.72), channel_id=1, source_target_pairs={{0,1},{1,0},{2,3},{3,2},{4,5},{5,4},{6,7},{7,6},{8,9},{9,8},{10,11... | collective-permute-start | bytes 1572872 | tf_op jit(solution)/shard_map/ppermute | solution.py:334
  67.7 0.7 collective-permute-start.21
  68.4 3.0 %shard_map.79 = (f32[128,1024]{1,0:T(8,128)S(1)}, f32[2,128,1024]{2,1,0:T(8,128)S(1)}, bf16[8,256,128]{2,1,0:T(8,128)(2,1)S(1)}, bf16[2,128,1024]{2,1,0:T(8,128)(2,1)S(1)}, bf16[2,128,1024]{2,1,0:T(8,128)(2,1)S(1)}) custom-call(bf16[1,128,2048]{2,1,0:T(8,128)(2,1)S(1)} %copy-done.1, bf16[2,1,128,2048]{3,2,1,0:T(8,128)(2,1)S(1)} %copy-done, ...), custom_call_target="tpu_custom_call" | custom-call | flops 503316480 | bytes 5242880 | tf_op jit(solution)/shard_map/pallas_call | solution.py:422
  71.5 3.2 %collective-permute-start.14 = (bf16[2,128,1024]{2,1,0:T(8,128)(2,1)S(1)}, bf16[2,128,1024]{2,1,0:T(8,128)(2,1)S(1)}, u32[]{:S(2)}, u32[]{:S(2)}) collective-permute-start(bf16[2,128,1024]{2,1,0:T(8,128)(2,1)S(1)} %get-tuple-element.60), channel_id=1, source_target_pairs={{0,1},{1,0},{2,3},{3,2},{4,5},{5,4},{6,7},{7,6},{8,9},{9,8},{10,11... | collective-permute-start | bytes 1572872 | tf_op jit(solution)/shard_map/ppermute | solution.py:334
  74.7 0.7 collective-permute-start.15
  75.4 5.0 %collective-permute-done.20.got1 = bf16[2,128,1024]{2,1,0:T(8,128)(2,1)S(1)} collective-permute-done((bf16[2,128,1024]{2,1,0:T(8,128)(2,1)S(1)}, bf16[2,128,1024]{2,1,0:T(8,128)(2,1)S(1)}, u32[]{:S(2)}, u32[]{:S(2)}) %collective-permute-start.20) | collective-permute-done | bytes 524320 | tf_op jit(solution)/shard_map/ppermute | solution.py:334
  80.4 1.5 %shard_map.83 = (bf16[1,128,2048]{2,1,0:T(8,128)(2,1)}, bf16[2,1,128,2048]{3,2,1,0:T(8,128)(2,1)}) custom-call(f32[128,1024]{1,0:T(8,128)S(1)} %get-tuple-element.69.dq_ref, f32[2,128,1024]{2,1,0:T(8,128)S(1)} %get-tuple-element.70.dkv_ref, bf16[8,256,128]{2,1,0:T(8,128)(2,1)S(1)} %get-tuple-element.71.p_ref, bf16[1,128,2048]{2,1,0:T(8,128)(2,1)S(1)} %copy-done.1, ...), custom_call_target="tpu_custom_call" | custom-call | bytes 2621440 | tf_op jit(solution)/shard_map/pallas_call | solution.py:435
  81.8 4.9 %collective-permute-done.14.got1 = bf16[2,128,1024]{2,1,0:T(8,128)(2,1)S(1)} collective-permute-done((bf16[2,128,1024]{2,1,0:T(8,128)(2,1)S(1)}, bf16[2,128,1024]{2,1,0:T(8,128)(2,1)S(1)}, u32[]{:S(2)}, u32[]{:S(2)}) %collective-permute-start.14) | collective-permute-done | bytes 524320 | tf_op jit(solution)/shard_map/ppermute | solution.py:334
  86.7 1.5 %shard_map.84 = (bf16[1,128,2048]{2,1,0:T(8,128)(2,1)}, bf16[2,1,128,2048]{3,2,1,0:T(8,128)(2,1)}) custom-call(f32[128,1024]{1,0:T(8,128)S(1)} %get-tuple-element.57.dq_ref, f32[2,128,1024]{2,1,0:T(8,128)S(1)} %get-tuple-element.58.dkv_ref, bf16[8,256,128]{2,1,0:T(8,128)(2,1)S(1)} %get-tuple-element.59.p_ref, ...), custom_call_target="tpu_custom_call", output_to_operand_aliasing={{0}: (8, {}), {1}: (9, {})} | custom-call | bytes 2621440 | tf_op jit(solution)/shard_map/pallas_call | solution.py:435
  (15 shorter events, 0.0 us)
Async XLA Ops:
  0.6 19.3 %copy-start.2 = (bf16[2,2048,256]{2,1,0:T(8,128)(2,1)S(1)}, bf16[2,2048,256]{2,1,0:T(8,128)(2,1)}, u32[]{:S(2)}) copy-start(bf16[2,2048,256]{2,1,0:T(8,128)(2,1)} %refs_4_.6) | copy-start | bytes 6291460
  0.6 19.2 %collective-permute-start.5 = (bf16[2,2048,256]{2,1,0:T(8,128)(2,1)}, bf16[2,2048,256]{2,1,0:T(8,128)(2,1)S(1)}, u32[]{:S(2)}, u32[]{:S(2)}) collective-permute-start(bf16[2,2048,256]{2,1,0:T(8,128)(2,1)} %refs_4_.6), channel_id=1, source_target_pairs={{0,4},{4,0},{8,12},{12,8},{16,20},{20,16},{24,28},{28,24},{1,5},{5... | collective-permute-start | bytes 6291464 | tf_op jit(solution)/shard_map/ppermute | solution.py:31
  2.4 7.7 %collective-permute-start.2 = (bf16[128,640]{1,0:T(8,128)(2,1)S(1)}, bf16[128,640]{1,0:T(8,128)(2,1)S(1)}, u32[]{:S(2)}, u32[]{:S(2)}) collective-permute-start(bf16[128,640]{1,0:T(8,128)(2,1)S(1)} %get-tuple-element.43), channel_id=1, source_target_pairs={{0,8},{4,12},{8,0},{12,4},{16,24},{20,28},{24,16},{28,20},{1,9},{5... | collective-permute-start | bytes 491528 | tf_op jit(solution)/shard_map/ppermute | solution.py:31
  5.0 9.7 %collective-permute-start.3 = (bf16[128,640]{1,0:T(8,128)(2,1)S(1)}, bf16[128,640]{1,0:T(8,128)(2,1)S(1)}, u32[]{:S(2)}, u32[]{:S(2)}) collective-permute-start(bf16[128,640]{1,0:T(8,128)(2,1)S(1)} %get-tuple-element.44), channel_id=1, source_target_pairs={{0,16},{4,20},{8,24},{12,28},{16,0},{20,4},{24,8},{28,12},{1,17},{... | collective-permute-start | bytes 491528 | tf_op jit(solution)/shard_map/ppermute | solution.py:31
  6.6 8.9 %collective-permute-start.4 = (bf16[128,640]{1,0:T(8,128)(2,1)S(1)}, bf16[128,640]{1,0:T(8,128)(2,1)S(1)}, u32[]{:S(2)}, u32[]{:S(2)}) collective-permute-start(bf16[128,640]{1,0:T(8,128)(2,1)S(1)} %get-tuple-element.45), channel_id=1, source_target_pairs={{0,24},{4,28},{8,16},{12,20},{16,8},{20,12},{24,0},{28,4},{1,25},{... | collective-permute-start | bytes 491528 | tf_op jit(solution)/shard_map/ppermute | solution.py:31
  8.0 14.9 %collective-permute-start = (bf16[128,2048]{1,0:T(8,128)(2,1)S(1)}, bf16[128,2048]{1,0:T(8,128)(2,1)S(1)}, u32[]{:S(2)}, u32[]{:S(2)}) collective-permute-start(bf16[128,2048]{1,0:T(8,128)(2,1)S(1)} %get-tuple-element.39), channel_id=1, source_target_pairs={{0,1},{1,0},{2,3},{3,2},{4,5},{5,4},{6,7},{7,6},{8,9},{9,8},{10,11... | collective-permute-start | bytes 1572872 | tf_op jit(solution)/shard_map/ppermute | solution.py:334
  10.1 12.8 %collective-permute-start.1 = (bf16[128,2048]{1,0:T(8,128)(2,1)S(1)}, bf16[128,2048]{1,0:T(8,128)(2,1)S(1)}, u32[]{:S(2)}, u32[]{:S(2)}) collective-permute-start(bf16[128,2048]{1,0:T(8,128)(2,1)S(1)} %get-tuple-element.40), channel_id=1, source_target_pairs={{0,0},{1,2},{2,1},{3,3},{4,4},{5,6},{6,5},{7,7},{8,8},{9,10},{10,9... | collective-permute-start | bytes 1572872 | tf_op jit(solution)/shard_map/ppermute | solution.py:334
  14.7 17.3 %collective-permute-start.10 = (bf16[128,2048]{1,0:T(8,128)(2,1)S(1)}, bf16[128,2048]{1,0:T(8,128)(2,1)S(1)}, u32[]{:S(2)}, u32[]{:S(2)}) collective-permute-start(bf16[128,2048]{1,0:T(8,128)(2,1)S(1)} %get-tuple-element.50), channel_id=1, source_target_pairs={{0,0},{1,2},{2,1},{3,3},{4,4},{5,6},{6,5},{7,7},{8,8},{9,10},{10,9... | collective-permute-start | bytes 1572872 | tf_op jit(solution)/shard_map/ppermute | solution.py:334
  15.4 19.3 %collective-permute-start.9 = (bf16[128,2048]{1,0:T(8,128)(2,1)S(1)}, bf16[128,2048]{1,0:T(8,128)(2,1)S(1)}, u32[]{:S(2)}, u32[]{:S(2)}) collective-permute-start(bf16[128,2048]{1,0:T(8,128)(2,1)S(1)} %get-tuple-element.50), channel_id=1, source_target_pairs={{0,1},{1,0},{2,3},{3,2},{4,5},{5,4},{6,7},{7,6},{8,9},{9,8},{10,11... | collective-permute-start | bytes 1572872 | tf_op jit(solution)/shard_map/ppermute | solution.py:334
  19.9 3.0 %copy-start = (bf16[2,1,128,2048]{3,2,1,0:T(8,128)(2,1)S(1)}, bf16[2,1,128,2048]{3,2,1,0:T(8,128)(2,1)}, u32[]{:S(2)}) copy-start(bf16[2,1,128,2048]{3,2,1,0:T(8,128)(2,1)} %kv_ref.11) | copy-start | bytes 3145732
  19.9 3.0 %copy-start.1 = (bf16[1,128,2048]{2,1,0:T(8,128)(2,1)S(1)}, bf16[1,128,2048]{2,1,0:T(8,128)(2,1)}, u32[]{:S(2)}) copy-start(bf16[1,128,2048]{2,1,0:T(8,128)(2,1)} %q_ref.11) | copy-start | bytes 1572868
  19.9 3.0 %copy-start.3 = (s32[1,512]{1,0:T(1,128)S(1)}, s32[1,512]{1,0:T(1,128)}, u32[]{:S(2)}) copy-start(s32[1,512]{1,0:T(1,128)} %segs.5) | copy-start | bytes 6148
  21.2 15.9 %collective-permute-start.16 = (bf16[128,1024]{1,0:T(8,128)(2,1)S(1)}, bf16[128,1024]{1,0:T(8,128)(2,1)S(1)}, u32[]{:S(2)}, u32[]{:S(2)}) collective-permute-start(bf16[128,1024]{1,0:T(8,128)(2,1)S(1)} %get-tuple-element.63), channel_id=1, source_target_pairs={{0,8},{4,12},{8,0},{12,4},{16,24},{20,28},{24,16},{28,20},{1,9},{5... | collective-permute-start | bytes 786440 | tf_op jit(solution)/shard_map/ppermute | solution.py:31
  24.4 11.1 %collective-permute-start.11 = (f32[2,16,128]{2,1,0:T(8,128)S(1)}, f32[2,16,128]{2,1,0:T(8,128)S(1)}, u32[]{:S(2)}, u32[]{:S(2)}) collective-permute-start(f32[2,16,128]{2,1,0:T(8,128)S(1)} %get-tuple-element.52.far_stats), channel_id=1, source_target_pairs={{0,1},{1,2},{2,3},{3,0},{4,5},{5,6},{6,7},{7,4},{8,9},{9,10},{10,1... | collective-permute-start | bytes 49160 | tf_op jit(solution)/shard_map/ppermute | solution.py:326
  30.5 11.6 %collective-permute-start.17 = (bf16[128,1024]{1,0:T(8,128)(2,1)S(1)}, bf16[128,1024]{1,0:T(8,128)(2,1)S(1)}, u32[]{:S(2)}, u32[]{:S(2)}) collective-permute-start(bf16[128,1024]{1,0:T(8,128)(2,1)S(1)} %get-tuple-element.64), channel_id=1, source_target_pairs={{0,16},{4,20},{8,24},{12,28},{16,0},{20,4},{24,8},{28,12},{1,17},{... | collective-permute-start | bytes 786440 | tf_op jit(solution)/shard_map/ppermute | solution.py:31
  32.0 10.2 %collective-permute-start.18 = (bf16[128,1024]{1,0:T(8,128)(2,1)S(1)}, bf16[128,1024]{1,0:T(8,128)(2,1)S(1)}, u32[]{:S(2)}, u32[]{:S(2)}) collective-permute-start(bf16[128,1024]{1,0:T(8,128)(2,1)S(1)} %get-tuple-element.65), channel_id=1, source_target_pairs={{0,24},{4,28},{8,16},{12,20},{16,8},{20,12},{24,0},{28,4},{1,25},{... | collective-permute-start | bytes 786440 | tf_op jit(solution)/shard_map/ppermute | solution.py:31
  34.8 11.0 %collective-permute-start.6 = (bf16[128,1024]{1,0:T(8,128)(2,1)S(1)}, bf16[128,1024]{1,0:T(8,128)(2,1)S(1)}, u32[]{:S(2)}, u32[]{:S(2)}) collective-permute-start(bf16[128,1024]{1,0:T(8,128)(2,1)S(1)} %get-tuple-element.47), channel_id=1, source_target_pairs={{0,8},{4,12},{8,0},{12,4},{16,24},{20,28},{24,16},{28,20},{1,9},{5... | collective-permute-start | bytes 786440 | tf_op jit(solution)/shard_map/ppermute | solution.py:31
  35.6 15.7 %collective-permute-start.7 = (bf16[128,1024]{1,0:T(8,128)(2,1)S(1)}, bf16[128,1024]{1,0:T(8,128)(2,1)S(1)}, u32[]{:S(2)}, u32[]{:S(2)}) collective-permute-start(bf16[128,1024]{1,0:T(8,128)(2,1)S(1)} %get-tuple-element.48), channel_id=1, source_target_pairs={{0,16},{4,20},{8,24},{12,28},{16,0},{20,4},{24,8},{28,12},{1,17},{... | collective-permute-start | bytes 786440 | tf_op jit(solution)/shard_map/ppermute | solution.py:31
  37.1 14.2 %collective-permute-start.8 = (bf16[128,1024]{1,0:T(8,128)(2,1)S(1)}, bf16[128,1024]{1,0:T(8,128)(2,1)S(1)}, u32[]{:S(2)}, u32[]{:S(2)}) collective-permute-start(bf16[128,1024]{1,0:T(8,128)(2,1)S(1)} %get-tuple-element.49), channel_id=1, source_target_pairs={{0,24},{4,28},{8,16},{12,20},{16,8},{20,12},{24,0},{28,4},{1,25},{... | collective-permute-start | bytes 786440 | tf_op jit(solution)/shard_map/ppermute | solution.py:31
  43.1 19.7 %collective-permute-start.19 = (bf16[144,1024]{1,0:T(8,128)(2,1)S(1)}, bf16[144,1024]{1,0:T(8,128)(2,1)S(1)}, u32[]{:S(2)}, u32[]{:S(2)}) collective-permute-start(bf16[144,1024]{1,0:T(8,128)(2,1)S(1)} %get-tuple-element.67.g_ref), channel_id=1, source_target_pairs={{0,3},{1,0},{2,1},{3,2},{4,7},{5,4},{6,5},{7,6},{8,11},{9,8},{10,9... | collective-permute-start | bytes 884744 | tf_op jit(solution)/shard_map/ppermute | solution.py:326
  52.2 16.2 %collective-permute-start.12 = (bf16[144,1024]{1,0:T(8,128)(2,1)S(1)}, bf16[144,1024]{1,0:T(8,128)(2,1)S(1)}, u32[]{:S(2)}, u32[]{:S(2)}) collective-permute-start(bf16[144,1024]{1,0:T(8,128)(2,1)S(1)} %get-tuple-element.55.g_ref), channel_id=1, source_target_pairs={{0,3},{1,0},{2,1},{3,2},{4,7},{5,4},{6,5},{7,6},{8,11},{9,8},{10,9... | collective-permute-start | bytes 884744 | tf_op jit(solution)/shard_map/ppermute | solution.py:326
  52.9 9.9 %collective-permute-start.13 = (f32[2,16,128]{2,1,0:T(8,128)S(1)}, f32[2,16,128]{2,1,0:T(8,128)S(1)}, u32[]{:S(2)}, u32[]{:S(2)}) collective-permute-start(f32[2,16,128]{2,1,0:T(8,128)S(1)} %get-tuple-element.51.refs_9_.own_stats), channel_id=1, source_target_pairs={{0,3},{1,0},{2,1},{3,2},{4,7},{5,4},{6,5},{7,6},{8,11},{9,8},{10,9... | collective-permute-start | bytes 49160 | tf_op jit(solution)/shard_map/ppermute | solution.py:326
  65.6 14.7 %collective-permute-start.20 = (bf16[2,128,1024]{2,1,0:T(8,128)(2,1)S(1)}, bf16[2,128,1024]{2,1,0:T(8,128)(2,1)S(1)}, u32[]{:S(2)}, u32[]{:S(2)}) collective-permute-start(bf16[2,128,1024]{2,1,0:T(8,128)(2,1)S(1)} %get-tuple-element.72), channel_id=1, source_target_pairs={{0,1},{1,0},{2,3},{3,2},{4,5},{5,4},{6,7},{7,6},{8,9},{9,8},{10,11... | collective-permute-start | bytes 1572872 | tf_op jit(solution)/shard_map/ppermute | solution.py:334
  67.7 12.6 %collective-permute-start.21 = (bf16[2,128,1024]{2,1,0:T(8,128)(2,1)S(1)}, bf16[2,128,1024]{2,1,0:T(8,128)(2,1)S(1)}, u32[]{:S(2)}, u32[]{:S(2)}) collective-permute-start(bf16[2,128,1024]{2,1,0:T(8,128)(2,1)S(1)} %get-tuple-element.73), channel_id=1, source_target_pairs={{0,0},{1,2},{2,1},{3,3},{4,4},{5,6},{6,5},{7,7},{8,8},{9,10},{10,9... | collective-permute-start | bytes 1572872 | tf_op jit(solution)/shard_map/ppermute | solution.py:334
  71.5 15.2 %collective-permute-start.14 = (bf16[2,128,1024]{2,1,0:T(8,128)(2,1)S(1)}, bf16[2,128,1024]{2,1,0:T(8,128)(2,1)S(1)}, u32[]{:S(2)}, u32[]{:S(2)}) collective-permute-start(bf16[2,128,1024]{2,1,0:T(8,128)(2,1)S(1)} %get-tuple-element.60), channel_id=1, source_target_pairs={{0,1},{1,0},{2,3},{3,2},{4,5},{5,4},{6,7},{7,6},{8,9},{9,8},{10,11... | collective-permute-start | bytes 1572872 | tf_op jit(solution)/shard_map/ppermute | solution.py:334
  74.7 12.1 %collective-permute-start.15 = (bf16[2,128,1024]{2,1,0:T(8,128)(2,1)S(1)}, bf16[2,128,1024]{2,1,0:T(8,128)(2,1)S(1)}, u32[]{:S(2)}, u32[]{:S(2)}) collective-permute-start(bf16[2,128,1024]{2,1,0:T(8,128)(2,1)S(1)} %get-tuple-element.61), channel_id=1, source_target_pairs={{0,0},{1,2},{2,1},{3,3},{4,4},{5,6},{6,5},{7,7},{8,8},{9,10},{10,9... | collective-permute-start | bytes 1572872 | tf_op jit(solution)/shard_map/ppermute | solution.py:334

commit v4 on v3

--- a/solution.py
+++ b/solution.py
@@ -13,6 +13,7 @@
 
 NEG = -1e30
 LANES = 128
+TAG_ROWS = 16
 BF16 = jnp.bfloat16
 F32 = jnp.float32
 NT = (((1,), (1,)), ((), ()))
@@ -40,30 +41,40 @@
 def grad_slices_kernel(grad_ref, tags_ref, *refs):
     outs, (tags, tag_sem, sem) = refs[:-3], refs[-3:]
     chip = lax.axis_index("dp") // 2
-    width = outs[0].shape[1] - LANES
+    rows = grad_ref.shape[1]
+    blocks = (outs[0].shape[0] - TAG_ROWS) // rows
     tag_copy = pltpu.make_async_copy(tags_ref, tags, tag_sem)
     copies = [
-        pltpu.make_async_copy(grad_ref.at[0, :, lane_slice((chip ^ k) * width, width)], out.at[:, :width], sem.at[k])
+        pltpu.make_async_copy(
+            grad_ref.at[0, :, lane_slice(((chip ^ k) * blocks + n) * LANES, LANES)],
+            out.at[n * rows : (n + 1) * rows],
+            sem.at[k, n],
+        )
         for k, out in enumerate(outs)
+        for n in range(blocks)
     ]
     for copy in [tag_copy] + copies:
         copy.start()
     tag_copy.wait()
-    tag = jnp.broadcast_to(column_of(tags[...]), (grad_ref.shape[1], LANES)).astype(BF16)
+    tag = jnp.broadcast_to(tags[...].astype(F32), (TAG_ROWS, LANES)).astype(BF16)
     for out in outs:
-        out[:, width:] = tag
+        out[blocks * rows :] = tag
     for copy in copies:
         copy.wait()
 
 
-def side_slices_kernel(q_ref, kv_ref, first, second, v_out, sem):
-    v_copy = pltpu.make_async_copy(kv_ref.at[1, 0], v_out, sem.at[0])
+def side_slices_kernel(cuts, q_ref, kv_ref, first, second, *refs):
+    v_outs, sem = refs[:-1], refs[-1]
+    v_copies = [
+        pltpu.make_async_copy(kv_ref.at[1, 0, :, at : at + width], out, sem.at[2 + n])
+        for n, ((at, width), out) in enumerate(zip(cuts, v_outs))
+    ]
 
     def sides(up, down):
         copies = [
             pltpu.make_async_copy(kv_ref.at[0, 0], up, sem.at[1]),
-            pltpu.make_async_copy(q_ref.at[0], down, sem.at[2]),
-            v_copy,
+            pltpu.make_async_copy(q_ref.at[0], down, sem.at[0]),
+            *v_copies,
         ]
         for copy in copies:
             copy.start()
@@ -83,16 +94,19 @@
 
 def project_kernel(chips, first, *refs):
     grads, (own_w, other_w), (mine, *parts, lhs) = refs[:chips], refs[chips : chips + 2], refs[chips + 2 :]
-    rows = grads[0].shape[0]
     depth = own_w.shape[2]
+    blocks = depth // LANES
+    rows = mine.shape[0]
     core = lax.axis_index("dp") % 2
-
     for k, grad in enumerate(grads):
-        text = grad[:, 2 * depth : 2 * depth + 1] == 1
+        text = column_of(grad[2 * blocks * rows : 2 * blocks * rows + 1]) == 1.0
         for side in range(2):
-            g = grad[:, lane_slice((core ^ side) * depth, depth)]
-            lhs[side, 0, k * rows : (k + 1) * rows] = jnp.where(text, jnp.zeros_like(g), g)
-            lhs[side, 1, k * rows : (k + 1) * rows] = jnp.where(text, g, jnp.zeros_like(g))
+            for n in range(blocks):
+                at = pl.ds(pl.multiple_of(((core ^ side) * blocks + n) * rows, rows), rows)
+                g = grad[at]
+                where = (slice(k * rows, (k + 1) * rows), slice(n * LANES, (n + 1) * LANES))
+                lhs[(side, 0, *where)] = jnp.where(text, jnp.zeros_like(g), g)
+                lhs[(side, 1, *where)] = jnp.where(text, g, jnp.zeros_like(g))
 
     total = None
     for side, w in enumerate((own_w, other_w)):
@@ -173,7 +187,9 @@
 
 def merged(one, two):
     top = jnp.maximum(one[0], two[0])
-    return top, 1.0 / (one[1] * jnp.exp(one[0] - top) + two[1] * jnp.exp(two[0] - top))
+    first = one[1] * jnp.exp(one[0] - top)
+    inverse = 1.0 / (first + two[1] * jnp.exp(two[0] - top))
+    return top, inverse, first * inverse
 
 
 def own_rows(index, own_stats, from_left, heads):
@@ -190,31 +206,29 @@
 
 def delta_kernel(count, first, terms, scale, mine, *refs):
     parts = refs[:terms]
-    q_ref, kv_ref, left_k, got1, got2, segs, own_stats, from_left, g_out, d_out, left_v = refs[terms:]
+    q_ref, kv_ref, left_k, left_v, segs, own_stats, g_out, d_out = refs[terms:]
     rows, span = mine.shape
+    heads = span // HEAD_DIM
     index = lax.axis_index("seq")
-    lanes = slice(first, first + span)
-    pair_of(index % 2 == 0, [(got2.at[:, lanes], left_v)], [(got1.at[:, lanes], left_v)])
-    total = mine[...]
-    for part in parts:
-        total = total + part[...].astype(F32)
-    g_out[:rows] = total.astype(BF16)
     pre, _, own, _ = masks(count, segs, index, rows)
-    heads = span // HEAD_DIM
-    top, inv = own_rows(index, own_stats, from_left, slice(first // HEAD_DIM, first // HEAD_DIM + heads))
     for h in range(heads):
         at = slice(h * HEAD_DIM, (h + 1) * HEAD_DIM)
         wide = slice(first + at.start, first + at.stop)
         row = slice(h, h + 1)
-        q, g = q_ref[0, :, wide], g_out[:rows, at]
+        stat = first // HEAD_DIM + h
+        total = mine[:, at]
+        for part in parts:
+            total = total + part[:, at].astype(F32)
+        g_out[h * rows : (h + 1) * rows] = total.astype(BF16)
+        q, g = q_ref[0, :, wide], g_out[h * rows : (h + 1) * rows]
         s_pre = score(left_k[:, wide], q, scale, pre)
         s_own = score(kv_ref[0, 0, :, wide], q, scale, own)
         d_pre = lax.dot_general(left_v[:, at], g, NT, preferred_element_type=F32)
         d_own = lax.dot_general(kv_ref[1, 0, :, wide], g, NT, preferred_element_type=F32)
-        terms_ = jnp.exp(s_pre - top[row]) * d_pre + jnp.exp(s_own - top[row]) * d_own
-        d_out[row] = jnp.sum(terms_, axis=0, keepdims=True) * inv[row]
-    g_out[rows:] = jnp.zeros((2 * heads, span), BF16)
-    g_out[rows:, :LANES] = split(d_out[...])
+        top = own_stats[0, stat : stat + 1]
+        weighed = jnp.exp(s_pre - top) * d_pre + jnp.exp(s_own - top) * d_own
+        d_out[row] = jnp.sum(weighed, axis=0, keepdims=True) / own_stats[1, stat : stat + 1]
+    g_out[heads * rows :] = split(d_out[...])
 
 
 def grads_kernel(count, first, scale, q_ref, kv_ref, left_k, left_v, right_q, g_ref, right_g, segs,
@@ -225,9 +239,10 @@
     heads = span // HEAD_DIM
     chosen = slice(first // HEAD_DIM, first // HEAD_DIM + heads)
     pre, far, own, nxt = masks(count, segs, index, rows)
-    top, inv = own_rows(index, own_stats, from_left, chosen)
-    r_top, r_inv = right_rows(index, count, far_stats, from_right, chosen)
-    right_delta = joined(right_g[rows:, :LANES])
+    top, inv, share = own_rows(index, own_stats, from_left, chosen)
+    r_top, r_inv, r_share = right_rows(index, count, far_stats, from_right, chosen)
+    own_delta = delta_own[...] * share
+    right_delta = joined(right_g[heads * rows :]) * r_share
 
     def run(up_out, down_out):
         for h in range(heads):
@@ -235,7 +250,8 @@
             wide = slice(first + at.start, first + at.stop)
             row = slice(h, h + 1)
             q2 = jnp.concatenate([q_ref[0, :, wide], right_q[:, wide]], axis=0)
-            g2 = jnp.concatenate([g_ref[:rows, at], right_g[:rows, at]], axis=0)
+            block = slice(h * rows, (h + 1) * rows)
+            g2 = jnp.concatenate([g_ref[block], right_g[block]], axis=0)
             k, kl = kv_ref[0, 0, :, wide], left_k[:, wide]
             s_left = lax.dot_general(kl, q2, NT, preferred_element_type=F32) * scale
             s_here = lax.dot_general(k, q2, NT, preferred_element_type=F32) * scale
@@ -248,8 +264,8 @@
             d_pre, d_far = d_left[:, :rows], d_left[:, rows:]
             extra = jnp.sum(p_far * d_far, axis=0, keepdims=True)
             far_delta[row] = extra
-            ds_pre = (p_pre * (d_pre - delta_own[row]) * scale).astype(BF16)
-            ds_own = (p_own * (d_own - delta_own[row]) * scale).astype(BF16)
+            ds_pre = (p_pre * (d_pre - own_delta[row]) * scale).astype(BF16)
+            ds_own = (p_own * (d_own - own_delta[row]) * scale).astype(BF16)
             ds_far = (p_far * (d_far - (right_delta[row] + extra)) * scale).astype(BF16)
             ds_nxt = (p_nxt * (extra * -scale)).astype(BF16)
             p_low = p_pre.astype(BF16)
@@ -326,6 +342,10 @@
     return lax.ppermute(value, "seq", [(i, (i + steps) % count) for i in range(count)])
 
 
+def passed_up(value):
+    return lax.ppermute(value, "seq", [(i, i + 1) for i in range(lax.axis_size("seq") - 1)])
+
+
 def neighbour_swaps(first, second):
     count = lax.axis_size("seq")
     one = [(i, min(i ^ 1, count - 1)) for i in range(count)]
@@ -358,30 +378,33 @@
     chips = lax.axis_size("dp") // 2
     count = lax.axis_size("seq")
     scale = HEAD_DIM ** (-0.5)
+    blocks = 2 * depth // LANES
 
     other_weight = swap(out_weight, "dp", 1)
     slices = pl.pallas_call(
         grad_slices_kernel,
         in_specs=[pl.BlockSpec(memory_space=pltpu.HBM)] * 2,
-        out_shape=[shape((rows, 2 * depth + LANES))] * chips,
+        out_shape=[shape((blocks * rows + TAG_ROWS, LANES))] * chips,
         scratch_shapes=[
-            pltpu.VMEM(tags.shape, tags.dtype), pltpu.SemaphoreType.DMA, pltpu.SemaphoreType.DMA((chips,))],
+            pltpu.VMEM(tags.shape, tags.dtype), pltpu.SemaphoreType.DMA, pltpu.SemaphoreType.DMA((chips, blocks))],
         compiler_params=params(4),
         name="grad_slices",
         cost_estimate=cost(0, 4 * grad_y.size),
     )(in_hbm(grad_y), in_hbm(tags))
     grads = [slices[0]] + [swap(slices[k], "dp", 2 * k) for k in range(1, chips)]
-    first, second, own_v = pl.pallas_call(
-        side_slices_kernel,
+    first, second, *own_vs = pl.pallas_call(
+        functools.partial(side_slices_kernel, chunks(hc)),
         in_specs=[pl.BlockSpec(memory_space=pltpu.HBM)] * 2,
-        out_shape=[shape((rows, hc))] * 3,
-        scratch_shapes=[pltpu.SemaphoreType.DMA((3,))],
+        out_shape=[shape((rows, hc))] * 2 + [shape((rows, width)) for _, width in chunks(hc)],
+        scratch_shapes=[pltpu.SemaphoreType.DMA((2 + PARTS,))],
         compiler_params=params(8),
         name="side_slices",
         cost_estimate=cost(0, 12 * query.size),
     )(in_hbm(query), in_hbm(key_value))
     sides = neighbour_swaps(first, second)
-    values = neighbour_swaps(own_v, own_v)
+    values = []
+    for own_v in own_vs:
+        values.append(passed_up(own_v))
 
     sums = []
     for first, span in chunks(hc):
@@ -407,18 +430,18 @@
     pieces = []
     for c, (first, span) in enumerate(chunks(hc)):
         heads = span // HEAD_DIM
-        gout, delta, left_v = pl.pallas_call(
+        gout, delta = pl.pallas_call(
             functools.partial(delta_kernel, count, first, chips - 1, scale),
-            out_shape=[shape((rows + 2 * heads, span)), shape((heads, rows), F32), shape((rows, span))],
+            out_shape=[shape((heads * rows + 2 * heads, HEAD_DIM)), shape((heads, rows), F32)],
             compiler_params=params(8),
             cost_estimate=cost(4 * 2 * rows * rows * span, 20 * rows * span),
-        )(*sums[c], query, key_value, left_k, *values, segments, own, from_left)
-        pieces.append((gout, delta, left_v, shifted(gout, -1)))
+        )(*sums[c], query, key_value, left_k, values[c], segments, own)
+        pieces.append((gout, delta, shifted(gout, -1)))
 
     parts = []
     for c, (first, span) in enumerate(chunks(hc)):
         heads, half = span // HEAD_DIM, shape((2, rows, span))
-        gout, delta, left_v, right_g = pieces[c]
+        gout, delta, right_g = pieces[c]
         *kept, to1, to2 = pl.pallas_call(
             functools.partial(grads_kernel, count, first, scale),
             out_shape=[
@@ -426,7 +449,7 @@
             scratch_shapes=[pltpu.VMEM((heads, rows), F32)],
             compiler_params=params(12),
             cost_estimate=cost(10 * 3 * rows * rows * span, 40 * rows * span),
-        )(query, key_value, left_k, left_v, right_q, gout, right_g, segments, own, far, from_left, from_right, delta)
+        )(query, key_value, left_k, values[c], right_q, gout, right_g, segments, own, far, from_left, from_right, delta)
         parts.append((*kept, query, key_value, left_k, *neighbour_swaps(to1, to2)))
 
     results = ()

time: 89.2 us -> 87 us (0.975)
  the two profiles are of different devices: /device:TPU:0 before, /device:TPU:18 now
where the time goes in v4:
time: 87 us; the launch traced here: 86.7 us
  waiting for transfers between devices  36.2 us (42%)
  starting transfers between devices  31.9 us (37%)
  Pallas kernels  17.6 us (20%)
  between operations  0.99 us (1%)
    ppermute x6, waiting for transfers between devices, neighbour_swaps(): return (lax.ppermute(first, 'seq', one), lax.ppermute(second, 'seq', two))  16 us
    ppermute x10, starting transfers between devices, swap(): lax.ppermute(value, axis, [(i, i ^ bits) for i in range(lax.axis_size(axi...  12.8 us
    ppermute x6, starting transfers between devices, neighbour_swaps(): return (lax.ppermute(first, 'seq', one), lax.ppermute(second, 'seq', two))  10.3 us
    ppermute x10, waiting for transfers between devices, swap(): lax.ppermute(value, axis, [(i, i ^ bits) for i in range(lax.axis_size(axi...  9.2 us
    ppermute x2, waiting for transfers between devices, passed_up(): lax.ppermute(value, 'seq', [(i, i + 1) for i in range(lax.axis_size('seq'...  6.15 us
    pallas_call x2, Pallas kernels, step(): pl.pallas_call(functools.partial(grads_kernel, count, first, scale), out_...  5.9 us
    ppermute x4, starting transfers between devices, shifted(): lax.ppermute(value, 'seq', [(i, (i + steps) % count) for i in range(count)])  5.02 us
    ppermute x4, waiting for transfers between devices, shifted(): lax.ppermute(value, 'seq', [(i, (i + steps) % count) for i in range(count)])  4.77 us
  transfers between devices with their start and end apart: 22, of which 10 were waited for; matrix products, arithmetic and copies ran while one was open for 0% of the time, Pallas kernels for 19%

profile of v4, /device:TPU:18, one launch (start us, length us, event | category | flops | bytes accessed | tf_op | source)
XLA Modules:
  0.0 86.7 jit_solution(15721133887972983747)
XLA Ops:
  0.6 0.1 collective-permute-start.6
  0.7 1.3 %grad_slices.1 = (bf16[528,128]{1,0:T(8,128)(2,1)S(1)}, bf16[528,128]{1,0:T(8,128)(2,1)S(1)}, bf16[528,128]{1,0:T(8,128)(2,1)S(1)}, bf16[528,128]{1,0:T(8,128)(2,1)S(1)}) custom-call(bf16[1,128,2048]{2,1,0:T(8,128)(2,1)} %grad_ref.1, s32[1,128]{1,0:T(1,128)} %tags_ref.1), custom_call_target="tpu_custom_call" | custom-call | bytes 1048576 | tf_op jit(solution)/shard_map/grad_slices/pallas_call | solution.py:384
  2.0 0.6 collective-permute-start.3
  2.6 1.4 %side_slices.1 = (bf16[128,2048]{1,0:T(8,128)(2,1)S(1)}, bf16[128,2048]{1,0:T(8,128)(2,1)S(1)}, bf16[128,1024]{1,0:T(8,128)(2,1)S(1)}, bf16[128,1024]{1,0:T(8,128)(2,1)S(1)}) custom-call(bf16[1,128,2048]{2,1,0:T(8,128)(2,1)} %q_ref.11, bf16[2,1,128,2048]{3,2,1,0:T(8,128)(2,1)} %kv_ref.11), custom_call_target="tpu_custom_call" | custom-call | bytes 3145728 | tf_op jit(solution)/shard_map/side_slices/pallas_call | solution.py:395
  4.0 1.6 %collective-permute-start = (bf16[128,2048]{1,0:T(8,128)(2,1)S(1)}, bf16[128,2048]{1,0:T(8,128)(2,1)S(1)}, u32[]{:S(2)}, u32[]{:S(2)}) collective-permute-start(bf16[128,2048]{1,0:T(8,128)(2,1)S(1)} %get-tuple-element.38), channel_id=1, source_target_pairs={{0,1},{1,0},{2,3},{3,2},{4,5},{5,4},{6,7},{7,6},{8,9},{9,8},{10,11... | collective-permute-start | bytes 1572872 | tf_op jit(solution)/shard_map/ppermute | solution.py:354
  5.7 1.9 %collective-permute-start.1 = (bf16[128,2048]{1,0:T(8,128)(2,1)S(1)}, bf16[128,2048]{1,0:T(8,128)(2,1)S(1)}, u32[]{:S(2)}, u32[]{:S(2)}) collective-permute-start(bf16[128,2048]{1,0:T(8,128)(2,1)S(1)} %get-tuple-element.39), channel_id=1, source_target_pairs={{0,0},{1,2},{2,1},{3,3},{4,4},{5,6},{6,5},{7,7},{8,8},{9,10},{10,9... | collective-permute-start | bytes 1572872 | tf_op jit(solution)/shard_map/ppermute | solution.py:354
  7.6 1.6 %collective-permute-start.4 = (bf16[528,128]{1,0:T(8,128)(2,1)S(1)}, bf16[528,128]{1,0:T(8,128)(2,1)S(1)}, u32[]{:S(2)}, u32[]{:S(2)}) collective-permute-start(bf16[528,128]{1,0:T(8,128)(2,1)S(1)} %get-tuple-element.45), channel_id=1, source_target_pairs={{0,16},{4,20},{8,24},{12,28},{16,0},{20,4},{24,8},{28,12},{1,17},{... | collective-permute-start | bytes 405512 | tf_op jit(solution)/shard_map/ppermute | solution.py:32
  9.2 0.0 collective-permute-done.3.refs_1_
  9.2 1.4 %collective-permute-start.5 = (bf16[528,128]{1,0:T(8,128)(2,1)S(1)}, bf16[528,128]{1,0:T(8,128)(2,1)S(1)}, u32[]{:S(2)}, u32[]{:S(2)}) collective-permute-start(bf16[528,128]{1,0:T(8,128)(2,1)S(1)} %get-tuple-element.46), channel_id=1, source_target_pairs={{0,24},{4,28},{8,16},{12,20},{16,8},{20,12},{24,0},{28,4},{1,25},{... | collective-permute-start | bytes 405512 | tf_op jit(solution)/shard_map/ppermute | solution.py:32
  10.6 5.2 %collective-permute-done.4.refs_2_ = bf16[528,128]{1,0:T(8,128)(2,1)S(1)} collective-permute-done((bf16[528,128]{1,0:T(8,128)(2,1)S(1)}, bf16[528,128]{1,0:T(8,128)(2,1)S(1)}, u32[]{:S(2)}, u32[]{:S(2)}) %collective-permute-start.4) | collective-permute-done | bytes 135200 | tf_op jit(solution)/shard_map/ppermute | solution.py:32
  15.8 1.9 %collective-permute-start.15 = (bf16[128,1024]{1,0:T(8,128)(2,1)S(1)}, bf16[128,1024]{1,0:T(8,128)(2,1)S(1)}, u32[]{:S(2)}, u32[]{:S(2)}) collective-permute-start(bf16[128,1024]{1,0:T(8,128)(2,1)S(1)} %get-tuple-element.60), channel_id=1, source_target_pairs={{0,1},{1,2},{2,3},{4,5},{5,6},{6,7},{8,9},{9,10},{10,11},{12,13},{... | collective-permute-start | bytes 786440 | tf_op jit(solution)/shard_map/ppermute | solution.py:346
  17.7 0.0 collective-permute-done.6.refs_5_
  17.8 1.4 %shard_map.80 = (f32[128,1024]{1,0:T(8,128)S(1)}, bf16[128,1024]{1,0:T(8,128)(2,1)S(1)}, bf16[128,1024]{1,0:T(8,128)(2,1)S(1)}, bf16[128,1024]{1,0:T(8,128)(2,1)S(1)}) custom-call(bf16[528,128]{1,0:T(8,128)(2,1)S(1)} %get-tuple-element.43.refs_0_, bf16[528,128]{1,0:T(8,128)(2,1)S(1)} %collective-permute-done.3.refs_1_, ...), custom_call_target="tpu_custom_call" | custom-call | flops 1073741824 | bytes 2097152 | tf_op jit(solution)/shard_map/pallas_call | solution.py:411
  19.2 1.6 %collective-permute-start.16 = (bf16[128,1024]{1,0:T(8,128)(2,1)S(1)}, bf16[128,1024]{1,0:T(8,128)(2,1)S(1)}, u32[]{:S(2)}, u32[]{:S(2)}) collective-permute-start(bf16[128,1024]{1,0:T(8,128)(2,1)S(1)} %get-tuple-element.62), channel_id=1, source_target_pairs={{0,8},{4,12},{8,0},{12,4},{16,24},{20,28},{24,16},{28,20},{1,9},{5... | collective-permute-start | bytes 786440 | tf_op jit(solution)/shard_map/ppermute | solution.py:32
  20.7 1.5 %collective-permute-start.17 = (bf16[128,1024]{1,0:T(8,128)(2,1)S(1)}, bf16[128,1024]{1,0:T(8,128)(2,1)S(1)}, u32[]{:S(2)}, u32[]{:S(2)}) collective-permute-start(bf16[128,1024]{1,0:T(8,128)(2,1)S(1)} %get-tuple-element.63), channel_id=1, source_target_pairs={{0,16},{4,20},{8,24},{12,28},{16,0},{20,4},{24,8},{28,12},{1,17},{... | collective-permute-start | bytes 786440 | tf_op jit(solution)/shard_map/ppermute | solution.py:32
  22.2 4.5 %collective-permute-done.15.refs_6_.left_v = bf16[128,1024]{1,0:T(8,128)(2,1)S(1)} collective-permute-done((bf16[128,1024]{1,0:T(8,128)(2,1)S(1)}, bf16[128,1024]{1,0:T(8,128)(2,1)S(1)}, u32[]{:S(2)}, u32[]{:S(2)}) %collective-permute-start.15) | collective-permute-done | bytes 262176 | tf_op jit(solution)/shard_map/ppermute | solution.py:346
  26.8 2.4 %collective-permute-start.18 = (bf16[128,1024]{1,0:T(8,128)(2,1)S(1)}, bf16[128,1024]{1,0:T(8,128)(2,1)S(1)}, u32[]{:S(2)}, u32[]{:S(2)}) collective-permute-start(bf16[128,1024]{1,0:T(8,128)(2,1)S(1)} %get-tuple-element.64), channel_id=1, source_target_pairs={{0,24},{4,28},{8,16},{12,20},{16,8},{20,12},{24,0},{28,4},{1,25},{... | collective-permute-start | bytes 786440 | tf_op jit(solution)/shard_map/ppermute | solution.py:32
  29.2 1.4 %shard_map.77 = (f32[128,1024]{1,0:T(8,128)S(1)}, bf16[128,1024]{1,0:T(8,128)(2,1)S(1)}, bf16[128,1024]{1,0:T(8,128)(2,1)S(1)}, bf16[128,1024]{1,0:T(8,128)(2,1)S(1)}) custom-call(bf16[528,128]{1,0:T(8,128)(2,1)S(1)} %get-tuple-element.43.refs_0_, bf16[528,128]{1,0:T(8,128)(2,1)S(1)} %collective-permute-done.3.refs_1_, ...), custom_call_target="tpu_custom_call" | custom-call | flops 1073741824 | bytes 2097152 | tf_op jit(solution)/shard_map/pallas_call | solution.py:411
  30.6 0.0 collective-permute-done.got1
  30.6 1.9 %collective-permute-start.2 = (bf16[128,1024]{1,0:T(8,128)(2,1)S(1)}, bf16[128,1024]{1,0:T(8,128)(2,1)S(1)}, u32[]{:S(2)}, u32[]{:S(2)}) collective-permute-start(bf16[128,1024]{1,0:T(8,128)(2,1)S(1)} %get-tuple-element.41), channel_id=1, source_target_pairs={{0,1},{1,2},{2,3},{4,5},{5,6},{6,7},{8,9},{9,10},{10,11},{12,13},{... | collective-permute-start | bytes 786440 | tf_op jit(solution)/shard_map/ppermute | solution.py:346
  32.6 0.0 collective-permute-done.1.got2
  32.6 0.6 collective-permute-start.7
  33.2 0.0 collective-permute-done.16.refs_0_
  33.2 0.5 collective-permute-start.8
  33.7 2.4 %collective-permute-start.9 = (bf16[128,1024]{1,0:T(8,128)(2,1)S(1)}, bf16[128,1024]{1,0:T(8,128)(2,1)S(1)}, u32[]{:S(2)}, u32[]{:S(2)}) collective-permute-start(bf16[128,1024]{1,0:T(8,128)(2,1)S(1)} %get-tuple-element.50), channel_id=1, source_target_pairs={{0,24},{4,28},{8,16},{12,20},{16,8},{20,12},{24,0},{28,4},{1,25},{... | collective-permute-start | bytes 786440 | tf_op jit(solution)/shard_map/ppermute | solution.py:32
  36.1 1.5 %stats.1 = (f32[2,16,128]{2,1,0:T(8,128)S(1)}, f32[2,16,128]{2,1,0:T(8,128)S(1)}, bf16[128,2048]{1,0:T(8,128)(2,1)S(1)}, bf16[128,2048]{1,0:T(8,128)(2,1)S(1)}) custom-call(bf16[1,128,2048]{2,1,0:T(8,128)(2,1)S(1)} %copy-done.1, bf16[2,1,128,2048]{3,2,1,0:T(8,128)(2,1)S(1)} %copy-done, bf16[128,2048]{1,0:T(8,128)(2,1)S(1)} %collective-permute-done.got1, ...), custom_call_target="tpu_custom_call" | custom-call | flops 201326592 | bytes 5242880 | tf_op jit(solution)/shard_map/stats/pallas_call | solution.py:421
  37.7 0.9 %shard_map.81 = (bf16[1040,128]{1,0:T(8,128)(2,1)S(1)}, f32[8,128]{1,0:T(8,128)S(1)}) custom-call(f32[128,1024]{1,0:T(8,128)S(1)} %get-tuple-element.61.mine, bf16[128,1024]{1,0:T(8,128)(2,1)S(1)} %collective-permute-done.16.refs_0_, bf16[128,1024]{1,0:T(8,128)(2,1)S(1)} %collective-permute-done.17.refs_1_, ...), custom_call_target="tpu_custom_call" | custom-call | flops 134217728 | bytes 2621440 | tf_op jit(solution)/shard_map/pallas_call | solution.py:433
  38.6 2.1 %collective-permute-start.19 = (bf16[1040,128]{1,0:T(8,128)(2,1)S(1)}, bf16[1040,128]{1,0:T(8,128)(2,1)S(1)}, u32[]{:S(2)}, u32[]{:S(2)}) collective-permute-start(bf16[1040,128]{1,0:T(8,128)(2,1)S(1)} %get-tuple-element.65.g_ref), channel_id=1, source_target_pairs={{0,3},{1,0},{2,1},{3,2},{4,7},{5,4},{6,5},{7,6},{8,11},{9,8},{10,9... | collective-permute-start | bytes 798728 | tf_op jit(solution)/shard_map/ppermute | solution.py:342
  40.7 1.6 %collective-permute-done.2.refs_6_.left_v = bf16[128,1024]{1,0:T(8,128)(2,1)S(1)} collective-permute-done((bf16[128,1024]{1,0:T(8,128)(2,1)S(1)}, bf16[128,1024]{1,0:T(8,128)(2,1)S(1)}, u32[]{:S(2)}, u32[]{:S(2)}) %collective-permute-start.2) | collective-permute-done | bytes 262176 | tf_op jit(solution)/shard_map/ppermute | solution.py:346
  42.3 4.0 %collective-permute-done.8.refs_1_ = bf16[128,1024]{1,0:T(8,128)(2,1)S(1)} collective-permute-done((bf16[128,1024]{1,0:T(8,128)(2,1)S(1)}, bf16[128,1024]{1,0:T(8,128)(2,1)S(1)}, u32[]{:S(2)}, u32[]{:S(2)}) %collective-permute-start.8) | collective-permute-done | bytes 262176 | tf_op jit(solution)/shard_map/ppermute | solution.py:32
  46.2 0.9 %shard_map.78 = (bf16[1040,128]{1,0:T(8,128)(2,1)S(1)}, f32[8,128]{1,0:T(8,128)S(1)}) custom-call(f32[128,1024]{1,0:T(8,128)S(1)} %get-tuple-element.47.mine, bf16[128,1024]{1,0:T(8,128)(2,1)S(1)} %collective-permute-done.7.refs_0_, bf16[128,1024]{1,0:T(8,128)(2,1)S(1)} %collective-permute-done.8.refs_1_, ...), custom_call_target="tpu_custom_call" | custom-call | flops 134217728 | bytes 2621440 | tf_op jit(solution)/shard_map/pallas_call | solution.py:433
  47.1 0.9 %collective-permute-start.10 = (bf16[1040,128]{1,0:T(8,128)(2,1)S(1)}, bf16[1040,128]{1,0:T(8,128)(2,1)S(1)}, u32[]{:S(2)}, u32[]{:S(2)}) collective-permute-start(bf16[1040,128]{1,0:T(8,128)(2,1)S(1)} %get-tuple-element.52.g_ref), channel_id=1, source_target_pairs={{0,3},{1,0},{2,1},{3,2},{4,7},{5,4},{6,5},{7,6},{8,11},{9,8},{10,9... | collective-permute-start | bytes 798728 | tf_op jit(solution)/shard_map/ppermute | solution.py:342
  48.1 1.1 %collective-permute-start.11 = (f32[2,16,128]{2,1,0:T(8,128)S(1)}, f32[2,16,128]{2,1,0:T(8,128)S(1)}, u32[]{:S(2)}, u32[]{:S(2)}) collective-permute-start(f32[2,16,128]{2,1,0:T(8,128)S(1)} %get-tuple-element.53.far_stats), channel_id=1, source_target_pairs={{0,1},{1,2},{2,3},{3,0},{4,5},{5,6},{6,7},{7,4},{8,9},{9,10},{10,1... | collective-permute-start | bytes 49160 | tf_op jit(solution)/shard_map/ppermute | solution.py:342
  49.2 0.9 %collective-permute-start.12 = (f32[2,16,128]{2,1,0:T(8,128)S(1)}, f32[2,16,128]{2,1,0:T(8,128)S(1)}, u32[]{:S(2)}, u32[]{:S(2)}) collective-permute-start(f32[2,16,128]{2,1,0:T(8,128)S(1)} %get-tuple-element.51.refs_8_.own_stats), channel_id=1, source_target_pairs={{0,3},{1,0},{2,1},{3,2},{4,7},{5,4},{6,5},{7,6},{8,11},{9,8},{10,9... | collective-permute-start | bytes 49160 | tf_op jit(solution)/shard_map/ppermute | solution.py:342
  50.1 3.9 %collective-permute-done.11.from_left = f32[2,16,128]{2,1,0:T(8,128)S(1)} collective-permute-done((f32[2,16,128]{2,1,0:T(8,128)S(1)}, f32[2,16,128]{2,1,0:T(8,128)S(1)}, u32[]{:S(2)}, u32[]{:S(2)}) %collective-permute-start.11) | collective-permute-done | bytes 16416 | tf_op jit(solution)/shard_map/ppermute | solution.py:342
  54.0 0.9 %collective-permute-done.12.from_right = f32[2,16,128]{2,1,0:T(8,128)S(1)} collective-permute-done((f32[2,16,128]{2,1,0:T(8,128)S(1)}, f32[2,16,128]{2,1,0:T(8,128)S(1)}, u32[]{:S(2)}, u32[]{:S(2)}) %collective-permute-start.12) | collective-permute-done | bytes 16416 | tf_op jit(solution)/shard_map/ppermute | solution.py:342
  54.9 2.9 %shard_map.82 = (f32[128,1024]{1,0:T(8,128)S(1)}, f32[2,128,1024]{2,1,0:T(8,128)S(1)}, bf16[8,256,128]{2,1,0:T(8,128)(2,1)S(1)}, bf16[2,128,1024]{2,1,0:T(8,128)(2,1)S(1)}, bf16[2,128,1024]{2,1,0:T(8,128)(2,1)S(1)}) custom-call(bf16[1,128,2048]{2,1,0:T(8,128)(2,1)S(1)} %copy-done.1, bf16[2,1,128,2048]{3,2,1,0:T(8,128)(2,1)S(1)} %copy-done, ...), custom_call_target="tpu_custom_call" | custom-call | flops 503316480 | bytes 5242880 | tf_op jit(solution)/shard_map/pallas_call | solution.py:445
  57.7 0.9 %collective-permute-start.20 = (bf16[2,128,1024]{2,1,0:T(8,128)(2,1)S(1)}, bf16[2,128,1024]{2,1,0:T(8,128)(2,1)S(1)}, u32[]{:S(2)}, u32[]{:S(2)}) collective-permute-start(bf16[2,128,1024]{2,1,0:T(8,128)(2,1)S(1)} %get-tuple-element.70), channel_id=1, source_target_pairs={{0,1},{1,0},{2,3},{3,2},{4,5},{5,4},{6,7},{7,6},{8,9},{9,8},{10,11... | collective-permute-start | bytes 1572872 | tf_op jit(solution)/shard_map/ppermute | solution.py:354
  58.6 3.8 %collective-permute-start.21 = (bf16[2,128,1024]{2,1,0:T(8,128)(2,1)S(1)}, bf16[2,128,1024]{2,1,0:T(8,128)(2,1)S(1)}, u32[]{:S(2)}, u32[]{:S(2)}) collective-permute-start(bf16[2,128,1024]{2,1,0:T(8,128)(2,1)S(1)} %get-tuple-element.71), channel_id=1, source_target_pairs={{0,0},{1,2},{2,1},{3,3},{4,4},{5,6},{6,5},{7,7},{8,8},{9,10},{10,9... | collective-permute-start | bytes 1572872 | tf_op jit(solution)/shard_map/ppermute | solution.py:354
  62.5 3.0 %shard_map.79 = (f32[128,1024]{1,0:T(8,128)S(1)}, f32[2,128,1024]{2,1,0:T(8,128)S(1)}, bf16[8,256,128]{2,1,0:T(8,128)(2,1)S(1)}, bf16[2,128,1024]{2,1,0:T(8,128)(2,1)S(1)}, bf16[2,128,1024]{2,1,0:T(8,128)(2,1)S(1)}) custom-call(bf16[1,128,2048]{2,1,0:T(8,128)(2,1)S(1)} %copy-done.1, bf16[2,1,128,2048]{3,2,1,0:T(8,128)(2,1)S(1)} %copy-done, ...), custom_call_target="tpu_custom_call" | custom-call | flops 503316480 | bytes 5242880 | tf_op jit(solution)/shard_map/pallas_call | solution.py:445
  65.5 0.1 collective-permute-start.13
  65.6 2.0 %collective-permute-start.14 = (bf16[2,128,1024]{2,1,0:T(8,128)(2,1)S(1)}, bf16[2,128,1024]{2,1,0:T(8,128)(2,1)S(1)}, u32[]{:S(2)}, u32[]{:S(2)}) collective-permute-start(bf16[2,128,1024]{2,1,0:T(8,128)(2,1)S(1)} %get-tuple-element.59), channel_id=1, source_target_pairs={{0,0},{1,2},{2,1},{3,3},{4,4},{5,6},{6,5},{7,7},{8,8},{9,10},{10,9... | collective-permute-start | bytes 1572872 | tf_op jit(solution)/shard_map/ppermute | solution.py:354
  67.6 5.0 %collective-permute-done.20.got1 = bf16[2,128,1024]{2,1,0:T(8,128)(2,1)S(1)} collective-permute-done((bf16[2,128,1024]{2,1,0:T(8,128)(2,1)S(1)}, bf16[2,128,1024]{2,1,0:T(8,128)(2,1)S(1)}, u32[]{:S(2)}, u32[]{:S(2)}) %collective-permute-start.20) | collective-permute-done | bytes 524320 | tf_op jit(solution)/shard_map/ppermute | solution.py:354
  72.6 2.7 %collective-permute-done.21.got2 = bf16[2,128,1024]{2,1,0:T(8,128)(2,1)S(1)} collective-permute-done((bf16[2,128,1024]{2,1,0:T(8,128)(2,1)S(1)}, bf16[2,128,1024]{2,1,0:T(8,128)(2,1)S(1)}, u32[]{:S(2)}, u32[]{:S(2)}) %collective-permute-start.21) | collective-permute-done | bytes 524320 | tf_op jit(solution)/shard_map/ppermute | solution.py:354
  75.3 1.4 %shard_map.83 = (bf16[1,128,2048]{2,1,0:T(8,128)(2,1)}, bf16[2,1,128,2048]{3,2,1,0:T(8,128)(2,1)}) custom-call(f32[128,1024]{1,0:T(8,128)S(1)} %get-tuple-element.67.dq_ref, f32[2,128,1024]{2,1,0:T(8,128)S(1)} %get-tuple-element.68.dkv_ref, bf16[8,256,128]{2,1,0:T(8,128)(2,1)S(1)} %get-tuple-element.69.p_ref, bf16[1,128,2048]{2,1,0:T(8,128)(2,1)S(1)} %copy-done.1, ...), custom_call_target="tpu_custom_call" | custom-call | bytes 2621440 | tf_op jit(solution)/shard_map/pallas_call | solution.py:458
  76.7 5.3 %collective-permute-done.13.got1 = bf16[2,128,1024]{2,1,0:T(8,128)(2,1)S(1)} collective-permute-done((bf16[2,128,1024]{2,1,0:T(8,128)(2,1)S(1)}, bf16[2,128,1024]{2,1,0:T(8,128)(2,1)S(1)}, u32[]{:S(2)}, u32[]{:S(2)}) %collective-permute-start.13) | collective-permute-done | bytes 524320 | tf_op jit(solution)/shard_map/ppermute | solution.py:354
  82.0 3.1 %collective-permute-done.14.got2 = bf16[2,128,1024]{2,1,0:T(8,128)(2,1)S(1)} collective-permute-done((bf16[2,128,1024]{2,1,0:T(8,128)(2,1)S(1)}, bf16[2,128,1024]{2,1,0:T(8,128)(2,1)S(1)}, u32[]{:S(2)}, u32[]{:S(2)}) %collective-permute-start.14) | collective-permute-done | bytes 524320 | tf_op jit(solution)/shard_map/ppermute | solution.py:354
  85.1 1.4 %shard_map.84 = (bf16[1,128,2048]{2,1,0:T(8,128)(2,1)}, bf16[2,1,128,2048]{3,2,1,0:T(8,128)(2,1)}) custom-call(f32[128,1024]{1,0:T(8,128)S(1)} %get-tuple-element.55.dq_ref, f32[2,128,1024]{2,1,0:T(8,128)S(1)} %get-tuple-element.56.dkv_ref, bf16[8,256,128]{2,1,0:T(8,128)(2,1)S(1)} %get-tuple-element.57.p_ref, ...), custom_call_target="tpu_custom_call", output_to_operand_aliasing={{0}: (8, {}), {1}: (9, {})} | custom-call | bytes 2621440 | tf_op jit(solution)/shard_map/pallas_call | solution.py:458
  (15 shorter events, 0.0 us)
Async XLA Ops:
  0.6 17.1 %copy-start.2 = (bf16[2,2048,256]{2,1,0:T(8,128)(2,1)S(1)}, bf16[2,2048,256]{2,1,0:T(8,128)(2,1)}, u32[]{:S(2)}) copy-start(bf16[2,2048,256]{2,1,0:T(8,128)(2,1)} %refs_4_.6) | copy-start | bytes 6291460
  0.6 17.1 %collective-permute-start.6 = (bf16[2,2048,256]{2,1,0:T(8,128)(2,1)}, bf16[2,2048,256]{2,1,0:T(8,128)(2,1)S(1)}, u32[]{:S(2)}, u32[]{:S(2)}) collective-permute-start(bf16[2,2048,256]{2,1,0:T(8,128)(2,1)} %refs_4_.6), channel_id=1, source_target_pairs={{0,4},{4,0},{8,12},{12,8},{16,20},{20,16},{24,28},{28,24},{1,5},{5... | collective-permute-start | bytes 6291464 | tf_op jit(solution)/shard_map/ppermute | solution.py:32
  2.0 7.1 %collective-permute-start.3 = (bf16[528,128]{1,0:T(8,128)(2,1)S(1)}, bf16[528,128]{1,0:T(8,128)(2,1)S(1)}, u32[]{:S(2)}, u32[]{:S(2)}) collective-permute-start(bf16[528,128]{1,0:T(8,128)(2,1)S(1)} %get-tuple-element.44), channel_id=1, source_target_pairs={{0,8},{4,12},{8,0},{12,4},{16,24},{20,28},{24,16},{28,20},{1,9},{5... | collective-permute-start | bytes 405512 | tf_op jit(solution)/shard_map/ppermute | solution.py:32
  4.0 26.6 %collective-permute-start = (bf16[128,2048]{1,0:T(8,128)(2,1)S(1)}, bf16[128,2048]{1,0:T(8,128)(2,1)S(1)}, u32[]{:S(2)}, u32[]{:S(2)}) collective-permute-start(bf16[128,2048]{1,0:T(8,128)(2,1)S(1)} %get-tuple-element.38), channel_id=1, source_target_pairs={{0,1},{1,0},{2,3},{3,2},{4,5},{5,4},{6,7},{7,6},{8,9},{9,8},{10,11... | collective-permute-start | bytes 1572872 | tf_op jit(solution)/shard_map/ppermute | solution.py:354
  5.7 26.9 %collective-permute-start.1 = (bf16[128,2048]{1,0:T(8,128)(2,1)S(1)}, bf16[128,2048]{1,0:T(8,128)(2,1)S(1)}, u32[]{:S(2)}, u32[]{:S(2)}) collective-permute-start(bf16[128,2048]{1,0:T(8,128)(2,1)S(1)} %get-tuple-element.39), channel_id=1, source_target_pairs={{0,0},{1,2},{2,1},{3,3},{4,4},{5,6},{6,5},{7,7},{8,8},{9,10},{10,9... | collective-permute-start | bytes 1572872 | tf_op jit(solution)/shard_map/ppermute | solution.py:354
  7.6 8.2 %collective-permute-start.4 = (bf16[528,128]{1,0:T(8,128)(2,1)S(1)}, bf16[528,128]{1,0:T(8,128)(2,1)S(1)}, u32[]{:S(2)}, u32[]{:S(2)}) collective-permute-start(bf16[528,128]{1,0:T(8,128)(2,1)S(1)} %get-tuple-element.45), channel_id=1, source_target_pairs={{0,16},{4,20},{8,24},{12,28},{16,0},{20,4},{24,8},{28,12},{1,17},{... | collective-permute-start | bytes 405512 | tf_op jit(solution)/shard_map/ppermute | solution.py:32
  9.2 8.6 %collective-permute-start.5 = (bf16[528,128]{1,0:T(8,128)(2,1)S(1)}, bf16[528,128]{1,0:T(8,128)(2,1)S(1)}, u32[]{:S(2)}, u32[]{:S(2)}) collective-permute-start(bf16[528,128]{1,0:T(8,128)(2,1)S(1)} %get-tuple-element.46), channel_id=1, source_target_pairs={{0,24},{4,28},{8,16},{12,20},{16,8},{20,12},{24,0},{28,4},{1,25},{... | collective-permute-start | bytes 405512 | tf_op jit(solution)/shard_map/ppermute | solution.py:32
  15.8 11.0 %collective-permute-start.15 = (bf16[128,1024]{1,0:T(8,128)(2,1)S(1)}, bf16[128,1024]{1,0:T(8,128)(2,1)S(1)}, u32[]{:S(2)}, u32[]{:S(2)}) collective-permute-start(bf16[128,1024]{1,0:T(8,128)(2,1)S(1)} %get-tuple-element.60), channel_id=1, source_target_pairs={{0,1},{1,2},{2,3},{4,5},{5,6},{6,7},{8,9},{9,10},{10,11},{12,13},{... | collective-permute-start | bytes 786440 | tf_op jit(solution)/shard_map/ppermute | solution.py:346
  19.2 14.0 %collective-permute-start.16 = (bf16[128,1024]{1,0:T(8,128)(2,1)S(1)}, bf16[128,1024]{1,0:T(8,128)(2,1)S(1)}, u32[]{:S(2)}, u32[]{:S(2)}) collective-permute-start(bf16[128,1024]{1,0:T(8,128)(2,1)S(1)} %get-tuple-element.62), channel_id=1, source_target_pairs={{0,8},{4,12},{8,0},{12,4},{16,24},{20,28},{24,16},{28,20},{1,9},{5... | collective-permute-start | bytes 786440 | tf_op jit(solution)/shard_map/ppermute | solution.py:32
  20.7 13.0 %collective-permute-start.17 = (bf16[128,1024]{1,0:T(8,128)(2,1)S(1)}, bf16[128,1024]{1,0:T(8,128)(2,1)S(1)}, u32[]{:S(2)}, u32[]{:S(2)}) collective-permute-start(bf16[128,1024]{1,0:T(8,128)(2,1)S(1)} %get-tuple-element.63), channel_id=1, source_target_pairs={{0,16},{4,20},{8,24},{12,28},{16,0},{20,4},{24,8},{28,12},{1,17},{... | collective-permute-start | bytes 786440 | tf_op jit(solution)/shard_map/ppermute | solution.py:32
  26.8 9.4 %copy-start = (bf16[2,1,128,2048]{3,2,1,0:T(8,128)(2,1)S(1)}, bf16[2,1,128,2048]{3,2,1,0:T(8,128)(2,1)}, u32[]{:S(2)}) copy-start(bf16[2,1,128,2048]{3,2,1,0:T(8,128)(2,1)} %kv_ref.11) | copy-start | bytes 3145732
  26.8 9.4 %copy-start.1 = (bf16[1,128,2048]{2,1,0:T(8,128)(2,1)S(1)}, bf16[1,128,2048]{2,1,0:T(8,128)(2,1)}, u32[]{:S(2)}) copy-start(bf16[1,128,2048]{2,1,0:T(8,128)(2,1)} %q_ref.11) | copy-start | bytes 1572868
  26.8 9.4 %copy-start.3 = (s32[1,512]{1,0:T(1,128)S(1)}, s32[1,512]{1,0:T(1,128)}, u32[]{:S(2)}) copy-start(s32[1,512]{1,0:T(1,128)} %segs.5) | copy-start | bytes 6148
  26.8 10.9 %collective-permute-start.18 = (bf16[128,1024]{1,0:T(8,128)(2,1)S(1)}, bf16[128,1024]{1,0:T(8,128)(2,1)S(1)}, u32[]{:S(2)}, u32[]{:S(2)}) collective-permute-start(bf16[128,1024]{1,0:T(8,128)(2,1)S(1)} %get-tuple-element.64), channel_id=1, source_target_pairs={{0,24},{4,28},{8,16},{12,20},{16,8},{20,12},{24,0},{28,4},{1,25},{... | collective-permute-start | bytes 786440 | tf_op jit(solution)/shard_map/ppermute | solution.py:32
  30.6 11.6 %collective-permute-start.2 = (bf16[128,1024]{1,0:T(8,128)(2,1)S(1)}, bf16[128,1024]{1,0:T(8,128)(2,1)S(1)}, u32[]{:S(2)}, u32[]{:S(2)}) collective-permute-start(bf16[128,1024]{1,0:T(8,128)(2,1)S(1)} %get-tuple-element.41), channel_id=1, source_target_pairs={{0,1},{1,2},{2,3},{4,5},{5,6},{6,7},{8,9},{9,10},{10,11},{12,13},{... | collective-permute-start | bytes 786440 | tf_op jit(solution)/shard_map/ppermute | solution.py:346
  32.6 9.7 %collective-permute-start.7 = (bf16[128,1024]{1,0:T(8,128)(2,1)S(1)}, bf16[128,1024]{1,0:T(8,128)(2,1)S(1)}, u32[]{:S(2)}, u32[]{:S(2)}) collective-permute-start(bf16[128,1024]{1,0:T(8,128)(2,1)S(1)} %get-tuple-element.48), channel_id=1, source_target_pairs={{0,8},{4,12},{8,0},{12,4},{16,24},{20,28},{24,16},{28,20},{1,9},{5... | collective-permute-start | bytes 786440 | tf_op jit(solution)/shard_map/ppermute | solution.py:32
  33.2 13.0 %collective-permute-start.8 = (bf16[128,1024]{1,0:T(8,128)(2,1)S(1)}, bf16[128,1024]{1,0:T(8,128)(2,1)S(1)}, u32[]{:S(2)}, u32[]{:S(2)}) collective-permute-start(bf16[128,1024]{1,0:T(8,128)(2,1)S(1)} %get-tuple-element.49), channel_id=1, source_target_pairs={{0,16},{4,20},{8,24},{12,28},{16,0},{20,4},{24,8},{28,12},{1,17},{... | collective-permute-start | bytes 786440 | tf_op jit(solution)/shard_map/ppermute | solution.py:32
  33.7 12.5 %collective-permute-start.9 = (bf16[128,1024]{1,0:T(8,128)(2,1)S(1)}, bf16[128,1024]{1,0:T(8,128)(2,1)S(1)}, u32[]{:S(2)}, u32[]{:S(2)}) collective-permute-start(bf16[128,1024]{1,0:T(8,128)(2,1)S(1)} %get-tuple-element.50), channel_id=1, source_target_pairs={{0,24},{4,28},{8,16},{12,20},{16,8},{20,12},{24,0},{28,4},{1,25},{... | collective-permute-start | bytes 786440 | tf_op jit(solution)/shard_map/ppermute | solution.py:32
  38.6 16.3 %collective-permute-start.19 = (bf16[1040,128]{1,0:T(8,128)(2,1)S(1)}, bf16[1040,128]{1,0:T(8,128)(2,1)S(1)}, u32[]{:S(2)}, u32[]{:S(2)}) collective-permute-start(bf16[1040,128]{1,0:T(8,128)(2,1)S(1)} %get-tuple-element.65.g_ref), channel_id=1, source_target_pairs={{0,3},{1,0},{2,1},{3,2},{4,7},{5,4},{6,5},{7,6},{8,11},{9,8},{10,9... | collective-permute-start | bytes 798728 | tf_op jit(solution)/shard_map/ppermute | solution.py:342
  47.1 15.3 %collective-permute-start.10 = (bf16[1040,128]{1,0:T(8,128)(2,1)S(1)}, bf16[1040,128]{1,0:T(8,128)(2,1)S(1)}, u32[]{:S(2)}, u32[]{:S(2)}) collective-permute-start(bf16[1040,128]{1,0:T(8,128)(2,1)S(1)} %get-tuple-element.52.g_ref), channel_id=1, source_target_pairs={{0,3},{1,0},{2,1},{3,2},{4,7},{5,4},{6,5},{7,6},{8,11},{9,8},{10,9... | collective-permute-start | bytes 798728 | tf_op jit(solution)/shard_map/ppermute | solution.py:342
  48.1 5.9 %collective-permute-start.11 = (f32[2,16,128]{2,1,0:T(8,128)S(1)}, f32[2,16,128]{2,1,0:T(8,128)S(1)}, u32[]{:S(2)}, u32[]{:S(2)}) collective-permute-start(f32[2,16,128]{2,1,0:T(8,128)S(1)} %get-tuple-element.53.far_stats), channel_id=1, source_target_pairs={{0,1},{1,2},{2,3},{3,0},{4,5},{5,6},{6,7},{7,4},{8,9},{9,10},{10,1... | collective-permute-start | bytes 49160 | tf_op jit(solution)/shard_map/ppermute | solution.py:342
  49.2 5.7 %collective-permute-start.12 = (f32[2,16,128]{2,1,0:T(8,128)S(1)}, f32[2,16,128]{2,1,0:T(8,128)S(1)}, u32[]{:S(2)}, u32[]{:S(2)}) collective-permute-start(f32[2,16,128]{2,1,0:T(8,128)S(1)} %get-tuple-element.51.refs_8_.own_stats), channel_id=1, source_target_pairs={{0,3},{1,0},{2,1},{3,2},{4,7},{5,4},{6,5},{7,6},{8,11},{9,8},{10,9... | collective-permute-start | bytes 49160 | tf_op jit(solution)/shard_map/ppermute | solution.py:342
  57.7 14.9 %collective-permute-start.20 = (bf16[2,128,1024]{2,1,0:T(8,128)(2,1)S(1)}, bf16[2,128,1024]{2,1,0:T(8,128)(2,1)S(1)}, u32[]{:S(2)}, u32[]{:S(2)}) collective-permute-start(bf16[2,128,1024]{2,1,0:T(8,128)(2,1)S(1)} %get-tuple-element.70), channel_id=1, source_target_pairs={{0,1},{1,0},{2,3},{3,2},{4,5},{5,4},{6,7},{7,6},{8,9},{9,8},{10,11... | collective-permute-start | bytes 1572872 | tf_op jit(solution)/shard_map/ppermute | solution.py:354
  58.6 16.7 %collective-permute-start.21 = (bf16[2,128,1024]{2,1,0:T(8,128)(2,1)S(1)}, bf16[2,128,1024]{2,1,0:T(8,128)(2,1)S(1)}, u32[]{:S(2)}, u32[]{:S(2)}) collective-permute-start(bf16[2,128,1024]{2,1,0:T(8,128)(2,1)S(1)} %get-tuple-element.71), channel_id=1, source_target_pairs={{0,0},{1,2},{2,1},{3,3},{4,4},{5,6},{6,5},{7,7},{8,8},{9,10},{10,9... | collective-permute-start | bytes 1572872 | tf_op jit(solution)/shard_map/ppermute | solution.py:354
  65.5 16.5 %collective-permute-start.13 = (bf16[2,128,1024]{2,1,0:T(8,128)(2,1)S(1)}, bf16[2,128,1024]{2,1,0:T(8,128)(2,1)S(1)}, u32[]{:S(2)}, u32[]{:S(2)}) collective-permute-start(bf16[2,128,1024]{2,1,0:T(8,128)(2,1)S(1)} %get-tuple-element.58), channel_id=1, source_target_pairs={{0,1},{1,0},{2,3},{3,2},{4,5},{5,4},{6,7},{7,6},{8,9},{9,8},{10,11... | collective-permute-start | bytes 1572872 | tf_op jit(solution)/shard_map/ppermute | solution.py:354
  65.6 19.5 %collective-permute-start.14 = (bf16[2,128,1024]{2,1,0:T(8,128)(2,1)S(1)}, bf16[2,128,1024]{2,1,0:T(8,128)(2,1)S(1)}, u32[]{:S(2)}, u32[]{:S(2)}) collective-permute-start(bf16[2,128,1024]{2,1,0:T(8,128)(2,1)S(1)} %get-tuple-element.59), channel_id=1, source_target_pairs={{0,0},{1,2},{2,1},{3,3},{4,4},{5,6},{6,5},{7,7},{8,8},{9,10},{10,9... | collective-permute-start | bytes 1572872 | tf_op jit(solution)/shard_map/ppermute | solution.py:354

commit v5 on v4

--- a/solution.py
+++ b/solution.py
@@ -299,8 +299,17 @@
     rows, span = dq_ref.shape
     heads = span // HEAD_DIM
 
+    lanes = slice(first, first + span)
+    copies = [
+        pltpu.make_async_copy(done.at[0], grad_q.at[0, :, lanes], sem.at[0]),
+        pltpu.make_async_copy(done.at[1], grad_kv.at[0, 0, :, lanes], sem.at[1]),
+        pltpu.make_async_copy(done.at[2], grad_kv.at[1, 0, :, lanes], sem.at[2]),
+    ]
+
     def add(from_left, from_right):
         no_left, no_right = index == 0, index == count - 1
+        done[2] = (dkv_ref[1] + jnp.where(no_right, 0.0, from_right[1].astype(F32))).astype(BF16)
+        copies[2].start()
         delta = jnp.where(no_left, 0.0, joined(from_left[1, : 2 * heads, :LANES]))
         for h in range(heads):
             at = slice(h * HEAD_DIM, (h + 1) * HEAD_DIM)
@@ -315,8 +324,6 @@
             dk = dkv_ref[0, :, at] + jnp.where(no_right, 0.0, from_right[0, :, at].astype(F32))
             dk = dk + jnp.dot(ds_own, q_ref[0, :, wide], preferred_element_type=F32)
             done[1, :, at] = dk.astype(BF16)
-            dv = dkv_ref[1, :, at] + jnp.where(no_right, 0.0, from_right[1, :, at].astype(F32))
-            done[2, :, at] = dv.astype(BF16)
 
     @pl.when(index % 2 == 0)
     def _():
@@ -326,24 +333,16 @@
     def _():
         add(got1, got2)
 
-    lanes = slice(first, first + span)
-    copies = [
-        pltpu.make_async_copy(done.at[0], grad_q.at[0, :, lanes], sem.at[0]),
-        pltpu.make_async_copy(done.at[1:], grad_kv.at[:, 0, :, lanes], sem.at[1]),
-    ]
-    for copy in copies:
+    for copy in copies[:2]:
         copy.start()
     for copy in copies:
         copy.wait()
 
 
-def shifted(value, steps):
+def passed(value, steps):
     count = lax.axis_size("seq")
-    return lax.ppermute(value, "seq", [(i, (i + steps) % count) for i in range(count)])
-
-
-def passed_up(value):
-    return lax.ppermute(value, "seq", [(i, i + 1) for i in range(lax.axis_size("seq") - 1)])
+    first, last = max(0, -steps), min(count, count - steps)
+    return lax.ppermute(value, "seq", [(i, i + steps) for i in range(first, last)])
 
 
 def neighbour_swaps(first, second):
@@ -404,7 +403,7 @@
     sides = neighbour_swaps(first, second)
     values = []
     for own_v in own_vs:
-        values.append(passed_up(own_v))
+        values.append(passed(own_v, 1))
 
     sums = []
     for first, span in chunks(hc):
@@ -425,7 +424,7 @@
         name="stats",
         cost_estimate=cost(2 * 3 * rows * rows * hc, 20 * rows * hc),
     )(query, key_value, *sides, segments)
-    from_right, from_left = shifted(own, -1), shifted(far, 1)
+    from_right, from_left = passed(own, -1), passed(far, 1)
 
     pieces = []
     for c, (first, span) in enumerate(chunks(hc)):
@@ -436,7 +435,7 @@
             compiler_params=params(8),
             cost_estimate=cost(4 * 2 * rows * rows * span, 20 * rows * span),
         )(*sums[c], query, key_value, left_k, values[c], segments, own)
-        pieces.append((gout, delta, shifted(gout, -1)))
+        pieces.append((gout, delta, passed(gout, -1)))
 
     parts = []
     for c, (first, span) in enumerate(chunks(hc)):
@@ -460,7 +459,7 @@
             in_specs=[pl.BlockSpec(memory_space=pltpu.VMEM)] * len(parts[c]) + [anywhere] * len(results),
             out_specs=[anywhere] * 2,
             out_shape=[shape(query.shape), shape(key_value.shape)],
-            scratch_shapes=[pltpu.VMEM((3, rows, span), BF16), pltpu.SemaphoreType.DMA((2,))],
+            scratch_shapes=[pltpu.VMEM((3, rows, span), BF16), pltpu.SemaphoreType.DMA((3,))],
             input_output_aliases={len(parts[c]) + n: n for n in range(len(results))},
             compiler_params=params(12),
             cost_estimate=cost(0, 20 * rows * span),

time: 87 us -> 88.7 us (1.020)
  the two profiles are of different devices: /device:TPU:18 before, /device:TPU:0 now
where the time goes in v5:
time: 88.7 us; the launch traced here: 87.8 us
  starting transfers between devices  43.6 us (49%)
  waiting for transfers between devices  25.8 us (29%)
  Pallas kernels  17.4 us (20%)
  between operations  1.02 us (1%)
    ppermute x6, starting transfers between devices, passed(): lax.ppermute(value, 'seq', [(i, i + steps) for i in range(first, last)])  18.8 us
    ppermute x10, starting transfers between devices, swap(): lax.ppermute(value, axis, [(i, i ^ bits) for i in range(lax.axis_size(axi...  17.2 us
    ppermute x6, waiting for transfers between devices, neighbour_swaps(): return (lax.ppermute(first, 'seq', one), lax.ppermute(second, 'seq', two))  11.5 us
    ppermute x10, waiting for transfers between devices, swap(): lax.ppermute(value, axis, [(i, i ^ bits) for i in range(lax.axis_size(axi...  9.66 us
    ppermute x6, starting transfers between devices, neighbour_swaps(): return (lax.ppermute(first, 'seq', one), lax.ppermute(second, 'seq', two))  7.57 us
    pallas_call x2, Pallas kernels, step(): pl.pallas_call(functools.partial(grads_kernel, count, first, scale), out_...  5.91 us
    ppermute x6, waiting for transfers between devices, passed(): lax.ppermute(value, 'seq', [(i, i + steps) for i in range(first, last)])  4.66 us
    pallas_call x2, Pallas kernels, step(): pl.pallas_call(functools.partial(project_kernel, chips, first), out_shape...  2.78 us
  transfers between devices with their start and end apart: 22, of which 7 were waited for; matrix products, arithmetic and copies ran while one was open for 0% of the time, Pallas kernels for 18%

profile of v5, /device:TPU:0, one launch (start us, length us, event | category | flops | bytes accessed | tf_op | source)
XLA Modules:
  0.0 87.8 jit_solution(3174715259137971704)
XLA Ops:
  0.6 0.6 collective-permute-start.6
  1.2 1.2 %grad_slices.1 = (bf16[528,128]{1,0:T(8,128)(2,1)S(1)}, bf16[528,128]{1,0:T(8,128)(2,1)S(1)}, bf16[528,128]{1,0:T(8,128)(2,1)S(1)}, bf16[528,128]{1,0:T(8,128)(2,1)S(1)}) custom-call(bf16[1,128,2048]{2,1,0:T(8,128)(2,1)} %grad_ref.1, s32[1,128]{1,0:T(1,128)} %tags_ref.1), custom_call_target="tpu_custom_call" | custom-call | bytes 1048576 | tf_op jit(solution)/shard_map/grad_slices/pallas_call | solution.py:383
  2.4 2.6 %collective-permute-start.3 = (bf16[528,128]{1,0:T(8,128)(2,1)S(1)}, bf16[528,128]{1,0:T(8,128)(2,1)S(1)}, u32[]{:S(2)}, u32[]{:S(2)}) collective-permute-start(bf16[528,128]{1,0:T(8,128)(2,1)S(1)} %get-tuple-element.44), channel_id=1, source_target_pairs={{0,8},{4,12},{8,0},{12,4},{16,24},{20,28},{24,16},{28,20},{1,9},{5... | collective-permute-start | bytes 405512 | tf_op jit(solution)/shard_map/ppermute | solution.py:32
  5.1 1.4 %side_slices.1 = (bf16[128,2048]{1,0:T(8,128)(2,1)S(1)}, bf16[128,2048]{1,0:T(8,128)(2,1)S(1)}, bf16[128,1024]{1,0:T(8,128)(2,1)S(1)}, bf16[128,1024]{1,0:T(8,128)(2,1)S(1)}) custom-call(bf16[1,128,2048]{2,1,0:T(8,128)(2,1)} %q_ref.11, bf16[2,1,128,2048]{3,2,1,0:T(8,128)(2,1)} %kv_ref.11), custom_call_target="tpu_custom_call" | custom-call | bytes 3145728 | tf_op jit(solution)/shard_map/side_slices/pallas_call | solution.py:394
  6.5 1.6 %collective-permute-start = (bf16[128,2048]{1,0:T(8,128)(2,1)S(1)}, bf16[128,2048]{1,0:T(8,128)(2,1)S(1)}, u32[]{:S(2)}, u32[]{:S(2)}) collective-permute-start(bf16[128,2048]{1,0:T(8,128)(2,1)S(1)} %get-tuple-element.38), channel_id=1, source_target_pairs={{0,1},{1,0},{2,3},{3,2},{4,5},{5,4},{6,7},{7,6},{8,9},{9,8},{10,11... | collective-permute-start | bytes 1572872 | tf_op jit(solution)/shard_map/ppermute | solution.py:353
  8.1 0.7 collective-permute-start.1
  8.8 1.6 %collective-permute-start.4 = (bf16[528,128]{1,0:T(8,128)(2,1)S(1)}, bf16[528,128]{1,0:T(8,128)(2,1)S(1)}, u32[]{:S(2)}, u32[]{:S(2)}) collective-permute-start(bf16[528,128]{1,0:T(8,128)(2,1)S(1)} %get-tuple-element.45), channel_id=1, source_target_pairs={{0,16},{4,20},{8,24},{12,28},{16,0},{20,4},{24,8},{28,12},{1,17},{... | collective-permute-start | bytes 405512 | tf_op jit(solution)/shard_map/ppermute | solution.py:32
  10.4 0.0 collective-permute-done.3.refs_1_
  10.4 1.5 %collective-permute-start.5 = (bf16[528,128]{1,0:T(8,128)(2,1)S(1)}, bf16[528,128]{1,0:T(8,128)(2,1)S(1)}, u32[]{:S(2)}, u32[]{:S(2)}) collective-permute-start(bf16[528,128]{1,0:T(8,128)(2,1)S(1)} %get-tuple-element.46), channel_id=1, source_target_pairs={{0,24},{4,28},{8,16},{12,20},{16,8},{20,12},{24,0},{28,4},{1,25},{... | collective-permute-start | bytes 405512 | tf_op jit(solution)/shard_map/ppermute | solution.py:32
  11.9 5.2 %collective-permute-done.4.refs_2_ = bf16[528,128]{1,0:T(8,128)(2,1)S(1)} collective-permute-done((bf16[528,128]{1,0:T(8,128)(2,1)S(1)}, bf16[528,128]{1,0:T(8,128)(2,1)S(1)}, u32[]{:S(2)}, u32[]{:S(2)}) %collective-permute-start.4) | collective-permute-done | bytes 135200 | tf_op jit(solution)/shard_map/ppermute | solution.py:32
  17.0 6.0 %collective-permute-start.15 = (bf16[128,1024]{1,0:T(8,128)(2,1)S(1)}, bf16[128,1024]{1,0:T(8,128)(2,1)S(1)}, u32[]{:S(2)}, u32[]{:S(2)}) collective-permute-start(bf16[128,1024]{1,0:T(8,128)(2,1)S(1)} %get-tuple-element.60), channel_id=1, source_target_pairs={{0,1},{1,2},{2,3},{4,5},{5,6},{6,7},{8,9},{9,10},{10,11},{12,13},{... | collective-permute-start | bytes 786440 | tf_op jit(solution)/shard_map/ppermute | solution.py:345
  23.1 0.0 collective-permute-done.6.refs_5_
  23.1 1.4 %shard_map.80 = (f32[128,1024]{1,0:T(8,128)S(1)}, bf16[128,1024]{1,0:T(8,128)(2,1)S(1)}, bf16[128,1024]{1,0:T(8,128)(2,1)S(1)}, bf16[128,1024]{1,0:T(8,128)(2,1)S(1)}) custom-call(bf16[528,128]{1,0:T(8,128)(2,1)S(1)} %get-tuple-element.43.refs_0_, bf16[528,128]{1,0:T(8,128)(2,1)S(1)} %collective-permute-done.3.refs_1_, ...), custom_call_target="tpu_custom_call" | custom-call | flops 1073741824 | bytes 2097152 | tf_op jit(solution)/shard_map/pallas_call | solution.py:410
  24.5 0.6 collective-permute-start.16
  25.1 1.5 %collective-permute-start.17 = (bf16[128,1024]{1,0:T(8,128)(2,1)S(1)}, bf16[128,1024]{1,0:T(8,128)(2,1)S(1)}, u32[]{:S(2)}, u32[]{:S(2)}) collective-permute-start(bf16[128,1024]{1,0:T(8,128)(2,1)S(1)} %get-tuple-element.63), channel_id=1, source_target_pairs={{0,16},{4,20},{8,24},{12,28},{16,0},{20,4},{24,8},{28,12},{1,17},{... | collective-permute-start | bytes 786440 | tf_op jit(solution)/shard_map/ppermute | solution.py:32
  26.6 0.3 collective-permute-done.15.refs_6_.left_v
  26.9 2.2 %collective-permute-start.18 = (bf16[128,1024]{1,0:T(8,128)(2,1)S(1)}, bf16[128,1024]{1,0:T(8,128)(2,1)S(1)}, u32[]{:S(2)}, u32[]{:S(2)}) collective-permute-start(bf16[128,1024]{1,0:T(8,128)(2,1)S(1)} %get-tuple-element.64), channel_id=1, source_target_pairs={{0,24},{4,28},{8,16},{12,20},{16,8},{20,12},{24,0},{28,4},{1,25},{... | collective-permute-start | bytes 786440 | tf_op jit(solution)/shard_map/ppermute | solution.py:32
  29.1 1.4 %shard_map.77 = (f32[128,1024]{1,0:T(8,128)S(1)}, bf16[128,1024]{1,0:T(8,128)(2,1)S(1)}, bf16[128,1024]{1,0:T(8,128)(2,1)S(1)}, bf16[128,1024]{1,0:T(8,128)(2,1)S(1)}) custom-call(bf16[528,128]{1,0:T(8,128)(2,1)S(1)} %get-tuple-element.43.refs_0_, bf16[528,128]{1,0:T(8,128)(2,1)S(1)} %collective-permute-done.3.refs_1_, ...), custom_call_target="tpu_custom_call" | custom-call | flops 1073741824 | bytes 2097152 | tf_op jit(solution)/shard_map/pallas_call | solution.py:410
  30.5 0.0 collective-permute-done.got1
  30.5 4.4 %collective-permute-start.2 = (bf16[128,1024]{1,0:T(8,128)(2,1)S(1)}, bf16[128,1024]{1,0:T(8,128)(2,1)S(1)}, u32[]{:S(2)}, u32[]{:S(2)}) collective-permute-start(bf16[128,1024]{1,0:T(8,128)(2,1)S(1)} %get-tuple-element.41), channel_id=1, source_target_pairs={{0,1},{1,2},{2,3},{4,5},{5,6},{6,7},{8,9},{9,10},{10,11},{12,13},{... | collective-permute-start | bytes 786440 | tf_op jit(solution)/shard_map/ppermute | solution.py:345
  34.9 1.6 %collective-permute-start.7 = (bf16[128,1024]{1,0:T(8,128)(2,1)S(1)}, bf16[128,1024]{1,0:T(8,128)(2,1)S(1)}, u32[]{:S(2)}, u32[]{:S(2)}) collective-permute-start(bf16[128,1024]{1,0:T(8,128)(2,1)S(1)} %get-tuple-element.48), channel_id=1, source_target_pairs={{0,8},{4,12},{8,0},{12,4},{16,24},{20,28},{24,16},{28,20},{1,9},{5... | collective-permute-start | bytes 786440 | tf_op jit(solution)/shard_map/ppermute | solution.py:32
  36.5 0.0 collective-permute-done.16.refs_0_
  36.5 0.3 collective-permute-start.8
  36.8 4.8 %collective-permute-start.9 = (bf16[128,1024]{1,0:T(8,128)(2,1)S(1)}, bf16[128,1024]{1,0:T(8,128)(2,1)S(1)}, u32[]{:S(2)}, u32[]{:S(2)}) collective-permute-start(bf16[128,1024]{1,0:T(8,128)(2,1)S(1)} %get-tuple-element.50), channel_id=1, source_target_pairs={{0,24},{4,28},{8,16},{12,20},{16,8},{20,12},{24,0},{28,4},{1,25},{... | collective-permute-start | bytes 786440 | tf_op jit(solution)/shard_map/ppermute | solution.py:32
  41.6 1.5 %stats.1 = (f32[2,16,128]{2,1,0:T(8,128)S(1)}, f32[2,16,128]{2,1,0:T(8,128)S(1)}, bf16[128,2048]{1,0:T(8,128)(2,1)S(1)}, bf16[128,2048]{1,0:T(8,128)(2,1)S(1)}) custom-call(bf16[1,128,2048]{2,1,0:T(8,128)(2,1)S(1)} %copy-done.1, bf16[2,1,128,2048]{3,2,1,0:T(8,128)(2,1)S(1)} %copy-done, bf16[128,2048]{1,0:T(8,128)(2,1)S(1)} %collective-permute-done.got1, ...), custom_call_target="tpu_custom_call" | custom-call | flops 201326592 | bytes 5242880 | tf_op jit(solution)/shard_map/stats/pallas_call | solution.py:420
  43.1 0.0 collective-permute-done.18.refs_2_
  43.1 0.9 %shard_map.81 = (bf16[1040,128]{1,0:T(8,128)(2,1)S(1)}, f32[8,128]{1,0:T(8,128)S(1)}) custom-call(f32[128,1024]{1,0:T(8,128)S(1)} %get-tuple-element.61.mine, bf16[128,1024]{1,0:T(8,128)(2,1)S(1)} %collective-permute-done.16.refs_0_, bf16[128,1024]{1,0:T(8,128)(2,1)S(1)} %collective-permute-done.17.refs_1_, ...), custom_call_target="tpu_custom_call" | custom-call | flops 134217728 | bytes 2621440 | tf_op jit(solution)/shard_map/pallas_call | solution.py:432
  44.0 1.3 %collective-permute-start.19 = (bf16[1040,128]{1,0:T(8,128)(2,1)S(1)}, bf16[1040,128]{1,0:T(8,128)(2,1)S(1)}, u32[]{:S(2)}, u32[]{:S(2)}) collective-permute-start(bf16[1040,128]{1,0:T(8,128)(2,1)S(1)} %get-tuple-element.65.g_ref), channel_id=1, source_target_pairs={{1,0},{2,1},{3,2},{5,4},{6,5},{7,6},{9,8},{10,9},{11,10},{13,12},{... | collective-permute-start | bytes 798728 | tf_op jit(solution)/shard_map/ppermute | solution.py:345
  45.3 0.0 collective-permute-done.2.refs_6_.left_v
  45.3 0.0 collective-permute-done.7.refs_0_
  45.3 4.5 %collective-permute-done.8.refs_1_ = bf16[128,1024]{1,0:T(8,128)(2,1)S(1)} collective-permute-done((bf16[128,1024]{1,0:T(8,128)(2,1)S(1)}, bf16[128,1024]{1,0:T(8,128)(2,1)S(1)}, u32[]{:S(2)}, u32[]{:S(2)}) %collective-permute-start.8) | collective-permute-done | bytes 262176 | tf_op jit(solution)/shard_map/ppermute | solution.py:32
  49.8 0.9 %shard_map.78 = (bf16[1040,128]{1,0:T(8,128)(2,1)S(1)}, f32[8,128]{1,0:T(8,128)S(1)}) custom-call(f32[128,1024]{1,0:T(8,128)S(1)} %get-tuple-element.47.mine, bf16[128,1024]{1,0:T(8,128)(2,1)S(1)} %collective-permute-done.7.refs_0_, bf16[128,1024]{1,0:T(8,128)(2,1)S(1)} %collective-permute-done.8.refs_1_, ...), custom_call_target="tpu_custom_call" | custom-call | flops 134217728 | bytes 2621440 | tf_op jit(solution)/shard_map/pallas_call | solution.py:432
  50.7 1.3 %collective-permute-start.10 = (bf16[1040,128]{1,0:T(8,128)(2,1)S(1)}, bf16[1040,128]{1,0:T(8,128)(2,1)S(1)}, u32[]{:S(2)}, u32[]{:S(2)}) collective-permute-start(bf16[1040,128]{1,0:T(8,128)(2,1)S(1)} %get-tuple-element.52.g_ref), channel_id=1, source_target_pairs={{1,0},{2,1},{3,2},{5,4},{6,5},{7,6},{9,8},{10,9},{11,10},{13,12},{... | collective-permute-start | bytes 798728 | tf_op jit(solution)/shard_map/ppermute | solution.py:345
  52.0 4.5 %collective-permute-start.11 = (f32[2,16,128]{2,1,0:T(8,128)S(1)}, f32[2,16,128]{2,1,0:T(8,128)S(1)}, u32[]{:S(2)}, u32[]{:S(2)}) collective-permute-start(f32[2,16,128]{2,1,0:T(8,128)S(1)} %get-tuple-element.53.far_stats), channel_id=1, source_target_pairs={{0,1},{1,2},{2,3},{4,5},{5,6},{6,7},{8,9},{9,10},{10,11},{12,13},{... | collective-permute-start | bytes 49160 | tf_op jit(solution)/shard_map/ppermute | solution.py:345
  56.6 1.3 %collective-permute-start.12 = (f32[2,16,128]{2,1,0:T(8,128)S(1)}, f32[2,16,128]{2,1,0:T(8,128)S(1)}, u32[]{:S(2)}, u32[]{:S(2)}) collective-permute-start(f32[2,16,128]{2,1,0:T(8,128)S(1)} %get-tuple-element.51.refs_8_.own_stats), channel_id=1, source_target_pairs={{1,0},{2,1},{3,2},{5,4},{6,5},{7,6},{9,8},{10,9},{11,10},{13,12},{... | collective-permute-start | bytes 49160 | tf_op jit(solution)/shard_map/ppermute | solution.py:345
  57.9 0.1 collective-permute-done.11.from_left
  58.0 4.2 %collective-permute-done.12.from_right = f32[2,16,128]{2,1,0:T(8,128)S(1)} collective-permute-done((f32[2,16,128]{2,1,0:T(8,128)S(1)}, f32[2,16,128]{2,1,0:T(8,128)S(1)}, u32[]{:S(2)}, u32[]{:S(2)}) %collective-permute-start.12) | collective-permute-done | bytes 16416 | tf_op jit(solution)/shard_map/ppermute | solution.py:345
  62.2 2.9 %shard_map.82 = (f32[128,1024]{1,0:T(8,128)S(1)}, f32[2,128,1024]{2,1,0:T(8,128)S(1)}, bf16[8,256,128]{2,1,0:T(8,128)(2,1)S(1)}, bf16[2,128,1024]{2,1,0:T(8,128)(2,1)S(1)}, bf16[2,128,1024]{2,1,0:T(8,128)(2,1)S(1)}) custom-call(bf16[1,128,2048]{2,1,0:T(8,128)(2,1)S(1)} %copy-done.1, bf16[2,1,128,2048]{3,2,1,0:T(8,128)(2,1)S(1)} %copy-done, ...), custom_call_target="tpu_custom_call" | custom-call | flops 503316480 | bytes 5242880 | tf_op jit(solution)/shard_map/pallas_call | solution.py:444
  65.1 1.0 %collective-permute-start.20 = (bf16[2,128,1024]{2,1,0:T(8,128)(2,1)S(1)}, bf16[2,128,1024]{2,1,0:T(8,128)(2,1)S(1)}, u32[]{:S(2)}, u32[]{:S(2)}) collective-permute-start(bf16[2,128,1024]{2,1,0:T(8,128)(2,1)S(1)} %get-tuple-element.70), channel_id=1, source_target_pairs={{0,1},{1,0},{2,3},{3,2},{4,5},{5,4},{6,7},{7,6},{8,9},{9,8},{10,11... | collective-permute-start | bytes 1572872 | tf_op jit(solution)/shard_map/ppermute | solution.py:353
  66.0 0.7 collective-permute-start.21
  66.7 3.0 %shard_map.79 = (f32[128,1024]{1,0:T(8,128)S(1)}, f32[2,128,1024]{2,1,0:T(8,128)S(1)}, bf16[8,256,128]{2,1,0:T(8,128)(2,1)S(1)}, bf16[2,128,1024]{2,1,0:T(8,128)(2,1)S(1)}, bf16[2,128,1024]{2,1,0:T(8,128)(2,1)S(1)}) custom-call(bf16[1,128,2048]{2,1,0:T(8,128)(2,1)S(1)} %copy-done.1, bf16[2,1,128,2048]{3,2,1,0:T(8,128)(2,1)S(1)} %copy-done, ...), custom_call_target="tpu_custom_call" | custom-call | flops 503316480 | bytes 5242880 | tf_op jit(solution)/shard_map/pallas_call | solution.py:444
  69.8 2.9 %collective-permute-start.13 = (bf16[2,128,1024]{2,1,0:T(8,128)(2,1)S(1)}, bf16[2,128,1024]{2,1,0:T(8,128)(2,1)S(1)}, u32[]{:S(2)}, u32[]{:S(2)}) collective-permute-start(bf16[2,128,1024]{2,1,0:T(8,128)(2,1)S(1)} %get-tuple-element.58), channel_id=1, source_target_pairs={{0,1},{1,0},{2,3},{3,2},{4,5},{5,4},{6,7},{7,6},{8,9},{9,8},{10,11... | collective-permute-start | bytes 1572872 | tf_op jit(solution)/shard_map/ppermute | solution.py:353
  72.7 0.7 collective-permute-start.14
  73.4 6.5 %collective-permute-done.20.got1 = bf16[2,128,1024]{2,1,0:T(8,128)(2,1)S(1)} collective-permute-done((bf16[2,128,1024]{2,1,0:T(8,128)(2,1)S(1)}, bf16[2,128,1024]{2,1,0:T(8,128)(2,1)S(1)}, u32[]{:S(2)}, u32[]{:S(2)}) %collective-permute-start.20) | collective-permute-done | bytes 524320 | tf_op jit(solution)/shard_map/ppermute | solution.py:353
  79.9 0.0 collective-permute-done.21.got2
  79.9 1.4 %shard_map.83 = (bf16[1,128,2048]{2,1,0:T(8,128)(2,1)}, bf16[2,1,128,2048]{3,2,1,0:T(8,128)(2,1)}) custom-call(f32[128,1024]{1,0:T(8,128)S(1)} %get-tuple-element.67.dq_ref, f32[2,128,1024]{2,1,0:T(8,128)S(1)} %get-tuple-element.68.dkv_ref, bf16[8,256,128]{2,1,0:T(8,128)(2,1)S(1)} %get-tuple-element.69.p_ref, bf16[1,128,2048]{2,1,0:T(8,128)(2,1)S(1)} %copy-done.1, ...), custom_call_target="tpu_custom_call" | custom-call | bytes 2621440 | tf_op jit(solution)/shard_map/pallas_call | solution.py:457
  81.3 4.9 %collective-permute-done.13.got1 = bf16[2,128,1024]{2,1,0:T(8,128)(2,1)S(1)} collective-permute-done((bf16[2,128,1024]{2,1,0:T(8,128)(2,1)S(1)}, bf16[2,128,1024]{2,1,0:T(8,128)(2,1)S(1)}, u32[]{:S(2)}, u32[]{:S(2)}) %collective-permute-start.13) | collective-permute-done | bytes 524320 | tf_op jit(solution)/shard_map/ppermute | solution.py:353
  86.2 1.4 %shard_map.84 = (bf16[1,128,2048]{2,1,0:T(8,128)(2,1)}, bf16[2,1,128,2048]{3,2,1,0:T(8,128)(2,1)}) custom-call(f32[128,1024]{1,0:T(8,128)S(1)} %get-tuple-element.55.dq_ref, f32[2,128,1024]{2,1,0:T(8,128)S(1)} %get-tuple-element.56.dkv_ref, bf16[8,256,128]{2,1,0:T(8,128)(2,1)S(1)} %get-tuple-element.57.p_ref, ...), custom_call_target="tpu_custom_call", output_to_operand_aliasing={{0}: (8, {}), {1}: (9, {})} | custom-call | bytes 2621440 | tf_op jit(solution)/shard_map/pallas_call | solution.py:457
  (15 shorter events, 0.0 us)
Async XLA Ops:
  0.6 22.4 %copy-start.2 = (bf16[2,2048,256]{2,1,0:T(8,128)(2,1)S(1)}, bf16[2,2048,256]{2,1,0:T(8,128)(2,1)}, u32[]{:S(2)}) copy-start(bf16[2,2048,256]{2,1,0:T(8,128)(2,1)} %refs_4_.6) | copy-start | bytes 6291460
  0.6 22.4 %collective-permute-start.6 = (bf16[2,2048,256]{2,1,0:T(8,128)(2,1)}, bf16[2,2048,256]{2,1,0:T(8,128)(2,1)S(1)}, u32[]{:S(2)}, u32[]{:S(2)}) collective-permute-start(bf16[2,2048,256]{2,1,0:T(8,128)(2,1)} %refs_4_.6), channel_id=1, source_target_pairs={{0,4},{4,0},{8,12},{12,8},{16,20},{20,16},{24,28},{28,24},{1,5},{5... | collective-permute-start | bytes 6291464 | tf_op jit(solution)/shard_map/ppermute | solution.py:32
  2.4 7.9 %collective-permute-start.3 = (bf16[528,128]{1,0:T(8,128)(2,1)S(1)}, bf16[528,128]{1,0:T(8,128)(2,1)S(1)}, u32[]{:S(2)}, u32[]{:S(2)}) collective-permute-start(bf16[528,128]{1,0:T(8,128)(2,1)S(1)} %get-tuple-element.44), channel_id=1, source_target_pairs={{0,8},{4,12},{8,0},{12,4},{16,24},{20,28},{24,16},{28,20},{1,9},{5... | collective-permute-start | bytes 405512 | tf_op jit(solution)/shard_map/ppermute | solution.py:32
  6.5 24.1 %collective-permute-start = (bf16[128,2048]{1,0:T(8,128)(2,1)S(1)}, bf16[128,2048]{1,0:T(8,128)(2,1)S(1)}, u32[]{:S(2)}, u32[]{:S(2)}) collective-permute-start(bf16[128,2048]{1,0:T(8,128)(2,1)S(1)} %get-tuple-element.38), channel_id=1, source_target_pairs={{0,1},{1,0},{2,3},{3,2},{4,5},{5,4},{6,7},{7,6},{8,9},{9,8},{10,11... | collective-permute-start | bytes 1572872 | tf_op jit(solution)/shard_map/ppermute | solution.py:353
  8.1 26.8 %collective-permute-start.1 = (bf16[128,2048]{1,0:T(8,128)(2,1)S(1)}, bf16[128,2048]{1,0:T(8,128)(2,1)S(1)}, u32[]{:S(2)}, u32[]{:S(2)}) collective-permute-start(bf16[128,2048]{1,0:T(8,128)(2,1)S(1)} %get-tuple-element.39), channel_id=1, source_target_pairs={{0,0},{1,2},{2,1},{3,3},{4,4},{5,6},{6,5},{7,7},{8,8},{9,10},{10,9... | collective-permute-start | bytes 1572872 | tf_op jit(solution)/shard_map/ppermute | solution.py:353
  8.8 8.2 %collective-permute-start.4 = (bf16[528,128]{1,0:T(8,128)(2,1)S(1)}, bf16[528,128]{1,0:T(8,128)(2,1)S(1)}, u32[]{:S(2)}, u32[]{:S(2)}) collective-permute-start(bf16[528,128]{1,0:T(8,128)(2,1)S(1)} %get-tuple-element.45), channel_id=1, source_target_pairs={{0,16},{4,20},{8,24},{12,28},{16,0},{20,4},{24,8},{28,12},{1,17},{... | collective-permute-start | bytes 405512 | tf_op jit(solution)/shard_map/ppermute | solution.py:32
  10.4 12.7 %collective-permute-start.5 = (bf16[528,128]{1,0:T(8,128)(2,1)S(1)}, bf16[528,128]{1,0:T(8,128)(2,1)S(1)}, u32[]{:S(2)}, u32[]{:S(2)}) collective-permute-start(bf16[528,128]{1,0:T(8,128)(2,1)S(1)} %get-tuple-element.46), channel_id=1, source_target_pairs={{0,24},{4,28},{8,16},{12,20},{16,8},{20,12},{24,0},{28,4},{1,25},{... | collective-permute-start | bytes 405512 | tf_op jit(solution)/shard_map/ppermute | solution.py:32
  17.0 9.9 %collective-permute-start.15 = (bf16[128,1024]{1,0:T(8,128)(2,1)S(1)}, bf16[128,1024]{1,0:T(8,128)(2,1)S(1)}, u32[]{:S(2)}, u32[]{:S(2)}) collective-permute-start(bf16[128,1024]{1,0:T(8,128)(2,1)S(1)} %get-tuple-element.60), channel_id=1, source_target_pairs={{0,1},{1,2},{2,3},{4,5},{5,6},{6,7},{8,9},{9,10},{10,11},{12,13},{... | collective-permute-start | bytes 786440 | tf_op jit(solution)/shard_map/ppermute | solution.py:345
  24.5 12.0 %collective-permute-start.16 = (bf16[128,1024]{1,0:T(8,128)(2,1)S(1)}, bf16[128,1024]{1,0:T(8,128)(2,1)S(1)}, u32[]{:S(2)}, u32[]{:S(2)}) collective-permute-start(bf16[128,1024]{1,0:T(8,128)(2,1)S(1)} %get-tuple-element.62), channel_id=1, source_target_pairs={{0,8},{4,12},{8,0},{12,4},{16,24},{20,28},{24,16},{28,20},{1,9},{5... | collective-permute-start | bytes 786440 | tf_op jit(solution)/shard_map/ppermute | solution.py:32
  25.1 11.7 %collective-permute-start.17 = (bf16[128,1024]{1,0:T(8,128)(2,1)S(1)}, bf16[128,1024]{1,0:T(8,128)(2,1)S(1)}, u32[]{:S(2)}, u32[]{:S(2)}) collective-permute-start(bf16[128,1024]{1,0:T(8,128)(2,1)S(1)} %get-tuple-element.63), channel_id=1, source_target_pairs={{0,16},{4,20},{8,24},{12,28},{16,0},{20,4},{24,8},{28,12},{1,17},{... | collective-permute-start | bytes 786440 | tf_op jit(solution)/shard_map/ppermute | solution.py:32
  26.9 14.7 %copy-start = (bf16[2,1,128,2048]{3,2,1,0:T(8,128)(2,1)S(1)}, bf16[2,1,128,2048]{3,2,1,0:T(8,128)(2,1)}, u32[]{:S(2)}) copy-start(bf16[2,1,128,2048]{3,2,1,0:T(8,128)(2,1)} %kv_ref.11) | copy-start | bytes 3145732
  26.9 14.7 %copy-start.1 = (bf16[1,128,2048]{2,1,0:T(8,128)(2,1)S(1)}, bf16[1,128,2048]{2,1,0:T(8,128)(2,1)}, u32[]{:S(2)}) copy-start(bf16[1,128,2048]{2,1,0:T(8,128)(2,1)} %q_ref.11) | copy-start | bytes 1572868
  26.9 14.7 %copy-start.3 = (s32[1,512]{1,0:T(1,128)S(1)}, s32[1,512]{1,0:T(1,128)}, u32[]{:S(2)}) copy-start(s32[1,512]{1,0:T(1,128)} %segs.5) | copy-start | bytes 6148
  26.9 16.2 %collective-permute-start.18 = (bf16[128,1024]{1,0:T(8,128)(2,1)S(1)}, bf16[128,1024]{1,0:T(8,128)(2,1)S(1)}, u32[]{:S(2)}, u32[]{:S(2)}) collective-permute-start(bf16[128,1024]{1,0:T(8,128)(2,1)S(1)} %get-tuple-element.64), channel_id=1, source_target_pairs={{0,24},{4,28},{8,16},{12,20},{16,8},{20,12},{24,0},{28,4},{1,25},{... | collective-permute-start | bytes 786440 | tf_op jit(solution)/shard_map/ppermute | solution.py:32
  30.5 14.8 %collective-permute-start.2 = (bf16[128,1024]{1,0:T(8,128)(2,1)S(1)}, bf16[128,1024]{1,0:T(8,128)(2,1)S(1)}, u32[]{:S(2)}, u32[]{:S(2)}) collective-permute-start(bf16[128,1024]{1,0:T(8,128)(2,1)S(1)} %get-tuple-element.41), channel_id=1, source_target_pairs={{0,1},{1,2},{2,3},{4,5},{5,6},{6,7},{8,9},{9,10},{10,11},{12,13},{... | collective-permute-start | bytes 786440 | tf_op jit(solution)/shard_map/ppermute | solution.py:345
  34.9 10.4 %collective-permute-start.7 = (bf16[128,1024]{1,0:T(8,128)(2,1)S(1)}, bf16[128,1024]{1,0:T(8,128)(2,1)S(1)}, u32[]{:S(2)}, u32[]{:S(2)}) collective-permute-start(bf16[128,1024]{1,0:T(8,128)(2,1)S(1)} %get-tuple-element.48), channel_id=1, source_target_pairs={{0,8},{4,12},{8,0},{12,4},{16,24},{20,28},{24,16},{28,20},{1,9},{5... | collective-permute-start | bytes 786440 | tf_op jit(solution)/shard_map/ppermute | solution.py:32
  36.5 13.3 %collective-permute-start.8 = (bf16[128,1024]{1,0:T(8,128)(2,1)S(1)}, bf16[128,1024]{1,0:T(8,128)(2,1)S(1)}, u32[]{:S(2)}, u32[]{:S(2)}) collective-permute-start(bf16[128,1024]{1,0:T(8,128)(2,1)S(1)} %get-tuple-element.49), channel_id=1, source_target_pairs={{0,16},{4,20},{8,24},{12,28},{16,0},{20,4},{24,8},{28,12},{1,17},{... | collective-permute-start | bytes 786440 | tf_op jit(solution)/shard_map/ppermute | solution.py:32
  36.8 13.0 %collective-permute-start.9 = (bf16[128,1024]{1,0:T(8,128)(2,1)S(1)}, bf16[128,1024]{1,0:T(8,128)(2,1)S(1)}, u32[]{:S(2)}, u32[]{:S(2)}) collective-permute-start(bf16[128,1024]{1,0:T(8,128)(2,1)S(1)} %get-tuple-element.50), channel_id=1, source_target_pairs={{0,24},{4,28},{8,16},{12,20},{16,8},{20,12},{24,0},{28,4},{1,25},{... | collective-permute-start | bytes 786440 | tf_op jit(solution)/shard_map/ppermute | solution.py:32
  44.0 18.2 %collective-permute-start.19 = (bf16[1040,128]{1,0:T(8,128)(2,1)S(1)}, bf16[1040,128]{1,0:T(8,128)(2,1)S(1)}, u32[]{:S(2)}, u32[]{:S(2)}) collective-permute-start(bf16[1040,128]{1,0:T(8,128)(2,1)S(1)} %get-tuple-element.65.g_ref), channel_id=1, source_target_pairs={{1,0},{2,1},{3,2},{5,4},{6,5},{7,6},{9,8},{10,9},{11,10},{13,12},{... | collective-permute-start | bytes 798728 | tf_op jit(solution)/shard_map/ppermute | solution.py:345
  50.7 16.0 %collective-permute-start.10 = (bf16[1040,128]{1,0:T(8,128)(2,1)S(1)}, bf16[1040,128]{1,0:T(8,128)(2,1)S(1)}, u32[]{:S(2)}, u32[]{:S(2)}) collective-permute-start(bf16[1040,128]{1,0:T(8,128)(2,1)S(1)} %get-tuple-element.52.g_ref), channel_id=1, source_target_pairs={{1,0},{2,1},{3,2},{5,4},{6,5},{7,6},{9,8},{10,9},{11,10},{13,12},{... | collective-permute-start | bytes 798728 | tf_op jit(solution)/shard_map/ppermute | solution.py:345
  52.0 6.0 %collective-permute-start.11 = (f32[2,16,128]{2,1,0:T(8,128)S(1)}, f32[2,16,128]{2,1,0:T(8,128)S(1)}, u32[]{:S(2)}, u32[]{:S(2)}) collective-permute-start(f32[2,16,128]{2,1,0:T(8,128)S(1)} %get-tuple-element.53.far_stats), channel_id=1, source_target_pairs={{0,1},{1,2},{2,3},{4,5},{5,6},{6,7},{8,9},{9,10},{10,11},{12,13},{... | collective-permute-start | bytes 49160 | tf_op jit(solution)/shard_map/ppermute | solution.py:345
  56.6 5.6 %collective-permute-start.12 = (f32[2,16,128]{2,1,0:T(8,128)S(1)}, f32[2,16,128]{2,1,0:T(8,128)S(1)}, u32[]{:S(2)}, u32[]{:S(2)}) collective-permute-start(f32[2,16,128]{2,1,0:T(8,128)S(1)} %get-tuple-element.51.refs_8_.own_stats), channel_id=1, source_target_pairs={{1,0},{2,1},{3,2},{5,4},{6,5},{7,6},{9,8},{10,9},{11,10},{13,12},{... | collective-permute-start | bytes 49160 | tf_op jit(solution)/shard_map/ppermute | solution.py:345
  65.1 14.9 %collective-permute-start.20 = (bf16[2,128,1024]{2,1,0:T(8,128)(2,1)S(1)}, bf16[2,128,1024]{2,1,0:T(8,128)(2,1)S(1)}, u32[]{:S(2)}, u32[]{:S(2)}) collective-permute-start(bf16[2,128,1024]{2,1,0:T(8,128)(2,1)S(1)} %get-tuple-element.70), channel_id=1, source_target_pairs={{0,1},{1,0},{2,3},{3,2},{4,5},{5,4},{6,7},{7,6},{8,9},{9,8},{10,11... | collective-permute-start | bytes 1572872 | tf_op jit(solution)/shard_map/ppermute | solution.py:353
  66.0 13.9 %collective-permute-start.21 = (bf16[2,128,1024]{2,1,0:T(8,128)(2,1)S(1)}, bf16[2,128,1024]{2,1,0:T(8,128)(2,1)S(1)}, u32[]{:S(2)}, u32[]{:S(2)}) collective-permute-start(bf16[2,128,1024]{2,1,0:T(8,128)(2,1)S(1)} %get-tuple-element.71), channel_id=1, source_target_pairs={{0,0},{1,2},{2,1},{3,3},{4,4},{5,6},{6,5},{7,7},{8,8},{9,10},{10,9... | collective-permute-start | bytes 1572872 | tf_op jit(solution)/shard_map/ppermute | solution.py:353
  69.8 16.5 %collective-permute-start.13 = (bf16[2,128,1024]{2,1,0:T(8,128)(2,1)S(1)}, bf16[2,128,1024]{2,1,0:T(8,128)(2,1)S(1)}, u32[]{:S(2)}, u32[]{:S(2)}) collective-permute-start(bf16[2,128,1024]{2,1,0:T(8,128)(2,1)S(1)} %get-tuple-element.58), channel_id=1, source_target_pairs={{0,1},{1,0},{2,3},{3,2},{4,5},{5,4},{6,7},{7,6},{8,9},{9,8},{10,11... | collective-permute-start | bytes 1572872 | tf_op jit(solution)/shard_map/ppermute | solution.py:353
  72.7 13.5 %collective-permute-start.14 = (bf16[2,128,1024]{2,1,0:T(8,128)(2,1)S(1)}, bf16[2,128,1024]{2,1,0:T(8,128)(2,1)S(1)}, u32[]{:S(2)}, u32[]{:S(2)}) collective-permute-start(bf16[2,128,1024]{2,1,0:T(8,128)(2,1)S(1)} %get-tuple-element.59), channel_id=1, source_target_pairs={{0,0},{1,2},{2,1},{3,3},{4,4},{5,6},{6,5},{7,7},{8,8},{9,10},{10,9... | collective-permute-start | bytes 1572872 | tf_op jit(solution)/shard_map/ppermute | solution.py:353

commit v6 on v5

--- a/solution.py
+++ b/solution.py
@@ -231,14 +231,14 @@
     g_out[heads * rows :] = split(d_out[...])
 
 
-def grads_kernel(count, first, scale, q_ref, kv_ref, left_k, left_v, right_q, g_ref, right_g, segs,
-                 own_stats, far_stats, from_left, from_right, delta_own,
-                 dq_out, dkv_out, p_out, to1, to2, far_delta):
+def left_kernel(count, first, scale, q_ref, left_k, left_v, right_q, g_ref, right_g, segs,
+                own_stats, far_stats, from_left, from_right, delta_own,
+                p_out, ds_out, far_delta, to1, to2):
     index = lax.axis_index("seq")
     rows, span = left_v.shape
     heads = span // HEAD_DIM
     chosen = slice(first // HEAD_DIM, first // HEAD_DIM + heads)
-    pre, far, own, nxt = masks(count, segs, index, rows)
+    pre, far, _, _ = masks(count, segs, index, rows)
     top, inv, share = own_rows(index, own_stats, from_left, chosen)
     r_top, r_inv, r_share = right_rows(index, count, far_stats, from_right, chosen)
     own_delta = delta_own[...] * share
@@ -248,39 +248,27 @@
         for h in range(heads):
             at = slice(h * HEAD_DIM, (h + 1) * HEAD_DIM)
             wide = slice(first + at.start, first + at.stop)
+            block = slice(h * rows, (h + 1) * rows)
             row = slice(h, h + 1)
             q2 = jnp.concatenate([q_ref[0, :, wide], right_q[:, wide]], axis=0)
-            block = slice(h * rows, (h + 1) * rows)
             g2 = jnp.concatenate([g_ref[block], right_g[block]], axis=0)
-            k, kl = kv_ref[0, 0, :, wide], left_k[:, wide]
+            kl = left_k[:, wide]
             s_left = lax.dot_general(kl, q2, NT, preferred_element_type=F32) * scale
-            s_here = lax.dot_general(k, q2, NT, preferred_element_type=F32) * scale
             d_left = lax.dot_general(left_v[:, at], g2, NT, preferred_element_type=F32)
-            d_own = lax.dot_general(kv_ref[1, 0, :, wide], g2[:rows], NT, preferred_element_type=F32)
             p_pre = jnp.exp(jnp.where(pre, s_left[:, :rows], NEG) - top[row]) * inv[row]
-            p_own = jnp.exp(jnp.where(own, s_here[:, :rows], NEG) - top[row]) * inv[row]
             p_far = jnp.exp(jnp.where(far, s_left[:, rows:], NEG) - r_top[row]) * r_inv[row]
-            p_nxt = jnp.exp(jnp.where(nxt, s_here[:, rows:], NEG) - r_top[row]) * r_inv[row]
             d_pre, d_far = d_left[:, :rows], d_left[:, rows:]
             extra = jnp.sum(p_far * d_far, axis=0, keepdims=True)
             far_delta[row] = extra
             ds_pre = (p_pre * (d_pre - own_delta[row]) * scale).astype(BF16)
-            ds_own = (p_own * (d_own - own_delta[row]) * scale).astype(BF16)
             ds_far = (p_far * (d_far - (right_delta[row] + extra)) * scale).astype(BF16)
-            ds_nxt = (p_nxt * (extra * -scale)).astype(BF16)
             p_low = p_pre.astype(BF16)
-            p_here = p_own.astype(BF16)
-            p_out[h, :rows] = p_low
-            p_out[h, rows:] = p_here
-            dkv_out[0, :, at] = jnp.dot(
-                jnp.concatenate([ds_own, ds_nxt], axis=1), q2, preferred_element_type=F32)
-            dkv_out[1, :, at] = jnp.dot(p_here, g2[:rows], preferred_element_type=F32)
+            p_out[h] = p_low
+            ds_out[h] = ds_pre
             down_out[0, :, at] = jnp.dot(
                 jnp.concatenate([ds_pre, ds_far], axis=1), q2, preferred_element_type=F32).astype(BF16)
             down_out[1, :, at] = jnp.dot(
                 jnp.concatenate([p_low, p_far.astype(BF16)], axis=1), g2, preferred_element_type=F32).astype(BF16)
-            dq_out[:, at] = lax.dot_general(ds_pre, kl, TN, preferred_element_type=F32) + lax.dot_general(
-                ds_own, k, TN, preferred_element_type=F32)
             up_out[0, :, at] = lax.dot_general(ds_far, kl, TN, preferred_element_type=F32).astype(BF16)
         up_out[1, : 2 * heads, :LANES] = split(far_delta[...])
 
@@ -293,10 +281,41 @@
         run(to2, to1)
 
 
-def finish_kernel(count, first, scale, dq_ref, dkv_ref, p_ref, q_ref, kv_ref, left_k, got1, got2, *refs):
+def own_kernel(count, first, scale, q_ref, kv_ref, left_k, right_q, g_ref, segs,
+               own_stats, far_stats, from_left, from_right, delta_own, ds_left, far_delta,
+               dq_out, dkv_out, p_out):
+    index = lax.axis_index("seq")
+    rows, span = dq_out.shape
+    heads = span // HEAD_DIM
+    chosen = slice(first // HEAD_DIM, first // HEAD_DIM + heads)
+    _, _, own, nxt = masks(count, segs, index, rows)
+    top, inv, share = own_rows(index, own_stats, from_left, chosen)
+    r_top, r_inv, _ = right_rows(index, count, far_stats, from_right, chosen)
+    own_delta = delta_own[...] * share
+    for h in range(heads):
+        at = slice(h * HEAD_DIM, (h + 1) * HEAD_DIM)
+        wide = slice(first + at.start, first + at.stop)
+        row = slice(h, h + 1)
+        q2 = jnp.concatenate([q_ref[0, :, wide], right_q[:, wide]], axis=0)
+        g, k = g_ref[h * rows : (h + 1) * rows], kv_ref[0, 0, :, wide]
+        s_here = lax.dot_general(k, q2, NT, preferred_element_type=F32) * scale
+        d_own = lax.dot_general(kv_ref[1, 0, :, wide], g, NT, preferred_element_type=F32)
+        p_own = jnp.exp(jnp.where(own, s_here[:, :rows], NEG) - top[row]) * inv[row]
+        p_nxt = jnp.exp(jnp.where(nxt, s_here[:, rows:], NEG) - r_top[row]) * r_inv[row]
+        ds_own = (p_own * (d_own - own_delta[row]) * scale).astype(BF16)
+        ds_nxt = (p_nxt * (far_delta[row] * -scale)).astype(BF16)
+        p_low = p_own.astype(BF16)
+        p_out[h] = p_low
+        dkv_out[0, :, at] = jnp.dot(jnp.concatenate([ds_own, ds_nxt], axis=1), q2, preferred_element_type=F32)
+        dkv_out[1, :, at] = jnp.dot(p_low, g, preferred_element_type=F32)
+        dq_out[:, at] = lax.dot_general(ds_left[h], left_k[:, wide], TN, preferred_element_type=F32) + lax.dot_general(
+            ds_own, k, TN, preferred_element_type=F32)
+
+
+def finish_kernel(count, first, scale, dq_ref, dkv_ref, p_own, p_left, q_ref, kv_ref, left_k, got1, got2, *refs):
     grad_q, grad_kv, done, sem = refs[-4:]
     index = lax.axis_index("seq")
-    rows, span = dq_ref.shape
+    _, span = dq_ref.shape
     heads = span // HEAD_DIM
 
     lanes = slice(first, first + span)
@@ -315,8 +334,8 @@
             at = slice(h * HEAD_DIM, (h + 1) * HEAD_DIM)
             wide = slice(first + at.start, first + at.stop)
             factor = delta[h : h + 1] * -scale
-            ds_pre = (p_ref[h, :rows].astype(F32) * factor).astype(BF16)
-            ds_own = (p_ref[h, rows:].astype(F32) * factor).astype(BF16)
+            ds_pre = (p_left[h].astype(F32) * factor).astype(BF16)
+            ds_own = (p_own[h].astype(F32) * factor).astype(BF16)
             dq = dq_ref[:, at] + jnp.where(no_left, 0.0, from_left[0, :, at].astype(F32))
             dq = dq + lax.dot_general(ds_pre, left_k[:, wide], TN, preferred_element_type=F32)
             dq = dq + lax.dot_general(ds_own, kv_ref[0, 0, :, wide], TN, preferred_element_type=F32)
@@ -441,15 +460,21 @@
     for c, (first, span) in enumerate(chunks(hc)):
         heads, half = span // HEAD_DIM, shape((2, rows, span))
         gout, delta, right_g = pieces[c]
-        *kept, to1, to2 = pl.pallas_call(
-            functools.partial(grads_kernel, count, first, scale),
-            out_shape=[
-                shape((rows, span), F32), shape((2, rows, span), F32), shape((heads, 2 * rows, rows)), half, half],
-            scratch_shapes=[pltpu.VMEM((heads, rows), F32)],
+        square, table = shape((heads, rows, rows)), (own, far, from_left, from_right, delta)
+        p_left, ds_left, far_delta, to1, to2 = pl.pallas_call(
+            functools.partial(left_kernel, count, first, scale),
+            out_shape=[square, square, shape((heads, rows), F32), half, half],
             compiler_params=params(12),
-            cost_estimate=cost(10 * 3 * rows * rows * span, 40 * rows * span),
-        )(query, key_value, left_k, values[c], right_q, gout, right_g, segments, own, far, from_left, from_right, delta)
-        parts.append((*kept, query, key_value, left_k, *neighbour_swaps(to1, to2)))
+            cost_estimate=cost(10 * 2 * rows * rows * span, 30 * rows * span),
+        )(query, left_k, values[c], right_q, gout, right_g, segments, *table)
+        got = neighbour_swaps(to1, to2)
+        kept = pl.pallas_call(
+            functools.partial(own_kernel, count, first, scale),
+            out_shape=[shape((rows, span), F32), shape((2, rows, span), F32), square],
+            compiler_params=params(12),
+            cost_estimate=cost(10 * 2 * rows * rows * span, 30 * rows * span),
+        )(query, key_value, left_k, right_q, gout, segments, *table, ds_left, far_delta)
+        parts.append((*kept, p_left, query, key_value, left_k, *got))
 
     results = ()
     anywhere = pl.BlockSpec(memory_space=pl.ANY)

time: 88.7 us -> 88.2 us (level)
  waiting for transfers between devices: 25.8 us -> 22.6 us
  Pallas kernels: 17.4 us -> 20.1 us
    ppermute x6, waiting for transfers between devices: 11.5 us -> 8.28 us  [neighbour_swaps(): return (lax.ppermute(first, 'seq', one), lax.ppermute(second, 'seq', two))]
    pallas_call x2 -> x4, Pallas kernels: 5.91 us -> 8.59 us  [the longest x2 4.86 us: step(): pl.pallas_call(functools.partial(left_kernel, count, first, scale), out_s...]
  transfers between devices with their start and end apart: 22 -> 22, of which waited for: 7 -> 7; matrix products, arithmetic and copies ran while one was open for 0% -> 0% of each run, Pallas kernels for 18% -> 21%
where the time goes in v6:
time: 88.2 us; the launch traced here: 87.3 us
  starting transfers between devices  43.6 us (49%)
  waiting for transfers between devices  22.6 us (26%)
  Pallas kernels  20.1 us (23%)
  between operations  1.02 us (1%)
    ppermute x6, starting transfers between devices, passed(): lax.ppermute(value, 'seq', [(i, i + steps) for i in range(first, last)])  18.8 us
    ppermute x10, starting transfers between devices, swap(): lax.ppermute(value, axis, [(i, i ^ bits) for i in range(lax.axis_size(axi...  17.2 us
    ppermute x10, waiting for transfers between devices, swap(): lax.ppermute(value, axis, [(i, i ^ bits) for i in range(lax.axis_size(axi...  9.66 us
    ppermute x6, waiting for transfers between devices, neighbour_swaps(): return (lax.ppermute(first, 'seq', one), lax.ppermute(second, 'seq', two))  8.28 us
    ppermute x6, starting transfers between devices, neighbour_swaps(): return (lax.ppermute(first, 'seq', one), lax.ppermute(second, 'seq', two))  7.56 us
    pallas_call x2, Pallas kernels, step(): pl.pallas_call(functools.partial(left_kernel, count, first, scale), out_s...  4.86 us
    ppermute x6, waiting for transfers between devices, passed(): lax.ppermute(value, 'seq', [(i, i + steps) for i in range(first, last)])  4.66 us
    pallas_call x2, Pallas kernels, step(): pl.pallas_call(functools.partial(own_kernel, count, first, scale), out_sh...  3.73 us
  transfers between devices with their start and end apart: 22, of which 7 were waited for; matrix products, arithmetic and copies ran while one was open for 0% of the time, Pallas kernels for 21%

profile of v6, /device:TPU:0, one launch (start us, length us, event | category | flops | bytes accessed | tf_op | source)
XLA Modules:
  0.0 87.3 jit_solution(10303289522474766661)
XLA Ops:
  0.6 0.6 collective-permute-start.5
  1.2 1.2 %grad_slices.1 = (bf16[528,128]{1,0:T(8,128)(2,1)S(1)}, bf16[528,128]{1,0:T(8,128)(2,1)S(1)}, bf16[528,128]{1,0:T(8,128)(2,1)S(1)}, bf16[528,128]{1,0:T(8,128)(2,1)S(1)}) custom-call(bf16[1,128,2048]{2,1,0:T(8,128)(2,1)} %grad_ref.1, s32[1,128]{1,0:T(1,128)} %tags_ref.1), custom_call_target="tpu_custom_call" | custom-call | bytes 1048576 | tf_op jit(solution)/shard_map/grad_slices/pallas_call | solution.py:402
  2.4 2.6 %collective-permute-start.2 = (bf16[528,128]{1,0:T(8,128)(2,1)S(1)}, bf16[528,128]{1,0:T(8,128)(2,1)S(1)}, u32[]{:S(2)}, u32[]{:S(2)}) collective-permute-start(bf16[528,128]{1,0:T(8,128)(2,1)S(1)} %get-tuple-element.49), channel_id=1, source_target_pairs={{0,8},{4,12},{8,0},{12,4},{16,24},{20,28},{24,16},{28,20},{1,9},{5... | collective-permute-start | bytes 405512 | tf_op jit(solution)/shard_map/ppermute | solution.py:32
  5.1 1.4 %side_slices.1 = (bf16[128,2048]{1,0:T(8,128)(2,1)S(1)}, bf16[128,2048]{1,0:T(8,128)(2,1)S(1)}, bf16[128,1024]{1,0:T(8,128)(2,1)S(1)}, bf16[128,1024]{1,0:T(8,128)(2,1)S(1)}) custom-call(bf16[1,128,2048]{2,1,0:T(8,128)(2,1)} %q_ref.15, bf16[2,1,128,2048]{3,2,1,0:T(8,128)(2,1)} %kv_ref.11), custom_call_target="tpu_custom_call" | custom-call | bytes 3145728 | tf_op jit(solution)/shard_map/side_slices/pallas_call | solution.py:413
  6.5 1.6 %collective-permute-start = (bf16[128,2048]{1,0:T(8,128)(2,1)S(1)}, bf16[128,2048]{1,0:T(8,128)(2,1)S(1)}, u32[]{:S(2)}, u32[]{:S(2)}) collective-permute-start(bf16[128,2048]{1,0:T(8,128)(2,1)S(1)} %get-tuple-element.44), channel_id=1, source_target_pairs={{0,1},{1,0},{2,3},{3,2},{4,5},{5,4},{6,7},{7,6},{8,9},{9,8},{10,11... | collective-permute-start | bytes 1572872 | tf_op jit(solution)/shard_map/ppermute | solution.py:372
  8.1 0.7 collective-permute-start.1
  8.8 1.6 %collective-permute-start.3 = (bf16[528,128]{1,0:T(8,128)(2,1)S(1)}, bf16[528,128]{1,0:T(8,128)(2,1)S(1)}, u32[]{:S(2)}, u32[]{:S(2)}) collective-permute-start(bf16[528,128]{1,0:T(8,128)(2,1)S(1)} %get-tuple-element.50), channel_id=1, source_target_pairs={{0,16},{4,20},{8,24},{12,28},{16,0},{20,4},{24,8},{28,12},{1,17},{... | collective-permute-start | bytes 405512 | tf_op jit(solution)/shard_map/ppermute | solution.py:32
  10.4 0.0 collective-permute-done.2.refs_1_
  10.4 1.5 %collective-permute-start.4 = (bf16[528,128]{1,0:T(8,128)(2,1)S(1)}, bf16[528,128]{1,0:T(8,128)(2,1)S(1)}, u32[]{:S(2)}, u32[]{:S(2)}) collective-permute-start(bf16[528,128]{1,0:T(8,128)(2,1)S(1)} %get-tuple-element.51), channel_id=1, source_target_pairs={{0,24},{4,28},{8,16},{12,20},{16,8},{20,12},{24,0},{28,4},{1,25},{... | collective-permute-start | bytes 405512 | tf_op jit(solution)/shard_map/ppermute | solution.py:32
  11.9 5.2 %collective-permute-done.3.refs_2_ = bf16[528,128]{1,0:T(8,128)(2,1)S(1)} collective-permute-done((bf16[528,128]{1,0:T(8,128)(2,1)S(1)}, bf16[528,128]{1,0:T(8,128)(2,1)S(1)}, u32[]{:S(2)}, u32[]{:S(2)}) %collective-permute-start.3) | collective-permute-done | bytes 135200 | tf_op jit(solution)/shard_map/ppermute | solution.py:32
  17.0 6.0 %collective-permute-start.18 = (bf16[128,1024]{1,0:T(8,128)(2,1)S(1)}, bf16[128,1024]{1,0:T(8,128)(2,1)S(1)}, u32[]{:S(2)}, u32[]{:S(2)}) collective-permute-start(bf16[128,1024]{1,0:T(8,128)(2,1)S(1)} %get-tuple-element.73), channel_id=1, source_target_pairs={{0,1},{1,2},{2,3},{4,5},{5,6},{6,7},{8,9},{9,10},{10,11},{12,13},{... | collective-permute-start | bytes 786440 | tf_op jit(solution)/shard_map/ppermute | solution.py:364
  23.1 0.0 collective-permute-done.5.refs_5_
  23.1 1.4 %shard_map.81 = (f32[128,1024]{1,0:T(8,128)S(1)}, bf16[128,1024]{1,0:T(8,128)(2,1)S(1)}, bf16[128,1024]{1,0:T(8,128)(2,1)S(1)}, bf16[128,1024]{1,0:T(8,128)(2,1)S(1)}) custom-call(bf16[528,128]{1,0:T(8,128)(2,1)S(1)} %get-tuple-element.48.refs_0_, bf16[528,128]{1,0:T(8,128)(2,1)S(1)} %collective-permute-done.2.refs_1_, ...), custom_call_target="tpu_custom_call" | custom-call | flops 1073741824 | bytes 2097152 | tf_op jit(solution)/shard_map/pallas_call | solution.py:429
  24.5 0.6 collective-permute-start.15
  25.1 1.5 %collective-permute-start.16 = (bf16[128,1024]{1,0:T(8,128)(2,1)S(1)}, bf16[128,1024]{1,0:T(8,128)(2,1)S(1)}, u32[]{:S(2)}, u32[]{:S(2)}) collective-permute-start(bf16[128,1024]{1,0:T(8,128)(2,1)S(1)} %get-tuple-element.71), channel_id=1, source_target_pairs={{0,16},{4,20},{8,24},{12,28},{16,0},{20,4},{24,8},{28,12},{1,17},{... | collective-permute-start | bytes 786440 | tf_op jit(solution)/shard_map/ppermute | solution.py:32
  26.6 0.3 collective-permute-done.18.refs_6_.left_v
  26.9 2.2 %collective-permute-start.17 = (bf16[128,1024]{1,0:T(8,128)(2,1)S(1)}, bf16[128,1024]{1,0:T(8,128)(2,1)S(1)}, u32[]{:S(2)}, u32[]{:S(2)}) collective-permute-start(bf16[128,1024]{1,0:T(8,128)(2,1)S(1)} %get-tuple-element.72), channel_id=1, source_target_pairs={{0,24},{4,28},{8,16},{12,20},{16,8},{20,12},{24,0},{28,4},{1,25},{... | collective-permute-start | bytes 786440 | tf_op jit(solution)/shard_map/ppermute | solution.py:32
  29.1 1.4 %shard_map.77 = (f32[128,1024]{1,0:T(8,128)S(1)}, bf16[128,1024]{1,0:T(8,128)(2,1)S(1)}, bf16[128,1024]{1,0:T(8,128)(2,1)S(1)}, bf16[128,1024]{1,0:T(8,128)(2,1)S(1)}) custom-call(bf16[528,128]{1,0:T(8,128)(2,1)S(1)} %get-tuple-element.48.refs_0_, bf16[528,128]{1,0:T(8,128)(2,1)S(1)} %collective-permute-done.2.refs_1_, ...), custom_call_target="tpu_custom_call" | custom-call | flops 1073741824 | bytes 2097152 | tf_op jit(solution)/shard_map/pallas_call | solution.py:429
  30.5 4.4 %collective-permute-start.9 = (bf16[128,1024]{1,0:T(8,128)(2,1)S(1)}, bf16[128,1024]{1,0:T(8,128)(2,1)S(1)}, u32[]{:S(2)}, u32[]{:S(2)}) collective-permute-start(bf16[128,1024]{1,0:T(8,128)(2,1)S(1)} %get-tuple-element.56), channel_id=1, source_target_pairs={{0,1},{1,2},{2,3},{4,5},{5,6},{6,7},{8,9},{9,10},{10,11},{12,13},{... | collective-permute-start | bytes 786440 | tf_op jit(solution)/shard_map/ppermute | solution.py:364
  34.9 0.0 collective-permute-done.1.got2
  34.9 1.6 %collective-permute-start.6 = (bf16[128,1024]{1,0:T(8,128)(2,1)S(1)}, bf16[128,1024]{1,0:T(8,128)(2,1)S(1)}, u32[]{:S(2)}, u32[]{:S(2)}) collective-permute-start(bf16[128,1024]{1,0:T(8,128)(2,1)S(1)} %get-tuple-element.53), channel_id=1, source_target_pairs={{0,8},{4,12},{8,0},{12,4},{16,24},{20,28},{24,16},{28,20},{1,9},{5... | collective-permute-start | bytes 786440 | tf_op jit(solution)/shard_map/ppermute | solution.py:32
  36.5 0.0 collective-permute-done.15.refs_0_
  36.5 0.3 collective-permute-start.7
  36.8 0.0 collective-permute-done.16.refs_1_
  36.8 4.8 %collective-permute-start.8 = (bf16[128,1024]{1,0:T(8,128)(2,1)S(1)}, bf16[128,1024]{1,0:T(8,128)(2,1)S(1)}, u32[]{:S(2)}, u32[]{:S(2)}) collective-permute-start(bf16[128,1024]{1,0:T(8,128)(2,1)S(1)} %get-tuple-element.55), channel_id=1, source_target_pairs={{0,24},{4,28},{8,16},{12,20},{16,8},{20,12},{24,0},{28,4},{1,25},{... | collective-permute-start | bytes 786440 | tf_op jit(solution)/shard_map/ppermute | solution.py:32
  41.6 1.5 %stats.1 = (f32[2,16,128]{2,1,0:T(8,128)S(1)}, f32[2,16,128]{2,1,0:T(8,128)S(1)}, bf16[128,2048]{1,0:T(8,128)(2,1)S(1)}, bf16[128,2048]{1,0:T(8,128)(2,1)S(1)}) custom-call(bf16[1,128,2048]{2,1,0:T(8,128)(2,1)S(1)} %copy-done.1, bf16[2,1,128,2048]{3,2,1,0:T(8,128)(2,1)S(1)} %copy-done, bf16[128,2048]{1,0:T(8,128)(2,1)S(1)} %collective-permute-done.got1, ...), custom_call_target="tpu_custom_call" | custom-call | flops 201326592 | bytes 5242880 | tf_op jit(solution)/shard_map/stats/pallas_call | solution.py:439
  43.1 0.0 collective-permute-done.17.refs_2_
  43.1 0.9 %shard_map.82 = (bf16[1040,128]{1,0:T(8,128)(2,1)S(1)}, f32[8,128]{1,0:T(8,128)S(1)}) custom-call(f32[128,1024]{1,0:T(8,128)S(1)} %get-tuple-element.69.mine, bf16[128,1024]{1,0:T(8,128)(2,1)S(1)} %collective-permute-done.15.refs_0_, bf16[128,1024]{1,0:T(8,128)(2,1)S(1)} %collective-permute-done.16.refs_1_, ...), custom_call_target="tpu_custom_call" | custom-call | flops 134217728 | bytes 2621440 | tf_op jit(solution)/shard_map/pallas_call | solution.py:451
  44.0 1.3 %collective-permute-start.19 = (bf16[1040,128]{1,0:T(8,128)(2,1)S(1)}, bf16[1040,128]{1,0:T(8,128)(2,1)S(1)}, u32[]{:S(2)}, u32[]{:S(2)}) collective-permute-start(bf16[1040,128]{1,0:T(8,128)(2,1)S(1)} %get-tuple-element.74.g_ref), channel_id=1, source_target_pairs={{1,0},{2,1},{3,2},{5,4},{6,5},{7,6},{9,8},{10,9},{11,10},{13,12},{... | collective-permute-start | bytes 798728 | tf_op jit(solution)/shard_map/ppermute | solution.py:364
  45.3 4.5 %collective-permute-done.7.refs_1_ = bf16[128,1024]{1,0:T(8,128)(2,1)S(1)} collective-permute-done((bf16[128,1024]{1,0:T(8,128)(2,1)S(1)}, bf16[128,1024]{1,0:T(8,128)(2,1)S(1)}, u32[]{:S(2)}, u32[]{:S(2)}) %collective-permute-start.7) | collective-permute-done | bytes 262176 | tf_op jit(solution)/shard_map/ppermute | solution.py:32
  49.8 0.9 %shard_map.78 = (bf16[1040,128]{1,0:T(8,128)(2,1)S(1)}, f32[8,128]{1,0:T(8,128)S(1)}) custom-call(f32[128,1024]{1,0:T(8,128)S(1)} %get-tuple-element.52.mine, bf16[128,1024]{1,0:T(8,128)(2,1)S(1)} %collective-permute-done.6.refs_0_, bf16[128,1024]{1,0:T(8,128)(2,1)S(1)} %collective-permute-done.7.refs_1_, ...), custom_call_target="tpu_custom_call" | custom-call | flops 134217728 | bytes 2621440 | tf_op jit(solution)/shard_map/pallas_call | solution.py:451
  50.7 1.3 %collective-permute-start.12 = (bf16[1040,128]{1,0:T(8,128)(2,1)S(1)}, bf16[1040,128]{1,0:T(8,128)(2,1)S(1)}, u32[]{:S(2)}, u32[]{:S(2)}) collective-permute-start(bf16[1040,128]{1,0:T(8,128)(2,1)S(1)} %get-tuple-element.58.g_ref), channel_id=1, source_target_pairs={{1,0},{2,1},{3,2},{5,4},{6,5},{7,6},{9,8},{10,9},{11,10},{13,12},{... | collective-permute-start | bytes 798728 | tf_op jit(solution)/shard_map/ppermute | solution.py:364
  52.0 4.5 %collective-permute-start.10 = (f32[2,16,128]{2,1,0:T(8,128)S(1)}, f32[2,16,128]{2,1,0:T(8,128)S(1)}, u32[]{:S(2)}, u32[]{:S(2)}) collective-permute-start(f32[2,16,128]{2,1,0:T(8,128)S(1)} %get-tuple-element.59.far_stats), channel_id=1, source_target_pairs={{0,1},{1,2},{2,3},{4,5},{5,6},{6,7},{8,9},{9,10},{10,11},{12,13},{... | collective-permute-start | bytes 49160 | tf_op jit(solution)/shard_map/ppermute | solution.py:364
  56.6 1.3 %collective-permute-start.11 = (f32[2,16,128]{2,1,0:T(8,128)S(1)}, f32[2,16,128]{2,1,0:T(8,128)S(1)}, u32[]{:S(2)}, u32[]{:S(2)}) collective-permute-start(f32[2,16,128]{2,1,0:T(8,128)S(1)} %get-tuple-element.57.refs_8_.own_stats), channel_id=1, source_target_pairs={{1,0},{2,1},{3,2},{5,4},{6,5},{7,6},{9,8},{10,9},{11,10},{13,12},{... | collective-permute-start | bytes 49160 | tf_op jit(solution)/shard_map/ppermute | solution.py:364
  57.9 0.1 collective-permute-done.10.from_left
  58.0 4.2 %collective-permute-done.11.from_right = f32[2,16,128]{2,1,0:T(8,128)S(1)} collective-permute-done((f32[2,16,128]{2,1,0:T(8,128)S(1)}, f32[2,16,128]{2,1,0:T(8,128)S(1)}, u32[]{:S(2)}, u32[]{:S(2)}) %collective-permute-start.11) | collective-permute-done | bytes 16416 | tf_op jit(solution)/shard_map/ppermute | solution.py:364
  62.2 2.3 %shard_map.83 = (bf16[8,128,128]{2,1,0:T(8,128)(2,1)S(1)}, bf16[8,128,128]{2,1,0:T(8,128)(2,1)S(1)}, f32[8,128]{1,0:T(8,128)S(1)}, bf16[2,128,1024]{2,1,0:T(8,128)(2,1)S(1)}, bf16[2,128,1024]{2,1,0:T(8,128)(2,1)S(1)}) custom-call(bf16[1,128,2048]{2,1,0:T(8,128)(2,1)S(1)} %copy-done.1, bf16[128,2048]{1,0:T(8,128)(2,1)S(1)} %get-tuple-element.46.refs_5_.left_k, ...), custom_call_target="tpu_custom_call" | custom-call | flops 335544320 | bytes 3932160 | tf_op jit(solution)/shard_map/pallas_call | solution.py:464
  64.5 1.0 %collective-permute-start.20 = (bf16[2,128,1024]{2,1,0:T(8,128)(2,1)S(1)}, bf16[2,128,1024]{2,1,0:T(8,128)(2,1)S(1)}, u32[]{:S(2)}, u32[]{:S(2)}) collective-permute-start(bf16[2,128,1024]{2,1,0:T(8,128)(2,1)S(1)} %get-tuple-element.82), channel_id=1, source_target_pairs={{0,1},{1,0},{2,3},{3,2},{4,5},{5,4},{6,7},{7,6},{8,9},{9,8},{10,11... | collective-permute-start | bytes 1572872 | tf_op jit(solution)/shard_map/ppermute | solution.py:372
  65.5 0.7 collective-permute-start.21
  66.2 2.5 %shard_map.79 = (bf16[8,128,128]{2,1,0:T(8,128)(2,1)S(1)}, bf16[8,128,128]{2,1,0:T(8,128)(2,1)S(1)}, f32[8,128]{1,0:T(8,128)S(1)}, bf16[2,128,1024]{2,1,0:T(8,128)(2,1)S(1)}, bf16[2,128,1024]{2,1,0:T(8,128)(2,1)S(1)}) custom-call(bf16[1,128,2048]{2,1,0:T(8,128)(2,1)S(1)} %copy-done.1, bf16[128,2048]{1,0:T(8,128)(2,1)S(1)} %get-tuple-element.46.refs_5_.left_k, ...), custom_call_target="tpu_custom_call" | custom-call | flops 335544320 | bytes 3932160 | tf_op jit(solution)/shard_map/pallas_call | solution.py:464
  68.7 2.9 %collective-permute-start.13 = (bf16[2,128,1024]{2,1,0:T(8,128)(2,1)S(1)}, bf16[2,128,1024]{2,1,0:T(8,128)(2,1)S(1)}, u32[]{:S(2)}, u32[]{:S(2)}) collective-permute-start(bf16[2,128,1024]{2,1,0:T(8,128)(2,1)S(1)} %get-tuple-element.67), channel_id=1, source_target_pairs={{0,1},{1,0},{2,3},{3,2},{4,5},{5,4},{6,7},{7,6},{8,9},{9,8},{10,11... | collective-permute-start | bytes 1572872 | tf_op jit(solution)/shard_map/ppermute | solution.py:372
  71.6 0.7 collective-permute-start.14
  72.3 1.9 %shard_map.80 = (f32[128,1024]{1,0:T(8,128)S(1)}, f32[2,128,1024]{2,1,0:T(8,128)S(1)}, bf16[8,128,128]{2,1,0:T(8,128)(2,1)S(1)}) custom-call(bf16[1,128,2048]{2,1,0:T(8,128)(2,1)S(1)} %copy-done.1, bf16[2,1,128,2048]{3,2,1,0:T(8,128)(2,1)S(1)} %copy-done, bf16[128,2048]{1,0:T(8,128)(2,1)S(1)} %get-tuple-element.46.refs_5_.left_k, ...), custom_call_target="tpu_custom_call" | custom-call | flops 335544320 | bytes 3932160 | tf_op jit(solution)/shard_map/pallas_call | solution.py:471
  74.2 1.9 %shard_map.84 = (f32[128,1024]{1,0:T(8,128)S(1)}, f32[2,128,1024]{2,1,0:T(8,128)S(1)}, bf16[8,128,128]{2,1,0:T(8,128)(2,1)S(1)}) custom-call(bf16[1,128,2048]{2,1,0:T(8,128)(2,1)S(1)} %copy-done.1, bf16[2,1,128,2048]{3,2,1,0:T(8,128)(2,1)S(1)} %copy-done, bf16[128,2048]{1,0:T(8,128)(2,1)S(1)} %get-tuple-element.46.refs_5_.left_k, ...), custom_call_target="tpu_custom_call" | custom-call | flops 335544320 | bytes 3932160 | tf_op jit(solution)/shard_map/pallas_call | solution.py:471
  76.1 3.3 %collective-permute-done.20.got1 = bf16[2,128,1024]{2,1,0:T(8,128)(2,1)S(1)} collective-permute-done((bf16[2,128,1024]{2,1,0:T(8,128)(2,1)S(1)}, bf16[2,128,1024]{2,1,0:T(8,128)(2,1)S(1)}, u32[]{:S(2)}, u32[]{:S(2)}) %collective-permute-start.20) | collective-permute-done | bytes 524320 | tf_op jit(solution)/shard_map/ppermute | solution.py:372
  79.4 1.4 %shard_map.85 = (bf16[1,128,2048]{2,1,0:T(8,128)(2,1)}, bf16[2,1,128,2048]{3,2,1,0:T(8,128)(2,1)}) custom-call(f32[128,1024]{1,0:T(8,128)S(1)} %get-tuple-element.78.dq_ref, f32[2,128,1024]{2,1,0:T(8,128)S(1)} %get-tuple-element.79.dkv_ref, bf16[8,128,128]{2,1,0:T(8,128)(2,1)S(1)} %get-tuple-element.80.p_own, ...), custom_call_target="tpu_custom_call" | custom-call | bytes 2621440 | tf_op jit(solution)/shard_map/pallas_call | solution.py:482
  80.8 4.9 %collective-permute-done.13.got1 = bf16[2,128,1024]{2,1,0:T(8,128)(2,1)S(1)} collective-permute-done((bf16[2,128,1024]{2,1,0:T(8,128)(2,1)S(1)}, bf16[2,128,1024]{2,1,0:T(8,128)(2,1)S(1)}, u32[]{:S(2)}, u32[]{:S(2)}) %collective-permute-start.13) | collective-permute-done | bytes 524320 | tf_op jit(solution)/shard_map/ppermute | solution.py:372
  85.7 1.4 %shard_map.86 = (bf16[1,128,2048]{2,1,0:T(8,128)(2,1)}, bf16[2,1,128,2048]{3,2,1,0:T(8,128)(2,1)}) custom-call(f32[128,1024]{1,0:T(8,128)S(1)} %get-tuple-element.63.dq_ref, f32[2,128,1024]{2,1,0:T(8,128)S(1)} %get-tuple-element.64.dkv_ref, bf16[8,128,128]{2,1,0:T(8,128)(2,1)S(1)} %get-tuple-element.65.p_own, ...), custom_call_target="tpu_custom_call", output_to_operand_aliasing={{0}: (9, {}), {1}: (10, {})} | custom-call | bytes 2621440 | tf_op jit(solution)/shard_map/pallas_call | solution.py:482
  (17 shorter events, 0.0 us)
Async XLA Ops:
  0.6 22.4 %copy-start.2 = (bf16[2,2048,256]{2,1,0:T(8,128)(2,1)S(1)}, bf16[2,2048,256]{2,1,0:T(8,128)(2,1)}, u32[]{:S(2)}) copy-start(bf16[2,2048,256]{2,1,0:T(8,128)(2,1)} %refs_4_.6) | copy-start | bytes 6291460
  0.6 22.4 %collective-permute-start.5 = (bf16[2,2048,256]{2,1,0:T(8,128)(2,1)}, bf16[2,2048,256]{2,1,0:T(8,128)(2,1)S(1)}, u32[]{:S(2)}, u32[]{:S(2)}) collective-permute-start(bf16[2,2048,256]{2,1,0:T(8,128)(2,1)} %refs_4_.6), channel_id=1, source_target_pairs={{0,4},{4,0},{8,12},{12,8},{16,20},{20,16},{24,28},{28,24},{1,5},{5... | collective-permute-start | bytes 6291464 | tf_op jit(solution)/shard_map/ppermute | solution.py:32
  2.4 7.9 %collective-permute-start.2 = (bf16[528,128]{1,0:T(8,128)(2,1)S(1)}, bf16[528,128]{1,0:T(8,128)(2,1)S(1)}, u32[]{:S(2)}, u32[]{:S(2)}) collective-permute-start(bf16[528,128]{1,0:T(8,128)(2,1)S(1)} %get-tuple-element.49), channel_id=1, source_target_pairs={{0,8},{4,12},{8,0},{12,4},{16,24},{20,28},{24,16},{28,20},{1,9},{5... | collective-permute-start | bytes 405512 | tf_op jit(solution)/shard_map/ppermute | solution.py:32
  6.5 24.1 %collective-permute-start = (bf16[128,2048]{1,0:T(8,128)(2,1)S(1)}, bf16[128,2048]{1,0:T(8,128)(2,1)S(1)}, u32[]{:S(2)}, u32[]{:S(2)}) collective-permute-start(bf16[128,2048]{1,0:T(8,128)(2,1)S(1)} %get-tuple-element.44), channel_id=1, source_target_pairs={{0,1},{1,0},{2,3},{3,2},{4,5},{5,4},{6,7},{7,6},{8,9},{9,8},{10,11... | collective-permute-start | bytes 1572872 | tf_op jit(solution)/shard_map/ppermute | solution.py:372
  8.1 26.8 %collective-permute-start.1 = (bf16[128,2048]{1,0:T(8,128)(2,1)S(1)}, bf16[128,2048]{1,0:T(8,128)(2,1)S(1)}, u32[]{:S(2)}, u32[]{:S(2)}) collective-permute-start(bf16[128,2048]{1,0:T(8,128)(2,1)S(1)} %get-tuple-element.45), channel_id=1, source_target_pairs={{0,0},{1,2},{2,1},{3,3},{4,4},{5,6},{6,5},{7,7},{8,8},{9,10},{10,9... | collective-permute-start | bytes 1572872 | tf_op jit(solution)/shard_map/ppermute | solution.py:372
  8.8 8.2 %collective-permute-start.3 = (bf16[528,128]{1,0:T(8,128)(2,1)S(1)}, bf16[528,128]{1,0:T(8,128)(2,1)S(1)}, u32[]{:S(2)}, u32[]{:S(2)}) collective-permute-start(bf16[528,128]{1,0:T(8,128)(2,1)S(1)} %get-tuple-element.50), channel_id=1, source_target_pairs={{0,16},{4,20},{8,24},{12,28},{16,0},{20,4},{24,8},{28,12},{1,17},{... | collective-permute-start | bytes 405512 | tf_op jit(solution)/shard_map/ppermute | solution.py:32
  10.4 12.7 %collective-permute-start.4 = (bf16[528,128]{1,0:T(8,128)(2,1)S(1)}, bf16[528,128]{1,0:T(8,128)(2,1)S(1)}, u32[]{:S(2)}, u32[]{:S(2)}) collective-permute-start(bf16[528,128]{1,0:T(8,128)(2,1)S(1)} %get-tuple-element.51), channel_id=1, source_target_pairs={{0,24},{4,28},{8,16},{12,20},{16,8},{20,12},{24,0},{28,4},{1,25},{... | collective-permute-start | bytes 405512 | tf_op jit(solution)/shard_map/ppermute | solution.py:32
  17.0 9.9 %collective-permute-start.18 = (bf16[128,1024]{1,0:T(8,128)(2,1)S(1)}, bf16[128,1024]{1,0:T(8,128)(2,1)S(1)}, u32[]{:S(2)}, u32[]{:S(2)}) collective-permute-start(bf16[128,1024]{1,0:T(8,128)(2,1)S(1)} %get-tuple-element.73), channel_id=1, source_target_pairs={{0,1},{1,2},{2,3},{4,5},{5,6},{6,7},{8,9},{9,10},{10,11},{12,13},{... | collective-permute-start | bytes 786440 | tf_op jit(solution)/shard_map/ppermute | solution.py:364
  24.5 12.0 %collective-permute-start.15 = (bf16[128,1024]{1,0:T(8,128)(2,1)S(1)}, bf16[128,1024]{1,0:T(8,128)(2,1)S(1)}, u32[]{:S(2)}, u32[]{:S(2)}) collective-permute-start(bf16[128,1024]{1,0:T(8,128)(2,1)S(1)} %get-tuple-element.70), channel_id=1, source_target_pairs={{0,8},{4,12},{8,0},{12,4},{16,24},{20,28},{24,16},{28,20},{1,9},{5... | collective-permute-start | bytes 786440 | tf_op jit(solution)/shard_map/ppermute | solution.py:32
  25.1 11.7 %collective-permute-start.16 = (bf16[128,1024]{1,0:T(8,128)(2,1)S(1)}, bf16[128,1024]{1,0:T(8,128)(2,1)S(1)}, u32[]{:S(2)}, u32[]{:S(2)}) collective-permute-start(bf16[128,1024]{1,0:T(8,128)(2,1)S(1)} %get-tuple-element.71), channel_id=1, source_target_pairs={{0,16},{4,20},{8,24},{12,28},{16,0},{20,4},{24,8},{28,12},{1,17},{... | collective-permute-start | bytes 786440 | tf_op jit(solution)/shard_map/ppermute | solution.py:32
  26.9 14.7 %copy-start = (bf16[2,1,128,2048]{3,2,1,0:T(8,128)(2,1)S(1)}, bf16[2,1,128,2048]{3,2,1,0:T(8,128)(2,1)}, u32[]{:S(2)}) copy-start(bf16[2,1,128,2048]{3,2,1,0:T(8,128)(2,1)} %kv_ref.11) | copy-start | bytes 3145732
  26.9 14.7 %copy-start.1 = (bf16[1,128,2048]{2,1,0:T(8,128)(2,1)S(1)}, bf16[1,128,2048]{2,1,0:T(8,128)(2,1)}, u32[]{:S(2)}) copy-start(bf16[1,128,2048]{2,1,0:T(8,128)(2,1)} %q_ref.15) | copy-start | bytes 1572868
  26.9 14.7 %copy-start.3 = (s32[1,512]{1,0:T(1,128)S(1)}, s32[1,512]{1,0:T(1,128)}, u32[]{:S(2)}) copy-start(s32[1,512]{1,0:T(1,128)} %segs.9) | copy-start | bytes 6148
  26.9 16.2 %collective-permute-start.17 = (bf16[128,1024]{1,0:T(8,128)(2,1)S(1)}, bf16[128,1024]{1,0:T(8,128)(2,1)S(1)}, u32[]{:S(2)}, u32[]{:S(2)}) collective-permute-start(bf16[128,1024]{1,0:T(8,128)(2,1)S(1)} %get-tuple-element.72), channel_id=1, source_target_pairs={{0,24},{4,28},{8,16},{12,20},{16,8},{20,12},{24,0},{28,4},{1,25},{... | collective-permute-start | bytes 786440 | tf_op jit(solution)/shard_map/ppermute | solution.py:32
  30.5 14.8 %collective-permute-start.9 = (bf16[128,1024]{1,0:T(8,128)(2,1)S(1)}, bf16[128,1024]{1,0:T(8,128)(2,1)S(1)}, u32[]{:S(2)}, u32[]{:S(2)}) collective-permute-start(bf16[128,1024]{1,0:T(8,128)(2,1)S(1)} %get-tuple-element.56), channel_id=1, source_target_pairs={{0,1},{1,2},{2,3},{4,5},{5,6},{6,7},{8,9},{9,10},{10,11},{12,13},{... | collective-permute-start | bytes 786440 | tf_op jit(solution)/shard_map/ppermute | solution.py:364
  34.9 10.4 %collective-permute-start.6 = (bf16[128,1024]{1,0:T(8,128)(2,1)S(1)}, bf16[128,1024]{1,0:T(8,128)(2,1)S(1)}, u32[]{:S(2)}, u32[]{:S(2)}) collective-permute-start(bf16[128,1024]{1,0:T(8,128)(2,1)S(1)} %get-tuple-element.53), channel_id=1, source_target_pairs={{0,8},{4,12},{8,0},{12,4},{16,24},{20,28},{24,16},{28,20},{1,9},{5... | collective-permute-start | bytes 786440 | tf_op jit(solution)/shard_map/ppermute | solution.py:32
  36.5 13.3 %collective-permute-start.7 = (bf16[128,1024]{1,0:T(8,128)(2,1)S(1)}, bf16[128,1024]{1,0:T(8,128)(2,1)S(1)}, u32[]{:S(2)}, u32[]{:S(2)}) collective-permute-start(bf16[128,1024]{1,0:T(8,128)(2,1)S(1)} %get-tuple-element.54), channel_id=1, source_target_pairs={{0,16},{4,20},{8,24},{12,28},{16,0},{20,4},{24,8},{28,12},{1,17},{... | collective-permute-start | bytes 786440 | tf_op jit(solution)/shard_map/ppermute | solution.py:32
  36.8 13.0 %collective-permute-start.8 = (bf16[128,1024]{1,0:T(8,128)(2,1)S(1)}, bf16[128,1024]{1,0:T(8,128)(2,1)S(1)}, u32[]{:S(2)}, u32[]{:S(2)}) collective-permute-start(bf16[128,1024]{1,0:T(8,128)(2,1)S(1)} %get-tuple-element.55), channel_id=1, source_target_pairs={{0,24},{4,28},{8,16},{12,20},{16,8},{20,12},{24,0},{28,4},{1,25},{... | collective-permute-start | bytes 786440 | tf_op jit(solution)/shard_map/ppermute | solution.py:32
  44.0 18.2 %collective-permute-start.19 = (bf16[1040,128]{1,0:T(8,128)(2,1)S(1)}, bf16[1040,128]{1,0:T(8,128)(2,1)S(1)}, u32[]{:S(2)}, u32[]{:S(2)}) collective-permute-start(bf16[1040,128]{1,0:T(8,128)(2,1)S(1)} %get-tuple-element.74.g_ref), channel_id=1, source_target_pairs={{1,0},{2,1},{3,2},{5,4},{6,5},{7,6},{9,8},{10,9},{11,10},{13,12},{... | collective-permute-start | bytes 798728 | tf_op jit(solution)/shard_map/ppermute | solution.py:364
  50.7 15.5 %collective-permute-start.12 = (bf16[1040,128]{1,0:T(8,128)(2,1)S(1)}, bf16[1040,128]{1,0:T(8,128)(2,1)S(1)}, u32[]{:S(2)}, u32[]{:S(2)}) collective-permute-start(bf16[1040,128]{1,0:T(8,128)(2,1)S(1)} %get-tuple-element.58.g_ref), channel_id=1, source_target_pairs={{1,0},{2,1},{3,2},{5,4},{6,5},{7,6},{9,8},{10,9},{11,10},{13,12},{... | collective-permute-start | bytes 798728 | tf_op jit(solution)/shard_map/ppermute | solution.py:364
  52.0 6.0 %collective-permute-start.10 = (f32[2,16,128]{2,1,0:T(8,128)S(1)}, f32[2,16,128]{2,1,0:T(8,128)S(1)}, u32[]{:S(2)}, u32[]{:S(2)}) collective-permute-start(f32[2,16,128]{2,1,0:T(8,128)S(1)} %get-tuple-element.59.far_stats), channel_id=1, source_target_pairs={{0,1},{1,2},{2,3},{4,5},{5,6},{6,7},{8,9},{9,10},{10,11},{12,13},{... | collective-permute-start | bytes 49160 | tf_op jit(solution)/shard_map/ppermute | solution.py:364
  56.6 5.6 %collective-permute-start.11 = (f32[2,16,128]{2,1,0:T(8,128)S(1)}, f32[2,16,128]{2,1,0:T(8,128)S(1)}, u32[]{:S(2)}, u32[]{:S(2)}) collective-permute-start(f32[2,16,128]{2,1,0:T(8,128)S(1)} %get-tuple-element.57.refs_8_.own_stats), channel_id=1, source_target_pairs={{1,0},{2,1},{3,2},{5,4},{6,5},{7,6},{9,8},{10,9},{11,10},{13,12},{... | collective-permute-start | bytes 49160 | tf_op jit(solution)/shard_map/ppermute | solution.py:364
  64.5 14.9 %collective-permute-start.20 = (bf16[2,128,1024]{2,1,0:T(8,128)(2,1)S(1)}, bf16[2,128,1024]{2,1,0:T(8,128)(2,1)S(1)}, u32[]{:S(2)}, u32[]{:S(2)}) collective-permute-start(bf16[2,128,1024]{2,1,0:T(8,128)(2,1)S(1)} %get-tuple-element.82), channel_id=1, source_target_pairs={{0,1},{1,0},{2,3},{3,2},{4,5},{5,4},{6,7},{7,6},{8,9},{9,8},{10,11... | collective-permute-start | bytes 1572872 | tf_op jit(solution)/shard_map/ppermute | solution.py:372
  65.5 13.9 %collective-permute-start.21 = (bf16[2,128,1024]{2,1,0:T(8,128)(2,1)S(1)}, bf16[2,128,1024]{2,1,0:T(8,128)(2,1)S(1)}, u32[]{:S(2)}, u32[]{:S(2)}) collective-permute-start(bf16[2,128,1024]{2,1,0:T(8,128)(2,1)S(1)} %get-tuple-element.83), channel_id=1, source_target_pairs={{0,0},{1,2},{2,1},{3,3},{4,4},{5,6},{6,5},{7,7},{8,8},{9,10},{10,9... | collective-permute-start | bytes 1572872 | tf_op jit(solution)/shard_map/ppermute | solution.py:372
  68.7 17.0 %collective-permute-start.13 = (bf16[2,128,1024]{2,1,0:T(8,128)(2,1)S(1)}, bf16[2,128,1024]{2,1,0:T(8,128)(2,1)S(1)}, u32[]{:S(2)}, u32[]{:S(2)}) collective-permute-start(bf16[2,128,1024]{2,1,0:T(8,128)(2,1)S(1)} %get-tuple-element.67), channel_id=1, source_target_pairs={{0,1},{1,0},{2,3},{3,2},{4,5},{5,4},{6,7},{7,6},{8,9},{9,8},{10,11... | collective-permute-start | bytes 1572872 | tf_op jit(solution)/shard_map/ppermute | solution.py:372
  71.6 14.1 %collective-permute-start.14 = (bf16[2,128,1024]{2,1,0:T(8,128)(2,1)S(1)}, bf16[2,128,1024]{2,1,0:T(8,128)(2,1)S(1)}, u32[]{:S(2)}, u32[]{:S(2)}) collective-permute-start(bf16[2,128,1024]{2,1,0:T(8,128)(2,1)S(1)} %get-tuple-element.68), channel_id=1, source_target_pairs={{0,0},{1,2},{2,1},{3,3},{4,4},{5,6},{6,5},{7,7},{8,8},{9,10},{10,9... | collective-permute-start | bytes 1572872 | tf_op jit(solution)/shard_map/ppermute | solution.py:372

commit v7 on v4

--- a/solution.py
+++ b/solution.py
@@ -342,8 +342,10 @@
     return lax.ppermute(value, "seq", [(i, (i + steps) % count) for i in range(count)])
 
 
-def passed_up(value):
-    return lax.ppermute(value, "seq", [(i, i + 1) for i in range(lax.axis_size("seq") - 1)])
+def passed(value, steps):
+    count = lax.axis_size("seq")
+    first, last = max(0, -steps), min(count, count - steps)
+    return lax.ppermute(value, "seq", [(i, i + steps) for i in range(first, last)])
 
 
 def neighbour_swaps(first, second):
@@ -404,7 +406,7 @@
     sides = neighbour_swaps(first, second)
     values = []
     for own_v in own_vs:
-        values.append(passed_up(own_v))
+        values.append(passed(own_v, 1))
 
     sums = []
     for first, span in chunks(hc):
@@ -436,7 +438,7 @@
             compiler_params=params(8),
             cost_estimate=cost(4 * 2 * rows * rows * span, 20 * rows * span),
         )(*sums[c], query, key_value, left_k, values[c], segments, own)
-        pieces.append((gout, delta, shifted(gout, -1)))
+        pieces.append((gout, delta, passed(gout, -1)))
 
     parts = []
     for c, (first, span) in enumerate(chunks(hc)):

time: 87 us -> 88 us (1.011)
  the two profiles are of different devices: /device:TPU:18 before, /device:TPU:0 now
where the time goes in v7:
time: 88 us; the launch traced here: 86.7 us
  starting transfers between devices  41.6 us (47%)
  waiting for transfers between devices  26.6 us (30%)
  Pallas kernels  17.5 us (20%)
  between operations  1.01 us (1%)
    ppermute x10, starting transfers between devices, swap(): lax.ppermute(value, axis, [(i, i ^ bits) for i in range(lax.axis_size(axi...  17.2 us
    ppermute x4, starting transfers between devices, passed(): lax.ppermute(value, 'seq', [(i, i + steps) for i in range(first, last)])  13 us
    ppermute x6, waiting for transfers between devices, neighbour_swaps(): return (lax.ppermute(first, 'seq', one), lax.ppermute(second, 'seq', two))  12.2 us
    ppermute x10, waiting for transfers between devices, swap(): lax.ppermute(value, axis, [(i, i ^ bits) for i in range(lax.axis_size(axi...  9.66 us
    ppermute x6, starting transfers between devices, neighbour_swaps(): return (lax.ppermute(first, 'seq', one), lax.ppermute(second, 'seq', two))  7.27 us
    pallas_call x2, Pallas kernels, step(): pl.pallas_call(functools.partial(grads_kernel, count, first, scale), out_...  5.91 us
    ppermute x2, waiting for transfers between devices, shifted(): lax.ppermute(value, 'seq', [(i, (i + steps) % count) for i in range(count)])  4.41 us
    ppermute x2, starting transfers between devices, shifted(): lax.ppermute(value, 'seq', [(i, (i + steps) % count) for i in range(count)])  4.15 us
  transfers between devices with their start and end apart: 22, of which 6 were waited for; matrix products, arithmetic and copies ran while one was open for 0% of the time, Pallas kernels for 19%

profile of v7, /device:TPU:0, one launch (start us, length us, event | category | flops | bytes accessed | tf_op | source)
XLA Modules:
  0.0 86.7 jit_solution(18079655784152672438)
XLA Ops:
  0.6 0.6 collective-permute-start.6
  1.2 1.2 %grad_slices.1 = (bf16[528,128]{1,0:T(8,128)(2,1)S(1)}, bf16[528,128]{1,0:T(8,128)(2,1)S(1)}, bf16[528,128]{1,0:T(8,128)(2,1)S(1)}, bf16[528,128]{1,0:T(8,128)(2,1)S(1)}) custom-call(bf16[1,128,2048]{2,1,0:T(8,128)(2,1)} %grad_ref.1, s32[1,128]{1,0:T(1,128)} %tags_ref.1), custom_call_target="tpu_custom_call" | custom-call | bytes 1048576 | tf_op jit(solution)/shard_map/grad_slices/pallas_call | solution.py:386
  2.4 2.6 %collective-permute-start.3 = (bf16[528,128]{1,0:T(8,128)(2,1)S(1)}, bf16[528,128]{1,0:T(8,128)(2,1)S(1)}, u32[]{:S(2)}, u32[]{:S(2)}) collective-permute-start(bf16[528,128]{1,0:T(8,128)(2,1)S(1)} %get-tuple-element.44), channel_id=1, source_target_pairs={{0,8},{4,12},{8,0},{12,4},{16,24},{20,28},{24,16},{28,20},{1,9},{5... | collective-permute-start | bytes 405512 | tf_op jit(solution)/shard_map/ppermute | solution.py:32
  5.1 1.4 %side_slices.1 = (bf16[128,2048]{1,0:T(8,128)(2,1)S(1)}, bf16[128,2048]{1,0:T(8,128)(2,1)S(1)}, bf16[128,1024]{1,0:T(8,128)(2,1)S(1)}, bf16[128,1024]{1,0:T(8,128)(2,1)S(1)}) custom-call(bf16[1,128,2048]{2,1,0:T(8,128)(2,1)} %q_ref.11, bf16[2,1,128,2048]{3,2,1,0:T(8,128)(2,1)} %kv_ref.11), custom_call_target="tpu_custom_call" | custom-call | bytes 3145728 | tf_op jit(solution)/shard_map/side_slices/pallas_call | solution.py:397
  6.5 1.6 %collective-permute-start = (bf16[128,2048]{1,0:T(8,128)(2,1)S(1)}, bf16[128,2048]{1,0:T(8,128)(2,1)S(1)}, u32[]{:S(2)}, u32[]{:S(2)}) collective-permute-start(bf16[128,2048]{1,0:T(8,128)(2,1)S(1)} %get-tuple-element.38), channel_id=1, source_target_pairs={{0,1},{1,0},{2,3},{3,2},{4,5},{5,4},{6,7},{7,6},{8,9},{9,8},{10,11... | collective-permute-start | bytes 1572872 | tf_op jit(solution)/shard_map/ppermute | solution.py:356
  8.1 0.7 collective-permute-start.1
  8.8 1.6 %collective-permute-start.4 = (bf16[528,128]{1,0:T(8,128)(2,1)S(1)}, bf16[528,128]{1,0:T(8,128)(2,1)S(1)}, u32[]{:S(2)}, u32[]{:S(2)}) collective-permute-start(bf16[528,128]{1,0:T(8,128)(2,1)S(1)} %get-tuple-element.45), channel_id=1, source_target_pairs={{0,16},{4,20},{8,24},{12,28},{16,0},{20,4},{24,8},{28,12},{1,17},{... | collective-permute-start | bytes 405512 | tf_op jit(solution)/shard_map/ppermute | solution.py:32
  10.4 0.0 collective-permute-done.3.refs_1_
  10.4 1.5 %collective-permute-start.5 = (bf16[528,128]{1,0:T(8,128)(2,1)S(1)}, bf16[528,128]{1,0:T(8,128)(2,1)S(1)}, u32[]{:S(2)}, u32[]{:S(2)}) collective-permute-start(bf16[528,128]{1,0:T(8,128)(2,1)S(1)} %get-tuple-element.46), channel_id=1, source_target_pairs={{0,24},{4,28},{8,16},{12,20},{16,8},{20,12},{24,0},{28,4},{1,25},{... | collective-permute-start | bytes 405512 | tf_op jit(solution)/shard_map/ppermute | solution.py:32
  11.9 5.2 %collective-permute-done.4.refs_2_ = bf16[528,128]{1,0:T(8,128)(2,1)S(1)} collective-permute-done((bf16[528,128]{1,0:T(8,128)(2,1)S(1)}, bf16[528,128]{1,0:T(8,128)(2,1)S(1)}, u32[]{:S(2)}, u32[]{:S(2)}) %collective-permute-start.4) | collective-permute-done | bytes 135200 | tf_op jit(solution)/shard_map/ppermute | solution.py:32
  17.0 6.0 %collective-permute-start.15 = (bf16[128,1024]{1,0:T(8,128)(2,1)S(1)}, bf16[128,1024]{1,0:T(8,128)(2,1)S(1)}, u32[]{:S(2)}, u32[]{:S(2)}) collective-permute-start(bf16[128,1024]{1,0:T(8,128)(2,1)S(1)} %get-tuple-element.60), channel_id=1, source_target_pairs={{0,1},{1,2},{2,3},{4,5},{5,6},{6,7},{8,9},{9,10},{10,11},{12,13},{... | collective-permute-start | bytes 786440 | tf_op jit(solution)/shard_map/ppermute | solution.py:348
  23.1 0.0 collective-permute-done.6.refs_5_
  23.1 1.4 %shard_map.80 = (f32[128,1024]{1,0:T(8,128)S(1)}, bf16[128,1024]{1,0:T(8,128)(2,1)S(1)}, bf16[128,1024]{1,0:T(8,128)(2,1)S(1)}, bf16[128,1024]{1,0:T(8,128)(2,1)S(1)}) custom-call(bf16[528,128]{1,0:T(8,128)(2,1)S(1)} %get-tuple-element.43.refs_0_, bf16[528,128]{1,0:T(8,128)(2,1)S(1)} %collective-permute-done.3.refs_1_, ...), custom_call_target="tpu_custom_call" | custom-call | flops 1073741824 | bytes 2097152 | tf_op jit(solution)/shard_map/pallas_call | solution.py:413
  24.5 0.6 collective-permute-start.16
  25.1 1.5 %collective-permute-start.17 = (bf16[128,1024]{1,0:T(8,128)(2,1)S(1)}, bf16[128,1024]{1,0:T(8,128)(2,1)S(1)}, u32[]{:S(2)}, u32[]{:S(2)}) collective-permute-start(bf16[128,1024]{1,0:T(8,128)(2,1)S(1)} %get-tuple-element.63), channel_id=1, source_target_pairs={{0,16},{4,20},{8,24},{12,28},{16,0},{20,4},{24,8},{28,12},{1,17},{... | collective-permute-start | bytes 786440 | tf_op jit(solution)/shard_map/ppermute | solution.py:32
  26.6 0.3 collective-permute-done.15.refs_6_.left_v
  26.9 2.2 %collective-permute-start.18 = (bf16[128,1024]{1,0:T(8,128)(2,1)S(1)}, bf16[128,1024]{1,0:T(8,128)(2,1)S(1)}, u32[]{:S(2)}, u32[]{:S(2)}) collective-permute-start(bf16[128,1024]{1,0:T(8,128)(2,1)S(1)} %get-tuple-element.64), channel_id=1, source_target_pairs={{0,24},{4,28},{8,16},{12,20},{16,8},{20,12},{24,0},{28,4},{1,25},{... | collective-permute-start | bytes 786440 | tf_op jit(solution)/shard_map/ppermute | solution.py:32
  29.1 1.4 %shard_map.77 = (f32[128,1024]{1,0:T(8,128)S(1)}, bf16[128,1024]{1,0:T(8,128)(2,1)S(1)}, bf16[128,1024]{1,0:T(8,128)(2,1)S(1)}, bf16[128,1024]{1,0:T(8,128)(2,1)S(1)}) custom-call(bf16[528,128]{1,0:T(8,128)(2,1)S(1)} %get-tuple-element.43.refs_0_, bf16[528,128]{1,0:T(8,128)(2,1)S(1)} %collective-permute-done.3.refs_1_, ...), custom_call_target="tpu_custom_call" | custom-call | flops 1073741824 | bytes 2097152 | tf_op jit(solution)/shard_map/pallas_call | solution.py:413
  30.5 0.0 collective-permute-done.got1
  30.5 4.4 %collective-permute-start.2 = (bf16[128,1024]{1,0:T(8,128)(2,1)S(1)}, bf16[128,1024]{1,0:T(8,128)(2,1)S(1)}, u32[]{:S(2)}, u32[]{:S(2)}) collective-permute-start(bf16[128,1024]{1,0:T(8,128)(2,1)S(1)} %get-tuple-element.41), channel_id=1, source_target_pairs={{0,1},{1,2},{2,3},{4,5},{5,6},{6,7},{8,9},{9,10},{10,11},{12,13},{... | collective-permute-start | bytes 786440 | tf_op jit(solution)/shard_map/ppermute | solution.py:348
  34.9 1.6 %collective-permute-start.7 = (bf16[128,1024]{1,0:T(8,128)(2,1)S(1)}, bf16[128,1024]{1,0:T(8,128)(2,1)S(1)}, u32[]{:S(2)}, u32[]{:S(2)}) collective-permute-start(bf16[128,1024]{1,0:T(8,128)(2,1)S(1)} %get-tuple-element.48), channel_id=1, source_target_pairs={{0,8},{4,12},{8,0},{12,4},{16,24},{20,28},{24,16},{28,20},{1,9},{5... | collective-permute-start | bytes 786440 | tf_op jit(solution)/shard_map/ppermute | solution.py:32
  36.5 0.0 collective-permute-done.16.refs_0_
  36.5 0.3 collective-permute-start.8
  36.8 4.8 %collective-permute-start.9 = (bf16[128,1024]{1,0:T(8,128)(2,1)S(1)}, bf16[128,1024]{1,0:T(8,128)(2,1)S(1)}, u32[]{:S(2)}, u32[]{:S(2)}) collective-permute-start(bf16[128,1024]{1,0:T(8,128)(2,1)S(1)} %get-tuple-element.50), channel_id=1, source_target_pairs={{0,24},{4,28},{8,16},{12,20},{16,8},{20,12},{24,0},{28,4},{1,25},{... | collective-permute-start | bytes 786440 | tf_op jit(solution)/shard_map/ppermute | solution.py:32
  41.6 1.5 %stats.1 = (f32[2,16,128]{2,1,0:T(8,128)S(1)}, f32[2,16,128]{2,1,0:T(8,128)S(1)}, bf16[128,2048]{1,0:T(8,128)(2,1)S(1)}, bf16[128,2048]{1,0:T(8,128)(2,1)S(1)}) custom-call(bf16[1,128,2048]{2,1,0:T(8,128)(2,1)S(1)} %copy-done.1, bf16[2,1,128,2048]{3,2,1,0:T(8,128)(2,1)S(1)} %copy-done, bf16[128,2048]{1,0:T(8,128)(2,1)S(1)} %collective-permute-done.got1, ...), custom_call_target="tpu_custom_call" | custom-call | flops 201326592 | bytes 5242880 | tf_op jit(solution)/shard_map/stats/pallas_call | solution.py:423
  43.1 0.0 collective-permute-done.18.refs_2_
  43.1 0.9 %shard_map.81 = (bf16[1040,128]{1,0:T(8,128)(2,1)S(1)}, f32[8,128]{1,0:T(8,128)S(1)}) custom-call(f32[128,1024]{1,0:T(8,128)S(1)} %get-tuple-element.61.mine, bf16[128,1024]{1,0:T(8,128)(2,1)S(1)} %collective-permute-done.16.refs_0_, bf16[128,1024]{1,0:T(8,128)(2,1)S(1)} %collective-permute-done.17.refs_1_, ...), custom_call_target="tpu_custom_call" | custom-call | flops 134217728 | bytes 2621440 | tf_op jit(solution)/shard_map/pallas_call | solution.py:435
  44.0 1.3 %collective-permute-start.19 = (bf16[1040,128]{1,0:T(8,128)(2,1)S(1)}, bf16[1040,128]{1,0:T(8,128)(2,1)S(1)}, u32[]{:S(2)}, u32[]{:S(2)}) collective-permute-start(bf16[1040,128]{1,0:T(8,128)(2,1)S(1)} %get-tuple-element.65.g_ref), channel_id=1, source_target_pairs={{1,0},{2,1},{3,2},{5,4},{6,5},{7,6},{9,8},{10,9},{11,10},{13,12},{... | collective-permute-start | bytes 798728 | tf_op jit(solution)/shard_map/ppermute | solution.py:348
  45.3 0.0 collective-permute-done.2.refs_6_.left_v
  45.3 0.0 collective-permute-done.7.refs_0_
  45.3 4.5 %collective-permute-done.8.refs_1_ = bf16[128,1024]{1,0:T(8,128)(2,1)S(1)} collective-permute-done((bf16[128,1024]{1,0:T(8,128)(2,1)S(1)}, bf16[128,1024]{1,0:T(8,128)(2,1)S(1)}, u32[]{:S(2)}, u32[]{:S(2)}) %collective-permute-start.8) | collective-permute-done | bytes 262176 | tf_op jit(solution)/shard_map/ppermute | solution.py:32
  49.8 0.9 %shard_map.78 = (bf16[1040,128]{1,0:T(8,128)(2,1)S(1)}, f32[8,128]{1,0:T(8,128)S(1)}) custom-call(f32[128,1024]{1,0:T(8,128)S(1)} %get-tuple-element.47.mine, bf16[128,1024]{1,0:T(8,128)(2,1)S(1)} %collective-permute-done.7.refs_0_, bf16[128,1024]{1,0:T(8,128)(2,1)S(1)} %collective-permute-done.8.refs_1_, ...), custom_call_target="tpu_custom_call" | custom-call | flops 134217728 | bytes 2621440 | tf_op jit(solution)/shard_map/pallas_call | solution.py:435
  50.7 1.3 %collective-permute-start.10 = (bf16[1040,128]{1,0:T(8,128)(2,1)S(1)}, bf16[1040,128]{1,0:T(8,128)(2,1)S(1)}, u32[]{:S(2)}, u32[]{:S(2)}) collective-permute-start(bf16[1040,128]{1,0:T(8,128)(2,1)S(1)} %get-tuple-element.52.g_ref), channel_id=1, source_target_pairs={{1,0},{2,1},{3,2},{5,4},{6,5},{7,6},{9,8},{10,9},{11,10},{13,12},{... | collective-permute-start | bytes 798728 | tf_op jit(solution)/shard_map/ppermute | solution.py:348
  52.0 2.7 %collective-permute-start.11 = (f32[2,16,128]{2,1,0:T(8,128)S(1)}, f32[2,16,128]{2,1,0:T(8,128)S(1)}, u32[]{:S(2)}, u32[]{:S(2)}) collective-permute-start(f32[2,16,128]{2,1,0:T(8,128)S(1)} %get-tuple-element.53.far_stats), channel_id=1, source_target_pairs={{0,1},{1,2},{2,3},{3,0},{4,5},{5,6},{6,7},{7,4},{8,9},{9,10},{10,1... | collective-permute-start | bytes 49160 | tf_op jit(solution)/shard_map/ppermute | solution.py:342
  54.7 1.5 %collective-permute-start.12 = (f32[2,16,128]{2,1,0:T(8,128)S(1)}, f32[2,16,128]{2,1,0:T(8,128)S(1)}, u32[]{:S(2)}, u32[]{:S(2)}) collective-permute-start(f32[2,16,128]{2,1,0:T(8,128)S(1)} %get-tuple-element.51.refs_8_.own_stats), channel_id=1, source_target_pairs={{0,3},{1,0},{2,1},{3,2},{4,7},{5,4},{6,5},{7,6},{8,11},{9,8},{10,9... | collective-permute-start | bytes 49160 | tf_op jit(solution)/shard_map/ppermute | solution.py:342
  56.1 4.4 %collective-permute-done.11.from_left = f32[2,16,128]{2,1,0:T(8,128)S(1)} collective-permute-done((f32[2,16,128]{2,1,0:T(8,128)S(1)}, f32[2,16,128]{2,1,0:T(8,128)S(1)}, u32[]{:S(2)}, u32[]{:S(2)}) %collective-permute-start.11) | collective-permute-done | bytes 16416 | tf_op jit(solution)/shard_map/ppermute | solution.py:342
  60.6 0.0 collective-permute-done.12.from_right
  60.6 0.0 collective-permute-done.19.right_g
  60.6 2.9 %shard_map.82 = (f32[128,1024]{1,0:T(8,128)S(1)}, f32[2,128,1024]{2,1,0:T(8,128)S(1)}, bf16[8,256,128]{2,1,0:T(8,128)(2,1)S(1)}, bf16[2,128,1024]{2,1,0:T(8,128)(2,1)S(1)}, bf16[2,128,1024]{2,1,0:T(8,128)(2,1)S(1)}) custom-call(bf16[1,128,2048]{2,1,0:T(8,128)(2,1)S(1)} %copy-done.1, bf16[2,1,128,2048]{3,2,1,0:T(8,128)(2,1)S(1)} %copy-done, ...), custom_call_target="tpu_custom_call" | custom-call | flops 503316480 | bytes 5242880 | tf_op jit(solution)/shard_map/pallas_call | solution.py:447
  63.4 0.1 collective-permute-start.20
  63.5 0.7 collective-permute-start.21
  64.2 3.0 %shard_map.79 = (f32[128,1024]{1,0:T(8,128)S(1)}, f32[2,128,1024]{2,1,0:T(8,128)S(1)}, bf16[8,256,128]{2,1,0:T(8,128)(2,1)S(1)}, bf16[2,128,1024]{2,1,0:T(8,128)(2,1)S(1)}, bf16[2,128,1024]{2,1,0:T(8,128)(2,1)S(1)}) custom-call(bf16[1,128,2048]{2,1,0:T(8,128)(2,1)S(1)} %copy-done.1, bf16[2,1,128,2048]{3,2,1,0:T(8,128)(2,1)S(1)} %copy-done, ...), custom_call_target="tpu_custom_call" | custom-call | flops 503316480 | bytes 5242880 | tf_op jit(solution)/shard_map/pallas_call | solution.py:447
  67.3 3.5 %collective-permute-start.13 = (bf16[2,128,1024]{2,1,0:T(8,128)(2,1)S(1)}, bf16[2,128,1024]{2,1,0:T(8,128)(2,1)S(1)}, u32[]{:S(2)}, u32[]{:S(2)}) collective-permute-start(bf16[2,128,1024]{2,1,0:T(8,128)(2,1)S(1)} %get-tuple-element.58), channel_id=1, source_target_pairs={{0,1},{1,0},{2,3},{3,2},{4,5},{5,4},{6,7},{7,6},{8,9},{9,8},{10,11... | collective-permute-start | bytes 1572872 | tf_op jit(solution)/shard_map/ppermute | solution.py:356
  70.8 0.7 collective-permute-start.14
  71.5 6.8 %collective-permute-done.20.got1 = bf16[2,128,1024]{2,1,0:T(8,128)(2,1)S(1)} collective-permute-done((bf16[2,128,1024]{2,1,0:T(8,128)(2,1)S(1)}, bf16[2,128,1024]{2,1,0:T(8,128)(2,1)S(1)}, u32[]{:S(2)}, u32[]{:S(2)}) %collective-permute-start.20) | collective-permute-done | bytes 524320 | tf_op jit(solution)/shard_map/ppermute | solution.py:356
  78.3 1.4 %shard_map.83 = (bf16[1,128,2048]{2,1,0:T(8,128)(2,1)}, bf16[2,1,128,2048]{3,2,1,0:T(8,128)(2,1)}) custom-call(f32[128,1024]{1,0:T(8,128)S(1)} %get-tuple-element.67.dq_ref, f32[2,128,1024]{2,1,0:T(8,128)S(1)} %get-tuple-element.68.dkv_ref, bf16[8,256,128]{2,1,0:T(8,128)(2,1)S(1)} %get-tuple-element.69.p_ref, bf16[1,128,2048]{2,1,0:T(8,128)(2,1)S(1)} %copy-done.1, ...), custom_call_target="tpu_custom_call" | custom-call | bytes 2621440 | tf_op jit(solution)/shard_map/pallas_call | solution.py:460
  79.7 5.3 %collective-permute-done.13.got1 = bf16[2,128,1024]{2,1,0:T(8,128)(2,1)S(1)} collective-permute-done((bf16[2,128,1024]{2,1,0:T(8,128)(2,1)S(1)}, bf16[2,128,1024]{2,1,0:T(8,128)(2,1)S(1)}, u32[]{:S(2)}, u32[]{:S(2)}) %collective-permute-start.13) | collective-permute-done | bytes 524320 | tf_op jit(solution)/shard_map/ppermute | solution.py:356
  85.1 1.5 %shard_map.84 = (bf16[1,128,2048]{2,1,0:T(8,128)(2,1)}, bf16[2,1,128,2048]{3,2,1,0:T(8,128)(2,1)}) custom-call(f32[128,1024]{1,0:T(8,128)S(1)} %get-tuple-element.55.dq_ref, f32[2,128,1024]{2,1,0:T(8,128)S(1)} %get-tuple-element.56.dkv_ref, bf16[8,256,128]{2,1,0:T(8,128)(2,1)S(1)} %get-tuple-element.57.p_ref, ...), custom_call_target="tpu_custom_call", output_to_operand_aliasing={{0}: (8, {}), {1}: (9, {})} | custom-call | bytes 2621440 | tf_op jit(solution)/shard_map/pallas_call | solution.py:460
  (15 shorter events, 0.0 us)
Async XLA Ops:
  0.6 22.4 %copy-start.2 = (bf16[2,2048,256]{2,1,0:T(8,128)(2,1)S(1)}, bf16[2,2048,256]{2,1,0:T(8,128)(2,1)}, u32[]{:S(2)}) copy-start(bf16[2,2048,256]{2,1,0:T(8,128)(2,1)} %refs_4_.6) | copy-start | bytes 6291460
  0.6 22.4 %collective-permute-start.6 = (bf16[2,2048,256]{2,1,0:T(8,128)(2,1)}, bf16[2,2048,256]{2,1,0:T(8,128)(2,1)S(1)}, u32[]{:S(2)}, u32[]{:S(2)}) collective-permute-start(bf16[2,2048,256]{2,1,0:T(8,128)(2,1)} %refs_4_.6), channel_id=1, source_target_pairs={{0,4},{4,0},{8,12},{12,8},{16,20},{20,16},{24,28},{28,24},{1,5},{5... | collective-permute-start | bytes 6291464 | tf_op jit(solution)/shard_map/ppermute | solution.py:32
  2.4 7.9 %collective-permute-start.3 = (bf16[528,128]{1,0:T(8,128)(2,1)S(1)}, bf16[528,128]{1,0:T(8,128)(2,1)S(1)}, u32[]{:S(2)}, u32[]{:S(2)}) collective-permute-start(bf16[528,128]{1,0:T(8,128)(2,1)S(1)} %get-tuple-element.44), channel_id=1, source_target_pairs={{0,8},{4,12},{8,0},{12,4},{16,24},{20,28},{24,16},{28,20},{1,9},{5... | collective-permute-start | bytes 405512 | tf_op jit(solution)/shard_map/ppermute | solution.py:32
  6.5 24.1 %collective-permute-start = (bf16[128,2048]{1,0:T(8,128)(2,1)S(1)}, bf16[128,2048]{1,0:T(8,128)(2,1)S(1)}, u32[]{:S(2)}, u32[]{:S(2)}) collective-permute-start(bf16[128,2048]{1,0:T(8,128)(2,1)S(1)} %get-tuple-element.38), channel_id=1, source_target_pairs={{0,1},{1,0},{2,3},{3,2},{4,5},{5,4},{6,7},{7,6},{8,9},{9,8},{10,11... | collective-permute-start | bytes 1572872 | tf_op jit(solution)/shard_map/ppermute | solution.py:356
  8.1 26.8 %collective-permute-start.1 = (bf16[128,2048]{1,0:T(8,128)(2,1)S(1)}, bf16[128,2048]{1,0:T(8,128)(2,1)S(1)}, u32[]{:S(2)}, u32[]{:S(2)}) collective-permute-start(bf16[128,2048]{1,0:T(8,128)(2,1)S(1)} %get-tuple-element.39), channel_id=1, source_target_pairs={{0,0},{1,2},{2,1},{3,3},{4,4},{5,6},{6,5},{7,7},{8,8},{9,10},{10,9... | collective-permute-start | bytes 1572872 | tf_op jit(solution)/shard_map/ppermute | solution.py:356
  8.8 8.2 %collective-permute-start.4 = (bf16[528,128]{1,0:T(8,128)(2,1)S(1)}, bf16[528,128]{1,0:T(8,128)(2,1)S(1)}, u32[]{:S(2)}, u32[]{:S(2)}) collective-permute-start(bf16[528,128]{1,0:T(8,128)(2,1)S(1)} %get-tuple-element.45), channel_id=1, source_target_pairs={{0,16},{4,20},{8,24},{12,28},{16,0},{20,4},{24,8},{28,12},{1,17},{... | collective-permute-start | bytes 405512 | tf_op jit(solution)/shard_map/ppermute | solution.py:32
  10.4 12.7 %collective-permute-start.5 = (bf16[528,128]{1,0:T(8,128)(2,1)S(1)}, bf16[528,128]{1,0:T(8,128)(2,1)S(1)}, u32[]{:S(2)}, u32[]{:S(2)}) collective-permute-start(bf16[528,128]{1,0:T(8,128)(2,1)S(1)} %get-tuple-element.46), channel_id=1, source_target_pairs={{0,24},{4,28},{8,16},{12,20},{16,8},{20,12},{24,0},{28,4},{1,25},{... | collective-permute-start | bytes 405512 | tf_op jit(solution)/shard_map/ppermute | solution.py:32
  17.0 9.9 %collective-permute-start.15 = (bf16[128,1024]{1,0:T(8,128)(2,1)S(1)}, bf16[128,1024]{1,0:T(8,128)(2,1)S(1)}, u32[]{:S(2)}, u32[]{:S(2)}) collective-permute-start(bf16[128,1024]{1,0:T(8,128)(2,1)S(1)} %get-tuple-element.60), channel_id=1, source_target_pairs={{0,1},{1,2},{2,3},{4,5},{5,6},{6,7},{8,9},{9,10},{10,11},{12,13},{... | collective-permute-start | bytes 786440 | tf_op jit(solution)/shard_map/ppermute | solution.py:348
  24.5 12.0 %collective-permute-start.16 = (bf16[128,1024]{1,0:T(8,128)(2,1)S(1)}, bf16[128,1024]{1,0:T(8,128)(2,1)S(1)}, u32[]{:S(2)}, u32[]{:S(2)}) collective-permute-start(bf16[128,1024]{1,0:T(8,128)(2,1)S(1)} %get-tuple-element.62), channel_id=1, source_target_pairs={{0,8},{4,12},{8,0},{12,4},{16,24},{20,28},{24,16},{28,20},{1,9},{5... | collective-permute-start | bytes 786440 | tf_op jit(solution)/shard_map/ppermute | solution.py:32
  25.1 11.7 %collective-permute-start.17 = (bf16[128,1024]{1,0:T(8,128)(2,1)S(1)}, bf16[128,1024]{1,0:T(8,128)(2,1)S(1)}, u32[]{:S(2)}, u32[]{:S(2)}) collective-permute-start(bf16[128,1024]{1,0:T(8,128)(2,1)S(1)} %get-tuple-element.63), channel_id=1, source_target_pairs={{0,16},{4,20},{8,24},{12,28},{16,0},{20,4},{24,8},{28,12},{1,17},{... | collective-permute-start | bytes 786440 | tf_op jit(solution)/shard_map/ppermute | solution.py:32
  26.9 14.7 %copy-start = (bf16[2,1,128,2048]{3,2,1,0:T(8,128)(2,1)S(1)}, bf16[2,1,128,2048]{3,2,1,0:T(8,128)(2,1)}, u32[]{:S(2)}) copy-start(bf16[2,1,128,2048]{3,2,1,0:T(8,128)(2,1)} %kv_ref.11) | copy-start | bytes 3145732
  26.9 14.7 %copy-start.1 = (bf16[1,128,2048]{2,1,0:T(8,128)(2,1)S(1)}, bf16[1,128,2048]{2,1,0:T(8,128)(2,1)}, u32[]{:S(2)}) copy-start(bf16[1,128,2048]{2,1,0:T(8,128)(2,1)} %q_ref.11) | copy-start | bytes 1572868
  26.9 14.7 %copy-start.3 = (s32[1,512]{1,0:T(1,128)S(1)}, s32[1,512]{1,0:T(1,128)}, u32[]{:S(2)}) copy-start(s32[1,512]{1,0:T(1,128)} %segs.5) | copy-start | bytes 6148
  26.9 16.2 %collective-permute-start.18 = (bf16[128,1024]{1,0:T(8,128)(2,1)S(1)}, bf16[128,1024]{1,0:T(8,128)(2,1)S(1)}, u32[]{:S(2)}, u32[]{:S(2)}) collective-permute-start(bf16[128,1024]{1,0:T(8,128)(2,1)S(1)} %get-tuple-element.64), channel_id=1, source_target_pairs={{0,24},{4,28},{8,16},{12,20},{16,8},{20,12},{24,0},{28,4},{1,25},{... | collective-permute-start | bytes 786440 | tf_op jit(solution)/shard_map/ppermute | solution.py:32
  30.5 14.8 %collective-permute-start.2 = (bf16[128,1024]{1,0:T(8,128)(2,1)S(1)}, bf16[128,1024]{1,0:T(8,128)(2,1)S(1)}, u32[]{:S(2)}, u32[]{:S(2)}) collective-permute-start(bf16[128,1024]{1,0:T(8,128)(2,1)S(1)} %get-tuple-element.41), channel_id=1, source_target_pairs={{0,1},{1,2},{2,3},{4,5},{5,6},{6,7},{8,9},{9,10},{10,11},{12,13},{... | collective-permute-start | bytes 786440 | tf_op jit(solution)/shard_map/ppermute | solution.py:348
  34.9 10.4 %collective-permute-start.7 = (bf16[128,1024]{1,0:T(8,128)(2,1)S(1)}, bf16[128,1024]{1,0:T(8,128)(2,1)S(1)}, u32[]{:S(2)}, u32[]{:S(2)}) collective-permute-start(bf16[128,1024]{1,0:T(8,128)(2,1)S(1)} %get-tuple-element.48), channel_id=1, source_target_pairs={{0,8},{4,12},{8,0},{12,4},{16,24},{20,28},{24,16},{28,20},{1,9},{5... | collective-permute-start | bytes 786440 | tf_op jit(solution)/shard_map/ppermute | solution.py:32
  36.5 13.3 %collective-permute-start.8 = (bf16[128,1024]{1,0:T(8,128)(2,1)S(1)}, bf16[128,1024]{1,0:T(8,128)(2,1)S(1)}, u32[]{:S(2)}, u32[]{:S(2)}) collective-permute-start(bf16[128,1024]{1,0:T(8,128)(2,1)S(1)} %get-tuple-element.49), channel_id=1, source_target_pairs={{0,16},{4,20},{8,24},{12,28},{16,0},{20,4},{24,8},{28,12},{1,17},{... | collective-permute-start | bytes 786440 | tf_op jit(solution)/shard_map/ppermute | solution.py:32
  36.8 13.0 %collective-permute-start.9 = (bf16[128,1024]{1,0:T(8,128)(2,1)S(1)}, bf16[128,1024]{1,0:T(8,128)(2,1)S(1)}, u32[]{:S(2)}, u32[]{:S(2)}) collective-permute-start(bf16[128,1024]{1,0:T(8,128)(2,1)S(1)} %get-tuple-element.50), channel_id=1, source_target_pairs={{0,24},{4,28},{8,16},{12,20},{16,8},{20,12},{24,0},{28,4},{1,25},{... | collective-permute-start | bytes 786440 | tf_op jit(solution)/shard_map/ppermute | solution.py:32
  44.0 16.6 %collective-permute-start.19 = (bf16[1040,128]{1,0:T(8,128)(2,1)S(1)}, bf16[1040,128]{1,0:T(8,128)(2,1)S(1)}, u32[]{:S(2)}, u32[]{:S(2)}) collective-permute-start(bf16[1040,128]{1,0:T(8,128)(2,1)S(1)} %get-tuple-element.65.g_ref), channel_id=1, source_target_pairs={{1,0},{2,1},{3,2},{5,4},{6,5},{7,6},{9,8},{10,9},{11,10},{13,12},{... | collective-permute-start | bytes 798728 | tf_op jit(solution)/shard_map/ppermute | solution.py:348
  50.7 13.5 %collective-permute-start.10 = (bf16[1040,128]{1,0:T(8,128)(2,1)S(1)}, bf16[1040,128]{1,0:T(8,128)(2,1)S(1)}, u32[]{:S(2)}, u32[]{:S(2)}) collective-permute-start(bf16[1040,128]{1,0:T(8,128)(2,1)S(1)} %get-tuple-element.52.g_ref), channel_id=1, source_target_pairs={{1,0},{2,1},{3,2},{5,4},{6,5},{7,6},{9,8},{10,9},{11,10},{13,12},{... | collective-permute-start | bytes 798728 | tf_op jit(solution)/shard_map/ppermute | solution.py:348
  52.0 8.6 %collective-permute-start.11 = (f32[2,16,128]{2,1,0:T(8,128)S(1)}, f32[2,16,128]{2,1,0:T(8,128)S(1)}, u32[]{:S(2)}, u32[]{:S(2)}) collective-permute-start(f32[2,16,128]{2,1,0:T(8,128)S(1)} %get-tuple-element.53.far_stats), channel_id=1, source_target_pairs={{0,1},{1,2},{2,3},{3,0},{4,5},{5,6},{6,7},{7,4},{8,9},{9,10},{10,1... | collective-permute-start | bytes 49160 | tf_op jit(solution)/shard_map/ppermute | solution.py:342
  54.7 5.9 %collective-permute-start.12 = (f32[2,16,128]{2,1,0:T(8,128)S(1)}, f32[2,16,128]{2,1,0:T(8,128)S(1)}, u32[]{:S(2)}, u32[]{:S(2)}) collective-permute-start(f32[2,16,128]{2,1,0:T(8,128)S(1)} %get-tuple-element.51.refs_8_.own_stats), channel_id=1, source_target_pairs={{0,3},{1,0},{2,1},{3,2},{4,7},{5,4},{6,5},{7,6},{8,11},{9,8},{10,9... | collective-permute-start | bytes 49160 | tf_op jit(solution)/shard_map/ppermute | solution.py:342
  63.4 14.9 %collective-permute-start.20 = (bf16[2,128,1024]{2,1,0:T(8,128)(2,1)S(1)}, bf16[2,128,1024]{2,1,0:T(8,128)(2,1)S(1)}, u32[]{:S(2)}, u32[]{:S(2)}) collective-permute-start(bf16[2,128,1024]{2,1,0:T(8,128)(2,1)S(1)} %get-tuple-element.70), channel_id=1, source_target_pairs={{0,1},{1,0},{2,3},{3,2},{4,5},{5,4},{6,7},{7,6},{8,9},{9,8},{10,11... | collective-permute-start | bytes 1572872 | tf_op jit(solution)/shard_map/ppermute | solution.py:356
  63.5 14.8 %collective-permute-start.21 = (bf16[2,128,1024]{2,1,0:T(8,128)(2,1)S(1)}, bf16[2,128,1024]{2,1,0:T(8,128)(2,1)S(1)}, u32[]{:S(2)}, u32[]{:S(2)}) collective-permute-start(bf16[2,128,1024]{2,1,0:T(8,128)(2,1)S(1)} %get-tuple-element.71), channel_id=1, source_target_pairs={{0,0},{1,2},{2,1},{3,3},{4,4},{5,6},{6,5},{7,7},{8,8},{9,10},{10,9... | collective-permute-start | bytes 1572872 | tf_op jit(solution)/shard_map/ppermute | solution.py:356
  67.3 17.8 %collective-permute-start.13 = (bf16[2,128,1024]{2,1,0:T(8,128)(2,1)S(1)}, bf16[2,128,1024]{2,1,0:T(8,128)(2,1)S(1)}, u32[]{:S(2)}, u32[]{:S(2)}) collective-permute-start(bf16[2,128,1024]{2,1,0:T(8,128)(2,1)S(1)} %get-tuple-element.58), channel_id=1, source_target_pairs={{0,1},{1,0},{2,3},{3,2},{4,5},{5,4},{6,7},{7,6},{8,9},{9,8},{10,11... | collective-permute-start | bytes 1572872 | tf_op jit(solution)/shard_map/ppermute | solution.py:356
  70.8 14.3 %collective-permute-start.14 = (bf16[2,128,1024]{2,1,0:T(8,128)(2,1)S(1)}, bf16[2,128,1024]{2,1,0:T(8,128)(2,1)S(1)}, u32[]{:S(2)}, u32[]{:S(2)}) collective-permute-start(bf16[2,128,1024]{2,1,0:T(8,128)(2,1)S(1)} %get-tuple-element.59), channel_id=1, source_target_pairs={{0,0},{1,2},{2,1},{3,3},{4,4},{5,6},{6,5},{7,7},{8,8},{9,10},{10,9... | collective-permute-start | bytes 1572872 | tf_op jit(solution)/shard_map/ppermute | solution.py:356
